TPU v7x, 32 devices: a whole 2x2x4 slice. The times are simulated.
32 devices in a mesh: runs: 2 (over x), sky: 16 (over z, y, core).
Axes of the slice: x: 2, y: 2, z: 4, core: 2. Of those that a mesh axis runs over, the one named last changes fastest.
Arguments:
- start_x: float32 [2048, 128], P(('runs', 'sky')), parts along dimension 0, may hold values from 2 to 125
- start_y: float32 [2048, 128], P(('runs', 'sky')), parts along dimension 0, may hold values from 2 to 13
- gradients: bfloat16 [3, 2, 8192, 256], P(None, None, ('runs', 'sky')), parts along dimension 2, may hold values from -6 to 6
- tile_map: int32 [3, 2048, 1], P(None, ('runs', 'sky')), parts along dimension 1, may hold values from 0 to 15; in each aligned block of 64 rows (0 to 63, 64 to 127, ..., all dimensions but the last counted through in order) at most 8 rows name the same one
- row_anchor: int32 [3, 2048], P(None, ('runs', 'sky')), parts along dimension 1, may hold values from 0 to 240
- col_anchor: int32 [3, 2048], P(None, ('runs', 'sky')), parts along dimension 1, may hold values from 0 to 128
Outputs:
- final_pos: float32 [2048, 2, 128], P(('runs', 'sky')), parts along dimension 0
- jacobian: float32 [2048, 4, 128], P(('runs', 'sky')), parts along dimension 0
There are 2 independent parts, one for each index of `runs`. A program takes and returns all parts, laid end to end along the dimension named above; each array names one. Nothing has to cross between parts.
Inputs may be any that keep to these rules, and one draw needn't show every extreme that they name: `tile_map`: in each plane at most 8 of one device's 64 ray blocks name the same tile, and that many do for some tile.
All inputs are finite; a program needn't handle non-finite values.
Results may differ from a plain program's by a relative error of at most 0.0033.
Values may be sent and summed in bfloat16 or wider, within the bound.
No kernel may reach another device: no remote copies, remote signals or barrier semaphores. Data moves between devices by JAX's collectives and lax.ppermute only.
A program may use at most 64 MiB of HBM per device.

v0:
```python
import math

import jax
import jax.numpy as jnp
from jax import lax
from jax.sharding import PartitionSpec as P

WR = 16
WC = 128
PLANES = 3


lens_ratio = (0.85, 0.7, 0.9)
lens_strength = (0.5, 0.6, 0.45)


def spline(dist):
    mag = jnp.abs(dist)
    inner = 2.0 / 3.0 - mag * mag + 0.5 * mag * mag * mag
    outer_base = jnp.maximum(2.0 - mag, 0.0)
    outer = outer_base * outer_base * outer_base / 6.0
    return jnp.where(mag < 1.0, inner, outer)


def spline_slope(dist):
    mag = jnp.abs(dist)
    inner = -2.0 * mag + 1.5 * mag * mag
    outer_base = jnp.maximum(2.0 - mag, 0.0)
    outer = -0.5 * outer_base * outer_base
    return jnp.where(dist < 0.0, -1.0, 1.0) * jnp.where(mag < 1.0, inner, outer)


def interp_group(pos, win):
    count = pos.shape[0]
    rays = pos.shape[2]
    cols = jnp.arange(WC).astype(jnp.float32)
    rows = jnp.arange(WR).astype(jnp.float32)
    dx = pos[:, 0, None, :] - cols[None, :, None]
    kern = jnp.concatenate([spline(dx), spline_slope(dx)], axis=2).astype(jnp.bfloat16)
    mixed = jnp.einsum(
        "nqs,nsr->nqr", win.reshape(count, 2 * WR, WC), kern, preferred_element_type=jnp.float32
    )
    mixed = mixed.reshape(count, 2, WR, 2, rays)
    dy = pos[:, 1, None, :] - rows[None, :, None]
    row_kern = spline(dy)[:, None]
    row_slope = spline_slope(dy)[:, None]
    alpha = jnp.sum(row_kern * mixed[:, :, :, 0], axis=2)
    along_x = jnp.sum(row_kern * mixed[:, :, :, 1], axis=2)
    along_y = jnp.sum(row_slope * mixed[:, :, :, 0], axis=2)
    return jnp.concatenate(
        [alpha, along_x[:, 0:1], along_y[:, 0:1], along_x[:, 1:2], along_y[:, 1:2]], axis=1
    )


def interpolate(pos, win):
    count = pos.shape[0]
    group = math.gcd(count, 16)
    steps_count = count // group
    rays = pos.shape[2]

    def one(items):
        return interp_group(items[0], items[1])

    local = lax.map(
        one, (pos.reshape(steps_count, group, 2, rays), win.reshape(steps_count, group, 2, WR, WC))
    )
    return local.reshape(count, 6, rays)


def advance(state, local, plane):
    pos, vel, jac, djac = state
    ratio = lens_ratio[plane]
    strength = lens_strength[plane]
    alpha = local[:, 0:2]
    hxx, hxy, hyx, hyy = (local[:, 2], local[:, 3], local[:, 4], local[:, 5])
    axx, axy, ayx, ayy = (jac[:, 0], jac[:, 1], jac[:, 2], jac[:, 3])
    product = jnp.stack(
        [
            hxx * axx + hxy * ayx,
            hxx * axy + hxy * ayy,
            hyx * axx + hyy * ayx,
            hyx * axy + hyy * ayy,
        ],
        axis=1,
    )
    vel = ratio * vel - strength * alpha
    pos = pos + vel
    djac = ratio * djac - strength * product
    jac = jac + djac
    return (pos, vel, jac, djac)


def cut_windows(sheet, rows, cols):

    def cut(row, col):
        zero = jnp.zeros((), jnp.int32)
        return lax.dynamic_slice(sheet, (zero, row, col), (2, WR, WC))

    return jax.vmap(cut)(rows, cols)


def slot_index(dest, peers, cap):
    onehot = (dest[:, None] == jnp.arange(peers, dtype=jnp.int32)[None, :]).astype(jnp.int32)
    before = jnp.cumsum(onehot, axis=0) - onehot
    slot = jnp.sum(before * onehot, axis=1)
    return dest * cap + slot


def body(start_x, start_y, gradients, tile_map, row_anchor, col_anchor):
    peers = lax.axis_size("sky")
    nblk = start_x.shape[0]
    rays = start_x.shape[1]
    cap = max(2, 2 * nblk // peers)
    pos = jnp.stack([start_x, start_y], axis=1)
    vel = jnp.zeros_like(pos)
    unit = jnp.array([1.0, 0.0, 0.0, 1.0], dtype=jnp.float32)
    jac = jnp.zeros((nblk, 4, rays), jnp.float32) + unit[None, :, None]
    djac = jnp.zeros_like(jac)
    state = (pos, vel, jac, djac)
    all_dest, all_rows, all_cols = (
        lax.all_gather(tile_map[:, :, 0], "sky", axis=1, tiled=True),
        lax.all_gather(row_anchor, "sky", axis=1, tiled=True),
        lax.all_gather(col_anchor, "sky", axis=1, tiled=True),
    )
    me = lax.axis_index("sky")
    for plane in range(PLANES):
        own_index = slot_index(tile_map[plane, :, 0], peers, cap)
        hit = (all_dest[plane].reshape(peers, nblk) == me).astype(jnp.int32)
        rank = jnp.cumsum(hit, axis=1) - hit
        sources = jnp.arange(peers, dtype=jnp.int32)[:, None]
        target = jnp.where(hit == 1, sources * cap + rank, peers * cap).reshape(-1)
        slot_rows = (
            jnp.zeros((peers * cap,), jnp.int32).at[target].set(all_rows[plane], mode="drop")
        )
        slot_cols = (
            jnp.zeros((peers * cap,), jnp.int32).at[target].set(all_cols[plane], mode="drop")
        )
        windows = cut_windows(gradients[plane], slot_rows, slot_cols).reshape(peers, cap, 2, WR, WC)
        received = lax.all_to_all(windows, "sky", split_axis=0, concat_axis=0, tiled=True)
        mine = received.reshape(peers * cap, 2, WR, WC)[own_index]
        local = interpolate(state[0], mine)
        state = advance(state, local, plane)
    return (state[0], state[2])


def solution(mesh):
    return jax.shard_map(
        body,
        mesh=mesh,
        in_specs=(
            P(("runs", "sky"), None),
            P(("runs", "sky"), None),
            P(None, None, ("runs", "sky"), None),
            P(None, ("runs", "sky"), None),
            P(None, ("runs", "sky")),
            P(None, ("runs", "sky")),
        ),
        out_specs=(P(("runs", "sky"), None, None), P(("runs", "sky"), None, None)),
        check_vma=False,
    )
```

profile of v0, /device:TPU:0, one launch (start us, length us, event | category | flops | bytes accessed | tf_op | source)
XLA Modules:
  0.0 1231.5 jit_solution(9916654076014263305)
XLA Ops:
  1.4 24.6 %all-gather = s32[3,1024,1]{0,2,1:T(1,128)S(1)} all-gather(s32[3,64,1]{0,2,1:T(1,128)S(1)} %copy.32), channel_id=2, replica_groups=mesh['runs'=2,'sky'=16] {'sky'}, dimensions={1}, use_global_device_ids=true | all-gather | bytes 13056 | tf_op jit(solution)/shard_map/all_gather | solution.py:121
  26.0 65.6 %fusion.113 = (s32[1024]{0:T(1024)S(1)}, s32[1024]{0:T(1024)S(1)}, s32[1024]{0:T(1024)S(1)}) fusion(s32[3,1024,1]{0,2,1:T(1,128)S(1)} %all-gather, s32[]{:T(128)S(6)} %axis_index.12), kind=kLoop, calls=%fused_computation.193 | loop fusion | flops 6144 | bytes 24580 | tf_op jit(solution)/shard_map/convert_element_type | solution.py:128
  92.9 17.5 %all-gather.1 = s32[16,64,3]{1,2,0:T(4,128)S(1)} all-gather(s32[1,64,3]{1,2,0:T(4,128)S(1)} %bitcast.259), channel_id=1, replica_groups=mesh['runs'=2,'sky'=16] {'sky'}, dimensions={0}, use_global_device_ids=true | all-gather | bytes 13056 | tf_op jit(solution)/shard_map/all_gather | solution.py:122
  110.5 18.8 %all-gather.2 = s32[16,64,3]{1,2,0:T(4,128)S(1)} all-gather(s32[1,64,3]{1,2,0:T(4,128)S(1)} %bitcast.260), channel_id=1, replica_groups=mesh['runs'=2,'sky'=16] {'sky'}, dimensions={0}, use_global_device_ids=true | all-gather | bytes 13056 | tf_op jit(solution)/shard_map/all_gather | solution.py:123
  129.5 4.3 scatter_custom_fusion
  133.8 4.3 scatter_custom_fusion.1
  138.1 4.3 scatter_custom_fusion.2
  142.4 4.3 scatter_custom_fusion.3
  146.7 4.3 scatter_custom_fusion.5
  151.0 4.3 scatter_custom_fusion.4
  156.7 333.8 %while.36 = (s32[]{:T(128)}, bf16[2,256,256]{2,1,0:T(8,128)(2,1)S(1)}, s32[128,3]{0,1:T(4,128)S(1)}, bf16[128,2,16,128]{3,2,1,0:T(8,128)(2,1)}, s32[]{:T(128)}) while((s32[]{:T(128)}, bf16[2,256,256]{2,1,0:T(8,128)(2,1)S(1)}, s32[128,3]{0,1:T(4,128)S(1)}, bf16[128,2,16,128]{3,2,1,0:T(8,128)(2,1)}, s32[]{:T(128)}) %tuple.193), condition=%wide.while_cond, body=%wide.while_body.sunk | while | flops 2 | bytes 18025 | solution.py:97
  490.5 3.7 all-to-all-start
  495.3 333.7 %while.37 = (s32[]{:T(128)}, bf16[2,256,256]{2,1,0:T(8,128)(2,1)S(1)}, s32[128,3]{0,1:T(4,128)S(1)}, bf16[128,2,16,128]{3,2,1,0:T(8,128)(2,1)}, s32[]{:T(128)}) while((s32[]{:T(128)}, bf16[2,256,256]{2,1,0:T(8,128)(2,1)S(1)}, s32[128,3]{0,1:T(4,128)S(1)}, bf16[128,2,16,128]{3,2,1,0:T(8,128)(2,1)}, s32[]{:T(128)}) %tuple.199), condition=%wide.while_cond.1, body=%wide.while_body.1.sunk | while | flops 2 | bytes 18025 | solution.py:97
  830.1 327.5 %while.38 = (s32[]{:T(128)}, bf16[2,256,256]{2,1,0:T(8,128)(2,1)S(1)}, s32[128,3]{0,1:T(4,128)S(1)}, bf16[128,2,16,128]{3,2,1,0:T(8,128)(2,1)}, s32[]{:T(128)}) while((s32[]{:T(128)}, bf16[2,256,256]{2,1,0:T(8,128)(2,1)S(1)}, s32[128,3]{0,1:T(4,128)S(1)}, bf16[128,2,16,128]{3,2,1,0:T(8,128)(2,1)}, s32[]{:T(128)}) %tuple.205), condition=%wide.while_cond.2, body=%wide.while_body.2.sunk | while | flops 2 | bytes 18025 | solution.py:97
  1050.8 2.0 bitcast_dynamic-update-slice_fusion.17
  1145.4 2.0 bitcast_dynamic-update-slice_fusion.17
  1148.0 2.0 bitcast_dynamic-update-slice_fusion.17
  1158.6 6.0 all-to-all-start.1
  1165.3 10.7 while.33
  1176.0 11.5 all-to-all-done.1
  1187.5 7.0 all-to-all-start.2
  1195.3 10.7 while.34
  1206.8 10.6 all-to-all-done.2
  1218.1 10.7 while.35
  (1398 shorter events, 1031.4 us)
Async XLA Ops:
  1.4 91.5 %copy-start.5 = (s32[3,64]{1,0:T(4,128)S(1)}, s32[3,64]{1,0:T(4,128)}, u32[]{:S(2)}) copy-start(s32[3,64]{1,0:T(4,128)} %param.17) | copy-start | bytes 2308
  26.0 84.5 %copy-start.6 = (s32[3,64]{1,0:T(4,128)S(1)}, s32[3,64]{1,0:T(4,128)}, u32[]{:S(2)}) copy-start(s32[3,64]{1,0:T(4,128)} %param.18) | copy-start | bytes 2308
  26.0 129.3 %copy-start = (bf16[3,2,256,256]{3,2,1,0:T(8,128)(2,1)S(1)}, bf16[3,2,256,256]{3,2,1,0:T(8,128)(2,1)}, u32[]{:S(2)}) copy-start(bf16[3,2,256,256]{3,2,1,0:T(8,128)(2,1)} %param.15) | copy-start | bytes 2359300
  490.5 668.1 %all-to-all-start = ((bf16[16,8,2,16,128]{4,3,2,1,0:T(8,128)(2,1)}), bf16[16,8,2,16,128]{4,3,2,1,0:T(8,128)(2,1)S(1)}, u32[]{:S(2)}, u32[]{:S(2)}) async-start(bf16[16,8,2,16,128]{4,3,2,1,0:T(8,128)(2,1)} %bitcast.37), calls=%async_computation | async-start | bytes 2097152 | tf_op jit(solution)/shard_map/all_to_all | solution.py:139
  495.3 662.4 %copy-start.3 = (s32[3,64,1]{1,2,0:T(1,128)S(1)}, s32[3,64,1]{1,2,0:T(1,128)}, u32[]{:S(2)}) copy-start(s32[3,64,1]{1,2,0:T(1,128)} %param.16) | copy-start | bytes 2308
  495.3 663.3 %copy-start.1 = (f32[64,128]{1,0:T(8,128)S(1)}, f32[64,128]{1,0:T(8,128)}, u32[]{:S(2)}) copy-start(f32[64,128]{1,0:T(8,128)} %param.14) | copy-start | bytes 98308
  495.3 663.3 %copy-start.2 = (f32[64,128]{1,0:T(8,128)S(1)}, f32[64,128]{1,0:T(8,128)}, u32[]{:S(2)}) copy-start(f32[64,128]{1,0:T(8,128)} %param.13) | copy-start | bytes 98308
  1158.6 28.9 %all-to-all-start.1 = ((bf16[16,8,2,16,128]{4,3,2,1,0:T(8,128)(2,1)}), bf16[16,8,2,16,128]{4,3,2,1,0:T(8,128)(2,1)S(1)}, u32[]{:S(2)}, u32[]{:S(2)}) async-start(bf16[16,8,2,16,128]{4,3,2,1,0:T(8,128)(2,1)} %bitcast.52), calls=%async_computation.1 | async-start | bytes 2097152 | tf_op jit(solution)/shard_map/all_to_all | solution.py:139
  1187.5 29.9 %all-to-all-start.2 = ((bf16[16,8,2,16,128]{4,3,2,1,0:T(8,128)(2,1)}), bf16[16,8,2,16,128]{4,3,2,1,0:T(8,128)(2,1)S(1)}, u32[]{:S(2)}, u32[]{:S(2)}) async-start(bf16[16,8,2,16,128]{4,3,2,1,0:T(8,128)(2,1)} %bitcast.67), calls=%async_computation.2 | async-start | bytes 2097152 | tf_op jit(solution)/shard_map/all_to_all | solution.py:139
  1195.3 10.9 copy-start.4
where the time goes:
time: 1240 us; the launch traced here: 1230 us
  local copies, waits for them, and re-layouts  1040 us (84%)
  other arithmetic  86.4 us (7%)
  blocking collectives  61 us (5%)
  waiting for transfers between devices  22.1 us (2%)
  starting transfers between devices  16.6 us (1%)
    gather x1152, local copies, waits for them, and re-layouts  994 us
    convert_element_type x1, other arithmetic, body(): hit = (all_dest[plane].reshape(peers, nblk) == me).astype(jnp.int32)  65.6 us
    scatter x6, local copies, waits for them, and re-layouts, body(): jnp.zeros((peers * cap,), jnp.int32).at[target]  25.8 us
  transfers between devices with their start and end apart: 3, of which 2 were waited for; matrix products, arithmetic and copies ran while one was open for 56% of the time, Pallas kernels for 0%

commit v1 on v0

v1 whole, which is shorter than its diff:
```python
import functools
import math

import jax
import jax.numpy as jnp
from jax import lax
from jax.experimental import pallas as pl
from jax.experimental.pallas import tpu as pltpu
from jax.sharding import PartitionSpec as P

WR = 16
WC = 128
PLANES = 3

lens_ratio = (0.85, 0.7, 0.9)
lens_strength = (0.5, 0.6, 0.45)

VMEM = pltpu.VMEM
SMEM = pltpu.SMEM


def whole(space=VMEM):
    return pl.BlockSpec(memory_space=space)


def dot_last(a, b):
    return lax.dot_general(
        a, b, (((1,), (1,)), ((), ())), preferred_element_type=jnp.float32
    )


def prep_kernel(peers, cap, tile_ref, row_ref, col_ref, req_ref, slot_ref):
    nblk = tile_ref.shape[1]
    lanes = req_ref.shape[1]
    owner = lax.broadcasted_iota(jnp.int32, (peers, nblk), 0)
    earlier = (
        lax.broadcasted_iota(jnp.int32, (nblk, nblk), 1)
        < lax.broadcasted_iota(jnp.int32, (nblk, nblk), 0)
    ).astype(jnp.float32).astype(jnp.bfloat16)
    lane = lax.broadcasted_iota(jnp.int32, (lanes, nblk), 0)
    rows = jnp.zeros((peers, lanes), jnp.float32)
    cols = jnp.zeros((peers, lanes), jnp.float32)
    for k in range(PLANES):
        tile = tile_ref[k : k + 1, :]
        hit = (owner == tile).astype(jnp.float32)
        hit16 = hit.astype(jnp.bfloat16)
        before = dot_last(hit16, earlier)
        rank = jnp.sum(before * hit, axis=0, keepdims=True).astype(jnp.int32)
        slot_ref[k : k + 1, :] = tile * cap + rank
        here = lane == (rank + k * cap)
        zero = jnp.zeros((), jnp.float32)
        row = jnp.where(here, row_ref[k : k + 1, :].astype(jnp.float32), zero)
        col = jnp.where(here, col_ref[k : k + 1, :].astype(jnp.float32), zero)
        rows += dot_last(hit16, row.astype(jnp.bfloat16))
        cols += dot_last(hit16, col.astype(jnp.bfloat16))
    req_ref[...] = rows.astype(jnp.int32) * 65536 + cols.astype(jnp.int32)


def prep(tile_map, row_anchor, col_anchor, peers, cap):
    nblk = tile_map.shape[1]
    lanes = -(-PLANES * cap // 128) * 128
    return pl.pallas_call(
        functools.partial(prep_kernel, peers, cap),
        out_shape=(
            jax.ShapeDtypeStruct((peers, lanes), jnp.int32),
            jax.ShapeDtypeStruct((PLANES, nblk), jnp.int32),
        ),
        in_specs=[whole()] * 3,
        out_specs=(whole(), whole()),
        name="prep",
    )(tile_map, row_anchor, col_anchor)


def cut_kernel(plane, cap, req_ref, sheet_ref, out_ref, half_ref):
    halves = sheet_ref.shape[3] // WC
    for c in range(2):
        for h in range(halves):
            half_ref[c * halves + h] = sheet_ref[plane, c, :, h * WC : (h + 1) * WC].astype(jnp.float32)
    lane = lax.broadcasted_iota(jnp.int32, (WR, WC), 1)

    def one(slot, carry):
        packed = req_ref[slot // cap, plane * cap + slot % cap]
        row = packed >> 16
        col = packed & 65535
        turn = (WC - col) & (WC - 1)
        left = lane < WC - col
        for c in range(2):
            part = [
                pltpu.roll(half_ref[c * halves + h, pl.ds(row, WR), :], turn, 1)
                for h in range(halves)
            ]
            out_ref[slot, c * WR : (c + 1) * WR, :] = jnp.where(left, part[0], part[1]).astype(jnp.bfloat16)
        return carry

    lax.fori_loop(0, out_ref.shape[0], one, 0, unroll=8)


def cut(plane, cap, requests, sheet):
    count = requests.shape[0] * cap
    return pl.pallas_call(
        functools.partial(cut_kernel, plane, cap),
        out_shape=jax.ShapeDtypeStruct((count, 2 * WR, WC), jnp.bfloat16),
        in_specs=[whole(SMEM), whole()],
        out_specs=whole(),
        scratch_shapes=[VMEM((2 * sheet.shape[3] // WC, sheet.shape[2], WC), jnp.float32)],
        name=f"cut{plane}",
    )(requests, sheet)


def taps(pos):
    cell = jnp.floor(pos)
    f = pos - cell
    g = 1.0 - f
    f2, g2 = f * f, g * g
    value = (
        g2 * g / 6.0,
        2.0 / 3.0 - f2 + 0.5 * f2 * f,
        2.0 / 3.0 - g2 + 0.5 * g2 * g,
        f2 * f / 6.0,
    )
    slope = (-0.5 * g2, -2.0 * f + 1.5 * f2, 2.0 * g - 1.5 * g2, 0.5 * f2)
    return cell, value, slope


def interp_kernel(plane, slot_ref, win_ref, *refs):
    first, last = plane == 0, plane == PLANES - 1
    if first:
        x_ref, y_ref = refs[:2]
        refs = refs[2:]
    else:
        state_ref = refs[0]
        refs = refs[1:]
    if last:
        pos_out, jac_out = refs[:2]
        refs = refs[2:]
    else:
        state_out = refs[0]
        refs = refs[1:]
    tap_ref, res_ref = refs
    nblk, rays = res_ref.shape[1:]

    if first:
        px, py = x_ref[...], y_ref[...]
    else:
        px, py = state_ref[0], state_ref[1]
    for at, pos in ((0, px), (9, py)):
        cell, value, slope = taps(pos)
        tap_ref[at] = cell
        for j in range(4):
            tap_ref[at + 1 + j] = value[j]
            tap_ref[at + 5 + j] = slope[j]

    def one(b, carry):
        def row(j):
            return tap_ref[j, pl.ds(b, 1), :]

        def spread(at, size):
            near = lax.broadcasted_iota(jnp.int32, (size, rays), 0).astype(jnp.float32) - row(at)
            zero = jnp.zeros((size, rays), jnp.float32)
            value, slope = zero, zero
            for j in range(4):
                here = near == (j - 1.0)
                value = jnp.where(here, row(at + 1 + j), value)
                slope = jnp.where(here, row(at + 5 + j), slope)
            return value, slope

        kx, kxd = spread(0, WC)
        kern = jnp.concatenate([kx.astype(jnp.bfloat16), kxd.astype(jnp.bfloat16)], axis=1)
        mixed = jnp.dot(win_ref[slot_ref[plane, b]], kern, preferred_element_type=jnp.float32)
        ky, kyd = spread(9, WR)
        for c in range(2):
            part = mixed[c * WR : (c + 1) * WR]
            mixed0, mixed1 = part[:, :rays], part[:, rays:]
            for at, product in ((0, ky * mixed0), (2, ky * mixed1), (4, kyd * mixed0)):
                res_ref[at + c, pl.ds(b, 1), :] = jnp.sum(product, axis=0, keepdims=True)
        return carry

    lax.fori_loop(0, nblk, one, 0, unroll=4)

    ratio, strength = lens_ratio[plane], lens_strength[plane]
    ax, ay = res_ref[0], res_ref[1]
    hxx, hyx, hxy, hyy = res_ref[2], res_ref[3], res_ref[4], res_ref[5]
    if first:
        vx, vy = -strength * ax, -strength * ay
        dj = [-strength * h for h in (hxx, hxy, hyx, hyy)]
        jac = [1.0 + dj[0], dj[1], dj[2], 1.0 + dj[3]]
    else:
        vx = ratio * state_ref[2] - strength * ax
        vy = ratio * state_ref[3] - strength * ay
        axx, axy, ayx, ayy = [state_ref[4 + j] for j in range(4)]
        product = (
            hxx * axx + hxy * ayx,
            hxx * axy + hxy * ayy,
            hyx * axx + hyy * ayx,
            hyx * axy + hyy * ayy,
        )
        dj = [ratio * state_ref[8 + j] - strength * product[j] for j in range(4)]
        jac = [old + d for old, d in zip((axx, axy, ayx, ayy), dj)]
    px, py = px + vx, py + vy
    if last:
        pos_out[:, 0, :] = px
        pos_out[:, 1, :] = py
        for j in range(4):
            jac_out[:, j, :] = jac[j]
    else:
        for j, value in enumerate([px, py, vx, vy] + jac + dj):
            state_out[j] = value


def interp(plane, slots, windows, state):
    nblk = slots.shape[1]
    rays = state[0].shape[-1]
    if plane == PLANES - 1:
        out_shape = (
            jax.ShapeDtypeStruct((nblk, 2, rays), jnp.float32),
            jax.ShapeDtypeStruct((nblk, 4, rays), jnp.float32),
        )
    else:
        out_shape = (jax.ShapeDtypeStruct((12, nblk, rays), jnp.float32),)
    return pl.pallas_call(
        functools.partial(interp_kernel, plane),
        out_shape=out_shape,
        in_specs=[whole(SMEM), whole()] + [whole()] * len(state),
        out_specs=(whole(),) * len(out_shape),
        scratch_shapes=[
            VMEM((18, nblk, rays), jnp.float32),
            VMEM((6, nblk, rays), jnp.float32),
        ],
        name=f"interp{plane}",
    )(slots, windows, *state)


def body(start_x, start_y, gradients, tile_map, row_anchor, col_anchor):
    peers = lax.axis_size("sky")
    nblk = start_x.shape[0]
    cap = max(2, 2 * nblk // peers)
    requests, slots = prep(tile_map[:, :, 0], row_anchor, col_anchor, peers, cap)
    asked = lax.all_to_all(requests, "sky", split_axis=0, concat_axis=0, tiled=True)
    received = []
    for plane in range(PLANES):
        windows = cut(plane, cap, asked, gradients)
        got = lax.all_to_all(
            windows.reshape(peers, cap, 2 * WR, WC), "sky", split_axis=0, concat_axis=0, tiled=True
        )
        received.append(got.reshape(peers * cap, 2 * WR, WC))
    state = (start_x, start_y)
    for plane in range(PLANES):
        state = interp(plane, slots, received[plane], state)
    return state


def solution(mesh):
    return jax.shard_map(
        body,
        mesh=mesh,
        in_specs=(
            P(("runs", "sky"), None),
            P(("runs", "sky"), None),
            P(None, None, ("runs", "sky"), None),
            P(None, ("runs", "sky"), None),
            P(None, ("runs", "sky")),
            P(None, ("runs", "sky")),
        ),
        out_specs=(P(("runs", "sky"), None, None), P(("runs", "sky"), None, None)),
        check_vma=False,
    )
```

time: 1240 us -> 119 us (0.10)
  local copies, waits for them, and re-layouts: 1040 us -> 4.22 us
  other arithmetic: 86.4 us -> 0 us
  blocking collectives: 61 us -> 13.9 us
  Pallas kernels: 0 us -> 34.4 us
  waiting for transfers between devices: 22.1 us -> 46.9 us
    gather x1155 -> x0, local copies, waits for them, and re-layouts: 996 us -> none
    convert_element_type x28 -> x0, other arithmetic: 65.9 us -> none  [the longest x1 65.6 us: body(): hit = (all_dest[plane].reshape(peers, nblk) == me).astype(jnp.int32)]
    all_gather x3 -> x0, blocking collectives: 61 us -> none  [the longest x1 24.6 us: body(): lax.all_gather(tile_map[:, :, 0], 'sky', axis=1, tiled=True)]
    pallas_call x0 -> x7, Pallas kernels: none -> 34.4 us  [the longest x3 19.5 us: interp(): pl.pallas_call(functools.partial(interp_kernel, plane), out_shape=out_sha...]
    scatter x6 -> x0, local copies, waits for them, and re-layouts: 25.8 us -> none  [body(): jnp.zeros((peers * cap,), jnp.int32).at[target]]
    all_to_all x3, waiting for transfers between devices: 22.1 us -> 46.9 us  [body(): lax.all_to_all(windows.reshape(peers, cap, 2 * WR, WC), 'sky', split_axis...]
    all_to_all x0 -> x1, blocking collectives: none -> 13.9 us  [body(): lax.all_to_all(requests, 'sky', split_axis=0, concat_axis=0, tiled=True)]
  transfers between devices with their start and end apart: 3 -> 3, of which waited for: 2 -> 3; matrix products, arithmetic and copies ran while one was open for 56% -> 0% of each run, Pallas kernels for 0% -> 19%
where the time goes in v1:
time: 119 us; the launch traced here: 117 us
  waiting for transfers between devices  46.9 us (39%)
  Pallas kernels  34.4 us (29%)
  starting transfers between devices  17.2 us (14%)
  blocking collectives  13.9 us (12%)
  local copies, waits for them, and re-layouts  4.22 us (4%)
    all_to_all x3, waiting for transfers between devices, body(): lax.all_to_all(windows.reshape(peers, cap, 2 * WR, WC), 'sky', split_axis...  46.9 us
    pallas_call x3, Pallas kernels, interp(): pl.pallas_call(functools.partial(interp_kernel, plane), out_shape=out_sha...  19.5 us
    all_to_all x3, starting transfers between devices, body(): lax.all_to_all(windows.reshape(peers, cap, 2 * WR, WC), 'sky', split_axis...  17.2 us
    all_to_all x1, blocking collectives, body(): lax.all_to_all(requests, 'sky', split_axis=0, concat_axis=0, tiled=True)  13.9 us
    pallas_call x3, Pallas kernels, cut(): pl.pallas_call(functools.partial(cut_kernel, plane, cap), out_shape=jax.S...  13.1 us
    unnamed x7, local copies, waits for them, and re-layouts  4.22 us
  transfers between devices with their start and end apart: 3, of which 3 were waited for; matrix products, arithmetic and copies ran while one was open for 0% of the time, Pallas kernels for 19%

profile of v1, /device:TPU:0, one launch (start us, length us, event | category | flops | bytes accessed | tf_op | source)
XLA Modules:
  0.0 117.2 jit_solution(626164323579218789)
XLA Ops:
  0.6 1.3 %copy.11 = s32[3,64,1]{1,0,2:T(4,128)} copy(s32[3,64,1]{1,2,0:T(1,128)} %param.9) | data formatting | bytes 1536
  1.9 1.8 %prep.1 = (s32[16,128]{1,0:T(8,128)}, s32[3,64]{1,0:T(4,128)}) custom-call(s32[3,64]{1,0:T(4,128)} %bitcast.22, s32[3,64]{1,0:T(4,128)} %row_ref.1, s32[3,64]{1,0:T(4,128)} %col_ref.1), custom_call_target="tpu_custom_call" | custom-call | tf_op jit(solution)/shard_map/prep/pallas_call | solution.py:62
  3.7 13.9 %all_to_all.26 = s32[16,1,128]{2,1,0:T(1,128)} all-to-all(s32[16,1,128]{2,1,0:T(1,128)} %bitcast.23), channel_id=1, replica_groups=mesh['runs'=2,'sky'=16] {'sky'}, dimensions={0} | all-to-all | bytes 16384 | tf_op jit(solution)/shard_map/all_to_all | solution.py:238
  17.6 4.3 %cut0.1 = bf16[128,32,128]{2,1,0:T(8,128)(2,1)} custom-call(s32[16,128]{1,0:T(8,128)} %bitcast.19, bf16[3,2,256,256]{3,2,1,0:T(8,128)(2,1)} %sheet_ref.5), custom_call_target="tpu_custom_call" | custom-call | tf_op jit(solution)/shard_map/cut0/pallas_call | solution.py:100
  21.9 3.7 %all-to-all-start.3 = ((bf16[16,8,32,128]{3,2,1,0:T(8,128)(2,1)}), bf16[16,8,32,128]{3,2,1,0:T(8,128)(2,1)S(1)}, u32[]{:S(2)}, u32[]{:S(2)}) async-start(bf16[16,8,32,128]{3,2,1,0:T(8,128)(2,1)} %bitcast.15), calls=%async_computation.3 | async-start | bytes 2097152 | tf_op jit(solution)/shard_map/all_to_all | solution.py:242
  25.6 4.4 %cut1.1 = bf16[128,32,128]{2,1,0:T(8,128)(2,1)} custom-call(s32[16,128]{1,0:T(8,128)} %bitcast.20, bf16[3,2,256,256]{3,2,1,0:T(8,128)(2,1)} %sheet_ref.5), custom_call_target="tpu_custom_call" | custom-call | tf_op jit(solution)/shard_map/cut1/pallas_call | solution.py:100
  30.0 18.5 %all-to-all-done.3 = bf16[16,8,32,128]{3,2,1,0:T(8,128)(2,1)S(1)} async-done(((bf16[16,8,32,128]{3,2,1,0:T(8,128)(2,1)}), bf16[16,8,32,128]{3,2,1,0:T(8,128)(2,1)S(1)}, u32[]{:S(2)}, u32[]{:S(2)}) %all-to-all-start.3) | async-done | bytes 1048608 | tf_op jit(solution)/shard_map/all_to_all | solution.py:242
  48.4 0.0 copy-start
  48.4 1.0 copy-done
  49.5 6.7 %all-to-all-start.2 = ((bf16[16,8,32,128]{3,2,1,0:T(8,128)(2,1)}), bf16[16,8,32,128]{3,2,1,0:T(8,128)(2,1)S(1)}, u32[]{:S(2)}, u32[]{:S(2)}) async-start(bf16[16,8,32,128]{3,2,1,0:T(8,128)(2,1)} %bitcast.14), calls=%async_computation.2 | async-start | bytes 2097152 | tf_op jit(solution)/shard_map/all_to_all | solution.py:242
  56.2 4.4 %cut2.1 = bf16[128,32,128]{2,1,0:T(8,128)(2,1)} custom-call(s32[16,128]{1,0:T(8,128)} %bitcast.21, bf16[3,2,256,256]{3,2,1,0:T(8,128)(2,1)} %sheet_ref.5), custom_call_target="tpu_custom_call" | custom-call | tf_op jit(solution)/shard_map/cut2/pallas_call | solution.py:100
  60.6 18.5 %all-to-all-done.2 = bf16[16,8,32,128]{3,2,1,0:T(8,128)(2,1)S(1)} async-done(((bf16[16,8,32,128]{3,2,1,0:T(8,128)(2,1)}), bf16[16,8,32,128]{3,2,1,0:T(8,128)(2,1)S(1)}, u32[]{:S(2)}, u32[]{:S(2)}) %all-to-all-start.2) | async-done | bytes 1048608 | tf_op jit(solution)/shard_map/all_to_all | solution.py:242
  79.1 0.0 copy-start.1
  79.1 1.0 copy-done.1
  80.1 6.8 %all-to-all-start.1 = ((bf16[16,8,32,128]{3,2,1,0:T(8,128)(2,1)}), bf16[16,8,32,128]{3,2,1,0:T(8,128)(2,1)S(1)}, u32[]{:S(2)}, u32[]{:S(2)}) async-start(bf16[16,8,32,128]{3,2,1,0:T(8,128)(2,1)} %bitcast.13), calls=%async_computation.1 | async-start | bytes 2097152 | tf_op jit(solution)/shard_map/all_to_all | solution.py:242
  86.9 6.4 %interp0.1.refs_0_ = f32[12,64,128]{2,1,0:T(8,128)} custom-call(s32[3,64]{1,0:T(4,128)} %get-tuple-element.4.slot_ref, bf16[128,32,128]{2,1,0:T(8,128)(2,1)} %bitcast.16, f32[64,128]{1,0:T(8,128)} %refs_0_.1, f32[64,128]{1,0:T(8,128)} %refs_1_.1), custom_call_target="tpu_custom_call" | custom-call | tf_op jit(solution)/shard_map/interp0/pallas_call | solution.py:220
  93.3 6.5 %interp1.1.refs_0_ = f32[12,64,128]{2,1,0:T(8,128)} custom-call(s32[3,64]{1,0:T(4,128)} %get-tuple-element.4.slot_ref, bf16[128,32,128]{2,1,0:T(8,128)(2,1)} %bitcast.17, f32[12,64,128]{2,1,0:T(8,128)} %interp0.1.refs_0_), custom_call_target="tpu_custom_call" | custom-call | tf_op jit(solution)/shard_map/interp1/pallas_call | solution.py:220
  99.8 9.9 %all-to-all-done.1 = bf16[16,8,32,128]{3,2,1,0:T(8,128)(2,1)S(1)} async-done(((bf16[16,8,32,128]{3,2,1,0:T(8,128)(2,1)}), bf16[16,8,32,128]{3,2,1,0:T(8,128)(2,1)S(1)}, u32[]{:S(2)}, u32[]{:S(2)}) %all-to-all-start.1) | async-done | bytes 1048608 | tf_op jit(solution)/shard_map/all_to_all | solution.py:242
  109.7 0.0 copy-start.2
  109.7 1.0 copy-done.2
  110.7 6.5 %interp2.1 = (f32[64,2,128]{2,1,0:T(2,128)}, f32[64,4,128]{2,1,0:T(4,128)}) custom-call(s32[3,64]{1,0:T(4,128)} %get-tuple-element.4.slot_ref, bf16[128,32,128]{2,1,0:T(8,128)(2,1)} %bitcast.18, f32[12,64,128]{2,1,0:T(8,128)} %interp1.1.refs_0_), custom_call_target="tpu_custom_call" | custom-call | tf_op jit(solution)/shard_map/interp2/pallas_call | solution.py:220
Async XLA Ops:
  21.9 26.5 %all-to-all-start.3 = ((bf16[16,8,32,128]{3,2,1,0:T(8,128)(2,1)}), bf16[16,8,32,128]{3,2,1,0:T(8,128)(2,1)S(1)}, u32[]{:S(2)}, u32[]{:S(2)}) async-start(bf16[16,8,32,128]{3,2,1,0:T(8,128)(2,1)} %bitcast.15), calls=%async_computation.3 | async-start | bytes 2097152 | tf_op jit(solution)/shard_map/all_to_all | solution.py:242
  48.4 1.0 copy-start
  49.5 29.6 %all-to-all-start.2 = ((bf16[16,8,32,128]{3,2,1,0:T(8,128)(2,1)}), bf16[16,8,32,128]{3,2,1,0:T(8,128)(2,1)S(1)}, u32[]{:S(2)}, u32[]{:S(2)}) async-start(bf16[16,8,32,128]{3,2,1,0:T(8,128)(2,1)} %bitcast.14), calls=%async_computation.2 | async-start | bytes 2097152 | tf_op jit(solution)/shard_map/all_to_all | solution.py:242
  79.1 1.0 copy-start.1
  80.1 29.7 %all-to-all-start.1 = ((bf16[16,8,32,128]{3,2,1,0:T(8,128)(2,1)}), bf16[16,8,32,128]{3,2,1,0:T(8,128)(2,1)S(1)}, u32[]{:S(2)}, u32[]{:S(2)}) async-start(bf16[16,8,32,128]{3,2,1,0:T(8,128)(2,1)} %bitcast.13), calls=%async_computation.1 | async-start | bytes 2097152 | tf_op jit(solution)/shard_map/all_to_all | solution.py:242
  109.7 1.0 copy-start.2

commit v2 on v1

--- a/solution.py
+++ b/solution.py
@@ -29,7 +29,8 @@
     )
 
 
-def prep_kernel(peers, cap, tile_ref, row_ref, col_ref, req_ref, slot_ref):
+def prep_kernel(peers, halves, cap, tile_ref, row_ref, col_ref, req_ref, slot_ref):
+    relays = peers // halves
     nblk = tile_ref.shape[1]
     lanes = req_ref.shape[1]
     owner = lax.broadcasted_iota(jnp.int32, (peers, nblk), 0)
@@ -38,31 +39,34 @@
         < lax.broadcasted_iota(jnp.int32, (nblk, nblk), 0)
     ).astype(jnp.float32).astype(jnp.bfloat16)
     lane = lax.broadcasted_iota(jnp.int32, (lanes, nblk), 0)
-    rows = jnp.zeros((peers, lanes), jnp.float32)
-    cols = jnp.zeros((peers, lanes), jnp.float32)
+    rows = jnp.zeros((relays, lanes), jnp.float32)
+    cols = jnp.zeros((relays, lanes), jnp.float32)
     for k in range(PLANES):
         tile = tile_ref[k : k + 1, :]
         hit = (owner == tile).astype(jnp.float32)
         hit16 = hit.astype(jnp.bfloat16)
         before = dot_last(hit16, earlier)
         rank = jnp.sum(before * hit, axis=0, keepdims=True).astype(jnp.int32)
-        slot_ref[k : k + 1, :] = tile * cap + rank
-        here = lane == (rank + k * cap)
+        side = tile // relays
+        rank = rank + side * cap
+        slot_ref[k : k + 1, :] = (tile - side * relays) * (halves * cap) + rank
+        here = lane == (rank + k * halves * cap)
         zero = jnp.zeros((), jnp.float32)
         row = jnp.where(here, row_ref[k : k + 1, :].astype(jnp.float32), zero)
         col = jnp.where(here, col_ref[k : k + 1, :].astype(jnp.float32), zero)
-        rows += dot_last(hit16, row.astype(jnp.bfloat16))
-        cols += dot_last(hit16, col.astype(jnp.bfloat16))
+        fold = sum(hit[h * relays : (h + 1) * relays] for h in range(halves)).astype(jnp.bfloat16)
+        rows += dot_last(fold, row.astype(jnp.bfloat16))
+        cols += dot_last(fold, col.astype(jnp.bfloat16))
     req_ref[...] = rows.astype(jnp.int32) * 65536 + cols.astype(jnp.int32)
 
 
-def prep(tile_map, row_anchor, col_anchor, peers, cap):
+def prep(tile_map, row_anchor, col_anchor, peers, halves, cap):
     nblk = tile_map.shape[1]
-    lanes = -(-PLANES * cap // 128) * 128
+    lanes = -(-PLANES * halves * cap // 128) * 128
     return pl.pallas_call(
-        functools.partial(prep_kernel, peers, cap),
+        functools.partial(prep_kernel, peers, halves, cap),
         out_shape=(
-            jax.ShapeDtypeStruct((peers, lanes), jnp.int32),
+            jax.ShapeDtypeStruct((peers // halves, lanes), jnp.int32),
             jax.ShapeDtypeStruct((PLANES, nblk), jnp.int32),
         ),
         in_specs=[whole()] * 3,
@@ -71,40 +75,48 @@
     )(tile_map, row_anchor, col_anchor)
 
 
-def cut_kernel(plane, cap, req_ref, sheet_ref, out_ref, half_ref):
-    halves = sheet_ref.shape[3] // WC
+def cut_kernel(plane, cap, side_ref, req_ref, own_ref, mirror_ref, out_ref, half_ref):
+    parts = own_ref.shape[3] // WC
     for c in range(2):
-        for h in range(halves):
-            half_ref[c * halves + h] = sheet_ref[plane, c, :, h * WC : (h + 1) * WC].astype(jnp.float32)
+        for h in range(parts):
+            lanes = slice(h * WC, (h + 1) * WC)
+            half_ref[c * parts + h] = own_ref[plane, c, :, lanes].astype(jnp.float32)
+            half_ref[(2 + c) * parts + h] = mirror_ref[c, :, lanes].astype(jnp.float32)
     lane = lax.broadcasted_iota(jnp.int32, (WR, WC), 1)
-
-    def one(slot, carry):
-        packed = req_ref[slot // cap, plane * cap + slot % cap]
-        row = packed >> 16
-        col = packed & 65535
-        turn = (WC - col) & (WC - 1)
-        left = lane < WC - col
-        for c in range(2):
-            part = [
-                pltpu.roll(half_ref[c * halves + h, pl.ds(row, WR), :], turn, 1)
-                for h in range(halves)
-            ]
-            out_ref[slot, c * WR : (c + 1) * WR, :] = jnp.where(left, part[0], part[1]).astype(jnp.bfloat16)
+    side = side_ref[0]
+    each = 2 * cap
+
+    def one(source, carry):
+        for place in range(each):
+            packed = req_ref[source, plane * each + place]
+            base = jnp.where(side == place // cap, 0, 2 * parts)
+            row = packed >> 16
+            col = packed & 65535
+            turn = (WC - col) & (WC - 1)
+            left = lane < WC - col
+            for c in range(2):
+                part = [
+                    pltpu.roll(half_ref[base + c * parts + h, pl.ds(row, WR), :], turn, 1)
+                    for h in range(parts)
+                ]
+                out_ref[source * each + place, c * WR : (c + 1) * WR, :] = jnp.where(
+                    left, part[0], part[1]
+                ).astype(jnp.bfloat16)
         return carry
 
-    lax.fori_loop(0, out_ref.shape[0], one, 0, unroll=8)
-
-
-def cut(plane, cap, requests, sheet):
-    count = requests.shape[0] * cap
+    lax.fori_loop(0, req_ref.shape[0], one, 0)
+
+
+def cut(plane, cap, side, requests, sheet, mirror):
+    count = requests.shape[0] * 2 * cap
     return pl.pallas_call(
         functools.partial(cut_kernel, plane, cap),
         out_shape=jax.ShapeDtypeStruct((count, 2 * WR, WC), jnp.bfloat16),
-        in_specs=[whole(SMEM), whole()],
+        in_specs=[whole(SMEM), whole(SMEM), whole(), whole()],
         out_specs=whole(),
-        scratch_shapes=[VMEM((2 * sheet.shape[3] // WC, sheet.shape[2], WC), jnp.float32)],
+        scratch_shapes=[VMEM((4 * sheet.shape[3] // WC, sheet.shape[2], WC), jnp.float32)],
         name=f"cut{plane}",
-    )(requests, sheet)
+    )(side, requests, sheet, mirror)
 
 
 def taps(pos):
@@ -234,14 +246,23 @@
     peers = lax.axis_size("sky")
     nblk = start_x.shape[0]
     cap = max(2, 2 * nblk // peers)
-    requests, slots = prep(tile_map[:, :, 0], row_anchor, col_anchor, peers, cap)
-    asked = lax.all_to_all(requests, "sky", split_axis=0, concat_axis=0, tiled=True)
+    relays = peers // 2
+    groups = [[h * relays + r for r in range(relays)] for h in range(2)]
+    swap = [(i, (i + relays) % peers) for i in range(peers)]
+    mirrors = [lax.ppermute(gradients[plane], "sky", swap) for plane in range(PLANES)]
+
+    def exchange(x):
+        return lax.all_to_all(
+            x, "sky", split_axis=0, concat_axis=0, axis_index_groups=groups, tiled=True
+        )
+
+    requests, slots = prep(tile_map[:, :, 0], row_anchor, col_anchor, peers, 2, cap)
+    asked = exchange(requests)
+    side = (lax.axis_index("sky") // relays).astype(jnp.int32).reshape(1)
     received = []
     for plane in range(PLANES):
-        windows = cut(plane, cap, asked, gradients)
-        got = lax.all_to_all(
-            windows.reshape(peers, cap, 2 * WR, WC), "sky", split_axis=0, concat_axis=0, tiled=True
-        )
+        windows = cut(plane, cap, side, asked, gradients, mirrors[plane])
+        got = exchange(windows.reshape(relays, 2 * cap, 2 * WR, WC))
         received.append(got.reshape(peers * cap, 2 * WR, WC))
     state = (start_x, start_y)
     for plane in range(PLANES):

time: 119 us -> 105 us (0.88); the launches traced: 117 us -> 105 us
  blocking collectives: 13.9 us -> 0 us
  starting transfers between devices: 17.2 us -> 25.4 us
  waiting for transfers between devices: 46.9 us -> 40.4 us
  Pallas kernels: 34.4 us -> 31.4 us
  local copies, waits for them, and re-layouts: 4.22 us -> 6.81 us
    all_to_all x3 -> x4, waiting for transfers between devices: 46.9 us -> 6.15 us  [exchange(): lax.all_to_all(x, 'sky', split_axis=0, concat_axis=0, axis_index_groups=g...]
    ppermute x0 -> x3, waiting for transfers between devices: none -> 34.2 us  [body(): lax.ppermute(gradients[plane], 'sky', swap)]
    all_to_all x1 -> x0, blocking collectives: 13.9 us -> none  [body(): lax.all_to_all(requests, 'sky', split_axis=0, concat_axis=0, tiled=True)]
    ppermute x0 -> x3, starting transfers between devices: none -> 6.88 us  [body(): lax.ppermute(gradients[plane], 'sky', swap)]
    pallas_call x3, Pallas kernels: 13.1 us -> 10.1 us  [cut(): pl.pallas_call(functools.partial(cut_kernel, plane, cap), out_shape=jax.S...]
    unnamed x7 -> x17, local copies, waits for them, and re-layouts: 4.22 us -> 5.65 us
    all_to_all x3 -> x4, starting transfers between devices: 17.2 us -> 18.5 us  [exchange(): lax.all_to_all(x, 'sky', split_axis=0, concat_axis=0, axis_index_groups=g...]
  transfers between devices with their start and end apart: 3 -> 7, of which waited for: 3 -> 5; matrix products, arithmetic and copies ran while one was open for 0% -> 1% of each run, Pallas kernels for 19% -> 21%
where the time goes in v2:
time: 105 us
  waiting for transfers between devices  40.4 us (38%)
  Pallas kernels  31.4 us (30%)
  starting transfers between devices  25.4 us (24%)
  local copies, waits for them, and re-layouts  6.81 us (6%)
    ppermute x3, waiting for transfers between devices, body(): lax.ppermute(gradients[plane], 'sky', swap)  34.2 us
    pallas_call x3, Pallas kernels, interp(): pl.pallas_call(functools.partial(interp_kernel, plane), out_shape=out_sha...  19.5 us
    all_to_all x4, starting transfers between devices, exchange(): lax.all_to_all(x, 'sky', split_axis=0, concat_axis=0, axis_index_groups=g...  18.5 us
    pallas_call x3, Pallas kernels, cut(): pl.pallas_call(functools.partial(cut_kernel, plane, cap), out_shape=jax.S...  10.1 us
    ppermute x3, starting transfers between devices, body(): lax.ppermute(gradients[plane], 'sky', swap)  6.88 us
    all_to_all x4, waiting for transfers between devices, exchange(): lax.all_to_all(x, 'sky', split_axis=0, concat_axis=0, axis_index_groups=g...  6.15 us
    unnamed x17, local copies, waits for them, and re-layouts  5.65 us
  transfers between devices with their start and end apart: 7, of which 5 were waited for; matrix products, arithmetic and copies ran while one was open for 1% of the time, Pallas kernels for 21%

profile of v2, /device:TPU:0, one launch (start us, length us, event | category | flops | bytes accessed | tf_op | source)
XLA Modules:
  0.0 104.7 jit_solution(14635257980040957331)
XLA Ops:
  0.6 1.2 %slice_bitcast_fusion = (bf16[2,256,256]{2,1,0:T(8,128)(2,1)S(1)}, bf16[2,256,256]{2,1,0:T(8,128)(2,1)S(1)}, bf16[2,256,256]{2,1,0:T(8,128)(2,1)S(1)}) fusion(bf16[3,2,256,256]{3,2,1,0:T(8,128)(2,1)} %own_ref.5), kind=kLoop, calls=%fused_computation | loop fusion | bytes 1572864 | tf_op jit(solution)/shard_map/squeeze | solution.py:252
  1.8 4.1 %collective-permute-start.2 = (bf16[2,256,256]{2,1,0:T(8,128)(2,1)S(1)}, bf16[2,256,256]{2,1,0:T(8,128)(2,1)S(1)}, u32[]{:S(2)}, u32[]{:S(2)}) collective-permute-start(bf16[2,256,256]{2,1,0:T(8,128)(2,1)S(1)} %get-tuple-element.6), channel_id=1, source_target_pairs={{0,8},{1,9},{2,10},{3,11},{4,12},{5,13},{6,14},{7,15},{8,0},{9,1},... | collective-permute-start | bytes 786440 | tf_op jit(solution)/shard_map/ppermute | solution.py:252
  6.5 1.8 %prep.1 = (s32[8,128]{1,0:T(8,128)}, s32[3,64]{1,0:T(4,128)}) custom-call(s32[3,64]{1,0:T(4,128)} %bitcast.29, s32[3,64]{1,0:T(4,128)} %row_ref.1, s32[3,64]{1,0:T(4,128)} %col_ref.1), custom_call_target="tpu_custom_call" | custom-call | tf_op jit(solution)/shard_map/prep/pallas_call | solution.py:66
  8.3 3.8 %all-to-all-start = ((s32[8,1,128]{2,1,0:T(1,128)}), s32[8,1,128]{2,1,0:T(1,128)S(1)}, u32[]{:S(2)}, u32[]{:S(2)}) async-start(s32[8,1,128]{2,1,0:T(1,128)} %bitcast.30), calls=%async_computation | async-start | bytes 8192 | tf_op jit(solution)/shard_map/all_to_all | solution.py:255
  12.2 4.6 %all-to-all-done = s32[8,1,128]{2,1,0:T(1,128)S(1)} async-done(((s32[8,1,128]{2,1,0:T(1,128)}), s32[8,1,128]{2,1,0:T(1,128)S(1)}, u32[]{:S(2)}, u32[]{:S(2)}) %all-to-all-start) | async-done | bytes 4128 | tf_op jit(solution)/shard_map/all_to_all | solution.py:255
  16.8 1.1 %collective-permute-done.2.mirror_ref = bf16[2,256,256]{2,1,0:T(8,128)(2,1)S(1)} collective-permute-done((bf16[2,256,256]{2,1,0:T(8,128)(2,1)S(1)}, bf16[2,256,256]{2,1,0:T(8,128)(2,1)S(1)}, u32[]{:S(2)}, u32[]{:S(2)}) %collective-permute-start.2) | collective-permute-done | bytes 262176 | tf_op jit(solution)/shard_map/ppermute | solution.py:252
  17.9 0.7 copy-done.3
  18.6 3.4 %cut0.1 = bf16[128,32,128]{2,1,0:T(8,128)(2,1)} custom-call(s32[1]{0:T(128)} %bitcast.side_ref, s32[8,128]{1,0:T(8,128)} %bitcast.26, bf16[3,2,256,256]{3,2,1,0:T(8,128)(2,1)} %own_ref.5, bf16[2,256,256]{2,1,0:T(8,128)(2,1)} %copy-done.3), custom_call_target="tpu_custom_call" | custom-call | tf_op jit(solution)/shard_map/cut0/pallas_call | solution.py:112
  22.0 3.6 %all-to-all-start.3 = ((bf16[8,16,32,128]{3,2,1,0:T(8,128)(2,1)}), bf16[8,16,32,128]{3,2,1,0:T(8,128)(2,1)S(1)}, u32[]{:S(2)}, u32[]{:S(2)}) async-start(bf16[8,16,32,128]{3,2,1,0:T(8,128)(2,1)} %bitcast.22), calls=%async_computation.3 | async-start | bytes 2097152 | tf_op jit(solution)/shard_map/all_to_all | solution.py:255
  25.6 2.7 %collective-permute-start.1 = (bf16[2,256,256]{2,1,0:T(8,128)(2,1)S(1)}, bf16[2,256,256]{2,1,0:T(8,128)(2,1)S(1)}, u32[]{:S(2)}, u32[]{:S(2)}) collective-permute-start(bf16[2,256,256]{2,1,0:T(8,128)(2,1)S(1)} %get-tuple-element.7), channel_id=1, source_target_pairs={{0,8},{1,9},{2,10},{3,11},{4,12},{5,13},{6,14},{7,15},{8,0},{9,1},... | collective-permute-start | bytes 786440 | tf_op jit(solution)/shard_map/ppermute | solution.py:252
  28.3 15.2 %collective-permute-done.1.mirror_ref = bf16[2,256,256]{2,1,0:T(8,128)(2,1)S(1)} collective-permute-done((bf16[2,256,256]{2,1,0:T(8,128)(2,1)S(1)}, bf16[2,256,256]{2,1,0:T(8,128)(2,1)S(1)}, u32[]{:S(2)}, u32[]{:S(2)}) %collective-permute-start.1) | collective-permute-done | bytes 262176 | tf_op jit(solution)/shard_map/ppermute | solution.py:252
  44.2 3.4 %cut1.1 = bf16[128,32,128]{2,1,0:T(8,128)(2,1)} custom-call(s32[1]{0:T(128)} %bitcast.side_ref, s32[8,128]{1,0:T(8,128)} %bitcast.27, bf16[3,2,256,256]{3,2,1,0:T(8,128)(2,1)} %own_ref.5, bf16[2,256,256]{2,1,0:T(8,128)(2,1)} %copy-done.5), custom_call_target="tpu_custom_call" | custom-call | tf_op jit(solution)/shard_map/cut1/pallas_call | solution.py:112
  47.5 1.0 copy-done
  48.5 7.1 %all-to-all-start.2 = ((bf16[8,16,32,128]{3,2,1,0:T(8,128)(2,1)}), bf16[8,16,32,128]{3,2,1,0:T(8,128)(2,1)S(1)}, u32[]{:S(2)}, u32[]{:S(2)}) async-start(bf16[8,16,32,128]{3,2,1,0:T(8,128)(2,1)} %bitcast.20), calls=%async_computation.2 | async-start | bytes 2097152 | tf_op jit(solution)/shard_map/all_to_all | solution.py:255
  55.6 18.0 %collective-permute-done.mirror_ref = bf16[2,256,256]{2,1,0:T(8,128)(2,1)S(1)} collective-permute-done((bf16[2,256,256]{2,1,0:T(8,128)(2,1)S(1)}, bf16[2,256,256]{2,1,0:T(8,128)(2,1)S(1)}, u32[]{:S(2)}, u32[]{:S(2)}) %collective-permute-start) | collective-permute-done | bytes 262176 | tf_op jit(solution)/shard_map/ppermute | solution.py:252
  73.6 0.7 copy-done.4
  74.3 3.4 %cut2.1 = bf16[128,32,128]{2,1,0:T(8,128)(2,1)} custom-call(s32[1]{0:T(128)} %bitcast.side_ref, s32[8,128]{1,0:T(8,128)} %bitcast.28, bf16[3,2,256,256]{3,2,1,0:T(8,128)(2,1)} %own_ref.5, bf16[2,256,256]{2,1,0:T(8,128)(2,1)} %copy-done.4), custom_call_target="tpu_custom_call" | custom-call | tf_op jit(solution)/shard_map/cut2/pallas_call | solution.py:112
  77.7 1.0 copy-done.1
  78.7 4.0 %all-to-all-start.1 = ((bf16[8,16,32,128]{3,2,1,0:T(8,128)(2,1)}), bf16[8,16,32,128]{3,2,1,0:T(8,128)(2,1)S(1)}, u32[]{:S(2)}, u32[]{:S(2)}) async-start(bf16[8,16,32,128]{3,2,1,0:T(8,128)(2,1)} %bitcast.21), calls=%async_computation.1 | async-start | bytes 2097152 | tf_op jit(solution)/shard_map/all_to_all | solution.py:255
  82.7 6.5 %interp0.1.refs_0_ = f32[12,64,128]{2,1,0:T(8,128)} custom-call(s32[3,64]{1,0:T(4,128)} %get-tuple-element.4.slot_ref, bf16[128,32,128]{2,1,0:T(8,128)(2,1)} %bitcast.23, f32[64,128]{1,0:T(8,128)} %refs_0_.1, f32[64,128]{1,0:T(8,128)} %refs_1_.1), custom_call_target="tpu_custom_call" | custom-call | tf_op jit(solution)/shard_map/interp0/pallas_call | solution.py:232
  89.2 6.5 %interp1.1.refs_0_ = f32[12,64,128]{2,1,0:T(8,128)} custom-call(s32[3,64]{1,0:T(4,128)} %get-tuple-element.4.slot_ref, bf16[128,32,128]{2,1,0:T(8,128)(2,1)} %bitcast.24, f32[12,64,128]{2,1,0:T(8,128)} %interp0.1.refs_0_), custom_call_target="tpu_custom_call" | custom-call | tf_op jit(solution)/shard_map/interp1/pallas_call | solution.py:232
  95.7 1.5 %all-to-all-done.1 = bf16[8,16,32,128]{3,2,1,0:T(8,128)(2,1)S(1)} async-done(((bf16[8,16,32,128]{3,2,1,0:T(8,128)(2,1)}), bf16[8,16,32,128]{3,2,1,0:T(8,128)(2,1)S(1)}, u32[]{:S(2)}, u32[]{:S(2)}) %all-to-all-start.1) | async-done | bytes 1048608 | tf_op jit(solution)/shard_map/all_to_all | solution.py:255
  97.2 1.0 copy-done.2
  98.2 6.5 %interp2.1 = (f32[64,2,128]{2,1,0:T(2,128)}, f32[64,4,128]{2,1,0:T(4,128)}) custom-call(s32[3,64]{1,0:T(4,128)} %get-tuple-element.4.slot_ref, bf16[128,32,128]{2,1,0:T(8,128)(2,1)} %bitcast.25, f32[12,64,128]{2,1,0:T(8,128)} %interp1.1.refs_0_), custom_call_target="tpu_custom_call" | custom-call | tf_op jit(solution)/shard_map/interp2/pallas_call | solution.py:232
  (15 shorter events, 1.3 us)
Async XLA Ops:
  1.8 4.1 %copy-start.7 = (s32[3,64,1]{1,2,0:T(1,128)S(1)}, s32[3,64,1]{1,2,0:T(1,128)}, u32[]{:S(2)}) copy-start(s32[3,64,1]{1,2,0:T(1,128)} %param.9) | copy-start | bytes 2308
  1.8 16.1 %collective-permute-start.2 = (bf16[2,256,256]{2,1,0:T(8,128)(2,1)S(1)}, bf16[2,256,256]{2,1,0:T(8,128)(2,1)S(1)}, u32[]{:S(2)}, u32[]{:S(2)}) collective-permute-start(bf16[2,256,256]{2,1,0:T(8,128)(2,1)S(1)} %get-tuple-element.6), channel_id=1, source_target_pairs={{0,8},{1,9},{2,10},{3,11},{4,12},{5,13},{6,14},{7,15},{8,0},{9,1},... | collective-permute-start | bytes 786440 | tf_op jit(solution)/shard_map/ppermute | solution.py:252
  8.3 8.5 %all-to-all-start = ((s32[8,1,128]{2,1,0:T(1,128)}), s32[8,1,128]{2,1,0:T(1,128)S(1)}, u32[]{:S(2)}, u32[]{:S(2)}) async-start(s32[8,1,128]{2,1,0:T(1,128)} %bitcast.30), calls=%async_computation | async-start | bytes 8192 | tf_op jit(solution)/shard_map/all_to_all | solution.py:255
  16.8 1.1 %copy-start.6 = (s32[8,1,128]{2,1,0:T(1,128)}, s32[8,1,128]{2,1,0:T(1,128)S(1)}, u32[]{:S(2)}) copy-start(s32[8,1,128]{2,1,0:T(1,128)S(1)} %all-to-all-done) | copy-start | bytes 12292
  17.9 0.7 copy-start.3
  22.0 25.5 %all-to-all-start.3 = ((bf16[8,16,32,128]{3,2,1,0:T(8,128)(2,1)}), bf16[8,16,32,128]{3,2,1,0:T(8,128)(2,1)S(1)}, u32[]{:S(2)}, u32[]{:S(2)}) async-start(bf16[8,16,32,128]{3,2,1,0:T(8,128)(2,1)} %bitcast.22), calls=%async_computation.3 | async-start | bytes 2097152 | tf_op jit(solution)/shard_map/all_to_all | solution.py:255
  25.6 17.9 %collective-permute-start.1 = (bf16[2,256,256]{2,1,0:T(8,128)(2,1)S(1)}, bf16[2,256,256]{2,1,0:T(8,128)(2,1)S(1)}, u32[]{:S(2)}, u32[]{:S(2)}) collective-permute-start(bf16[2,256,256]{2,1,0:T(8,128)(2,1)S(1)} %get-tuple-element.7), channel_id=1, source_target_pairs={{0,8},{1,9},{2,10},{3,11},{4,12},{5,13},{6,14},{7,15},{8,0},{9,1},... | collective-permute-start | bytes 786440 | tf_op jit(solution)/shard_map/ppermute | solution.py:252
  43.5 0.7 copy-start.5
  47.5 1.0 copy-start
  48.5 29.2 %all-to-all-start.2 = ((bf16[8,16,32,128]{3,2,1,0:T(8,128)(2,1)}), bf16[8,16,32,128]{3,2,1,0:T(8,128)(2,1)S(1)}, u32[]{:S(2)}, u32[]{:S(2)}) async-start(bf16[8,16,32,128]{3,2,1,0:T(8,128)(2,1)} %bitcast.20), calls=%async_computation.2 | async-start | bytes 2097152 | tf_op jit(solution)/shard_map/all_to_all | solution.py:255
  55.6 18.0 %collective-permute-start = (bf16[2,256,256]{2,1,0:T(8,128)(2,1)S(1)}, bf16[2,256,256]{2,1,0:T(8,128)(2,1)S(1)}, u32[]{:S(2)}, u32[]{:S(2)}) collective-permute-start(bf16[2,256,256]{2,1,0:T(8,128)(2,1)S(1)} %get-tuple-element.8), channel_id=1, source_target_pairs={{0,8},{1,9},{2,10},{3,11},{4,12},{5,13},{6,14},{7,15},{8,0},{9,1},... | collective-permute-start | bytes 786440 | tf_op jit(solution)/shard_map/ppermute | solution.py:252
  73.6 0.7 copy-start.4
  77.7 1.0 copy-start.1
  78.7 18.5 %all-to-all-start.1 = ((bf16[8,16,32,128]{3,2,1,0:T(8,128)(2,1)}), bf16[8,16,32,128]{3,2,1,0:T(8,128)(2,1)S(1)}, u32[]{:S(2)}, u32[]{:S(2)}) async-start(bf16[8,16,32,128]{3,2,1,0:T(8,128)(2,1)} %bitcast.21), calls=%async_computation.1 | async-start | bytes 2097152 | tf_op jit(solution)/shard_map/all_to_all | solution.py:255
  97.2 1.0 copy-start.2

commit v3 on v2

--- a/solution.py
+++ b/solution.py
@@ -1,5 +1,4 @@
 import functools
-import math
 
 import jax
 import jax.numpy as jnp
@@ -7,6 +6,7 @@
 from jax.experimental import pallas as pl
 from jax.experimental.pallas import tpu as pltpu
 from jax.sharding import PartitionSpec as P
+
 
 WR = 16
 WC = 128
@@ -115,7 +115,6 @@
         in_specs=[whole(SMEM), whole(SMEM), whole(), whole()],
         out_specs=whole(),
         scratch_shapes=[VMEM((4 * sheet.shape[3] // WC, sheet.shape[2], WC), jnp.float32)],
-        name=f"cut{plane}",
     )(side, requests, sheet, mirror)
 
 
@@ -238,7 +237,6 @@
             VMEM((18, nblk, rays), jnp.float32),
             VMEM((6, nblk, rays), jnp.float32),
         ],
-        name=f"interp{plane}",
     )(slots, windows, *state)
 
 
@@ -249,7 +247,9 @@
     relays = peers // 2
     groups = [[h * relays + r for r in range(relays)] for h in range(2)]
     swap = [(i, (i + relays) % peers) for i in range(peers)]
-    mirrors = [lax.ppermute(gradients[plane], "sky", swap) for plane in range(PLANES)]
+    mirrors = []
+    for plane in range(PLANES):
+        mirrors.append(lax.ppermute(gradients[plane], "sky", swap))
 
     def exchange(x):
         return lax.all_to_all(

time: 105 us -> 105 us (level)
  no operation moved by 1% of the time
where the time goes in v3:
time: 105 us
  waiting for transfers between devices  40.4 us (38%)
  Pallas kernels  31.4 us (30%)
  starting transfers between devices  25.4 us (24%)
  local copies, waits for them, and re-layouts  6.81 us (6%)
    ppermute x3, waiting for transfers between devices, body(): mirrors.append(lax.ppermute(gradients[plane], 'sky', swap))  34.2 us
    pallas_call x3, Pallas kernels, interp(): pl.pallas_call(functools.partial(interp_kernel, plane), out_shape=out_sha...  19.5 us
    all_to_all x4, starting transfers between devices, exchange(): lax.all_to_all(x, 'sky', split_axis=0, concat_axis=0, axis_index_groups=g...  18.5 us
    pallas_call x3, Pallas kernels, cut(): pl.pallas_call(functools.partial(cut_kernel, plane, cap), out_shape=jax.S...  10.1 us
    ppermute x3, starting transfers between devices, body(): mirrors.append(lax.ppermute(gradients[plane], 'sky', swap))  6.88 us
    all_to_all x4, waiting for transfers between devices, exchange(): lax.all_to_all(x, 'sky', split_axis=0, concat_axis=0, axis_index_groups=g...  6.15 us
    unnamed x17, local copies, waits for them, and re-layouts  5.65 us
  transfers between devices with their start and end apart: 7, of which 5 were waited for; matrix products, arithmetic and copies ran while one was open for 1% of the time, Pallas kernels for 21%

profile of v3, /device:TPU:0, one launch (start us, length us, event | category | flops | bytes accessed | tf_op | source)
XLA Modules:
  0.0 104.7 jit_solution(14635257980040957331)
XLA Ops:
  0.6 1.2 %slice_bitcast_fusion = (bf16[2,256,256]{2,1,0:T(8,128)(2,1)S(1)}, bf16[2,256,256]{2,1,0:T(8,128)(2,1)S(1)}, bf16[2,256,256]{2,1,0:T(8,128)(2,1)S(1)}) fusion(bf16[3,2,256,256]{3,2,1,0:T(8,128)(2,1)} %own_ref.5), kind=kLoop, calls=%fused_computation | loop fusion | bytes 1572864 | tf_op jit(solution)/shard_map/squeeze | solution.py:252
  1.8 4.1 %collective-permute-start.2 = (bf16[2,256,256]{2,1,0:T(8,128)(2,1)S(1)}, bf16[2,256,256]{2,1,0:T(8,128)(2,1)S(1)}, u32[]{:S(2)}, u32[]{:S(2)}) collective-permute-start(bf16[2,256,256]{2,1,0:T(8,128)(2,1)S(1)} %get-tuple-element.6), channel_id=1, source_target_pairs={{0,8},{1,9},{2,10},{3,11},{4,12},{5,13},{6,14},{7,15},{8,0},{9,1},... | collective-permute-start | bytes 786440 | tf_op jit(solution)/shard_map/ppermute | solution.py:252
  6.5 1.8 %prep.1 = (s32[8,128]{1,0:T(8,128)}, s32[3,64]{1,0:T(4,128)}) custom-call(s32[3,64]{1,0:T(4,128)} %bitcast.29, s32[3,64]{1,0:T(4,128)} %row_ref.1, s32[3,64]{1,0:T(4,128)} %col_ref.1), custom_call_target="tpu_custom_call" | custom-call | tf_op jit(solution)/shard_map/prep/pallas_call | solution.py:66
  8.3 3.8 %all-to-all-start = ((s32[8,1,128]{2,1,0:T(1,128)}), s32[8,1,128]{2,1,0:T(1,128)S(1)}, u32[]{:S(2)}, u32[]{:S(2)}) async-start(s32[8,1,128]{2,1,0:T(1,128)} %bitcast.30), calls=%async_computation | async-start | bytes 8192 | tf_op jit(solution)/shard_map/all_to_all | solution.py:255
  12.2 4.6 %all-to-all-done = s32[8,1,128]{2,1,0:T(1,128)S(1)} async-done(((s32[8,1,128]{2,1,0:T(1,128)}), s32[8,1,128]{2,1,0:T(1,128)S(1)}, u32[]{:S(2)}, u32[]{:S(2)}) %all-to-all-start) | async-done | bytes 4128 | tf_op jit(solution)/shard_map/all_to_all | solution.py:255
  16.8 1.1 %collective-permute-done.2.mirror_ref = bf16[2,256,256]{2,1,0:T(8,128)(2,1)S(1)} collective-permute-done((bf16[2,256,256]{2,1,0:T(8,128)(2,1)S(1)}, bf16[2,256,256]{2,1,0:T(8,128)(2,1)S(1)}, u32[]{:S(2)}, u32[]{:S(2)}) %collective-permute-start.2) | collective-permute-done | bytes 262176 | tf_op jit(solution)/shard_map/ppermute | solution.py:252
  17.9 0.7 copy-done.3
  18.6 3.4 %shard_map.79 = bf16[128,32,128]{2,1,0:T(8,128)(2,1)} custom-call(s32[1]{0:T(128)} %bitcast.side_ref, s32[8,128]{1,0:T(8,128)} %bitcast.26, bf16[3,2,256,256]{3,2,1,0:T(8,128)(2,1)} %own_ref.5, bf16[2,256,256]{2,1,0:T(8,128)(2,1)} %copy-done.3), custom_call_target="tpu_custom_call" | custom-call | tf_op jit(solution)/shard_map/pallas_call | solution.py:112
  22.0 3.6 %all-to-all-start.3 = ((bf16[8,16,32,128]{3,2,1,0:T(8,128)(2,1)}), bf16[8,16,32,128]{3,2,1,0:T(8,128)(2,1)S(1)}, u32[]{:S(2)}, u32[]{:S(2)}) async-start(bf16[8,16,32,128]{3,2,1,0:T(8,128)(2,1)} %bitcast.22), calls=%async_computation.3 | async-start | bytes 2097152 | tf_op jit(solution)/shard_map/all_to_all | solution.py:255
  25.6 2.7 %collective-permute-start.1 = (bf16[2,256,256]{2,1,0:T(8,128)(2,1)S(1)}, bf16[2,256,256]{2,1,0:T(8,128)(2,1)S(1)}, u32[]{:S(2)}, u32[]{:S(2)}) collective-permute-start(bf16[2,256,256]{2,1,0:T(8,128)(2,1)S(1)} %get-tuple-element.7), channel_id=1, source_target_pairs={{0,8},{1,9},{2,10},{3,11},{4,12},{5,13},{6,14},{7,15},{8,0},{9,1},... | collective-permute-start | bytes 786440 | tf_op jit(solution)/shard_map/ppermute | solution.py:252
  28.3 15.2 %collective-permute-done.1.mirror_ref = bf16[2,256,256]{2,1,0:T(8,128)(2,1)S(1)} collective-permute-done((bf16[2,256,256]{2,1,0:T(8,128)(2,1)S(1)}, bf16[2,256,256]{2,1,0:T(8,128)(2,1)S(1)}, u32[]{:S(2)}, u32[]{:S(2)}) %collective-permute-start.1) | collective-permute-done | bytes 262176 | tf_op jit(solution)/shard_map/ppermute | solution.py:252
  44.2 3.4 %shard_map.78 = bf16[128,32,128]{2,1,0:T(8,128)(2,1)} custom-call(s32[1]{0:T(128)} %bitcast.side_ref, s32[8,128]{1,0:T(8,128)} %bitcast.27, bf16[3,2,256,256]{3,2,1,0:T(8,128)(2,1)} %own_ref.5, bf16[2,256,256]{2,1,0:T(8,128)(2,1)} %copy-done.5), custom_call_target="tpu_custom_call" | custom-call | tf_op jit(solution)/shard_map/pallas_call | solution.py:112
  47.5 1.0 copy-done
  48.5 7.1 %all-to-all-start.2 = ((bf16[8,16,32,128]{3,2,1,0:T(8,128)(2,1)}), bf16[8,16,32,128]{3,2,1,0:T(8,128)(2,1)S(1)}, u32[]{:S(2)}, u32[]{:S(2)}) async-start(bf16[8,16,32,128]{3,2,1,0:T(8,128)(2,1)} %bitcast.20), calls=%async_computation.2 | async-start | bytes 2097152 | tf_op jit(solution)/shard_map/all_to_all | solution.py:255
  55.6 18.0 %collective-permute-done.mirror_ref = bf16[2,256,256]{2,1,0:T(8,128)(2,1)S(1)} collective-permute-done((bf16[2,256,256]{2,1,0:T(8,128)(2,1)S(1)}, bf16[2,256,256]{2,1,0:T(8,128)(2,1)S(1)}, u32[]{:S(2)}, u32[]{:S(2)}) %collective-permute-start) | collective-permute-done | bytes 262176 | tf_op jit(solution)/shard_map/ppermute | solution.py:252
  73.6 0.7 copy-done.4
  74.3 3.4 %shard_map.77 = bf16[128,32,128]{2,1,0:T(8,128)(2,1)} custom-call(s32[1]{0:T(128)} %bitcast.side_ref, s32[8,128]{1,0:T(8,128)} %bitcast.28, bf16[3,2,256,256]{3,2,1,0:T(8,128)(2,1)} %own_ref.5, bf16[2,256,256]{2,1,0:T(8,128)(2,1)} %copy-done.4), custom_call_target="tpu_custom_call" | custom-call | tf_op jit(solution)/shard_map/pallas_call | solution.py:112
  77.7 1.0 copy-done.1
  78.7 4.0 %all-to-all-start.1 = ((bf16[8,16,32,128]{3,2,1,0:T(8,128)(2,1)}), bf16[8,16,32,128]{3,2,1,0:T(8,128)(2,1)S(1)}, u32[]{:S(2)}, u32[]{:S(2)}) async-start(bf16[8,16,32,128]{3,2,1,0:T(8,128)(2,1)} %bitcast.21), calls=%async_computation.1 | async-start | bytes 2097152 | tf_op jit(solution)/shard_map/all_to_all | solution.py:255
  82.7 6.5 %shard_map.80.refs_0_ = f32[12,64,128]{2,1,0:T(8,128)} custom-call(s32[3,64]{1,0:T(4,128)} %get-tuple-element.4.slot_ref, bf16[128,32,128]{2,1,0:T(8,128)(2,1)} %bitcast.23, f32[64,128]{1,0:T(8,128)} %refs_0_.1, f32[64,128]{1,0:T(8,128)} %refs_1_.1), custom_call_target="tpu_custom_call" | custom-call | tf_op jit(solution)/shard_map/pallas_call | solution.py:231
  89.2 6.5 %shard_map.81.refs_0_ = f32[12,64,128]{2,1,0:T(8,128)} custom-call(s32[3,64]{1,0:T(4,128)} %get-tuple-element.4.slot_ref, bf16[128,32,128]{2,1,0:T(8,128)(2,1)} %bitcast.24, f32[12,64,128]{2,1,0:T(8,128)} %shard_map.80.refs_0_), custom_call_target="tpu_custom_call" | custom-call | tf_op jit(solution)/shard_map/pallas_call | solution.py:231
  95.7 1.5 %all-to-all-done.1 = bf16[8,16,32,128]{3,2,1,0:T(8,128)(2,1)S(1)} async-done(((bf16[8,16,32,128]{3,2,1,0:T(8,128)(2,1)}), bf16[8,16,32,128]{3,2,1,0:T(8,128)(2,1)S(1)}, u32[]{:S(2)}, u32[]{:S(2)}) %all-to-all-start.1) | async-done | bytes 1048608 | tf_op jit(solution)/shard_map/all_to_all | solution.py:255
  97.2 1.0 copy-done.2
  98.2 6.5 %shard_map.82 = (f32[64,2,128]{2,1,0:T(2,128)}, f32[64,4,128]{2,1,0:T(4,128)}) custom-call(s32[3,64]{1,0:T(4,128)} %get-tuple-element.4.slot_ref, bf16[128,32,128]{2,1,0:T(8,128)(2,1)} %bitcast.25, f32[12,64,128]{2,1,0:T(8,128)} %shard_map.81.refs_0_), custom_call_target="tpu_custom_call" | custom-call | tf_op jit(solution)/shard_map/pallas_call | solution.py:231
  (15 shorter events, 1.3 us)
Async XLA Ops:
  1.8 4.1 %copy-start.7 = (s32[3,64,1]{1,2,0:T(1,128)S(1)}, s32[3,64,1]{1,2,0:T(1,128)}, u32[]{:S(2)}) copy-start(s32[3,64,1]{1,2,0:T(1,128)} %param.9) | copy-start | bytes 2308
  1.8 16.1 %collective-permute-start.2 = (bf16[2,256,256]{2,1,0:T(8,128)(2,1)S(1)}, bf16[2,256,256]{2,1,0:T(8,128)(2,1)S(1)}, u32[]{:S(2)}, u32[]{:S(2)}) collective-permute-start(bf16[2,256,256]{2,1,0:T(8,128)(2,1)S(1)} %get-tuple-element.6), channel_id=1, source_target_pairs={{0,8},{1,9},{2,10},{3,11},{4,12},{5,13},{6,14},{7,15},{8,0},{9,1},... | collective-permute-start | bytes 786440 | tf_op jit(solution)/shard_map/ppermute | solution.py:252
  8.3 8.5 %all-to-all-start = ((s32[8,1,128]{2,1,0:T(1,128)}), s32[8,1,128]{2,1,0:T(1,128)S(1)}, u32[]{:S(2)}, u32[]{:S(2)}) async-start(s32[8,1,128]{2,1,0:T(1,128)} %bitcast.30), calls=%async_computation | async-start | bytes 8192 | tf_op jit(solution)/shard_map/all_to_all | solution.py:255
  16.8 1.1 %copy-start.6 = (s32[8,1,128]{2,1,0:T(1,128)}, s32[8,1,128]{2,1,0:T(1,128)S(1)}, u32[]{:S(2)}) copy-start(s32[8,1,128]{2,1,0:T(1,128)S(1)} %all-to-all-done) | copy-start | bytes 12292
  17.9 0.7 copy-start.3
  22.0 25.5 %all-to-all-start.3 = ((bf16[8,16,32,128]{3,2,1,0:T(8,128)(2,1)}), bf16[8,16,32,128]{3,2,1,0:T(8,128)(2,1)S(1)}, u32[]{:S(2)}, u32[]{:S(2)}) async-start(bf16[8,16,32,128]{3,2,1,0:T(8,128)(2,1)} %bitcast.22), calls=%async_computation.3 | async-start | bytes 2097152 | tf_op jit(solution)/shard_map/all_to_all | solution.py:255
  25.6 17.9 %collective-permute-start.1 = (bf16[2,256,256]{2,1,0:T(8,128)(2,1)S(1)}, bf16[2,256,256]{2,1,0:T(8,128)(2,1)S(1)}, u32[]{:S(2)}, u32[]{:S(2)}) collective-permute-start(bf16[2,256,256]{2,1,0:T(8,128)(2,1)S(1)} %get-tuple-element.7), channel_id=1, source_target_pairs={{0,8},{1,9},{2,10},{3,11},{4,12},{5,13},{6,14},{7,15},{8,0},{9,1},... | collective-permute-start | bytes 786440 | tf_op jit(solution)/shard_map/ppermute | solution.py:252
  43.5 0.7 copy-start.5
  47.5 1.0 copy-start
  48.5 29.2 %all-to-all-start.2 = ((bf16[8,16,32,128]{3,2,1,0:T(8,128)(2,1)}), bf16[8,16,32,128]{3,2,1,0:T(8,128)(2,1)S(1)}, u32[]{:S(2)}, u32[]{:S(2)}) async-start(bf16[8,16,32,128]{3,2,1,0:T(8,128)(2,1)} %bitcast.20), calls=%async_computation.2 | async-start | bytes 2097152 | tf_op jit(solution)/shard_map/all_to_all | solution.py:255
  55.6 18.0 %collective-permute-start = (bf16[2,256,256]{2,1,0:T(8,128)(2,1)S(1)}, bf16[2,256,256]{2,1,0:T(8,128)(2,1)S(1)}, u32[]{:S(2)}, u32[]{:S(2)}) collective-permute-start(bf16[2,256,256]{2,1,0:T(8,128)(2,1)S(1)} %get-tuple-element.8), channel_id=1, source_target_pairs={{0,8},{1,9},{2,10},{3,11},{4,12},{5,13},{6,14},{7,15},{8,0},{9,1},... | collective-permute-start | bytes 786440 | tf_op jit(solution)/shard_map/ppermute | solution.py:252
  73.6 0.7 copy-start.4
  77.7 1.0 copy-start.1
  78.7 18.5 %all-to-all-start.1 = ((bf16[8,16,32,128]{3,2,1,0:T(8,128)(2,1)}), bf16[8,16,32,128]{3,2,1,0:T(8,128)(2,1)S(1)}, u32[]{:S(2)}, u32[]{:S(2)}) async-start(bf16[8,16,32,128]{3,2,1,0:T(8,128)(2,1)} %bitcast.21), calls=%async_computation.1 | async-start | bytes 2097152 | tf_op jit(solution)/shard_map/all_to_all | solution.py:255
  97.2 1.0 copy-start.2

commit v4 on v3

--- a/solution.py
+++ b/solution.py
@@ -15,6 +15,7 @@
 lens_ratio = (0.85, 0.7, 0.9)
 lens_strength = (0.5, 0.6, 0.45)
 
+GRANT = pltpu.CompilerParams(vmem_limit_bytes=16 << 20)
 VMEM = pltpu.VMEM
 SMEM = pltpu.SMEM
 
@@ -115,6 +116,7 @@
         in_specs=[whole(SMEM), whole(SMEM), whole(), whole()],
         out_specs=whole(),
         scratch_shapes=[VMEM((4 * sheet.shape[3] // WC, sheet.shape[2], WC), jnp.float32)],
+        compiler_params=GRANT,
     )(side, requests, sheet, mirror)
 
 
@@ -156,7 +158,7 @@
         px, py = state_ref[0], state_ref[1]
     for at, pos in ((0, px), (9, py)):
         cell, value, slope = taps(pos)
-        tap_ref[at] = cell
+        tap_ref[at] = jnp.clip(cell, -4.0, WC + 4.0)
         for j in range(4):
             tap_ref[at + 1 + j] = value[j]
             tap_ref[at + 5 + j] = slope[j]
@@ -165,20 +167,26 @@
         def row(j):
             return tap_ref[j, pl.ds(b, 1), :]
 
-        def spread(at, size):
-            near = lax.broadcasted_iota(jnp.int32, (size, rays), 0).astype(jnp.float32) - row(at)
-            zero = jnp.zeros((size, rays), jnp.float32)
-            value, slope = zero, zero
+        def spread(at, size, dtype):
+            tile = 8 * 4 // jnp.dtype(dtype).itemsize
+
+            def lay(j):
+                return jnp.broadcast_to(row(j), (tile, rays)).astype(dtype)[None]
+
+            place = lax.broadcasted_iota(jnp.int32, (size // tile, tile, rays), 0) * tile
+            place = (place + lax.broadcasted_iota(jnp.int32, place.shape, 1)).astype(jnp.float32)
+            near = place.astype(dtype) - lay(at)
+            value = jnp.zeros(near.shape, dtype)
+            slope = value
             for j in range(4):
-                here = near == (j - 1.0)
-                value = jnp.where(here, row(at + 1 + j), value)
-                slope = jnp.where(here, row(at + 5 + j), slope)
-            return value, slope
-
-        kx, kxd = spread(0, WC)
-        kern = jnp.concatenate([kx.astype(jnp.bfloat16), kxd.astype(jnp.bfloat16)], axis=1)
+                here = near == jnp.asarray(j - 1, dtype)
+                value = jnp.where(here, lay(at + 1 + j), value)
+                slope = jnp.where(here, lay(at + 5 + j), slope)
+            return value.reshape(size, rays), slope.reshape(size, rays)
+
+        kern = jnp.concatenate(spread(0, WC, jnp.bfloat16), axis=1)
         mixed = jnp.dot(win_ref[slot_ref[plane, b]], kern, preferred_element_type=jnp.float32)
-        ky, kyd = spread(9, WR)
+        ky, kyd = spread(9, WR, jnp.float32)
         for c in range(2):
             part = mixed[c * WR : (c + 1) * WR]
             mixed0, mixed1 = part[:, :rays], part[:, rays:]
@@ -186,7 +194,7 @@
                 res_ref[at + c, pl.ds(b, 1), :] = jnp.sum(product, axis=0, keepdims=True)
         return carry
 
-    lax.fori_loop(0, nblk, one, 0, unroll=4)
+    lax.fori_loop(0, nblk, one, 0, unroll=16)
 
     ratio, strength = lens_ratio[plane], lens_strength[plane]
     ax, ay = res_ref[0], res_ref[1]
@@ -237,6 +245,7 @@
             VMEM((18, nblk, rays), jnp.float32),
             VMEM((6, nblk, rays), jnp.float32),
         ],
+        compiler_params=GRANT,
     )(slots, windows, *state)
 
 

time: 105 us -> 96.5 us (0.919)
  Pallas kernels: 31.4 us -> 19.8 us
  waiting for transfers between devices: 40.4 us -> 47.2 us
  local copies, waits for them, and re-layouts: 6.81 us -> 2.48 us
    pallas_call x3, Pallas kernels: 19.5 us -> 9.63 us  [interp(): pl.pallas_call(functools.partial(interp_kernel, plane), out_shape=out_sha...]
    all_to_all x4, waiting for transfers between devices: 6.15 us -> 13 us  [exchange(): lax.all_to_all(x, 'sky', split_axis=0, concat_axis=0, axis_index_groups=g...]
    unnamed x17 -> x11, local copies, waits for them, and re-layouts: 5.65 us -> 1.25 us
    pallas_call x3, Pallas kernels: 10.1 us -> 8.34 us  [cut(): pl.pallas_call(functools.partial(cut_kernel, plane, cap), out_shape=jax.S...]
  transfers between devices with their start and end apart: 7 -> 7, of which waited for: 5 -> 5; matrix products, arithmetic and copies ran while one was open for 1% -> 1% of each run, Pallas kernels for 21% -> 13%
where the time goes in v4:
time: 96.5 us; the launch traced here: 96 us
  waiting for transfers between devices  47.2 us (49%)
  starting transfers between devices  25.7 us (27%)
  Pallas kernels  19.8 us (21%)
  local copies, waits for them, and re-layouts  2.48 us (3%)
    ppermute x3, waiting for transfers between devices, body(): mirrors.append(lax.ppermute(gradients[plane], 'sky', swap))  34.2 us
    all_to_all x4, starting transfers between devices, exchange(): lax.all_to_all(x, 'sky', split_axis=0, concat_axis=0, axis_index_groups=g...  18.9 us
    all_to_all x4, waiting for transfers between devices, exchange(): lax.all_to_all(x, 'sky', split_axis=0, concat_axis=0, axis_index_groups=g...  13 us
    pallas_call x3, Pallas kernels, interp(): pl.pallas_call(functools.partial(interp_kernel, plane), out_shape=out_sha...  9.63 us
    pallas_call x3, Pallas kernels, cut(): pl.pallas_call(functools.partial(cut_kernel, plane, cap), out_shape=jax.S...  8.34 us
    ppermute x3, starting transfers between devices, body(): mirrors.append(lax.ppermute(gradients[plane], 'sky', swap))  6.88 us
  transfers between devices with their start and end apart: 7, of which 5 were waited for; matrix products, arithmetic and copies ran while one was open for 1% of the time, Pallas kernels for 13%

profile of v4, /device:TPU:0, one launch (start us, length us, event | category | flops | bytes accessed | tf_op | source)
XLA Modules:
  0.0 96.0 jit_solution(12930279644489585076)
XLA Ops:
  0.6 1.2 %slice_bitcast_fusion = (bf16[2,256,256]{2,1,0:T(8,128)(2,1)S(1)}, bf16[2,256,256]{2,1,0:T(8,128)(2,1)S(1)}, bf16[2,256,256]{2,1,0:T(8,128)(2,1)S(1)}) fusion(bf16[3,2,256,256]{3,2,1,0:T(8,128)(2,1)} %own_ref.5), kind=kLoop, calls=%fused_computation | loop fusion | bytes 1572864 | tf_op jit(solution)/shard_map/squeeze | solution.py:261
  1.9 0.0 copy-start.4
  1.9 4.1 %collective-permute-start.2 = (bf16[2,256,256]{2,1,0:T(8,128)(2,1)S(1)}, bf16[2,256,256]{2,1,0:T(8,128)(2,1)S(1)}, u32[]{:S(2)}, u32[]{:S(2)}) collective-permute-start(bf16[2,256,256]{2,1,0:T(8,128)(2,1)S(1)} %get-tuple-element.6), channel_id=1, source_target_pairs={{0,8},{1,9},{2,10},{3,11},{4,12},{5,13},{6,14},{7,15},{8,0},{9,1},... | collective-permute-start | bytes 786440 | tf_op jit(solution)/shard_map/ppermute | solution.py:261
  6.0 0.6 copy.11
  6.6 1.8 %prep.1 = (s32[8,128]{1,0:T(8,128)}, s32[3,64]{1,0:T(4,128)}) custom-call(s32[3,64]{1,0:T(4,128)} %bitcast.25, s32[3,64]{1,0:T(4,128)} %row_ref.1, s32[3,64]{1,0:T(4,128)} %col_ref.1), custom_call_target="tpu_custom_call" | custom-call | tf_op jit(solution)/shard_map/prep/pallas_call | solution.py:67
  8.4 3.8 %all-to-all-start = ((s32[8,1,128]{2,1,0:T(1,128)}), s32[8,1,128]{2,1,0:T(1,128)S(1)}, u32[]{:S(2)}, u32[]{:S(2)}) async-start(s32[8,1,128]{2,1,0:T(1,128)} %bitcast.26), calls=%async_computation | async-start | bytes 8192 | tf_op jit(solution)/shard_map/all_to_all | solution.py:264
  12.2 4.6 %all-to-all-done = s32[8,1,128]{2,1,0:T(1,128)S(1)} async-done(((s32[8,1,128]{2,1,0:T(1,128)}), s32[8,1,128]{2,1,0:T(1,128)S(1)}, u32[]{:S(2)}, u32[]{:S(2)}) %all-to-all-start) | async-done | bytes 4128 | tf_op jit(solution)/shard_map/all_to_all | solution.py:264
  16.9 1.1 %collective-permute-done.2.mirror_ref = bf16[2,256,256]{2,1,0:T(8,128)(2,1)S(1)} collective-permute-done((bf16[2,256,256]{2,1,0:T(8,128)(2,1)S(1)}, bf16[2,256,256]{2,1,0:T(8,128)(2,1)S(1)}, u32[]{:S(2)}, u32[]{:S(2)}) %collective-permute-start.2) | collective-permute-done | bytes 262176 | tf_op jit(solution)/shard_map/ppermute | solution.py:261
  18.0 2.8 %shard_map.79 = bf16[128,32,128]{2,1,0:T(8,128)(2,1)} custom-call(s32[1]{0:T(128)} %bitcast.side_ref, s32[8,128]{1,0:T(8,128)S(1)} %bitcast.22, bf16[3,2,256,256]{3,2,1,0:T(8,128)(2,1)S(1)} %copy-done, bf16[2,256,256]{2,1,0:T(8,128)(2,1)S(1)} %collective-permute-done.2.mirror_ref), custom_call_target="tpu_custom_call" | custom-call | tf_op jit(solution)/shard_map/pallas_call | solution.py:113
  20.8 3.6 %all-to-all-start.3 = ((bf16[8,16,32,128]{3,2,1,0:T(8,128)(2,1)}), bf16[8,16,32,128]{3,2,1,0:T(8,128)(2,1)S(1)}, u32[]{:S(2)}, u32[]{:S(2)}) async-start(bf16[8,16,32,128]{3,2,1,0:T(8,128)(2,1)} %bitcast.11), calls=%async_computation.3 | async-start | bytes 2097152 | tf_op jit(solution)/shard_map/all_to_all | solution.py:264
  24.3 2.7 %collective-permute-start.1 = (bf16[2,256,256]{2,1,0:T(8,128)(2,1)S(1)}, bf16[2,256,256]{2,1,0:T(8,128)(2,1)S(1)}, u32[]{:S(2)}, u32[]{:S(2)}) collective-permute-start(bf16[2,256,256]{2,1,0:T(8,128)(2,1)S(1)} %get-tuple-element.7), channel_id=1, source_target_pairs={{0,8},{1,9},{2,10},{3,11},{4,12},{5,13},{6,14},{7,15},{8,0},{9,1},... | collective-permute-start | bytes 786440 | tf_op jit(solution)/shard_map/ppermute | solution.py:261
  27.1 15.2 %collective-permute-done.1.mirror_ref = bf16[2,256,256]{2,1,0:T(8,128)(2,1)S(1)} collective-permute-done((bf16[2,256,256]{2,1,0:T(8,128)(2,1)S(1)}, bf16[2,256,256]{2,1,0:T(8,128)(2,1)S(1)}, u32[]{:S(2)}, u32[]{:S(2)}) %collective-permute-start.1) | collective-permute-done | bytes 262176 | tf_op jit(solution)/shard_map/ppermute | solution.py:261
  42.2 2.8 %shard_map.78 = bf16[128,32,128]{2,1,0:T(8,128)(2,1)} custom-call(s32[1]{0:T(128)} %bitcast.side_ref, s32[8,128]{1,0:T(8,128)S(1)} %bitcast.23, bf16[3,2,256,256]{3,2,1,0:T(8,128)(2,1)S(1)} %copy-done, bf16[2,256,256]{2,1,0:T(8,128)(2,1)S(1)} %collective-permute-done.1.mirror_ref), custom_call_target="tpu_custom_call" | custom-call | tf_op jit(solution)/shard_map/pallas_call | solution.py:113
  45.0 0.0 all-to-all-done.3
  45.0 7.1 %all-to-all-start.2 = ((bf16[8,16,32,128]{3,2,1,0:T(8,128)(2,1)}), bf16[8,16,32,128]{3,2,1,0:T(8,128)(2,1)S(1)}, u32[]{:S(2)}, u32[]{:S(2)}) async-start(bf16[8,16,32,128]{3,2,1,0:T(8,128)(2,1)} %bitcast.8), calls=%async_computation.2 | async-start | bytes 2097152 | tf_op jit(solution)/shard_map/all_to_all | solution.py:264
  52.2 18.0 %collective-permute-done.mirror_ref = bf16[2,256,256]{2,1,0:T(8,128)(2,1)S(1)} collective-permute-done((bf16[2,256,256]{2,1,0:T(8,128)(2,1)S(1)}, bf16[2,256,256]{2,1,0:T(8,128)(2,1)S(1)}, u32[]{:S(2)}, u32[]{:S(2)}) %collective-permute-start) | collective-permute-done | bytes 262176 | tf_op jit(solution)/shard_map/ppermute | solution.py:261
  70.1 2.8 %shard_map.77 = bf16[128,32,128]{2,1,0:T(8,128)(2,1)} custom-call(s32[1]{0:T(128)} %bitcast.side_ref, s32[8,128]{1,0:T(8,128)S(1)} %bitcast.24, bf16[3,2,256,256]{3,2,1,0:T(8,128)(2,1)S(1)} %copy-done, bf16[2,256,256]{2,1,0:T(8,128)(2,1)S(1)} %collective-permute-done.mirror_ref), custom_call_target="tpu_custom_call" | custom-call | tf_op jit(solution)/shard_map/pallas_call | solution.py:113
  72.9 0.0 all-to-all-done.2
  72.9 4.4 %all-to-all-start.1 = ((bf16[8,16,32,128]{3,2,1,0:T(8,128)(2,1)}), bf16[8,16,32,128]{3,2,1,0:T(8,128)(2,1)}, u32[]{:S(2)}, u32[]{:S(2)}) async-start(bf16[8,16,32,128]{3,2,1,0:T(8,128)(2,1)} %bitcast.5), calls=%async_computation.1 | async-start | bytes 2097152 | tf_op jit(solution)/shard_map/all_to_all | solution.py:264
  77.4 0.7 copy-done.3
  78.0 2.7 %shard_map.80.refs_0_ = f32[12,64,128]{2,1,0:T(8,128)S(1)} custom-call(s32[3,64]{1,0:T(4,128)S(1)} %copy-done.3, bf16[128,32,128]{2,1,0:T(8,128)(2,1)S(1)} %bitcast.20, f32[64,128]{1,0:T(8,128)S(1)} %copy-done.1, f32[64,128]{1,0:T(8,128)S(1)} %copy-done.2), custom_call_target="tpu_custom_call" | custom-call | tf_op jit(solution)/shard_map/pallas_call | solution.py:239
  80.7 2.7 %shard_map.81.refs_0_ = f32[12,64,128]{2,1,0:T(8,128)S(1)} custom-call(s32[3,64]{1,0:T(4,128)S(1)} %copy-done.3, bf16[128,32,128]{2,1,0:T(8,128)(2,1)S(1)} %bitcast.21, f32[12,64,128]{2,1,0:T(8,128)S(1)} %shard_map.80.refs_0_), custom_call_target="tpu_custom_call" | custom-call | tf_op jit(solution)/shard_map/pallas_call | solution.py:239
  83.5 8.3 %all-to-all-done.1 = bf16[8,16,32,128]{3,2,1,0:T(8,128)(2,1)} async-done(((bf16[8,16,32,128]{3,2,1,0:T(8,128)(2,1)}), bf16[8,16,32,128]{3,2,1,0:T(8,128)(2,1)}, u32[]{:S(2)}, u32[]{:S(2)}) %all-to-all-start.1) | async-done | bytes 1048608 | tf_op jit(solution)/shard_map/all_to_all | solution.py:264
  91.8 4.2 %shard_map.82 = (f32[64,2,128]{2,1,0:T(2,128)}, f32[64,4,128]{2,1,0:T(4,128)}) custom-call(s32[3,64]{1,0:T(4,128)S(1)} %copy-done.3, bf16[128,32,128]{2,1,0:T(8,128)(2,1)} %bitcast.6.win_ref, f32[12,64,128]{2,1,0:T(8,128)S(1)} %shard_map.81.refs_0_), custom_call_target="tpu_custom_call" | custom-call | tf_op jit(solution)/shard_map/pallas_call | solution.py:239
  (9 shorter events, 0.0 us)
Async XLA Ops:
  0.6 17.4 %copy-start = (bf16[3,2,256,256]{3,2,1,0:T(8,128)(2,1)S(1)}, bf16[3,2,256,256]{3,2,1,0:T(8,128)(2,1)}, u32[]{:S(2)}) copy-start(bf16[3,2,256,256]{3,2,1,0:T(8,128)(2,1)} %own_ref.5) | copy-start | bytes 2359300
  1.9 4.1 %copy-start.4 = (s32[3,64,1]{1,2,0:T(1,128)S(1)}, s32[3,64,1]{1,2,0:T(1,128)}, u32[]{:S(2)}) copy-start(s32[3,64,1]{1,2,0:T(1,128)} %param.9) | copy-start | bytes 2308
  1.9 16.1 %collective-permute-start.2 = (bf16[2,256,256]{2,1,0:T(8,128)(2,1)S(1)}, bf16[2,256,256]{2,1,0:T(8,128)(2,1)S(1)}, u32[]{:S(2)}, u32[]{:S(2)}) collective-permute-start(bf16[2,256,256]{2,1,0:T(8,128)(2,1)S(1)} %get-tuple-element.6), channel_id=1, source_target_pairs={{0,8},{1,9},{2,10},{3,11},{4,12},{5,13},{6,14},{7,15},{8,0},{9,1},... | collective-permute-start | bytes 786440 | tf_op jit(solution)/shard_map/ppermute | solution.py:261
  8.4 8.5 %all-to-all-start = ((s32[8,1,128]{2,1,0:T(1,128)}), s32[8,1,128]{2,1,0:T(1,128)S(1)}, u32[]{:S(2)}, u32[]{:S(2)}) async-start(s32[8,1,128]{2,1,0:T(1,128)} %bitcast.26), calls=%async_computation | async-start | bytes 8192 | tf_op jit(solution)/shard_map/all_to_all | solution.py:264
  20.8 24.3 %all-to-all-start.3 = ((bf16[8,16,32,128]{3,2,1,0:T(8,128)(2,1)}), bf16[8,16,32,128]{3,2,1,0:T(8,128)(2,1)S(1)}, u32[]{:S(2)}, u32[]{:S(2)}) async-start(bf16[8,16,32,128]{3,2,1,0:T(8,128)(2,1)} %bitcast.11), calls=%async_computation.3 | async-start | bytes 2097152 | tf_op jit(solution)/shard_map/all_to_all | solution.py:264
  24.3 17.9 %collective-permute-start.1 = (bf16[2,256,256]{2,1,0:T(8,128)(2,1)S(1)}, bf16[2,256,256]{2,1,0:T(8,128)(2,1)S(1)}, u32[]{:S(2)}, u32[]{:S(2)}) collective-permute-start(bf16[2,256,256]{2,1,0:T(8,128)(2,1)S(1)} %get-tuple-element.7), channel_id=1, source_target_pairs={{0,8},{1,9},{2,10},{3,11},{4,12},{5,13},{6,14},{7,15},{8,0},{9,1},... | collective-permute-start | bytes 786440 | tf_op jit(solution)/shard_map/ppermute | solution.py:261
  45.0 27.9 %all-to-all-start.2 = ((bf16[8,16,32,128]{3,2,1,0:T(8,128)(2,1)}), bf16[8,16,32,128]{3,2,1,0:T(8,128)(2,1)S(1)}, u32[]{:S(2)}, u32[]{:S(2)}) async-start(bf16[8,16,32,128]{3,2,1,0:T(8,128)(2,1)} %bitcast.8), calls=%async_computation.2 | async-start | bytes 2097152 | tf_op jit(solution)/shard_map/all_to_all | solution.py:264
  52.1 18.0 %collective-permute-start = (bf16[2,256,256]{2,1,0:T(8,128)(2,1)S(1)}, bf16[2,256,256]{2,1,0:T(8,128)(2,1)S(1)}, u32[]{:S(2)}, u32[]{:S(2)}) collective-permute-start(bf16[2,256,256]{2,1,0:T(8,128)(2,1)S(1)} %get-tuple-element.8), channel_id=1, source_target_pairs={{0,8},{1,9},{2,10},{3,11},{4,12},{5,13},{6,14},{7,15},{8,0},{9,1},... | collective-permute-start | bytes 786440 | tf_op jit(solution)/shard_map/ppermute | solution.py:261
  72.9 4.4 %copy-start.1 = (f32[64,128]{1,0:T(8,128)S(1)}, f32[64,128]{1,0:T(8,128)}, u32[]{:S(2)}) copy-start(f32[64,128]{1,0:T(8,128)} %refs_0_.1) | copy-start | bytes 98308
  72.9 4.4 %copy-start.2 = (f32[64,128]{1,0:T(8,128)S(1)}, f32[64,128]{1,0:T(8,128)}, u32[]{:S(2)}) copy-start(f32[64,128]{1,0:T(8,128)} %refs_1_.1) | copy-start | bytes 98308
  72.9 18.9 %all-to-all-start.1 = ((bf16[8,16,32,128]{3,2,1,0:T(8,128)(2,1)}), bf16[8,16,32,128]{3,2,1,0:T(8,128)(2,1)}, u32[]{:S(2)}, u32[]{:S(2)}) async-start(bf16[8,16,32,128]{3,2,1,0:T(8,128)(2,1)} %bitcast.5), calls=%async_computation.1 | async-start | bytes 2097152 | tf_op jit(solution)/shard_map/all_to_all | solution.py:264
  77.3 0.7 copy-start.3

commit v5 on v4

--- a/solution.py
+++ b/solution.py
@@ -30,7 +30,7 @@
     )
 
 
-def prep_kernel(peers, halves, cap, tile_ref, row_ref, col_ref, req_ref, slot_ref):
+def prep_kernel(peers, halves, cap, direct, me_ref, tile_ref, row_ref, col_ref, req_ref, slot_ref):
     relays = peers // halves
     nblk = tile_ref.shape[1]
     lanes = req_ref.shape[1]
@@ -50,7 +50,10 @@
         rank = jnp.sum(before * hit, axis=0, keepdims=True).astype(jnp.int32)
         side = tile // relays
         rank = rank + side * cap
-        slot_ref[k : k + 1, :] = (tile - side * relays) * (halves * cap) + rank
+        relay = (tile - side * relays) ^ me_ref[0]
+        if not direct:
+            relay = (relay & 1) * (relays // 2) + (relay >> 1)
+        slot_ref[k : k + 1, :] = relay * (halves * cap) + rank
         here = lane == (rank + k * halves * cap)
         zero = jnp.zeros((), jnp.float32)
         row = jnp.where(here, row_ref[k : k + 1, :].astype(jnp.float32), zero)
@@ -61,22 +64,23 @@
     req_ref[...] = rows.astype(jnp.int32) * 65536 + cols.astype(jnp.int32)
 
 
-def prep(tile_map, row_anchor, col_anchor, peers, halves, cap):
+def prep(me, tile_map, row_anchor, col_anchor, peers, halves, cap, direct):
     nblk = tile_map.shape[1]
     lanes = -(-PLANES * halves * cap // 128) * 128
     return pl.pallas_call(
-        functools.partial(prep_kernel, peers, halves, cap),
+        functools.partial(prep_kernel, peers, halves, cap, direct),
         out_shape=(
             jax.ShapeDtypeStruct((peers // halves, lanes), jnp.int32),
             jax.ShapeDtypeStruct((PLANES, nblk), jnp.int32),
         ),
-        in_specs=[whole()] * 3,
+        in_specs=[whole(SMEM)] + [whole()] * 3,
         out_specs=(whole(), whole()),
         name="prep",
-    )(tile_map, row_anchor, col_anchor)
-
-
-def cut_kernel(plane, cap, side_ref, req_ref, own_ref, mirror_ref, out_ref, half_ref):
+    )(me, tile_map, row_anchor, col_anchor)
+
+
+def cut_kernel(plane, cap, place_ref, req_ref, own_ref, mirror_ref, *refs):
+    out_refs, half_ref = refs[:-1], refs[-1]
     parts = own_ref.shape[3] // WC
     for c in range(2):
         for h in range(parts):
@@ -84,40 +88,43 @@
             half_ref[c * parts + h] = own_ref[plane, c, :, lanes].astype(jnp.float32)
             half_ref[(2 + c) * parts + h] = mirror_ref[c, :, lanes].astype(jnp.float32)
     lane = lax.broadcasted_iota(jnp.int32, (WR, WC), 1)
-    side = side_ref[0]
+    side, me = place_ref[0], place_ref[1]
     each = 2 * cap
-
-    def one(source, carry):
-        for place in range(each):
-            packed = req_ref[source, plane * each + place]
-            base = jnp.where(side == place // cap, 0, 2 * parts)
-            row = packed >> 16
-            col = packed & 65535
-            turn = (WC - col) & (WC - 1)
-            left = lane < WC - col
-            for c in range(2):
-                part = [
-                    pltpu.roll(half_ref[base + c * parts + h, pl.ds(row, WR), :], turn, 1)
-                    for h in range(parts)
-                ]
-                out_ref[source * each + place, c * WR : (c + 1) * WR, :] = jnp.where(
-                    left, part[0], part[1]
-                ).astype(jnp.bfloat16)
+    span = req_ref.shape[0] // len(out_refs)
+
+    def one(at, carry):
+        for m, out_ref in enumerate(out_refs):
+            source = (m * span + at) ^ me
+            for place in range(each):
+                packed = req_ref[source, plane * each + place]
+                base = jnp.where(side == place // cap, 0, 2 * parts)
+                row = packed >> 16
+                col = packed & 65535
+                turn = (WC - col) & (WC - 1)
+                left = lane < WC - col
+                for c in range(2):
+                    part = [
+                        pltpu.roll(half_ref[base + c * parts + h, pl.ds(row, WR), :], turn, 1)
+                        for h in range(parts)
+                    ]
+                    out_ref[at * each + place, c * WR : (c + 1) * WR, :] = jnp.where(
+                        left, part[0], part[1]
+                    ).astype(jnp.bfloat16)
         return carry
 
-    lax.fori_loop(0, req_ref.shape[0], one, 0)
-
-
-def cut(plane, cap, side, requests, sheet, mirror):
-    count = requests.shape[0] * 2 * cap
+    lax.fori_loop(0, span, one, 0)
+
+
+def cut(plane, cap, outs, place, requests, sheet, mirror):
+    count = requests.shape[0] // outs * 2 * cap
     return pl.pallas_call(
         functools.partial(cut_kernel, plane, cap),
-        out_shape=jax.ShapeDtypeStruct((count, 2 * WR, WC), jnp.bfloat16),
+        out_shape=(jax.ShapeDtypeStruct((count, 2 * WR, WC), jnp.bfloat16),) * outs,
         in_specs=[whole(SMEM), whole(SMEM), whole(), whole()],
-        out_specs=whole(),
+        out_specs=(whole(),) * outs,
         scratch_shapes=[VMEM((4 * sheet.shape[3] // WC, sheet.shape[2], WC), jnp.float32)],
         compiler_params=GRANT,
-    )(side, requests, sheet, mirror)
+    )(place, requests, sheet, mirror)
 
 
 def taps(pos):
@@ -254,25 +261,46 @@
     nblk = start_x.shape[0]
     cap = max(2, 2 * nblk // peers)
     relays = peers // 2
+    chips = relays // 2
+    direct = chips > 4 or chips & (chips - 1) != 0
     groups = [[h * relays + r for r in range(relays)] for h in range(2)]
-    swap = [(i, (i + relays) % peers) for i in range(peers)]
+
+    def swap(bits):
+        return [(i, i ^ bits) for i in range(peers)]
+
+    mirror_pairs = [(i, (i + relays) % peers) for i in range(peers)]
     mirrors = []
     for plane in range(PLANES):
-        mirrors.append(lax.ppermute(gradients[plane], "sky", swap))
+        mirrors.append(lax.ppermute(gradients[plane], "sky", mirror_pairs))
 
     def exchange(x):
         return lax.all_to_all(
             x, "sky", split_axis=0, concat_axis=0, axis_index_groups=groups, tiled=True
         )
 
-    requests, slots = prep(tile_map[:, :, 0], row_anchor, col_anchor, peers, 2, cap)
+    def send(outs):
+        if direct:
+            got = exchange(outs[0].reshape(relays, 2 * cap, 2 * WR, WC))
+            return got.reshape(peers * cap, 2 * WR, WC)
+        got = [outs[0]]
+        for m in range(1, chips):
+            got.append(lax.ppermute(outs[m], "sky", swap(2 * m)))
+        mine = [part[: 2 * cap] for part in got]
+        other = jnp.concatenate([part[2 * cap :] for part in got], axis=0)
+        other = lax.ppermute(other, "sky", swap(1))
+        return jnp.concatenate(mine + [other], axis=0)
+
+    index = lax.axis_index("sky").astype(jnp.int32)
+    me = jnp.zeros_like(index) if direct else index % relays
+    place = jnp.stack([index // relays, me])
+    requests, slots = prep(
+        me.reshape(1), tile_map[:, :, 0], row_anchor, col_anchor, peers, 2, cap, direct
+    )
     asked = exchange(requests)
-    side = (lax.axis_index("sky") // relays).astype(jnp.int32).reshape(1)
     received = []
     for plane in range(PLANES):
-        windows = cut(plane, cap, side, asked, gradients, mirrors[plane])
-        got = exchange(windows.reshape(relays, 2 * cap, 2 * WR, WC))
-        received.append(got.reshape(peers * cap, 2 * WR, WC))
+        outs = cut(plane, cap, 1 if direct else chips, place, asked, gradients, mirrors[plane])
+        received.append(send(outs))
     state = (start_x, start_y)
     for plane in range(PLANES):
         state = interp(plane, slots, received[plane], state)

time: 96.5 us -> 85.6 us (0.89)
  Pallas kernels: 19.8 us -> 14.9 us
  waiting for transfers between devices: 47.2 us -> 42.6 us
  starting transfers between devices: 25.7 us -> 23 us
  local copies, waits for them, and re-layouts: 2.48 us -> 3.68 us
    all_to_all x4 -> x1, starting transfers between devices: 18.9 us -> 3.81 us  [exchange(): lax.all_to_all(x, 'sky', split_axis=0, concat_axis=0, axis_index_groups=g...]
    ppermute x3 -> x15, starting transfers between devices: 6.88 us -> 19.2 us  [the longest x9 12 us: send(): got.append(lax.ppermute(outs[m], 'sky', swap(2 * m)))]
    all_to_all x4 -> x1, waiting for transfers between devices: 13 us -> 1.65 us  [exchange(): lax.all_to_all(x, 'sky', split_axis=0, concat_axis=0, axis_index_groups=g...]
    ppermute x3 -> x15, waiting for transfers between devices: 34.2 us -> 40.9 us  [the longest x9 26.1 us: send(): got.append(lax.ppermute(outs[m], 'sky', swap(2 * m)))]
    pallas_call x4, Pallas kernels: 10.2 us -> 5.93 us  [the longest x3 4.11 us: cut(): pl.pallas_call(functools.partial(cut_kernel, plane, cap), out_shape=(jax....]
  transfers between devices with their start and end apart: 7 -> 16, of which waited for: 5 -> 10; matrix products, arithmetic and copies ran while one was open for 1% -> 2% of each run, Pallas kernels for 13% -> 13%
where the time goes in v5:
time: 85.6 us; the launch traced here: 85.3 us
  waiting for transfers between devices  42.6 us (50%)
  starting transfers between devices  23 us (27%)
  Pallas kernels  14.9 us (17%)
  local copies, waits for them, and re-layouts  3.68 us (4%)
  between operations  0.88 us (1%)
    ppermute x9, waiting for transfers between devices, send(): got.append(lax.ppermute(outs[m], 'sky', swap(2 * m)))  26.1 us
    ppermute x3, waiting for transfers between devices, body(): mirrors.append(lax.ppermute(gradients[plane], 'sky', mirror_pairs))  14.8 us
    ppermute x9, starting transfers between devices, send(): got.append(lax.ppermute(outs[m], 'sky', swap(2 * m)))  12 us
    pallas_call x3, Pallas kernels, interp(): pl.pallas_call(functools.partial(interp_kernel, plane), out_shape=out_sha...  8.93 us
    ppermute x3, starting transfers between devices, body(): mirrors.append(lax.ppermute(gradients[plane], 'sky', mirror_pairs))  7.05 us
    pallas_call x3, Pallas kernels, cut(): pl.pallas_call(functools.partial(cut_kernel, plane, cap), out_shape=(jax....  4.11 us
    all_to_all x1, starting transfers between devices, exchange(): lax.all_to_all(x, 'sky', split_axis=0, concat_axis=0, axis_index_groups=g...  3.81 us
    unnamed x11, local copies, waits for them, and re-layouts  1.94 us
  transfers between devices with their start and end apart: 16, of which 10 were waited for; matrix products, arithmetic and copies ran while one was open for 2% of the time, Pallas kernels for 13%

profile of v5, /device:TPU:0, one launch (start us, length us, event | category | flops | bytes accessed | tf_op | source)
XLA Modules:
  0.0 85.3 jit_solution(7798794805825537423)
XLA Ops:
  1.9 4.1 %collective-permute-start.10 = (bf16[2,256,256]{2,1,0:T(8,128)(2,1)S(1)}, bf16[2,256,256]{2,1,0:T(8,128)(2,1)S(1)}, u32[]{:S(2)}, u32[]{:S(2)}) collective-permute-start(bf16[2,256,256]{2,1,0:T(8,128)(2,1)S(1)} %get-tuple-element.30), channel_id=1, source_target_pairs={{0,8},{1,9},{2,10},{3,11},{4,12},{5,13},{6,14},{7,15},{8,0},{9,1},... | collective-permute-start | bytes 786440 | tf_op jit(solution)/shard_map/ppermute | solution.py:274
  7.3 1.8 %prep.1 = (s32[8,128]{1,0:T(8,128)}, s32[3,64]{1,0:T(4,128)}) custom-call(s32[1]{0:T(128)} %bitcast.me_ref, s32[3,64]{1,0:T(4,128)} %bitcast.18, s32[3,64]{1,0:T(4,128)} %row_ref.1, s32[3,64]{1,0:T(4,128)} %col_ref.1), custom_call_target="tpu_custom_call" | custom-call | tf_op jit(solution)/shard_map/prep/pallas_call | solution.py:70
  9.1 3.8 %all-to-all-start = ((s32[8,1,128]{2,1,0:T(1,128)}), s32[8,1,128]{2,1,0:T(1,128)S(1)}, u32[]{:S(2)}, u32[]{:S(2)}) async-start(s32[8,1,128]{2,1,0:T(1,128)} %bitcast.19), calls=%async_computation | async-start | bytes 8192 | tf_op jit(solution)/shard_map/all_to_all | solution.py:277
  13.2 2.6 %collective-permute-start = (bf16[2,256,256]{2,1,0:T(8,128)(2,1)S(1)}, bf16[2,256,256]{2,1,0:T(8,128)(2,1)S(1)}, u32[]{:S(2)}, u32[]{:S(2)}) collective-permute-start(bf16[2,256,256]{2,1,0:T(8,128)(2,1)S(1)} %get-tuple-element.32), channel_id=1, source_target_pairs={{0,8},{1,9},{2,10},{3,11},{4,12},{5,13},{6,14},{7,15},{8,0},{9,1},... | collective-permute-start | bytes 786440 | tf_op jit(solution)/shard_map/ppermute | solution.py:274
  15.9 1.6 %all-to-all-done = s32[8,1,128]{2,1,0:T(1,128)S(1)} async-done(((s32[8,1,128]{2,1,0:T(1,128)}), s32[8,1,128]{2,1,0:T(1,128)S(1)}, u32[]{:S(2)}, u32[]{:S(2)}) %all-to-all-start) | async-done | bytes 4128 | tf_op jit(solution)/shard_map/all_to_all | solution.py:277
  17.6 12.5 %collective-permute-done.10.mirror_ref = bf16[2,256,256]{2,1,0:T(8,128)(2,1)S(1)} collective-permute-done((bf16[2,256,256]{2,1,0:T(8,128)(2,1)S(1)}, bf16[2,256,256]{2,1,0:T(8,128)(2,1)S(1)}, u32[]{:S(2)}, u32[]{:S(2)}) %collective-permute-start.10) | collective-permute-done | bytes 262176 | tf_op jit(solution)/shard_map/ppermute | solution.py:274
  30.0 1.4 %shard_map.79 = (bf16[32,32,128]{2,1,0:T(8,128)(2,1)S(1)}, bf16[32,32,128]{2,1,0:T(8,128)(2,1)S(1)}, bf16[32,32,128]{2,1,0:T(8,128)(2,1)S(1)}, bf16[32,32,128]{2,1,0:T(8,128)(2,1)S(1)}) custom-call(s32[2]{0:T(128)S(1)} %pad_add_fusion.place_ref, s32[8,128]{1,0:T(8,128)S(1)} %bitcast.15, bf16[3,2,256,256]{3,2,1,0:T(8,128)(2,1)S(1)} %copy-done, ...), custom_call_target="tpu_custom_call" | custom-call | tf_op jit(solution)/shard_map/pallas_call | solution.py:120
  31.4 1.7 %collective-permute-start.11 = (bf16[32,32,128]{2,1,0:T(8,128)(2,1)S(1)}, bf16[32,32,128]{2,1,0:T(8,128)(2,1)S(1)}, u32[]{:S(2)}, u32[]{:S(2)}) collective-permute-start(bf16[32,32,128]{2,1,0:T(8,128)(2,1)S(1)} %get-tuple-element.27), channel_id=1, source_target_pairs={{0,2},{1,3},{2,0},{3,1},{4,6},{5,7},{6,4},{7,5},{8,10},{9,11},{10,... | collective-permute-start | bytes 786440 | tf_op jit(solution)/shard_map/ppermute | solution.py:287
  33.2 1.8 %collective-permute-start.13 = (bf16[32,32,128]{2,1,0:T(8,128)(2,1)S(1)}, bf16[32,32,128]{2,1,0:T(8,128)(2,1)S(1)}, u32[]{:S(2)}, u32[]{:S(2)}) collective-permute-start(bf16[32,32,128]{2,1,0:T(8,128)(2,1)S(1)} %get-tuple-element.29), channel_id=1, source_target_pairs={{0,6},{1,7},{2,4},{3,5},{4,2},{5,3},{6,0},{7,1},{8,14},{9,15},{10,... | collective-permute-start | bytes 786440 | tf_op jit(solution)/shard_map/ppermute | solution.py:287
  35.7 1.4 %shard_map.78 = (bf16[32,32,128]{2,1,0:T(8,128)(2,1)S(1)}, bf16[32,32,128]{2,1,0:T(8,128)(2,1)S(1)}, bf16[32,32,128]{2,1,0:T(8,128)(2,1)S(1)}, bf16[32,32,128]{2,1,0:T(8,128)(2,1)S(1)}) custom-call(s32[2]{0:T(128)S(1)} %pad_add_fusion.place_ref, s32[8,128]{1,0:T(8,128)S(1)} %bitcast.16, bf16[3,2,256,256]{3,2,1,0:T(8,128)(2,1)S(1)} %copy-done, ...), custom_call_target="tpu_custom_call" | custom-call | tf_op jit(solution)/shard_map/pallas_call | solution.py:120
  37.1 1.8 %collective-permute-start.6 = (bf16[32,32,128]{2,1,0:T(8,128)(2,1)S(1)}, bf16[32,32,128]{2,1,0:T(8,128)(2,1)S(1)}, u32[]{:S(2)}, u32[]{:S(2)}) collective-permute-start(bf16[32,32,128]{2,1,0:T(8,128)(2,1)S(1)} %get-tuple-element.23), channel_id=1, source_target_pairs={{0,2},{1,3},{2,0},{3,1},{4,6},{5,7},{6,4},{7,5},{8,10},{9,11},{10,... | collective-permute-start | bytes 786440 | tf_op jit(solution)/shard_map/ppermute | solution.py:287
  38.9 1.6 %collective-permute-done.mirror_ref = bf16[2,256,256]{2,1,0:T(8,128)(2,1)S(1)} collective-permute-done((bf16[2,256,256]{2,1,0:T(8,128)(2,1)S(1)}, bf16[2,256,256]{2,1,0:T(8,128)(2,1)S(1)}, u32[]{:S(2)}, u32[]{:S(2)}) %collective-permute-start) | collective-permute-done | bytes 262176 | tf_op jit(solution)/shard_map/ppermute | solution.py:274
  41.2 1.4 %shard_map.77 = (bf16[32,32,128]{2,1,0:T(8,128)(2,1)S(1)}, bf16[32,32,128]{2,1,0:T(8,128)(2,1)S(1)}, bf16[32,32,128]{2,1,0:T(8,128)(2,1)S(1)}, bf16[32,32,128]{2,1,0:T(8,128)(2,1)S(1)}) custom-call(s32[2]{0:T(128)S(1)} %pad_add_fusion.place_ref, s32[8,128]{1,0:T(8,128)S(1)} %bitcast.17, bf16[3,2,256,256]{3,2,1,0:T(8,128)(2,1)S(1)} %copy-done, ...), custom_call_target="tpu_custom_call" | custom-call | tf_op jit(solution)/shard_map/pallas_call | solution.py:120
  42.6 2.4 %collective-permute-start.8 = (bf16[32,32,128]{2,1,0:T(8,128)(2,1)S(1)}, bf16[32,32,128]{2,1,0:T(8,128)(2,1)S(1)}, u32[]{:S(2)}, u32[]{:S(2)}) collective-permute-start(bf16[32,32,128]{2,1,0:T(8,128)(2,1)S(1)} %get-tuple-element.25), channel_id=1, source_target_pairs={{0,6},{1,7},{2,4},{3,5},{4,2},{5,3},{6,0},{7,1},{8,14},{9,15},{10,... | collective-permute-start | bytes 786440 | tf_op jit(solution)/shard_map/ppermute | solution.py:287
  46.1 1.6 %collective-permute-start.1 = (bf16[32,32,128]{2,1,0:T(8,128)(2,1)S(1)}, bf16[32,32,128]{2,1,0:T(8,128)(2,1)S(1)}, u32[]{:S(2)}, u32[]{:S(2)}) collective-permute-start(bf16[32,32,128]{2,1,0:T(8,128)(2,1)S(1)} %get-tuple-element.19), channel_id=1, source_target_pairs={{0,2},{1,3},{2,0},{3,1},{4,6},{5,7},{6,4},{7,5},{8,10},{9,11},{10,... | collective-permute-start | bytes 786440 | tf_op jit(solution)/shard_map/ppermute | solution.py:287
  47.7 5.1 %collective-permute-done.13 = bf16[32,32,128]{2,1,0:T(8,128)(2,1)S(1)} collective-permute-done((bf16[32,32,128]{2,1,0:T(8,128)(2,1)S(1)}, bf16[32,32,128]{2,1,0:T(8,128)(2,1)S(1)}, u32[]{:S(2)}, u32[]{:S(2)}) %collective-permute-start.13) | collective-permute-done | bytes 262176 | tf_op jit(solution)/shard_map/ppermute | solution.py:287
  52.8 2.0 %collective-permute-start.3 = (bf16[32,32,128]{2,1,0:T(8,128)(2,1)S(1)}, bf16[32,32,128]{2,1,0:T(8,128)(2,1)S(1)}, u32[]{:S(2)}, u32[]{:S(2)}) collective-permute-start(bf16[32,32,128]{2,1,0:T(8,128)(2,1)S(1)} %get-tuple-element.21), channel_id=1, source_target_pairs={{0,6},{1,7},{2,4},{3,5},{4,2},{5,3},{6,0},{7,1},{8,14},{9,15},{10,... | collective-permute-start | bytes 786440 | tf_op jit(solution)/shard_map/ppermute | solution.py:287
  54.9 2.5 %collective-permute-done.7 = bf16[32,32,128]{2,1,0:T(8,128)(2,1)S(1)} collective-permute-done((bf16[32,32,128]{2,1,0:T(8,128)(2,1)S(1)}, bf16[32,32,128]{2,1,0:T(8,128)(2,1)S(1)}, u32[]{:S(2)}, u32[]{:S(2)}) %collective-permute-start.7) | collective-permute-done | bytes 262176 | tf_op jit(solution)/shard_map/ppermute | solution.py:287
  57.4 6.6 %collective-permute-done.8 = bf16[32,32,128]{2,1,0:T(8,128)(2,1)S(1)} collective-permute-done((bf16[32,32,128]{2,1,0:T(8,128)(2,1)S(1)}, bf16[32,32,128]{2,1,0:T(8,128)(2,1)S(1)}, u32[]{:S(2)}, u32[]{:S(2)}) %collective-permute-start.8) | collective-permute-done | bytes 262176 | tf_op jit(solution)/shard_map/ppermute | solution.py:287
  64.2 4.4 %collective-permute-done.2 = bf16[32,32,128]{2,1,0:T(8,128)(2,1)S(1)} collective-permute-done((bf16[32,32,128]{2,1,0:T(8,128)(2,1)S(1)}, bf16[32,32,128]{2,1,0:T(8,128)(2,1)S(1)}, u32[]{:S(2)}, u32[]{:S(2)}) %collective-permute-start.2) | collective-permute-done | bytes 262176 | tf_op jit(solution)/shard_map/ppermute | solution.py:287
  68.7 6.5 %collective-permute-done.3 = bf16[32,32,128]{2,1,0:T(8,128)(2,1)S(1)} collective-permute-done((bf16[32,32,128]{2,1,0:T(8,128)(2,1)S(1)}, bf16[32,32,128]{2,1,0:T(8,128)(2,1)S(1)}, u32[]{:S(2)}, u32[]{:S(2)}) %collective-permute-start.3) | collective-permute-done | bytes 262176 | tf_op jit(solution)/shard_map/ppermute | solution.py:287
  76.1 2.7 %shard_map.80.refs_0_ = f32[12,64,128]{2,1,0:T(8,128)S(1)} custom-call(s32[3,64]{1,0:T(4,128)S(1)} %copy-done.3, bf16[128,32,128]{2,1,0:T(8,128)(2,1)S(1)} %constant_dynamic-update-slice_fusion.2.win_ref, f32[64,128]{1,0:T(8,128)S(1)} %copy-done.1, f32[64,128]{1,0:T(8,128)S(1)} %copy-done.2), custom_call_target="tpu_custom_call" | custom-call | tf_op jit(solution)/shard_map/pallas_call | solution.py:246
  78.9 2.7 %shard_map.81.refs_0_ = f32[12,64,128]{2,1,0:T(8,128)S(1)} custom-call(s32[3,64]{1,0:T(4,128)S(1)} %copy-done.3, bf16[128,32,128]{2,1,0:T(8,128)(2,1)S(1)} %constant_dynamic-update-slice_fusion.1.win_ref, f32[12,64,128]{2,1,0:T(8,128)S(1)} %shard_map.80.refs_0_), custom_call_target="tpu_custom_call" | custom-call | tf_op jit(solution)/shard_map/pallas_call | solution.py:246
  81.8 3.5 %shard_map.82 = (f32[64,2,128]{2,1,0:T(2,128)}, f32[64,4,128]{2,1,0:T(4,128)}) custom-call(s32[3,64]{1,0:T(4,128)S(1)} %copy-done.3, bf16[128,32,128]{2,1,0:T(8,128)(2,1)S(1)} %constant_dynamic-update-slice_fusion.win_ref, f32[12,64,128]{2,1,0:T(8,128)S(1)} %shard_map.81.refs_0_), custom_call_target="tpu_custom_call" | custom-call | tf_op jit(solution)/shard_map/pallas_call | solution.py:246
  (46 shorter events, 7.0 us)
Async XLA Ops:
  0.6 29.4 %copy-start = (bf16[3,2,256,256]{3,2,1,0:T(8,128)(2,1)S(1)}, bf16[3,2,256,256]{3,2,1,0:T(8,128)(2,1)}, u32[]{:S(2)}) copy-start(bf16[3,2,256,256]{3,2,1,0:T(8,128)(2,1)} %own_ref.5) | copy-start | bytes 2359300
  1.9 28.1 %collective-permute-start.10 = (bf16[2,256,256]{2,1,0:T(8,128)(2,1)S(1)}, bf16[2,256,256]{2,1,0:T(8,128)(2,1)S(1)}, u32[]{:S(2)}, u32[]{:S(2)}) collective-permute-start(bf16[2,256,256]{2,1,0:T(8,128)(2,1)S(1)} %get-tuple-element.30), channel_id=1, source_target_pairs={{0,8},{1,9},{2,10},{3,11},{4,12},{5,13},{6,14},{7,15},{8,0},{9,1},... | collective-permute-start | bytes 786440 | tf_op jit(solution)/shard_map/ppermute | solution.py:274
  6.0 0.7 copy-start.4
  9.1 8.5 %all-to-all-start = ((s32[8,1,128]{2,1,0:T(1,128)}), s32[8,1,128]{2,1,0:T(1,128)S(1)}, u32[]{:S(2)}, u32[]{:S(2)}) async-start(s32[8,1,128]{2,1,0:T(1,128)} %bitcast.19), calls=%async_computation | async-start | bytes 8192 | tf_op jit(solution)/shard_map/all_to_all | solution.py:277
  12.9 22.8 %collective-permute-start.5 = (bf16[2,256,256]{2,1,0:T(8,128)(2,1)S(1)}, bf16[2,256,256]{2,1,0:T(8,128)(2,1)S(1)}, u32[]{:S(2)}, u32[]{:S(2)}) collective-permute-start(bf16[2,256,256]{2,1,0:T(8,128)(2,1)S(1)} %get-tuple-element.31), channel_id=1, source_target_pairs={{0,8},{1,9},{2,10},{3,11},{4,12},{5,13},{6,14},{7,15},{8,0},{9,1},... | collective-permute-start | bytes 786440 | tf_op jit(solution)/shard_map/ppermute | solution.py:274
  13.2 27.3 %collective-permute-start = (bf16[2,256,256]{2,1,0:T(8,128)(2,1)S(1)}, bf16[2,256,256]{2,1,0:T(8,128)(2,1)S(1)}, u32[]{:S(2)}, u32[]{:S(2)}) collective-permute-start(bf16[2,256,256]{2,1,0:T(8,128)(2,1)S(1)} %get-tuple-element.32), channel_id=1, source_target_pairs={{0,8},{1,9},{2,10},{3,11},{4,12},{5,13},{6,14},{7,15},{8,0},{9,1},... | collective-permute-start | bytes 786440 | tf_op jit(solution)/shard_map/ppermute | solution.py:274
  31.4 11.2 %collective-permute-start.11 = (bf16[32,32,128]{2,1,0:T(8,128)(2,1)S(1)}, bf16[32,32,128]{2,1,0:T(8,128)(2,1)S(1)}, u32[]{:S(2)}, u32[]{:S(2)}) collective-permute-start(bf16[32,32,128]{2,1,0:T(8,128)(2,1)S(1)} %get-tuple-element.27), channel_id=1, source_target_pairs={{0,2},{1,3},{2,0},{3,1},{4,6},{5,7},{6,4},{7,5},{8,10},{9,11},{10,... | collective-permute-start | bytes 786440 | tf_op jit(solution)/shard_map/ppermute | solution.py:287
  33.2 12.9 %collective-permute-start.12 = (bf16[32,32,128]{2,1,0:T(8,128)(2,1)S(1)}, bf16[32,32,128]{2,1,0:T(8,128)(2,1)S(1)}, u32[]{:S(2)}, u32[]{:S(2)}) collective-permute-start(bf16[32,32,128]{2,1,0:T(8,128)(2,1)S(1)} %get-tuple-element.28), channel_id=1, source_target_pairs={{0,4},{1,5},{2,6},{3,7},{4,0},{5,1},{6,2},{7,3},{8,12},{9,13},{10,... | collective-permute-start | bytes 786440 | tf_op jit(solution)/shard_map/ppermute | solution.py:287
  33.2 19.6 %collective-permute-start.13 = (bf16[32,32,128]{2,1,0:T(8,128)(2,1)S(1)}, bf16[32,32,128]{2,1,0:T(8,128)(2,1)S(1)}, u32[]{:S(2)}, u32[]{:S(2)}) collective-permute-start(bf16[32,32,128]{2,1,0:T(8,128)(2,1)S(1)} %get-tuple-element.29), channel_id=1, source_target_pairs={{0,6},{1,7},{2,4},{3,5},{4,2},{5,3},{6,0},{7,1},{8,14},{9,15},{10,... | collective-permute-start | bytes 786440 | tf_op jit(solution)/shard_map/ppermute | solution.py:287
  37.1 15.7 %collective-permute-start.6 = (bf16[32,32,128]{2,1,0:T(8,128)(2,1)S(1)}, bf16[32,32,128]{2,1,0:T(8,128)(2,1)S(1)}, u32[]{:S(2)}, u32[]{:S(2)}) collective-permute-start(bf16[32,32,128]{2,1,0:T(8,128)(2,1)S(1)} %get-tuple-element.23), channel_id=1, source_target_pairs={{0,2},{1,3},{2,0},{3,1},{4,6},{5,7},{6,4},{7,5},{8,10},{9,11},{10,... | collective-permute-start | bytes 786440 | tf_op jit(solution)/shard_map/ppermute | solution.py:287
  40.5 16.9 %collective-permute-start.7 = (bf16[32,32,128]{2,1,0:T(8,128)(2,1)S(1)}, bf16[32,32,128]{2,1,0:T(8,128)(2,1)S(1)}, u32[]{:S(2)}, u32[]{:S(2)}) collective-permute-start(bf16[32,32,128]{2,1,0:T(8,128)(2,1)S(1)} %get-tuple-element.24), channel_id=1, source_target_pairs={{0,4},{1,5},{2,6},{3,7},{4,0},{5,1},{6,2},{7,3},{8,12},{9,13},{10,... | collective-permute-start | bytes 786440 | tf_op jit(solution)/shard_map/ppermute | solution.py:287
  42.6 21.4 %collective-permute-start.8 = (bf16[32,32,128]{2,1,0:T(8,128)(2,1)S(1)}, bf16[32,32,128]{2,1,0:T(8,128)(2,1)S(1)}, u32[]{:S(2)}, u32[]{:S(2)}) collective-permute-start(bf16[32,32,128]{2,1,0:T(8,128)(2,1)S(1)} %get-tuple-element.25), channel_id=1, source_target_pairs={{0,6},{1,7},{2,4},{3,5},{4,2},{5,3},{6,0},{7,1},{8,14},{9,15},{10,... | collective-permute-start | bytes 786440 | tf_op jit(solution)/shard_map/ppermute | solution.py:287
  46.1 18.1 %collective-permute-start.1 = (bf16[32,32,128]{2,1,0:T(8,128)(2,1)S(1)}, bf16[32,32,128]{2,1,0:T(8,128)(2,1)S(1)}, u32[]{:S(2)}, u32[]{:S(2)}) collective-permute-start(bf16[32,32,128]{2,1,0:T(8,128)(2,1)S(1)} %get-tuple-element.19), channel_id=1, source_target_pairs={{0,2},{1,3},{2,0},{3,1},{4,6},{5,7},{6,4},{7,5},{8,10},{9,11},{10,... | collective-permute-start | bytes 786440 | tf_op jit(solution)/shard_map/ppermute | solution.py:287
  52.8 15.8 %collective-permute-start.2 = (bf16[32,32,128]{2,1,0:T(8,128)(2,1)S(1)}, bf16[32,32,128]{2,1,0:T(8,128)(2,1)S(1)}, u32[]{:S(2)}, u32[]{:S(2)}) collective-permute-start(bf16[32,32,128]{2,1,0:T(8,128)(2,1)S(1)} %get-tuple-element.20), channel_id=1, source_target_pairs={{0,4},{1,5},{2,6},{3,7},{4,0},{5,1},{6,2},{7,3},{8,12},{9,13},{10,... | collective-permute-start | bytes 786440 | tf_op jit(solution)/shard_map/ppermute | solution.py:287
  52.8 22.3 %collective-permute-start.3 = (bf16[32,32,128]{2,1,0:T(8,128)(2,1)S(1)}, bf16[32,32,128]{2,1,0:T(8,128)(2,1)S(1)}, u32[]{:S(2)}, u32[]{:S(2)}) collective-permute-start(bf16[32,32,128]{2,1,0:T(8,128)(2,1)S(1)} %get-tuple-element.21), channel_id=1, source_target_pairs={{0,6},{1,7},{2,4},{3,5},{4,2},{5,3},{6,0},{7,1},{8,14},{9,15},{10,... | collective-permute-start | bytes 786440 | tf_op jit(solution)/shard_map/ppermute | solution.py:287
  57.4 18.0 %collective-permute-start.14 = (bf16[64,32,128]{2,1,0:T(8,128)(2,1)S(1)}, bf16[64,32,128]{2,1,0:T(8,128)(2,1)S(1)}, u32[]{:S(2)}, u32[]{:S(2)}) collective-permute-start(bf16[64,32,128]{2,1,0:T(8,128)(2,1)S(1)} %pad_maximum_fusion.2), channel_id=1, source_target_pairs={{0,1},{1,0},{2,3},{3,2},{4,5},{5,4},{6,7},{7,6},{8,9},{9,8},{10,11... | collective-permute-start | bytes 1572872 | tf_op jit(solution)/shard_map/ppermute | solution.py:290
  64.1 14.7 %collective-permute-start.9 = (bf16[64,32,128]{2,1,0:T(8,128)(2,1)S(1)}, bf16[64,32,128]{2,1,0:T(8,128)(2,1)S(1)}, u32[]{:S(2)}, u32[]{:S(2)}) collective-permute-start(bf16[64,32,128]{2,1,0:T(8,128)(2,1)S(1)} %pad_maximum_fusion.1), channel_id=1, source_target_pairs={{0,1},{1,0},{2,3},{3,2},{4,5},{5,4},{6,7},{7,6},{8,9},{9,8},{10,11... | collective-permute-start | bytes 1572872 | tf_op jit(solution)/shard_map/ppermute | solution.py:290
  75.3 6.4 %collective-permute-start.4 = (bf16[64,32,128]{2,1,0:T(8,128)(2,1)S(1)}, bf16[64,32,128]{2,1,0:T(8,128)(2,1)S(1)}, u32[]{:S(2)}, u32[]{:S(2)}) collective-permute-start(bf16[64,32,128]{2,1,0:T(8,128)(2,1)S(1)} %pad_maximum_fusion), channel_id=1, source_target_pairs={{0,1},{1,0},{2,3},{3,2},{4,5},{5,4},{6,7},{7,6},{8,9},{9,8},{10,11... | collective-permute-start | bytes 1572872 | tf_op jit(solution)/shard_map/ppermute | solution.py:290
  75.4 0.8 copy-start.1
  75.4 0.8 copy-start.2
  75.4 0.8 copy-start.3

commit v6 on v4

--- a/solution.py
+++ b/solution.py
@@ -30,94 +30,120 @@
     )
 
 
-def prep_kernel(peers, halves, cap, tile_ref, row_ref, col_ref, req_ref, slot_ref):
-    relays = peers // halves
-    nblk = tile_ref.shape[1]
-    lanes = req_ref.shape[1]
-    owner = lax.broadcasted_iota(jnp.int32, (peers, nblk), 0)
+def ranks(peers, tile_ref, plane):
+    nblk = tile_ref.shape[2]
+    tile = tile_ref[plane]
+    hit = (lax.broadcasted_iota(jnp.int32, (peers, nblk), 0) == tile).astype(jnp.float32)
     earlier = (
         lax.broadcasted_iota(jnp.int32, (nblk, nblk), 1)
         < lax.broadcasted_iota(jnp.int32, (nblk, nblk), 0)
     ).astype(jnp.float32).astype(jnp.bfloat16)
+    before = dot_last(hit.astype(jnp.bfloat16), earlier)
+    return tile, hit, jnp.sum(before * hit, axis=0, keepdims=True).astype(jnp.int32)
+
+
+def want_kernel(peers, cap, tile_ref, row_ref, col_ref, req_ref):
+    nblk = tile_ref.shape[2]
+    relays, lanes = req_ref.shape
     lane = lax.broadcasted_iota(jnp.int32, (lanes, nblk), 0)
     rows = jnp.zeros((relays, lanes), jnp.float32)
     cols = jnp.zeros((relays, lanes), jnp.float32)
     for k in range(PLANES):
-        tile = tile_ref[k : k + 1, :]
-        hit = (owner == tile).astype(jnp.float32)
-        hit16 = hit.astype(jnp.bfloat16)
-        before = dot_last(hit16, earlier)
-        rank = jnp.sum(before * hit, axis=0, keepdims=True).astype(jnp.int32)
-        side = tile // relays
-        rank = rank + side * cap
-        slot_ref[k : k + 1, :] = (tile - side * relays) * (halves * cap) + rank
-        here = lane == (rank + k * halves * cap)
+        tile, hit, rank = ranks(peers, tile_ref, k)
+        here = lane == (rank + (tile // relays + 2 * k) * cap)
         zero = jnp.zeros((), jnp.float32)
         row = jnp.where(here, row_ref[k : k + 1, :].astype(jnp.float32), zero)
         col = jnp.where(here, col_ref[k : k + 1, :].astype(jnp.float32), zero)
-        fold = sum(hit[h * relays : (h + 1) * relays] for h in range(halves)).astype(jnp.bfloat16)
+        fold = (hit[:relays] + hit[relays:]).astype(jnp.bfloat16)
         rows += dot_last(fold, row.astype(jnp.bfloat16))
         cols += dot_last(fold, col.astype(jnp.bfloat16))
     req_ref[...] = rows.astype(jnp.int32) * 65536 + cols.astype(jnp.int32)
 
 
-def prep(tile_map, row_anchor, col_anchor, peers, halves, cap):
-    nblk = tile_map.shape[1]
-    lanes = -(-PLANES * halves * cap // 128) * 128
+def want(tile_map, row_anchor, col_anchor, peers, cap):
+    lanes = -(-PLANES * 2 * cap // 128) * 128
     return pl.pallas_call(
-        functools.partial(prep_kernel, peers, halves, cap),
-        out_shape=(
-            jax.ShapeDtypeStruct((peers // halves, lanes), jnp.int32),
-            jax.ShapeDtypeStruct((PLANES, nblk), jnp.int32),
-        ),
+        functools.partial(want_kernel, peers, cap),
+        out_shape=jax.ShapeDtypeStruct((peers // 2, lanes), jnp.int32),
         in_specs=[whole()] * 3,
-        out_specs=(whole(), whole()),
-        name="prep",
+        out_specs=whole(),
+        name="want",
     )(tile_map, row_anchor, col_anchor)
 
 
-def cut_kernel(plane, cap, side_ref, req_ref, own_ref, mirror_ref, out_ref, half_ref):
-    parts = own_ref.shape[3] // WC
-    for c in range(2):
-        for h in range(parts):
-            lanes = slice(h * WC, (h + 1) * WC)
-            half_ref[c * parts + h] = own_ref[plane, c, :, lanes].astype(jnp.float32)
-            half_ref[(2 + c) * parts + h] = mirror_ref[c, :, lanes].astype(jnp.float32)
+def slot_kernel(peers, cap, direct, place_ref, tile_ref, slot_ref):
+    relays = peers // 2
+    for k in range(PLANES):
+        tile, _, rank = ranks(peers, tile_ref, k)
+        side = tile // relays
+        relay = (tile - side * relays) ^ place_ref[1]
+        if not direct:
+            relay = (relay & 1) * (relays // 2) + (relay >> 1)
+        far = (side != place_ref[0]).astype(jnp.int32)
+        slot_ref[k : k + 1, :] = (far * relays + relay) * cap + rank
+
+
+def find_slots(place, tile_map, peers, cap, direct):
+    return pl.pallas_call(
+        functools.partial(slot_kernel, peers, cap, direct),
+        out_shape=jax.ShapeDtypeStruct((PLANES, tile_map.shape[2]), jnp.int32),
+        in_specs=[whole(SMEM), whole()],
+        out_specs=whole(),
+        name="slots",
+    )(place, tile_map)
+
+
+def cut_kernel(planes, cap, mirrored, place_ref, req_ref, sheet_ref, *refs):
+    out_refs, half_ref = refs[:-1], refs[-1]
+    parts = sheet_ref.shape[-1] // WC
+    for at, k in enumerate(planes):
+        for c in range(2):
+            for h in range(parts):
+                lanes = slice(h * WC, (h + 1) * WC)
+                part = sheet_ref[c, :, lanes] if mirrored else sheet_ref[k, c, :, lanes]
+                half_ref[(at * 2 + c) * parts + h] = part.astype(jnp.float32)
     lane = lax.broadcasted_iota(jnp.int32, (WR, WC), 1)
-    side = side_ref[0]
-    each = 2 * cap
-
-    def one(source, carry):
-        for place in range(each):
-            packed = req_ref[source, plane * each + place]
-            base = jnp.where(side == place // cap, 0, 2 * parts)
-            row = packed >> 16
-            col = packed & 65535
-            turn = (WC - col) & (WC - 1)
-            left = lane < WC - col
-            for c in range(2):
-                part = [
-                    pltpu.roll(half_ref[base + c * parts + h, pl.ds(row, WR), :], turn, 1)
-                    for h in range(parts)
-                ]
-                out_ref[source * each + place, c * WR : (c + 1) * WR, :] = jnp.where(
-                    left, part[0], part[1]
-                ).astype(jnp.bfloat16)
+    me = place_ref[1]
+    side = 1 - place_ref[0] if mirrored else place_ref[0]
+    span = req_ref.shape[0] // len(out_refs)
+
+    def one(now, carry):
+        for m, out_ref in enumerate(out_refs):
+            source = (m * span + now) ^ me
+            for at, k in enumerate(planes):
+                for place in range(cap):
+                    packed = req_ref[source, (2 * k + side) * cap + place]
+                    row = packed >> 16
+                    col = packed & 65535
+                    turn = (WC - col) & (WC - 1)
+                    left = lane < WC - col
+                    slot = (now * len(planes) + at) * cap + place
+                    for c in range(2):
+                        part = [
+                            pltpu.roll(half_ref[(at * 2 + c) * parts + h, pl.ds(row, WR), :], turn, 1)
+                            for h in range(parts)
+                        ]
+                        out_ref[slot, c * WR : (c + 1) * WR, :] = jnp.where(
+                            left, part[0], part[1]
+                        ).astype(jnp.bfloat16)
         return carry
 
-    lax.fori_loop(0, req_ref.shape[0], one, 0)
-
-
-def cut(plane, cap, side, requests, sheet, mirror):
-    count = requests.shape[0] * 2 * cap
+    lax.fori_loop(0, span, one, 0)
+
+
+def cut(planes, cap, outs, place, requests, sheet):
+    mirrored = sheet.ndim == 3
+    count = requests.shape[0] // outs * len(planes) * cap
+    height, width = sheet.shape[-2:]
     return pl.pallas_call(
-        functools.partial(cut_kernel, plane, cap),
-        out_shape=jax.ShapeDtypeStruct((count, 2 * WR, WC), jnp.bfloat16),
-        in_specs=[whole(SMEM), whole(SMEM), whole(), whole()],
-        out_specs=whole(),
-        scratch_shapes=[VMEM((4 * sheet.shape[3] // WC, sheet.shape[2], WC), jnp.float32)],
+        functools.partial(cut_kernel, planes, cap, mirrored),
+        out_shape=(jax.ShapeDtypeStruct((count, 2 * WR, WC), jnp.bfloat16),) * outs,
+        in_specs=[whole(SMEM), whole(SMEM), whole()],
+        out_specs=(whole(),) * outs,
+        scratch_shapes=[VMEM((len(planes) * 2 * width // WC, height, WC), jnp.float32)],
         compiler_params=GRANT,
-    )(side, requests, sheet, mirror)
+        name="cut",
+    )(place, requests, sheet)
 
 
 def taps(pos):
@@ -254,28 +280,52 @@
     nblk = start_x.shape[0]
     cap = max(2, 2 * nblk // peers)
     relays = peers // 2
+    chips = relays // 2
+    direct = chips > 4 or chips & (chips - 1) != 0
+    outs = 1 if direct else chips
     groups = [[h * relays + r for r in range(relays)] for h in range(2)]
-    swap = [(i, (i + relays) % peers) for i in range(peers)]
-    mirrors = []
-    for plane in range(PLANES):
-        mirrors.append(lax.ppermute(gradients[plane], "sky", swap))
+    mirror_pairs = [(i, (i + relays) % peers) for i in range(peers)]
+
+    def swap(bits):
+        return [(i, i ^ bits) for i in range(peers)]
 
     def exchange(x):
         return lax.all_to_all(
             x, "sky", split_axis=0, concat_axis=0, axis_index_groups=groups, tiled=True
         )
 
-    requests, slots = prep(tile_map[:, :, 0], row_anchor, col_anchor, peers, 2, cap)
+    def ship(parts):
+        if direct:
+            return exchange(parts[0].reshape(relays, -1, 2 * WR, WC))
+        got = [parts[0]]
+        for m in range(1, chips):
+            got.append(lax.ppermute(parts[m], "sky", swap(2 * m)))
+        half = parts[0].shape[0] // 2
+        mine = [part[:half] for part in got]
+        other = jnp.concatenate([part[half:] for part in got], axis=0)
+        other = lax.ppermute(other, "sky", swap(1))
+        return jnp.concatenate(mine + [other], axis=0).reshape(relays, -1, 2 * WR, WC)
+
+    mirrors = []
+    for plane in range(PLANES):
+        mirrors.append(lax.ppermute(gradients[plane], "sky", mirror_pairs))
+    index = lax.axis_index("sky").astype(jnp.int32)
+    place = jnp.stack([index // relays, jnp.zeros_like(index) if direct else index % relays])
+    tiles = tile_map.transpose(0, 2, 1)
+    requests = want(tiles, row_anchor, col_anchor, peers, cap)
     asked = exchange(requests)
-    side = (lax.axis_index("sky") // relays).astype(jnp.int32).reshape(1)
-    received = []
+    slots = find_slots(place, tiles, peers, cap, direct)
+    parts = cut(tuple(range(PLANES)), cap, outs, place, asked, gradients)
+    own = ship(parts).reshape(relays, PLANES, cap, 2 * WR, WC)
+    windows = []
     for plane in range(PLANES):
-        windows = cut(plane, cap, side, asked, gradients, mirrors[plane])
-        got = exchange(windows.reshape(relays, 2 * cap, 2 * WR, WC))
-        received.append(got.reshape(peers * cap, 2 * WR, WC))
+        parts = cut((plane,), cap, outs, place, asked, mirrors[plane])
+        far = ship(parts)
+        both = [x.reshape(relays * cap, 2 * WR, WC) for x in (own[:, plane], far)]
+        windows.append(jnp.concatenate(both, axis=0))
     state = (start_x, start_y)
     for plane in range(PLANES):
-        state = interp(plane, slots, received[plane], state)
+        state = interp(plane, slots, windows[plane], state)
     return state
 
 

time: 96.5 us -> 106 us (1.098)
  waiting for transfers between devices: 47.2 us -> 60.2 us
  starting transfers between devices: 25.7 us -> 19.8 us
  local copies, waits for them, and re-layouts: 2.48 us -> 5.78 us
  Pallas kernels: 19.8 us -> 17 us
  other arithmetic: 0 us -> 1.72 us
    ppermute x3 -> x19, waiting for transfers between devices: 34.2 us -> 55.7 us  [the longest x3 29.3 us: body(): mirrors.append(lax.ppermute(gradients[plane], 'sky', mirror_pairs))]
    all_to_all x4 -> x1, starting transfers between devices: 18.9 us -> 5.28 us  [exchange(): lax.all_to_all(x, 'sky', split_axis=0, concat_axis=0, axis_index_groups=g...]
    all_to_all x4 -> x1, waiting for transfers between devices: 13 us -> 4.52 us  [exchange(): lax.all_to_all(x, 'sky', split_axis=0, concat_axis=0, axis_index_groups=g...]
    ppermute x3 -> x19, starting transfers between devices: 6.88 us -> 14.5 us  [the longest x12 8.81 us: ship(): got.append(lax.ppermute(parts[m], 'sky', swap(2 * m)))]
    concatenate x0 -> x4, local copies, waits for them, and re-layouts: none -> 3.06 us  [the longest x3 2.96 us: body(): windows.append(jnp.concatenate(both, axis=0))]
    pallas_call x4 -> x6, Pallas kernels: 10.2 us -> 8.12 us  [the longest x4 4.87 us: cut(): pl.pallas_call(functools.partial(cut_kernel, planes, cap, mirrored), out_...]
    concatenate x0 -> x4, other arithmetic: none -> 1.65 us  [ship(): other = jnp.concatenate([part[half:] for part in got], axis=0)]
    squeeze x1, local copies, waits for them, and re-layouts: 1.23 us -> 0.05 us  [body(): mirrors.append(lax.ppermute(gradients[plane], 'sky', mirror_pairs))]
  transfers between devices with their start and end apart: 7 -> 20, of which waited for: 5 -> 11; matrix products, arithmetic and copies ran while one was open for 1% -> 4% of each run, Pallas kernels for 13% -> 10%
where the time goes in v6:
time: 106 us; the launch traced here: 105 us
  waiting for transfers between devices  60.2 us (57%)
  starting transfers between devices  19.8 us (19%)
  Pallas kernels  17 us (16%)
  local copies, waits for them, and re-layouts  5.78 us (5%)
  other arithmetic  1.72 us (2%)
    ppermute x3, waiting for transfers between devices, body(): mirrors.append(lax.ppermute(gradients[plane], 'sky', mirror_pairs))  29.3 us
    ppermute x12, waiting for transfers between devices, ship(): got.append(lax.ppermute(parts[m], 'sky', swap(2 * m)))  26.4 us
    pallas_call x3, Pallas kernels, interp(): pl.pallas_call(functools.partial(interp_kernel, plane), out_shape=out_sha...  8.92 us
    ppermute x12, starting transfers between devices, ship(): got.append(lax.ppermute(parts[m], 'sky', swap(2 * m)))  8.81 us
    ppermute x3, starting transfers between devices, body(): mirrors.append(lax.ppermute(gradients[plane], 'sky', mirror_pairs))  5.58 us
    all_to_all x1, starting transfers between devices, exchange(): lax.all_to_all(x, 'sky', split_axis=0, concat_axis=0, axis_index_groups=g...  5.28 us
    pallas_call x4, Pallas kernels, cut(): pl.pallas_call(functools.partial(cut_kernel, planes, cap, mirrored), out_...  4.87 us
    all_to_all x1, waiting for transfers between devices, exchange(): lax.all_to_all(x, 'sky', split_axis=0, concat_axis=0, axis_index_groups=g...  4.52 us
  transfers between devices with their start and end apart: 20, of which 11 were waited for; matrix products, arithmetic and copies ran while one was open for 4% of the time, Pallas kernels for 10%

profile of v6, /device:TPU:0, one launch (start us, length us, event | category | flops | bytes accessed | tf_op | source)
XLA Modules:
  0.0 105.5 jit_solution(16672750626984697516)
XLA Ops:
  0.6 1.8 %want.1 = s32[8,128]{1,0:T(8,128)} custom-call(s32[3,1,64]{2,1,0:T(1,128)} %bitcast.32, s32[3,64]{1,0:T(4,128)} %row_ref.1, s32[3,64]{1,0:T(4,128)} %col_ref.1), custom_call_target="tpu_custom_call" | custom-call | tf_op jit(solution)/shard_map/want/pallas_call | solution.py:65
  2.5 5.3 %all-to-all-start = ((s32[8,1,128]{2,1,0:T(1,128)}), s32[8,1,128]{2,1,0:T(1,128)S(1)}, u32[]{:S(2)}, u32[]{:S(2)}) async-start(s32[8,1,128]{2,1,0:T(1,128)} %bitcast.31), calls=%async_computation | async-start | bytes 8192 | tf_op jit(solution)/shard_map/all_to_all | solution.py:293
  7.8 4.5 %all-to-all-done = s32[8,1,128]{2,1,0:T(1,128)S(1)} async-done(((s32[8,1,128]{2,1,0:T(1,128)}), s32[8,1,128]{2,1,0:T(1,128)S(1)}, u32[]{:S(2)}, u32[]{:S(2)}) %all-to-all-start) | async-done | bytes 4128 | tf_op jit(solution)/shard_map/all_to_all | solution.py:293
  12.3 1.1 %copy-done = bf16[3,2,256,256]{3,2,1,0:T(8,128)(2,1)S(1)} copy-done((bf16[3,2,256,256]{3,2,1,0:T(8,128)(2,1)S(1)}, bf16[3,2,256,256]{3,2,1,0:T(8,128)(2,1)}, u32[]{:S(2)}) %copy-start) | copy-done | bytes 786456
  13.5 1.7 %cut.4 = (bf16[48,32,128]{2,1,0:T(8,128)(2,1)S(1)}, bf16[48,32,128]{2,1,0:T(8,128)(2,1)S(1)}, bf16[48,32,128]{2,1,0:T(8,128)(2,1)S(1)}, bf16[48,32,128]{2,1,0:T(8,128)(2,1)S(1)}) custom-call(s32[2]{0:T(128)S(1)} %pad_add_fusion.place_ref, s32[8,128]{1,0:T(8,128)S(1)} %bitcast.23, bf16[3,2,256,256]{3,2,1,0:T(8,128)(2,1)S(1)} %copy-done), custom_call_target="tpu_custom_call" | custom-call | tf_op jit(solution)/shard_map/cut/pallas_call | solution.py:138
  16.4 2.4 %collective-permute-start.2 = (bf16[48,32,128]{2,1,0:T(8,128)(2,1)S(1)}, bf16[48,32,128]{2,1,0:T(8,128)(2,1)S(1)}, u32[]{:S(2)}, u32[]{:S(2)}) collective-permute-start(bf16[48,32,128]{2,1,0:T(8,128)(2,1)S(1)} %get-tuple-element.21), channel_id=1, source_target_pairs={{0,6},{1,7},{2,4},{3,5},{4,2},{5,3},{6,0},{7,1},{8,14},{9,15},{10,... | collective-permute-start | bytes 1179656 | tf_op jit(solution)/shard_map/ppermute | solution.py:302
  18.7 7.6 %collective-permute-done = bf16[48,32,128]{2,1,0:T(8,128)(2,1)S(1)} collective-permute-done((bf16[48,32,128]{2,1,0:T(8,128)(2,1)S(1)}, bf16[48,32,128]{2,1,0:T(8,128)(2,1)S(1)}, u32[]{:S(2)}, u32[]{:S(2)}) %collective-permute-start) | collective-permute-done | bytes 393248 | tf_op jit(solution)/shard_map/ppermute | solution.py:302
  26.3 1.4 %collective-permute-done.1 = bf16[48,32,128]{2,1,0:T(8,128)(2,1)S(1)} collective-permute-done((bf16[48,32,128]{2,1,0:T(8,128)(2,1)S(1)}, bf16[48,32,128]{2,1,0:T(8,128)(2,1)S(1)}, u32[]{:S(2)}, u32[]{:S(2)}) %collective-permute-start.1) | collective-permute-done | bytes 393248 | tf_op jit(solution)/shard_map/ppermute | solution.py:302
  27.8 7.8 %collective-permute-done.2 = bf16[48,32,128]{2,1,0:T(8,128)(2,1)S(1)} collective-permute-done((bf16[48,32,128]{2,1,0:T(8,128)(2,1)S(1)}, bf16[48,32,128]{2,1,0:T(8,128)(2,1)S(1)}, u32[]{:S(2)}, u32[]{:S(2)}) %collective-permute-start.2) | collective-permute-done | bytes 393248 | tf_op jit(solution)/shard_map/ppermute | solution.py:302
  36.0 2.7 %collective-permute-start.14 = (bf16[2,256,256]{2,1,0:T(8,128)(2,1)S(1)}, bf16[2,256,256]{2,1,0:T(8,128)(2,1)S(1)}, u32[]{:S(2)}, u32[]{:S(2)}) collective-permute-start(bf16[2,256,256]{2,1,0:T(8,128)(2,1)S(1)} %get-tuple-element.37), channel_id=1, source_target_pairs={{0,8},{1,9},{2,10},{3,11},{4,12},{5,13},{6,14},{7,15},{8,0},{9,1},... | collective-permute-start | bytes 786440 | tf_op jit(solution)/shard_map/ppermute | solution.py:311
  39.0 2.6 %collective-permute-start.4 = (bf16[2,256,256]{2,1,0:T(8,128)(2,1)S(1)}, bf16[2,256,256]{2,1,0:T(8,128)(2,1)S(1)}, u32[]{:S(2)}, u32[]{:S(2)}) collective-permute-start(bf16[2,256,256]{2,1,0:T(8,128)(2,1)S(1)} %get-tuple-element.38), channel_id=1, source_target_pairs={{0,8},{1,9},{2,10},{3,11},{4,12},{5,13},{6,14},{7,15},{8,0},{9,1},... | collective-permute-start | bytes 786440 | tf_op jit(solution)/shard_map/ppermute | solution.py:311
  41.6 21.0 %collective-permute-done.14.sheet_ref = bf16[2,256,256]{2,1,0:T(8,128)(2,1)S(1)} collective-permute-done((bf16[2,256,256]{2,1,0:T(8,128)(2,1)S(1)}, bf16[2,256,256]{2,1,0:T(8,128)(2,1)S(1)}, u32[]{:S(2)}, u32[]{:S(2)}) %collective-permute-start.14) | collective-permute-done | bytes 262176 | tf_op jit(solution)/shard_map/ppermute | solution.py:311
  64.4 3.9 %collective-permute-done.9.sheet_ref = bf16[2,256,256]{2,1,0:T(8,128)(2,1)S(1)} collective-permute-done((bf16[2,256,256]{2,1,0:T(8,128)(2,1)S(1)}, bf16[2,256,256]{2,1,0:T(8,128)(2,1)S(1)}, u32[]{:S(2)}, u32[]{:S(2)}) %collective-permute-start.9) | collective-permute-done | bytes 262176 | tf_op jit(solution)/shard_map/ppermute | solution.py:311
  69.4 4.4 %collective-permute-done.4.sheet_ref = bf16[2,256,256]{2,1,0:T(8,128)(2,1)S(1)} collective-permute-done((bf16[2,256,256]{2,1,0:T(8,128)(2,1)S(1)}, bf16[2,256,256]{2,1,0:T(8,128)(2,1)S(1)}, u32[]{:S(2)}, u32[]{:S(2)}) %collective-permute-start.4) | collective-permute-done | bytes 262176 | tf_op jit(solution)/shard_map/ppermute | solution.py:311
  74.4 1.1 %cut.5 = (bf16[16,32,128]{2,1,0:T(8,128)(2,1)S(1)}, bf16[16,32,128]{2,1,0:T(8,128)(2,1)S(1)}, bf16[16,32,128]{2,1,0:T(8,128)(2,1)S(1)}, bf16[16,32,128]{2,1,0:T(8,128)(2,1)S(1)}) custom-call(s32[2]{0:T(128)S(1)} %pad_add_fusion.place_ref, s32[8,128]{1,0:T(8,128)S(1)} %bitcast.26, bf16[2,256,256]{2,1,0:T(8,128)(2,1)S(1)} %collective-permute-done.4.sheet_ref), custom_call_target="tpu_custom_call" | custom-call | tf_op jit(solution)/shard_map/cut/pallas_call | solution.py:138
  76.2 3.0 %collective-permute-start.12 = (bf16[16,32,128]{2,1,0:T(8,128)(2,1)S(1)}, bf16[16,32,128]{2,1,0:T(8,128)(2,1)S(1)}, u32[]{:S(2)}, u32[]{:S(2)}) collective-permute-start(bf16[16,32,128]{2,1,0:T(8,128)(2,1)S(1)} %get-tuple-element.29), channel_id=1, source_target_pairs={{0,6},{1,7},{2,4},{3,5},{4,2},{5,3},{6,0},{7,1},{8,14},{9,15},{10,... | collective-permute-start | bytes 393224 | tf_op jit(solution)/shard_map/ppermute | solution.py:302
  80.0 2.9 %collective-permute-done.10 = bf16[16,32,128]{2,1,0:T(8,128)(2,1)S(1)} collective-permute-done((bf16[16,32,128]{2,1,0:T(8,128)(2,1)S(1)}, bf16[16,32,128]{2,1,0:T(8,128)(2,1)S(1)}, u32[]{:S(2)}, u32[]{:S(2)}) %collective-permute-start.10) | collective-permute-done | bytes 131104 | tf_op jit(solution)/shard_map/ppermute | solution.py:302
  83.1 2.5 %collective-permute-done.12 = bf16[16,32,128]{2,1,0:T(8,128)(2,1)S(1)} collective-permute-done((bf16[16,32,128]{2,1,0:T(8,128)(2,1)S(1)}, bf16[16,32,128]{2,1,0:T(8,128)(2,1)S(1)}, u32[]{:S(2)}, u32[]{:S(2)}) %collective-permute-start.12) | collective-permute-done | bytes 131104 | tf_op jit(solution)/shard_map/ppermute | solution.py:302
  86.5 1.4 %collective-permute-done.5 = bf16[16,32,128]{2,1,0:T(8,128)(2,1)S(1)} collective-permute-done((bf16[16,32,128]{2,1,0:T(8,128)(2,1)S(1)}, bf16[16,32,128]{2,1,0:T(8,128)(2,1)S(1)}, u32[]{:S(2)}, u32[]{:S(2)}) %collective-permute-start.5) | collective-permute-done | bytes 131104 | tf_op jit(solution)/shard_map/ppermute | solution.py:302
  88.0 2.7 %collective-permute-done.7 = bf16[16,32,128]{2,1,0:T(8,128)(2,1)S(1)} collective-permute-done((bf16[16,32,128]{2,1,0:T(8,128)(2,1)S(1)}, bf16[16,32,128]{2,1,0:T(8,128)(2,1)S(1)}, u32[]{:S(2)}, u32[]{:S(2)}) %collective-permute-start.7) | collective-permute-done | bytes 131104 | tf_op jit(solution)/shard_map/ppermute | solution.py:302
  91.4 1.4 %slots.1.slot_ref = s32[3,64]{1,0:T(4,128)} custom-call(s32[2]{0:T(128)} %copy-done.5, s32[3,1,64]{2,1,0:T(1,128)} %bitcast.33), custom_call_target="tpu_custom_call" | custom-call | tf_op jit(solution)/shard_map/slots/pallas_call | solution.py:87
  94.6 2.7 %shard_map.77.refs_0_ = f32[12,64,128]{2,1,0:T(8,128)S(1)} custom-call(s32[3,64]{1,0:T(4,128)S(1)} %copy-done.4, bf16[128,32,128]{2,1,0:T(8,128)(2,1)S(1)} %constant_dynamic-update-slice_fusion.5.win_ref, f32[64,128]{1,0:T(8,128)S(1)} %copy-done.2, f32[64,128]{1,0:T(8,128)S(1)} %copy-done.3), custom_call_target="tpu_custom_call" | custom-call | tf_op jit(solution)/shard_map/pallas_call | solution.py:265
  98.3 2.7 %shard_map.78.refs_0_ = f32[12,64,128]{2,1,0:T(8,128)S(1)} custom-call(s32[3,64]{1,0:T(4,128)S(1)} %copy-done.4, bf16[128,32,128]{2,1,0:T(8,128)(2,1)S(1)} %constant_dynamic-update-slice_fusion.3.win_ref, f32[12,64,128]{2,1,0:T(8,128)S(1)} %shard_map.77.refs_0_), custom_call_target="tpu_custom_call" | custom-call | tf_op jit(solution)/shard_map/pallas_call | solution.py:265
  102.0 3.5 %shard_map.79 = (f32[64,2,128]{2,1,0:T(2,128)}, f32[64,4,128]{2,1,0:T(4,128)}) custom-call(s32[3,64]{1,0:T(4,128)S(1)} %copy-done.4, bf16[128,32,128]{2,1,0:T(8,128)(2,1)S(1)} %constant_dynamic-update-slice_fusion.1.win_ref, f32[12,64,128]{2,1,0:T(8,128)S(1)} %shard_map.78.refs_0_), custom_call_target="tpu_custom_call" | custom-call | tf_op jit(solution)/shard_map/pallas_call | solution.py:265
  (67 shorter events, 12.5 us)
Async XLA Ops:
  2.5 9.9 %all-to-all-start = ((s32[8,1,128]{2,1,0:T(1,128)}), s32[8,1,128]{2,1,0:T(1,128)S(1)}, u32[]{:S(2)}, u32[]{:S(2)}) async-start(s32[8,1,128]{2,1,0:T(1,128)} %bitcast.31), calls=%async_computation | async-start | bytes 8192 | tf_op jit(solution)/shard_map/all_to_all | solution.py:293
  7.8 66.6 %copy-start.5 = (s32[2]{0:T(128)}, s32[2]{0:T(128)S(1)}, u32[]{:S(2)}) copy-start(s32[2]{0:T(128)S(1)} %pad_add_fusion.place_ref) | copy-start | bytes 28
  15.2 11.1 %collective-permute-start = (bf16[48,32,128]{2,1,0:T(8,128)(2,1)S(1)}, bf16[48,32,128]{2,1,0:T(8,128)(2,1)S(1)}, u32[]{:S(2)}, u32[]{:S(2)}) collective-permute-start(bf16[48,32,128]{2,1,0:T(8,128)(2,1)S(1)} %get-tuple-element.19), channel_id=1, source_target_pairs={{0,2},{1,3},{2,0},{3,1},{4,6},{5,7},{6,4},{7,5},{8,10},{9,11},{10,... | collective-permute-start | bytes 1179656 | tf_op jit(solution)/shard_map/ppermute | solution.py:302
  15.8 12.0 %collective-permute-start.1 = (bf16[48,32,128]{2,1,0:T(8,128)(2,1)S(1)}, bf16[48,32,128]{2,1,0:T(8,128)(2,1)S(1)}, u32[]{:S(2)}, u32[]{:S(2)}) collective-permute-start(bf16[48,32,128]{2,1,0:T(8,128)(2,1)S(1)} %get-tuple-element.20), channel_id=1, source_target_pairs={{0,4},{1,5},{2,6},{3,7},{4,0},{5,1},{6,2},{7,3},{8,12},{9,13},{10,... | collective-permute-start | bytes 1179656 | tf_op jit(solution)/shard_map/ppermute | solution.py:302
  16.4 19.3 %collective-permute-start.2 = (bf16[48,32,128]{2,1,0:T(8,128)(2,1)S(1)}, bf16[48,32,128]{2,1,0:T(8,128)(2,1)S(1)}, u32[]{:S(2)}, u32[]{:S(2)}) collective-permute-start(bf16[48,32,128]{2,1,0:T(8,128)(2,1)S(1)} %get-tuple-element.21), channel_id=1, source_target_pairs={{0,6},{1,7},{2,4},{3,5},{4,2},{5,3},{6,0},{7,1},{8,14},{9,15},{10,... | collective-permute-start | bytes 1179656 | tf_op jit(solution)/shard_map/ppermute | solution.py:302
  27.8 8.1 %copy-start.1 = (bf16[3,2,256,256]{3,2,1,0:T(8,128)(2,1)S(1)}, bf16[3,2,256,256]{3,2,1,0:T(8,128)(2,1)}, u32[]{:S(2)}) copy-start(bf16[3,2,256,256]{3,2,1,0:T(8,128)(2,1)} %sheet_ref.1) | copy-start | bytes 2359300
  35.8 39.6 %collective-permute-start.3 = (bf16[96,32,128]{2,1,0:T(8,128)(2,1)S(1)}, bf16[96,32,128]{2,1,0:T(8,128)(2,1)S(1)}, u32[]{:S(2)}, u32[]{:S(2)}) collective-permute-start(bf16[96,32,128]{2,1,0:T(8,128)(2,1)S(1)} %pad_maximum_fusion), channel_id=1, source_target_pairs={{0,1},{1,0},{2,3},{3,2},{4,5},{5,4},{6,7},{7,6},{8,9},{9,8},{10,11... | collective-permute-start | bytes 2359304 | tf_op jit(solution)/shard_map/ppermute | solution.py:306
  36.0 26.6 %collective-permute-start.14 = (bf16[2,256,256]{2,1,0:T(8,128)(2,1)S(1)}, bf16[2,256,256]{2,1,0:T(8,128)(2,1)S(1)}, u32[]{:S(2)}, u32[]{:S(2)}) collective-permute-start(bf16[2,256,256]{2,1,0:T(8,128)(2,1)S(1)} %get-tuple-element.37), channel_id=1, source_target_pairs={{0,8},{1,9},{2,10},{3,11},{4,12},{5,13},{6,14},{7,15},{8,0},{9,1},... | collective-permute-start | bytes 786440 | tf_op jit(solution)/shard_map/ppermute | solution.py:311
  38.6 29.7 %collective-permute-start.9 = (bf16[2,256,256]{2,1,0:T(8,128)(2,1)S(1)}, bf16[2,256,256]{2,1,0:T(8,128)(2,1)S(1)}, u32[]{:S(2)}, u32[]{:S(2)}) collective-permute-start(bf16[2,256,256]{2,1,0:T(8,128)(2,1)S(1)} %get-tuple-element.39), channel_id=1, source_target_pairs={{0,8},{1,9},{2,10},{3,11},{4,12},{5,13},{6,14},{7,15},{8,0},{9,1},... | collective-permute-start | bytes 786440 | tf_op jit(solution)/shard_map/ppermute | solution.py:311
  39.0 34.9 %collective-permute-start.4 = (bf16[2,256,256]{2,1,0:T(8,128)(2,1)S(1)}, bf16[2,256,256]{2,1,0:T(8,128)(2,1)S(1)}, u32[]{:S(2)}, u32[]{:S(2)}) collective-permute-start(bf16[2,256,256]{2,1,0:T(8,128)(2,1)S(1)} %get-tuple-element.38), channel_id=1, source_target_pairs={{0,8},{1,9},{2,10},{3,11},{4,12},{5,13},{6,14},{7,15},{8,0},{9,1},... | collective-permute-start | bytes 786440 | tf_op jit(solution)/shard_map/ppermute | solution.py:311
  63.7 12.5 %collective-permute-start.15 = (bf16[16,32,128]{2,1,0:T(8,128)(2,1)S(1)}, bf16[16,32,128]{2,1,0:T(8,128)(2,1)S(1)}, u32[]{:S(2)}, u32[]{:S(2)}) collective-permute-start(bf16[16,32,128]{2,1,0:T(8,128)(2,1)S(1)} %get-tuple-element.31), channel_id=1, source_target_pairs={{0,2},{1,3},{2,0},{3,1},{4,6},{5,7},{6,4},{7,5},{8,10},{9,11},{10,... | collective-permute-start | bytes 393224 | tf_op jit(solution)/shard_map/ppermute | solution.py:302
  64.2 15.0 %collective-permute-start.16 = (bf16[16,32,128]{2,1,0:T(8,128)(2,1)S(1)}, bf16[16,32,128]{2,1,0:T(8,128)(2,1)S(1)}, u32[]{:S(2)}, u32[]{:S(2)}) collective-permute-start(bf16[16,32,128]{2,1,0:T(8,128)(2,1)S(1)} %get-tuple-element.32), channel_id=1, source_target_pairs={{0,4},{1,5},{2,6},{3,7},{4,0},{5,1},{6,2},{7,3},{8,12},{9,13},{10,... | collective-permute-start | bytes 393224 | tf_op jit(solution)/shard_map/ppermute | solution.py:302
  68.3 11.6 %collective-permute-start.17 = (bf16[16,32,128]{2,1,0:T(8,128)(2,1)S(1)}, bf16[16,32,128]{2,1,0:T(8,128)(2,1)S(1)}, u32[]{:S(2)}, u32[]{:S(2)}) collective-permute-start(bf16[16,32,128]{2,1,0:T(8,128)(2,1)S(1)} %get-tuple-element.33), channel_id=1, source_target_pairs={{0,6},{1,7},{2,4},{3,5},{4,2},{5,3},{6,0},{7,1},{8,14},{9,15},{10,... | collective-permute-start | bytes 393224 | tf_op jit(solution)/shard_map/ppermute | solution.py:302
  73.8 9.0 %collective-permute-start.10 = (bf16[16,32,128]{2,1,0:T(8,128)(2,1)S(1)}, bf16[16,32,128]{2,1,0:T(8,128)(2,1)S(1)}, u32[]{:S(2)}, u32[]{:S(2)}) collective-permute-start(bf16[16,32,128]{2,1,0:T(8,128)(2,1)S(1)} %get-tuple-element.27), channel_id=1, source_target_pairs={{0,2},{1,3},{2,0},{3,1},{4,6},{5,7},{6,4},{7,5},{8,10},{9,11},{10,... | collective-permute-start | bytes 393224 | tf_op jit(solution)/shard_map/ppermute | solution.py:302
  75.5 7.5 %collective-permute-start.11 = (bf16[16,32,128]{2,1,0:T(8,128)(2,1)S(1)}, bf16[16,32,128]{2,1,0:T(8,128)(2,1)S(1)}, u32[]{:S(2)}, u32[]{:S(2)}) collective-permute-start(bf16[16,32,128]{2,1,0:T(8,128)(2,1)S(1)} %get-tuple-element.28), channel_id=1, source_target_pairs={{0,4},{1,5},{2,6},{3,7},{4,0},{5,1},{6,2},{7,3},{8,12},{9,13},{10,... | collective-permute-start | bytes 393224 | tf_op jit(solution)/shard_map/ppermute | solution.py:302
  76.2 9.4 %collective-permute-start.12 = (bf16[16,32,128]{2,1,0:T(8,128)(2,1)S(1)}, bf16[16,32,128]{2,1,0:T(8,128)(2,1)S(1)}, u32[]{:S(2)}, u32[]{:S(2)}) collective-permute-start(bf16[16,32,128]{2,1,0:T(8,128)(2,1)S(1)} %get-tuple-element.29), channel_id=1, source_target_pairs={{0,6},{1,7},{2,4},{3,5},{4,2},{5,3},{6,0},{7,1},{8,14},{9,15},{10,... | collective-permute-start | bytes 393224 | tf_op jit(solution)/shard_map/ppermute | solution.py:302
  79.2 8.7 %collective-permute-start.5 = (bf16[16,32,128]{2,1,0:T(8,128)(2,1)S(1)}, bf16[16,32,128]{2,1,0:T(8,128)(2,1)S(1)}, u32[]{:S(2)}, u32[]{:S(2)}) collective-permute-start(bf16[16,32,128]{2,1,0:T(8,128)(2,1)S(1)} %get-tuple-element.23), channel_id=1, source_target_pairs={{0,2},{1,3},{2,0},{3,1},{4,6},{5,7},{6,4},{7,5},{8,10},{9,11},{10,... | collective-permute-start | bytes 393224 | tf_op jit(solution)/shard_map/ppermute | solution.py:302
  79.9 8.1 %collective-permute-start.6 = (bf16[16,32,128]{2,1,0:T(8,128)(2,1)S(1)}, bf16[16,32,128]{2,1,0:T(8,128)(2,1)S(1)}, u32[]{:S(2)}, u32[]{:S(2)}) collective-permute-start(bf16[16,32,128]{2,1,0:T(8,128)(2,1)S(1)} %get-tuple-element.24), channel_id=1, source_target_pairs={{0,4},{1,5},{2,6},{3,7},{4,0},{5,1},{6,2},{7,3},{8,12},{9,13},{10,... | collective-permute-start | bytes 393224 | tf_op jit(solution)/shard_map/ppermute | solution.py:302
  82.9 7.8 %collective-permute-start.7 = (bf16[16,32,128]{2,1,0:T(8,128)(2,1)S(1)}, bf16[16,32,128]{2,1,0:T(8,128)(2,1)S(1)}, u32[]{:S(2)}, u32[]{:S(2)}) collective-permute-start(bf16[16,32,128]{2,1,0:T(8,128)(2,1)S(1)} %get-tuple-element.25), channel_id=1, source_target_pairs={{0,6},{1,7},{2,4},{3,5},{4,2},{5,3},{6,0},{7,1},{8,14},{9,15},{10,... | collective-permute-start | bytes 393224 | tf_op jit(solution)/shard_map/ppermute | solution.py:302
  83.0 9.9 %collective-permute-start.18 = (bf16[32,32,128]{2,1,0:T(8,128)(2,1)S(1)}, bf16[32,32,128]{2,1,0:T(8,128)(2,1)}, u32[]{:S(2)}, u32[]{:S(2)}) collective-permute-start(bf16[32,32,128]{2,1,0:T(8,128)(2,1)S(1)} %pad_maximum_fusion.3), channel_id=1, source_target_pairs={{0,1},{1,0},{2,3},{3,2},{4,5},{5,4},{6,7},{7,6},{8,9},{9,8},{10,11... | collective-permute-start | bytes 786440 | tf_op jit(solution)/shard_map/ppermute | solution.py:306
  86.4 10.8 %collective-permute-start.13 = (bf16[32,32,128]{2,1,0:T(8,128)(2,1)}, bf16[32,32,128]{2,1,0:T(8,128)(2,1)}, u32[]{:S(2)}, u32[]{:S(2)}) collective-permute-start(bf16[32,32,128]{2,1,0:T(8,128)(2,1)} %pad_maximum_fusion.2), channel_id=1, source_target_pairs={{0,1},{1,0},{2,3},{3,2},{4,5},{5,4},{6,7},{7,6},{8,9},{9,8},{10,11... | collective-permute-start | bytes 786440 | tf_op jit(solution)/shard_map/ppermute | solution.py:306
  86.4 7.4 %copy-start.2 = (f32[64,128]{1,0:T(8,128)S(1)}, f32[64,128]{1,0:T(8,128)}, u32[]{:S(2)}) copy-start(f32[64,128]{1,0:T(8,128)} %refs_0_.1) | copy-start | bytes 98308
  86.4 7.4 %copy-start.3 = (f32[64,128]{1,0:T(8,128)S(1)}, f32[64,128]{1,0:T(8,128)}, u32[]{:S(2)}) copy-start(f32[64,128]{1,0:T(8,128)} %refs_1_.1) | copy-start | bytes 98308
  91.4 9.6 %collective-permute-start.8 = (bf16[32,32,128]{2,1,0:T(8,128)(2,1)}, bf16[32,32,128]{2,1,0:T(8,128)(2,1)}, u32[]{:S(2)}, u32[]{:S(2)}) collective-permute-start(bf16[32,32,128]{2,1,0:T(8,128)(2,1)} %pad_maximum_fusion.1), channel_id=1, source_target_pairs={{0,1},{1,0},{2,3},{3,2},{4,5},{5,4},{6,7},{7,6},{8,9},{9,8},{10,11... | collective-permute-start | bytes 786440 | tf_op jit(solution)/shard_map/ppermute | solution.py:306
  (2 other events, 1.8 us)

commit v7 on v6

--- a/solution.py
+++ b/solution.py
@@ -89,6 +89,7 @@
         out_shape=jax.ShapeDtypeStruct((PLANES, tile_map.shape[2]), jnp.int32),
         in_specs=[whole(SMEM), whole()],
         out_specs=whole(),
+        compiler_params=GRANT,
         name="slots",
     )(place, tile_map)
 
@@ -306,13 +307,16 @@
         other = lax.ppermute(other, "sky", swap(1))
         return jnp.concatenate(mine + [other], axis=0).reshape(relays, -1, 2 * WR, WC)
 
-    mirrors = []
-    for plane in range(PLANES):
-        mirrors.append(lax.ppermute(gradients[plane], "sky", mirror_pairs))
+    def mirror(plane, sheet):
+        return lax.ppermute(sheet[plane], "sky", mirror_pairs)
+
     index = lax.axis_index("sky").astype(jnp.int32)
     place = jnp.stack([index // relays, jnp.zeros_like(index) if direct else index % relays])
     tiles = tile_map.transpose(0, 2, 1)
     requests = want(tiles, row_anchor, col_anchor, peers, cap)
+    mirrors = [mirror(0, gradients)]
+    requests, late = lax.optimization_barrier((requests, gradients))
+    mirrors += [mirror(plane, late) for plane in range(1, PLANES)]
     asked = exchange(requests)
     slots = find_slots(place, tiles, peers, cap, direct)
     parts = cut(tuple(range(PLANES)), cap, outs, place, asked, gradients)

time: 106 us -> 101 us (0.953)
  local copies, waits for them, and re-layouts: 5.78 us -> 2.26 us
  other arithmetic: 1.72 us -> 0.29 us
    concatenate x3, local copies, waits for them, and re-layouts: 2.96 us -> 0.11 us  [body(): windows.append(jnp.concatenate(both, axis=0))]
    concatenate x4, other arithmetic: 1.65 us -> 0.21 us  [ship(): other = jnp.concatenate([part[half:] for part in got], axis=0)]
  transfers between devices with their start and end apart: 20 -> 20, of which waited for: 11 -> 11; matrix products, arithmetic and copies ran while one was open for 4% -> 1% of each run, Pallas kernels for 10% -> 9%
where the time goes in v7:
time: 101 us
  waiting for transfers between devices  60.7 us (60%)
  starting transfers between devices  20 us (20%)
  Pallas kernels  16.3 us (16%)
  local copies, waits for them, and re-layouts  2.26 us (2%)
  between operations  1.02 us (1%)
    ppermute x3, waiting for transfers between devices, mirror(): return lax.ppermute(sheet[plane], 'sky', mirror_pairs)  29.2 us
    ppermute x12, waiting for transfers between devices, ship(): got.append(lax.ppermute(parts[m], 'sky', swap(2 * m)))  27 us
    pallas_call x3, Pallas kernels, interp(): pl.pallas_call(functools.partial(interp_kernel, plane), out_shape=out_sha...  8.95 us
    ppermute x12, starting transfers between devices, ship(): got.append(lax.ppermute(parts[m], 'sky', swap(2 * m)))  8.81 us
    ppermute x3, starting transfers between devices, mirror(): return lax.ppermute(sheet[plane], 'sky', mirror_pairs)  5.64 us
    all_to_all x1, starting transfers between devices, exchange(): lax.all_to_all(x, 'sky', split_axis=0, concat_axis=0, axis_index_groups=g...  5.28 us
    pallas_call x4, Pallas kernels, cut(): pl.pallas_call(functools.partial(cut_kernel, planes, cap, mirrored), out_...  4.87 us
    all_to_all x1, waiting for transfers between devices, exchange(): lax.all_to_all(x, 'sky', split_axis=0, concat_axis=0, axis_index_groups=g...  4.53 us
  transfers between devices with their start and end apart: 20, of which 11 were waited for; matrix products, arithmetic and copies ran while one was open for 1% of the time, Pallas kernels for 9%

profile of v7, /device:TPU:0, one launch (start us, length us, event | category | flops | bytes accessed | tf_op | source)
XLA Modules:
  0.0 100.6 jit_solution(8366759998749194086)
XLA Ops:
  0.6 1.8 %want.1 = s32[8,128]{1,0:T(8,128)} custom-call(s32[3,1,64]{2,1,0:T(1,128)} %bitcast.27, s32[3,64]{1,0:T(4,128)} %row_ref.1, s32[3,64]{1,0:T(4,128)} %col_ref.1), custom_call_target="tpu_custom_call" | custom-call | tf_op jit(solution)/shard_map/want/pallas_call | solution.py:65
  2.5 5.3 %all-to-all-start = ((s32[8,1,128]{2,1,0:T(1,128)}), s32[8,1,128]{2,1,0:T(1,128)S(1)}, u32[]{:S(2)}, u32[]{:S(2)}) async-start(s32[8,1,128]{2,1,0:T(1,128)} %bitcast.33), calls=%async_computation | async-start | bytes 8192 | tf_op jit(solution)/shard_map/all_to_all | solution.py:294
  7.8 4.5 %all-to-all-done = s32[8,1,128]{2,1,0:T(1,128)S(1)} async-done(((s32[8,1,128]{2,1,0:T(1,128)}), s32[8,1,128]{2,1,0:T(1,128)S(1)}, u32[]{:S(2)}, u32[]{:S(2)}) %all-to-all-start) | async-done | bytes 4128 | tf_op jit(solution)/shard_map/all_to_all | solution.py:294
  12.3 1.1 %copy-done = bf16[3,2,256,256]{3,2,1,0:T(8,128)(2,1)S(1)} copy-done((bf16[3,2,256,256]{3,2,1,0:T(8,128)(2,1)S(1)}, bf16[3,2,256,256]{3,2,1,0:T(8,128)(2,1)}, u32[]{:S(2)}) %copy-start) | copy-done | bytes 786456
  13.5 1.7 %cut.4 = (bf16[48,32,128]{2,1,0:T(8,128)(2,1)S(1)}, bf16[48,32,128]{2,1,0:T(8,128)(2,1)S(1)}, bf16[48,32,128]{2,1,0:T(8,128)(2,1)S(1)}, bf16[48,32,128]{2,1,0:T(8,128)(2,1)S(1)}) custom-call(s32[2]{0:T(128)S(1)} %pad_add_fusion.place_ref, s32[8,128]{1,0:T(8,128)S(1)} %bitcast.23, bf16[3,2,256,256]{3,2,1,0:T(8,128)(2,1)S(1)} %copy-done), custom_call_target="tpu_custom_call" | custom-call | tf_op jit(solution)/shard_map/cut/pallas_call | solution.py:139
  16.4 2.4 %collective-permute-start.2 = (bf16[48,32,128]{2,1,0:T(8,128)(2,1)S(1)}, bf16[48,32,128]{2,1,0:T(8,128)(2,1)S(1)}, u32[]{:S(2)}, u32[]{:S(2)}) collective-permute-start(bf16[48,32,128]{2,1,0:T(8,128)(2,1)S(1)} %get-tuple-element.24), channel_id=1, source_target_pairs={{0,6},{1,7},{2,4},{3,5},{4,2},{5,3},{6,0},{7,1},{8,14},{9,15},{10,... | collective-permute-start | bytes 1179656 | tf_op jit(solution)/shard_map/ppermute | solution.py:303
  18.7 7.6 %collective-permute-done = bf16[48,32,128]{2,1,0:T(8,128)(2,1)S(1)} collective-permute-done((bf16[48,32,128]{2,1,0:T(8,128)(2,1)S(1)}, bf16[48,32,128]{2,1,0:T(8,128)(2,1)S(1)}, u32[]{:S(2)}, u32[]{:S(2)}) %collective-permute-start) | collective-permute-done | bytes 393248 | tf_op jit(solution)/shard_map/ppermute | solution.py:303
  26.3 1.4 %collective-permute-done.1 = bf16[48,32,128]{2,1,0:T(8,128)(2,1)S(1)} collective-permute-done((bf16[48,32,128]{2,1,0:T(8,128)(2,1)S(1)}, bf16[48,32,128]{2,1,0:T(8,128)(2,1)S(1)}, u32[]{:S(2)}, u32[]{:S(2)}) %collective-permute-start.1) | collective-permute-done | bytes 393248 | tf_op jit(solution)/shard_map/ppermute | solution.py:303
  27.8 7.8 %collective-permute-done.2 = bf16[48,32,128]{2,1,0:T(8,128)(2,1)S(1)} collective-permute-done((bf16[48,32,128]{2,1,0:T(8,128)(2,1)S(1)}, bf16[48,32,128]{2,1,0:T(8,128)(2,1)S(1)}, u32[]{:S(2)}, u32[]{:S(2)}) %collective-permute-start.2) | collective-permute-done | bytes 393248 | tf_op jit(solution)/shard_map/ppermute | solution.py:303
  35.9 2.7 %collective-permute-start.14 = (bf16[2,256,256]{2,1,0:T(8,128)(2,1)S(1)}, bf16[2,256,256]{2,1,0:T(8,128)(2,1)S(1)}, u32[]{:S(2)}, u32[]{:S(2)}) collective-permute-start(bf16[2,256,256]{2,1,0:T(8,128)(2,1)S(1)} %slice_bitcast_fusion), channel_id=1, source_target_pairs={{0,8},{1,9},{2,10},{3,11},{4,12},{5,13},{6,14},{7,15},{8,0},{9,1},... | collective-permute-start | bytes 786440 | tf_op jit(solution)/shard_map/ppermute | solution.py:311
  39.0 2.6 %collective-permute-start.4 = (bf16[2,256,256]{2,1,0:T(8,128)(2,1)S(1)}, bf16[2,256,256]{2,1,0:T(8,128)(2,1)S(1)}, u32[]{:S(2)}, u32[]{:S(2)}) collective-permute-start(bf16[2,256,256]{2,1,0:T(8,128)(2,1)S(1)} %get-tuple-element.42), channel_id=1, source_target_pairs={{0,8},{1,9},{2,10},{3,11},{4,12},{5,13},{6,14},{7,15},{8,0},{9,1},... | collective-permute-start | bytes 786440 | tf_op jit(solution)/shard_map/ppermute | solution.py:311
  41.6 20.9 %collective-permute-done.14.sheet_ref = bf16[2,256,256]{2,1,0:T(8,128)(2,1)S(1)} collective-permute-done((bf16[2,256,256]{2,1,0:T(8,128)(2,1)S(1)}, bf16[2,256,256]{2,1,0:T(8,128)(2,1)S(1)}, u32[]{:S(2)}, u32[]{:S(2)}) %collective-permute-start.14) | collective-permute-done | bytes 262176 | tf_op jit(solution)/shard_map/ppermute | solution.py:311
  64.4 3.9 %collective-permute-done.9.sheet_ref = bf16[2,256,256]{2,1,0:T(8,128)(2,1)S(1)} collective-permute-done((bf16[2,256,256]{2,1,0:T(8,128)(2,1)S(1)}, bf16[2,256,256]{2,1,0:T(8,128)(2,1)S(1)}, u32[]{:S(2)}, u32[]{:S(2)}) %collective-permute-start.9) | collective-permute-done | bytes 262176 | tf_op jit(solution)/shard_map/ppermute | solution.py:311
  68.3 1.1 %cut.6 = (bf16[16,32,128]{2,1,0:T(8,128)(2,1)S(1)}, bf16[16,32,128]{2,1,0:T(8,128)(2,1)S(1)}, bf16[16,32,128]{2,1,0:T(8,128)(2,1)S(1)}, bf16[16,32,128]{2,1,0:T(8,128)(2,1)S(1)}) custom-call(s32[2]{0:T(128)S(1)} %pad_add_fusion.place_ref, s32[8,128]{1,0:T(8,128)S(1)} %bitcast.25, bf16[2,256,256]{2,1,0:T(8,128)(2,1)S(1)} %collective-permute-done.9.sheet_ref), custom_call_target="tpu_custom_call" | custom-call | tf_op jit(solution)/shard_map/cut/pallas_call | solution.py:139
  69.4 4.4 %collective-permute-done.4.sheet_ref = bf16[2,256,256]{2,1,0:T(8,128)(2,1)S(1)} collective-permute-done((bf16[2,256,256]{2,1,0:T(8,128)(2,1)S(1)}, bf16[2,256,256]{2,1,0:T(8,128)(2,1)S(1)}, u32[]{:S(2)}, u32[]{:S(2)}) %collective-permute-start.4) | collective-permute-done | bytes 262176 | tf_op jit(solution)/shard_map/ppermute | solution.py:311
  74.4 1.1 %cut.5 = (bf16[16,32,128]{2,1,0:T(8,128)(2,1)S(1)}, bf16[16,32,128]{2,1,0:T(8,128)(2,1)S(1)}, bf16[16,32,128]{2,1,0:T(8,128)(2,1)S(1)}, bf16[16,32,128]{2,1,0:T(8,128)(2,1)S(1)}) custom-call(s32[2]{0:T(128)S(1)} %pad_add_fusion.place_ref, s32[8,128]{1,0:T(8,128)S(1)} %bitcast.26, bf16[2,256,256]{2,1,0:T(8,128)(2,1)S(1)} %collective-permute-done.4.sheet_ref), custom_call_target="tpu_custom_call" | custom-call | tf_op jit(solution)/shard_map/cut/pallas_call | solution.py:139
  76.2 3.0 %collective-permute-start.12 = (bf16[16,32,128]{2,1,0:T(8,128)(2,1)S(1)}, bf16[16,32,128]{2,1,0:T(8,128)(2,1)S(1)}, u32[]{:S(2)}, u32[]{:S(2)}) collective-permute-start(bf16[16,32,128]{2,1,0:T(8,128)(2,1)S(1)} %get-tuple-element.33), channel_id=1, source_target_pairs={{0,6},{1,7},{2,4},{3,5},{4,2},{5,3},{6,0},{7,1},{8,14},{9,15},{10,... | collective-permute-start | bytes 393224 | tf_op jit(solution)/shard_map/ppermute | solution.py:303
  79.9 2.9 %collective-permute-done.10 = bf16[16,32,128]{2,1,0:T(8,128)(2,1)S(1)} collective-permute-done((bf16[16,32,128]{2,1,0:T(8,128)(2,1)S(1)}, bf16[16,32,128]{2,1,0:T(8,128)(2,1)S(1)}, u32[]{:S(2)}, u32[]{:S(2)}) %collective-permute-start.10) | collective-permute-done | bytes 131104 | tf_op jit(solution)/shard_map/ppermute | solution.py:303
  83.1 2.5 %collective-permute-done.12 = bf16[16,32,128]{2,1,0:T(8,128)(2,1)S(1)} collective-permute-done((bf16[16,32,128]{2,1,0:T(8,128)(2,1)S(1)}, bf16[16,32,128]{2,1,0:T(8,128)(2,1)S(1)}, u32[]{:S(2)}, u32[]{:S(2)}) %collective-permute-start.12) | collective-permute-done | bytes 131104 | tf_op jit(solution)/shard_map/ppermute | solution.py:303
  85.9 2.0 %collective-permute-done.5 = bf16[16,32,128]{2,1,0:T(8,128)(2,1)S(1)} collective-permute-done((bf16[16,32,128]{2,1,0:T(8,128)(2,1)S(1)}, bf16[16,32,128]{2,1,0:T(8,128)(2,1)S(1)}, u32[]{:S(2)}, u32[]{:S(2)}) %collective-permute-start.5) | collective-permute-done | bytes 131104 | tf_op jit(solution)/shard_map/ppermute | solution.py:303
  87.9 2.7 %collective-permute-done.7 = bf16[16,32,128]{2,1,0:T(8,128)(2,1)S(1)} collective-permute-done((bf16[16,32,128]{2,1,0:T(8,128)(2,1)S(1)}, bf16[16,32,128]{2,1,0:T(8,128)(2,1)S(1)}, u32[]{:S(2)}, u32[]{:S(2)}) %collective-permute-start.7) | collective-permute-done | bytes 131104 | tf_op jit(solution)/shard_map/ppermute | solution.py:303
  91.6 2.7 %shard_map.77.refs_0_ = f32[12,64,128]{2,1,0:T(8,128)S(1)} custom-call(s32[3,64]{1,0:T(4,128)S(1)} %slots.1.slot_ref, bf16[128,32,128]{2,1,0:T(8,128)(2,1)S(1)} %constant_dynamic-update-slice_fusion.5.win_ref, f32[64,128]{1,0:T(8,128)S(1)} %copy-done.2, f32[64,128]{1,0:T(8,128)S(1)} %copy-done.3), custom_call_target="tpu_custom_call" | custom-call | tf_op jit(solution)/shard_map/pallas_call | solution.py:266
  94.3 2.7 %shard_map.78.refs_0_ = f32[12,64,128]{2,1,0:T(8,128)S(1)} custom-call(s32[3,64]{1,0:T(4,128)S(1)} %slots.1.slot_ref, bf16[128,32,128]{2,1,0:T(8,128)(2,1)S(1)} %constant_dynamic-update-slice_fusion.3.win_ref, f32[12,64,128]{2,1,0:T(8,128)S(1)} %shard_map.77.refs_0_), custom_call_target="tpu_custom_call" | custom-call | tf_op jit(solution)/shard_map/pallas_call | solution.py:266
  97.1 3.5 %shard_map.79 = (f32[64,2,128]{2,1,0:T(2,128)}, f32[64,4,128]{2,1,0:T(4,128)}) custom-call(s32[3,64]{1,0:T(4,128)S(1)} %slots.1.slot_ref, bf16[128,32,128]{2,1,0:T(8,128)(2,1)S(1)} %constant_dynamic-update-slice_fusion.1.win_ref, f32[12,64,128]{2,1,0:T(8,128)S(1)} %shard_map.78.refs_0_), custom_call_target="tpu_custom_call" | custom-call | tf_op jit(solution)/shard_map/pallas_call | solution.py:266
  (66 shorter events, 7.4 us)
Async XLA Ops:
  2.5 9.9 %all-to-all-start = ((s32[8,1,128]{2,1,0:T(1,128)}), s32[8,1,128]{2,1,0:T(1,128)S(1)}, u32[]{:S(2)}, u32[]{:S(2)}) async-start(s32[8,1,128]{2,1,0:T(1,128)} %bitcast.33), calls=%async_computation | async-start | bytes 8192 | tf_op jit(solution)/shard_map/all_to_all | solution.py:294
  15.2 11.1 %collective-permute-start = (bf16[48,32,128]{2,1,0:T(8,128)(2,1)S(1)}, bf16[48,32,128]{2,1,0:T(8,128)(2,1)S(1)}, u32[]{:S(2)}, u32[]{:S(2)}) collective-permute-start(bf16[48,32,128]{2,1,0:T(8,128)(2,1)S(1)} %get-tuple-element.22), channel_id=1, source_target_pairs={{0,2},{1,3},{2,0},{3,1},{4,6},{5,7},{6,4},{7,5},{8,10},{9,11},{10,... | collective-permute-start | bytes 1179656 | tf_op jit(solution)/shard_map/ppermute | solution.py:303
  15.8 12.0 %collective-permute-start.1 = (bf16[48,32,128]{2,1,0:T(8,128)(2,1)S(1)}, bf16[48,32,128]{2,1,0:T(8,128)(2,1)S(1)}, u32[]{:S(2)}, u32[]{:S(2)}) collective-permute-start(bf16[48,32,128]{2,1,0:T(8,128)(2,1)S(1)} %get-tuple-element.23), channel_id=1, source_target_pairs={{0,4},{1,5},{2,6},{3,7},{4,0},{5,1},{6,2},{7,3},{8,12},{9,13},{10,... | collective-permute-start | bytes 1179656 | tf_op jit(solution)/shard_map/ppermute | solution.py:303
  16.4 19.3 %collective-permute-start.2 = (bf16[48,32,128]{2,1,0:T(8,128)(2,1)S(1)}, bf16[48,32,128]{2,1,0:T(8,128)(2,1)S(1)}, u32[]{:S(2)}, u32[]{:S(2)}) collective-permute-start(bf16[48,32,128]{2,1,0:T(8,128)(2,1)S(1)} %get-tuple-element.24), channel_id=1, source_target_pairs={{0,6},{1,7},{2,4},{3,5},{4,2},{5,3},{6,0},{7,1},{8,14},{9,15},{10,... | collective-permute-start | bytes 1179656 | tf_op jit(solution)/shard_map/ppermute | solution.py:303
  27.8 8.1 %copy-start.1 = (bf16[3,2,256,256]{3,2,1,0:T(8,128)(2,1)S(1)}, bf16[3,2,256,256]{3,2,1,0:T(8,128)(2,1)}, u32[]{:S(2)}) copy-start(bf16[3,2,256,256]{3,2,1,0:T(8,128)(2,1)} %sheet_ref.1) | copy-start | bytes 2359300
  35.8 39.6 %collective-permute-start.3 = (bf16[96,32,128]{2,1,0:T(8,128)(2,1)S(1)}, bf16[96,32,128]{2,1,0:T(8,128)(2,1)S(1)}, u32[]{:S(2)}, u32[]{:S(2)}) collective-permute-start(bf16[96,32,128]{2,1,0:T(8,128)(2,1)S(1)} %pad_maximum_fusion), channel_id=1, source_target_pairs={{0,1},{1,0},{2,3},{3,2},{4,5},{5,4},{6,7},{7,6},{8,9},{9,8},{10,11... | collective-permute-start | bytes 2359304 | tf_op jit(solution)/shard_map/ppermute | solution.py:307
  35.9 26.6 %collective-permute-start.14 = (bf16[2,256,256]{2,1,0:T(8,128)(2,1)S(1)}, bf16[2,256,256]{2,1,0:T(8,128)(2,1)S(1)}, u32[]{:S(2)}, u32[]{:S(2)}) collective-permute-start(bf16[2,256,256]{2,1,0:T(8,128)(2,1)S(1)} %slice_bitcast_fusion), channel_id=1, source_target_pairs={{0,8},{1,9},{2,10},{3,11},{4,12},{5,13},{6,14},{7,15},{8,0},{9,1},... | collective-permute-start | bytes 786440 | tf_op jit(solution)/shard_map/ppermute | solution.py:311
  38.6 29.6 %collective-permute-start.9 = (bf16[2,256,256]{2,1,0:T(8,128)(2,1)S(1)}, bf16[2,256,256]{2,1,0:T(8,128)(2,1)S(1)}, u32[]{:S(2)}, u32[]{:S(2)}) collective-permute-start(bf16[2,256,256]{2,1,0:T(8,128)(2,1)S(1)} %get-tuple-element.41), channel_id=1, source_target_pairs={{0,8},{1,9},{2,10},{3,11},{4,12},{5,13},{6,14},{7,15},{8,0},{9,1},... | collective-permute-start | bytes 786440 | tf_op jit(solution)/shard_map/ppermute | solution.py:311
  39.0 34.8 %collective-permute-start.4 = (bf16[2,256,256]{2,1,0:T(8,128)(2,1)S(1)}, bf16[2,256,256]{2,1,0:T(8,128)(2,1)S(1)}, u32[]{:S(2)}, u32[]{:S(2)}) collective-permute-start(bf16[2,256,256]{2,1,0:T(8,128)(2,1)S(1)} %get-tuple-element.42), channel_id=1, source_target_pairs={{0,8},{1,9},{2,10},{3,11},{4,12},{5,13},{6,14},{7,15},{8,0},{9,1},... | collective-permute-start | bytes 786440 | tf_op jit(solution)/shard_map/ppermute | solution.py:311
  63.6 12.5 %collective-permute-start.15 = (bf16[16,32,128]{2,1,0:T(8,128)(2,1)S(1)}, bf16[16,32,128]{2,1,0:T(8,128)(2,1)S(1)}, u32[]{:S(2)}, u32[]{:S(2)}) collective-permute-start(bf16[16,32,128]{2,1,0:T(8,128)(2,1)S(1)} %get-tuple-element.35), channel_id=1, source_target_pairs={{0,2},{1,3},{2,0},{3,1},{4,6},{5,7},{6,4},{7,5},{8,10},{9,11},{10,... | collective-permute-start | bytes 393224 | tf_op jit(solution)/shard_map/ppermute | solution.py:303
  64.2 15.0 %collective-permute-start.16 = (bf16[16,32,128]{2,1,0:T(8,128)(2,1)S(1)}, bf16[16,32,128]{2,1,0:T(8,128)(2,1)S(1)}, u32[]{:S(2)}, u32[]{:S(2)}) collective-permute-start(bf16[16,32,128]{2,1,0:T(8,128)(2,1)S(1)} %get-tuple-element.36), channel_id=1, source_target_pairs={{0,4},{1,5},{2,6},{3,7},{4,0},{5,1},{6,2},{7,3},{8,12},{9,13},{10,... | collective-permute-start | bytes 393224 | tf_op jit(solution)/shard_map/ppermute | solution.py:303
  68.3 11.6 %collective-permute-start.17 = (bf16[16,32,128]{2,1,0:T(8,128)(2,1)S(1)}, bf16[16,32,128]{2,1,0:T(8,128)(2,1)S(1)}, u32[]{:S(2)}, u32[]{:S(2)}) collective-permute-start(bf16[16,32,128]{2,1,0:T(8,128)(2,1)S(1)} %get-tuple-element.37), channel_id=1, source_target_pairs={{0,6},{1,7},{2,4},{3,5},{4,2},{5,3},{6,0},{7,1},{8,14},{9,15},{10,... | collective-permute-start | bytes 393224 | tf_op jit(solution)/shard_map/ppermute | solution.py:303
  73.8 9.0 %collective-permute-start.10 = (bf16[16,32,128]{2,1,0:T(8,128)(2,1)S(1)}, bf16[16,32,128]{2,1,0:T(8,128)(2,1)S(1)}, u32[]{:S(2)}, u32[]{:S(2)}) collective-permute-start(bf16[16,32,128]{2,1,0:T(8,128)(2,1)S(1)} %get-tuple-element.31), channel_id=1, source_target_pairs={{0,2},{1,3},{2,0},{3,1},{4,6},{5,7},{6,4},{7,5},{8,10},{9,11},{10,... | collective-permute-start | bytes 393224 | tf_op jit(solution)/shard_map/ppermute | solution.py:303
  75.4 7.5 %collective-permute-start.11 = (bf16[16,32,128]{2,1,0:T(8,128)(2,1)S(1)}, bf16[16,32,128]{2,1,0:T(8,128)(2,1)S(1)}, u32[]{:S(2)}, u32[]{:S(2)}) collective-permute-start(bf16[16,32,128]{2,1,0:T(8,128)(2,1)S(1)} %get-tuple-element.32), channel_id=1, source_target_pairs={{0,4},{1,5},{2,6},{3,7},{4,0},{5,1},{6,2},{7,3},{8,12},{9,13},{10,... | collective-permute-start | bytes 393224 | tf_op jit(solution)/shard_map/ppermute | solution.py:303
  76.2 9.4 %collective-permute-start.12 = (bf16[16,32,128]{2,1,0:T(8,128)(2,1)S(1)}, bf16[16,32,128]{2,1,0:T(8,128)(2,1)S(1)}, u32[]{:S(2)}, u32[]{:S(2)}) collective-permute-start(bf16[16,32,128]{2,1,0:T(8,128)(2,1)S(1)} %get-tuple-element.33), channel_id=1, source_target_pairs={{0,6},{1,7},{2,4},{3,5},{4,2},{5,3},{6,0},{7,1},{8,14},{9,15},{10,... | collective-permute-start | bytes 393224 | tf_op jit(solution)/shard_map/ppermute | solution.py:303
  79.2 8.7 %collective-permute-start.5 = (bf16[16,32,128]{2,1,0:T(8,128)(2,1)S(1)}, bf16[16,32,128]{2,1,0:T(8,128)(2,1)S(1)}, u32[]{:S(2)}, u32[]{:S(2)}) collective-permute-start(bf16[16,32,128]{2,1,0:T(8,128)(2,1)S(1)} %get-tuple-element.27), channel_id=1, source_target_pairs={{0,2},{1,3},{2,0},{3,1},{4,6},{5,7},{6,4},{7,5},{8,10},{9,11},{10,... | collective-permute-start | bytes 393224 | tf_op jit(solution)/shard_map/ppermute | solution.py:303
  79.8 8.1 %collective-permute-start.6 = (bf16[16,32,128]{2,1,0:T(8,128)(2,1)S(1)}, bf16[16,32,128]{2,1,0:T(8,128)(2,1)S(1)}, u32[]{:S(2)}, u32[]{:S(2)}) collective-permute-start(bf16[16,32,128]{2,1,0:T(8,128)(2,1)S(1)} %get-tuple-element.28), channel_id=1, source_target_pairs={{0,4},{1,5},{2,6},{3,7},{4,0},{5,1},{6,2},{7,3},{8,12},{9,13},{10,... | collective-permute-start | bytes 393224 | tf_op jit(solution)/shard_map/ppermute | solution.py:303
  82.8 7.8 %collective-permute-start.7 = (bf16[16,32,128]{2,1,0:T(8,128)(2,1)S(1)}, bf16[16,32,128]{2,1,0:T(8,128)(2,1)S(1)}, u32[]{:S(2)}, u32[]{:S(2)}) collective-permute-start(bf16[16,32,128]{2,1,0:T(8,128)(2,1)S(1)} %get-tuple-element.29), channel_id=1, source_target_pairs={{0,6},{1,7},{2,4},{3,5},{4,2},{5,3},{6,0},{7,1},{8,14},{9,15},{10,... | collective-permute-start | bytes 393224 | tf_op jit(solution)/shard_map/ppermute | solution.py:303
  83.0 8.5 %collective-permute-start.18 = (bf16[32,32,128]{2,1,0:T(8,128)(2,1)S(1)}, bf16[32,32,128]{2,1,0:T(8,128)(2,1)S(1)}, u32[]{:S(2)}, u32[]{:S(2)}) collective-permute-start(bf16[32,32,128]{2,1,0:T(8,128)(2,1)S(1)} %pad_maximum_fusion.3), channel_id=1, source_target_pairs={{0,1},{1,0},{2,3},{3,2},{4,5},{5,4},{6,7},{7,6},{8,9},{9,8},{10,11... | collective-permute-start | bytes 786440 | tf_op jit(solution)/shard_map/ppermute | solution.py:307
  85.6 5.1 %copy-start.4 = (s32[3,64,1]{1,2,0:T(1,128)S(1)}, s32[3,64,1]{1,2,0:T(1,128)}, u32[]{:S(2)}) copy-start(s32[3,64,1]{1,2,0:T(1,128)} %param.9) | copy-start | bytes 2308
  85.7 8.6 %collective-permute-start.13 = (bf16[32,32,128]{2,1,0:T(8,128)(2,1)S(1)}, bf16[32,32,128]{2,1,0:T(8,128)(2,1)S(1)}, u32[]{:S(2)}, u32[]{:S(2)}) collective-permute-start(bf16[32,32,128]{2,1,0:T(8,128)(2,1)S(1)} %pad_maximum_fusion.2), channel_id=1, source_target_pairs={{0,1},{1,0},{2,3},{3,2},{4,5},{5,4},{6,7},{7,6},{8,9},{9,8},{10,11... | collective-permute-start | bytes 786440 | tf_op jit(solution)/shard_map/ppermute | solution.py:307
  85.8 5.8 %copy-start.2 = (f32[64,128]{1,0:T(8,128)S(1)}, f32[64,128]{1,0:T(8,128)}, u32[]{:S(2)}) copy-start(f32[64,128]{1,0:T(8,128)} %refs_0_.1) | copy-start | bytes 98308
  85.8 5.8 %copy-start.3 = (f32[64,128]{1,0:T(8,128)S(1)}, f32[64,128]{1,0:T(8,128)}, u32[]{:S(2)}) copy-start(f32[64,128]{1,0:T(8,128)} %refs_1_.1) | copy-start | bytes 98308
  90.7 6.4 %collective-permute-start.8 = (bf16[32,32,128]{2,1,0:T(8,128)(2,1)S(1)}, bf16[32,32,128]{2,1,0:T(8,128)(2,1)S(1)}, u32[]{:S(2)}, u32[]{:S(2)}) collective-permute-start(bf16[32,32,128]{2,1,0:T(8,128)(2,1)S(1)} %pad_maximum_fusion.1), channel_id=1, source_target_pairs={{0,1},{1,0},{2,3},{3,2},{4,5},{5,4},{6,7},{7,6},{8,9},{9,8},{10,11... | collective-permute-start | bytes 786440 | tf_op jit(solution)/shard_map/ppermute | solution.py:307
  (1 other events, 1.1 us)

commit v8 on v7

--- a/solution.py
+++ b/solution.py
@@ -94,14 +94,13 @@
     )(place, tile_map)
 
 
-def cut_kernel(planes, cap, mirrored, place_ref, req_ref, sheet_ref, *refs):
-    out_refs, half_ref = refs[:-1], refs[-1]
-    parts = sheet_ref.shape[-1] // WC
-    for at, k in enumerate(planes):
+def cut_kernel(planes, cap, mirrored, place_ref, req_ref, *refs):
+    sheet_refs, out_refs, half_ref = refs[: len(planes)], refs[len(planes) : -1], refs[-1]
+    parts = sheet_refs[0].shape[-1] // WC
+    for at, sheet_ref in enumerate(sheet_refs):
         for c in range(2):
             for h in range(parts):
-                lanes = slice(h * WC, (h + 1) * WC)
-                part = sheet_ref[c, :, lanes] if mirrored else sheet_ref[k, c, :, lanes]
+                part = sheet_ref[c, :, h * WC : (h + 1) * WC]
                 half_ref[(at * 2 + c) * parts + h] = part.astype(jnp.float32)
     lane = lax.broadcasted_iota(jnp.int32, (WR, WC), 1)
     me = place_ref[1]
@@ -132,19 +131,18 @@
     lax.fori_loop(0, span, one, 0)
 
 
-def cut(planes, cap, outs, place, requests, sheet):
-    mirrored = sheet.ndim == 3
+def cut(planes, cap, outs, mirrored, place, requests, sheets):
     count = requests.shape[0] // outs * len(planes) * cap
-    height, width = sheet.shape[-2:]
+    height, width = sheets[0].shape[-2:]
     return pl.pallas_call(
         functools.partial(cut_kernel, planes, cap, mirrored),
         out_shape=(jax.ShapeDtypeStruct((count, 2 * WR, WC), jnp.bfloat16),) * outs,
-        in_specs=[whole(SMEM), whole(SMEM), whole()],
+        in_specs=[whole(SMEM), whole(SMEM)] + [whole()] * len(planes),
         out_specs=(whole(),) * outs,
         scratch_shapes=[VMEM((len(planes) * 2 * width // WC, height, WC), jnp.float32)],
         compiler_params=GRANT,
         name="cut",
-    )(place, requests, sheet)
+    )(place, requests, *sheets)
 
 
 def taps(pos):
@@ -295,41 +293,61 @@
             x, "sky", split_axis=0, concat_axis=0, axis_index_groups=groups, tiled=True
         )
 
-    def ship(parts):
+    def ship(parts, count):
         if direct:
-            return exchange(parts[0].reshape(relays, -1, 2 * WR, WC))
+            got = exchange(parts[0].reshape(relays, -1, 2 * WR, WC))
+            got = got.reshape(relays, count, cap, 2 * WR, WC)
+            return [([got[:, at].reshape(relays * cap, 2 * WR, WC)], []) for at in range(count)]
         got = [parts[0]]
         for m in range(1, chips):
             got.append(lax.ppermute(parts[m], "sky", swap(2 * m)))
-        half = parts[0].shape[0] // 2
-        mine = [part[:half] for part in got]
-        other = jnp.concatenate([part[half:] for part in got], axis=0)
-        other = lax.ppermute(other, "sky", swap(1))
-        return jnp.concatenate(mine + [other], axis=0).reshape(relays, -1, 2 * WR, WC)
-
-    def mirror(plane, sheet):
-        return lax.ppermute(sheet[plane], "sky", mirror_pairs)
+
+        def pieces(at):
+            return [part[at * cap : (at + 1) * cap] for part in got]
+
+        return [(pieces(at), pieces(count + at)) for at in range(count)]
+
+    def across(lists):
+        if direct:
+            return [[] for _ in lists]
+        got = lax.ppermute(jnp.concatenate(sum(lists, []), axis=0), "sky", swap(1))
+        size = chips * cap
+        return [[got[at * size : (at + 1) * size]] for at in range(len(lists))]
+
+    def tile(plane, sheet):
+        return sheet[plane]
+
+    def mirror(plane):
+        return lax.ppermute(sheets[plane], "sky", mirror_pairs)
+
+    def cut_sent(planes, mirrored, tiles_of):
+        parts = cut(planes, cap, outs, mirrored, place, asked, tiles_of)
+        return ship(parts, len(planes))
 
     index = lax.axis_index("sky").astype(jnp.int32)
     place = jnp.stack([index // relays, jnp.zeros_like(index) if direct else index % relays])
     tiles = tile_map.transpose(0, 2, 1)
     requests = want(tiles, row_anchor, col_anchor, peers, cap)
-    mirrors = [mirror(0, gradients)]
     requests, late = lax.optimization_barrier((requests, gradients))
-    mirrors += [mirror(plane, late) for plane in range(1, PLANES)]
+    sheets = [tile(0, gradients)] + [tile(plane, late) for plane in range(1, PLANES)]
+    mirrors = [mirror(plane) for plane in range(PLANES)]
     asked = exchange(requests)
     slots = find_slots(place, tiles, peers, cap, direct)
-    parts = cut(tuple(range(PLANES)), cap, outs, place, asked, gradients)
-    own = ship(parts).reshape(relays, PLANES, cap, 2 * WR, WC)
-    windows = []
+    rest = tuple(range(1, PLANES))
+    own = cut_sent((0,), False, sheets[:1])
+    far = cut_sent((0,), True, mirrors[:1])
+    own += cut_sent(rest, False, sheets[1:])
+    for plane in rest:
+        far += cut_sent((plane,), True, mirrors[plane : plane + 1])
+    state = (start_x, start_y)
+    held = {}
     for plane in range(PLANES):
-        parts = cut((plane,), cap, outs, place, asked, mirrors[plane])
-        far = ship(parts)
-        both = [x.reshape(relays * cap, 2 * WR, WC) for x in (own[:, plane], far)]
-        windows.append(jnp.concatenate(both, axis=0))
-    state = (start_x, start_y)
-    for plane in range(PLANES):
-        state = interp(plane, slots, windows[plane], state)
+        news = [("own", plane)] if plane == 0 else [("own", k) for k in rest] if plane == 1 else []
+        news.append(("far", plane))
+        source = {"own": own, "far": far}
+        held.update(zip(news, across([source[kind][k][1] for kind, k in news])))
+        windows = own[plane][0] + held["own", plane] + far[plane][0] + held["far", plane]
+        state = interp(plane, slots, jnp.concatenate(windows, axis=0), state)
     return state
 
 

time: 101 us -> 115 us (1.14)
  starting transfers between devices: 20 us -> 28.5 us
  waiting for transfers between devices: 60.7 us -> 64 us
  local copies, waits for them, and re-layouts: 2.26 us -> 4.07 us
    ppermute x12 -> x15, waiting for transfers between devices: 27 us -> 61.9 us  [ship(): got.append(lax.ppermute(parts[m], 'sky', swap(2 * m)))]
    ppermute x7 -> x6, waiting for transfers between devices: 29.2 us -> 2.17 us  [the longest x3 2.17 us: across(): got = lax.ppermute(jnp.concatenate(sum(lists, []), axis=0), 'sky', swap(1))]
    ppermute x12 -> x15, starting transfers between devices: 8.81 us -> 17.3 us  [ship(): got.append(lax.ppermute(parts[m], 'sky', swap(2 * m)))]
    all_to_all x1, waiting for transfers between devices: 4.53 us -> 0.01 us  [exchange(): lax.all_to_all(x, 'sky', split_axis=0, concat_axis=0, axis_index_groups=g...]
    squeeze x2, local copies, waits for them, and re-layouts: 0.05 us -> 2.03 us  [tile(): return sheet[plane]]
    pallas_call x4 -> x5, Pallas kernels: 4.87 us -> 5.63 us  [cut(): pl.pallas_call(functools.partial(cut_kernel, planes, cap, mirrored), out_...]
    ppermute x7 -> x6, starting transfers between devices: 5.93 us -> 5.99 us  [the longest x3 5.64 us: mirror(): return lax.ppermute(sheets[plane], 'sky', mirror_pairs)]
  transfers between devices with their start and end apart: 20 -> 22, of which waited for: 11 -> 10; matrix products, arithmetic and copies ran while one was open for 1% -> 2% of each run, Pallas kernels for 9% -> 10%
where the time goes in v8:
time: 115 us
  waiting for transfers between devices  64 us (56%)
  starting transfers between devices  28.5 us (25%)
  Pallas kernels  17.1 us (15%)
  local copies, waits for them, and re-layouts  4.07 us (4%)
    ppermute x15, waiting for transfers between devices, ship(): got.append(lax.ppermute(parts[m], 'sky', swap(2 * m)))  61.9 us
    ppermute x15, starting transfers between devices, ship(): got.append(lax.ppermute(parts[m], 'sky', swap(2 * m)))  17.3 us
    pallas_call x3, Pallas kernels, interp(): pl.pallas_call(functools.partial(interp_kernel, plane), out_shape=out_sha...  8.92 us
    ppermute x3, starting transfers between devices, mirror(): return lax.ppermute(sheets[plane], 'sky', mirror_pairs)  5.64 us
    pallas_call x5, Pallas kernels, cut(): pl.pallas_call(functools.partial(cut_kernel, planes, cap, mirrored), out_...  5.63 us
    all_to_all x1, starting transfers between devices, exchange(): lax.all_to_all(x, 'sky', split_axis=0, concat_axis=0, axis_index_groups=g...  5.28 us
  transfers between devices with their start and end apart: 22, of which 10 were waited for; matrix products, arithmetic and copies ran while one was open for 2% of the time, Pallas kernels for 10%

profile of v8, /device:TPU:0, one launch (start us, length us, event | category | flops | bytes accessed | tf_op | source)
XLA Modules:
  0.0 114.8 jit_solution(6656891948661561477)
XLA Ops:
  0.6 1.8 %want.1 = s32[8,128]{1,0:T(8,128)} custom-call(s32[3,1,64]{2,1,0:T(1,128)} %bitcast.18, s32[3,64]{1,0:T(4,128)} %row_ref.1, s32[3,64]{1,0:T(4,128)} %col_ref.1), custom_call_target="tpu_custom_call" | custom-call | tf_op jit(solution)/shard_map/want/pallas_call | solution.py:65
  2.5 5.3 %all-to-all-start = ((s32[8,1,128]{2,1,0:T(1,128)}), s32[8,1,128]{2,1,0:T(1,128)S(1)}, u32[]{:S(2)}, u32[]{:S(2)}) async-start(s32[8,1,128]{2,1,0:T(1,128)} %bitcast.20), calls=%async_computation | async-start | bytes 8192 | tf_op jit(solution)/shard_map/all_to_all | solution.py:292
  8.8 2.7 %collective-permute-start.8 = (bf16[2,256,256]{2,1,0:T(8,128)(2,1)S(1)}, bf16[2,256,256]{2,1,0:T(8,128)(2,1)S(1)}, u32[]{:S(2)}, u32[]{:S(2)}) collective-permute-start(bf16[2,256,256]{2,1,0:T(8,128)(2,1)S(1)} %get-tuple-element.48.refs_1_), channel_id=1, source_target_pairs={{0,8},{1,9},{2,10},{3,11},{4,12},{5,13},{6,14},{7,15},{8,0},{9,1},... | collective-permute-start | bytes 786440 | tf_op jit(solution)/shard_map/ppermute | solution.py:321
  12.8 2.7 %collective-permute-start.16 = (bf16[2,256,256]{2,1,0:T(8,128)(2,1)S(1)}, bf16[2,256,256]{2,1,0:T(8,128)(2,1)S(1)}, u32[]{:S(2)}, u32[]{:S(2)}) collective-permute-start(bf16[2,256,256]{2,1,0:T(8,128)(2,1)S(1)} %slice_bitcast_fusion.refs_0_), channel_id=1, source_target_pairs={{0,8},{1,9},{2,10},{3,11},{4,12},{5,13},{6,14},{7,15},{8,0},{9,1},... | collective-permute-start | bytes 786440 | tf_op jit(solution)/shard_map/ppermute | solution.py:321
  19.3 2.1 %collective-permute-start = (bf16[32,32,128]{2,1,0:T(8,128)(2,1)S(1)}, bf16[32,32,128]{2,1,0:T(8,128)(2,1)S(1)}, u32[]{:S(2)}, u32[]{:S(2)}) collective-permute-start(bf16[32,32,128]{2,1,0:T(8,128)(2,1)S(1)} %get-tuple-element.27), channel_id=1, source_target_pairs={{0,2},{1,3},{2,0},{3,1},{4,6},{5,7},{6,4},{7,5},{8,10},{9,11},{10,... | collective-permute-start | bytes 786440 | tf_op jit(solution)/shard_map/ppermute | solution.py:303
  21.5 8.6 %collective-permute-done.13 = bf16[16,32,128]{2,1,0:T(8,128)(2,1)S(1)} collective-permute-done((bf16[16,32,128]{2,1,0:T(8,128)(2,1)S(1)}, bf16[16,32,128]{2,1,0:T(8,128)(2,1)S(1)}, u32[]{:S(2)}, u32[]{:S(2)}) %collective-permute-start.13) | collective-permute-done | bytes 131104 | tf_op jit(solution)/shard_map/ppermute | solution.py:303
  30.0 1.6 %collective-permute-start.14 = (bf16[16,32,128]{2,1,0:T(8,128)(2,1)S(1)}, bf16[16,32,128]{2,1,0:T(8,128)(2,1)S(1)}, u32[]{:S(2)}, u32[]{:S(2)}) collective-permute-start(bf16[16,32,128]{2,1,0:T(8,128)(2,1)S(1)} %get-tuple-element.40), channel_id=1, source_target_pairs={{0,4},{1,5},{2,6},{3,7},{4,0},{5,1},{6,2},{7,3},{8,12},{9,13},{10,... | collective-permute-start | bytes 393224 | tf_op jit(solution)/shard_map/ppermute | solution.py:303
  31.7 17.7 %collective-permute-done.14 = bf16[16,32,128]{2,1,0:T(8,128)(2,1)S(1)} collective-permute-done((bf16[16,32,128]{2,1,0:T(8,128)(2,1)S(1)}, bf16[16,32,128]{2,1,0:T(8,128)(2,1)S(1)}, u32[]{:S(2)}, u32[]{:S(2)}) %collective-permute-start.14) | collective-permute-done | bytes 131104 | tf_op jit(solution)/shard_map/ppermute | solution.py:303
  50.0 5.7 %collective-permute-done.15 = bf16[16,32,128]{2,1,0:T(8,128)(2,1)S(1)} collective-permute-done((bf16[16,32,128]{2,1,0:T(8,128)(2,1)S(1)}, bf16[16,32,128]{2,1,0:T(8,128)(2,1)S(1)}, u32[]{:S(2)}, u32[]{:S(2)}) %collective-permute-start.15) | collective-permute-done | bytes 131104 | tf_op jit(solution)/shard_map/ppermute | solution.py:303
  56.2 2.7 %collective-permute-start.2 = (bf16[32,32,128]{2,1,0:T(8,128)(2,1)S(1)}, bf16[32,32,128]{2,1,0:T(8,128)(2,1)S(1)}, u32[]{:S(2)}, u32[]{:S(2)}) collective-permute-start(bf16[32,32,128]{2,1,0:T(8,128)(2,1)S(1)} %get-tuple-element.29), channel_id=1, source_target_pairs={{0,6},{1,7},{2,4},{3,5},{4,2},{5,3},{6,0},{7,1},{8,14},{9,15},{10,... | collective-permute-start | bytes 786440 | tf_op jit(solution)/shard_map/ppermute | solution.py:303
  61.4 1.6 %collective-permute-start.10 = (bf16[16,32,128]{2,1,0:T(8,128)(2,1)S(1)}, bf16[16,32,128]{2,1,0:T(8,128)(2,1)S(1)}, u32[]{:S(2)}, u32[]{:S(2)}) collective-permute-start(bf16[16,32,128]{2,1,0:T(8,128)(2,1)S(1)} %get-tuple-element.36), channel_id=1, source_target_pairs={{0,4},{1,5},{2,6},{3,7},{4,0},{5,1},{6,2},{7,3},{8,12},{9,13},{10,... | collective-permute-start | bytes 393224 | tf_op jit(solution)/shard_map/ppermute | solution.py:303
  64.1 1.7 %collective-permute-start.9 = (bf16[16,32,128]{2,1,0:T(8,128)(2,1)S(1)}, bf16[16,32,128]{2,1,0:T(8,128)(2,1)S(1)}, u32[]{:S(2)}, u32[]{:S(2)}) collective-permute-start(bf16[16,32,128]{2,1,0:T(8,128)(2,1)S(1)} %get-tuple-element.35), channel_id=1, source_target_pairs={{0,2},{1,3},{2,0},{3,1},{4,6},{5,7},{6,4},{7,5},{8,10},{9,11},{10,... | collective-permute-start | bytes 393224 | tf_op jit(solution)/shard_map/ppermute | solution.py:303
  66.5 5.1 %collective-permute-done.2 = bf16[32,32,128]{2,1,0:T(8,128)(2,1)S(1)} collective-permute-done((bf16[32,32,128]{2,1,0:T(8,128)(2,1)S(1)}, bf16[32,32,128]{2,1,0:T(8,128)(2,1)S(1)}, u32[]{:S(2)}, u32[]{:S(2)}) %collective-permute-start.2) | collective-permute-done | bytes 262176 | tf_op jit(solution)/shard_map/ppermute | solution.py:303
  72.2 8.3 %collective-permute-done.17 = bf16[16,32,128]{2,1,0:T(8,128)(2,1)S(1)} collective-permute-done((bf16[16,32,128]{2,1,0:T(8,128)(2,1)S(1)}, bf16[16,32,128]{2,1,0:T(8,128)(2,1)S(1)}, u32[]{:S(2)}, u32[]{:S(2)}) %collective-permute-start.17) | collective-permute-done | bytes 131104 | tf_op jit(solution)/shard_map/ppermute | solution.py:303
  81.1 4.3 %collective-permute-done.18 = bf16[16,32,128]{2,1,0:T(8,128)(2,1)S(1)} collective-permute-done((bf16[16,32,128]{2,1,0:T(8,128)(2,1)S(1)}, bf16[16,32,128]{2,1,0:T(8,128)(2,1)S(1)}, u32[]{:S(2)}, u32[]{:S(2)}) %collective-permute-start.18) | collective-permute-done | bytes 131104 | tf_op jit(solution)/shard_map/ppermute | solution.py:303
  85.4 1.5 %collective-permute-start.19 = (bf16[16,32,128]{2,1,0:T(8,128)(2,1)S(1)}, bf16[16,32,128]{2,1,0:T(8,128)(2,1)S(1)}, u32[]{:S(2)}, u32[]{:S(2)}) collective-permute-start(bf16[16,32,128]{2,1,0:T(8,128)(2,1)S(1)} %get-tuple-element.45), channel_id=1, source_target_pairs={{0,6},{1,7},{2,4},{3,5},{4,2},{5,3},{6,0},{7,1},{8,14},{9,15},{10,... | collective-permute-start | bytes 393224 | tf_op jit(solution)/shard_map/ppermute | solution.py:303
  87.0 4.3 %collective-permute-done.19 = bf16[16,32,128]{2,1,0:T(8,128)(2,1)S(1)} collective-permute-done((bf16[16,32,128]{2,1,0:T(8,128)(2,1)S(1)}, bf16[16,32,128]{2,1,0:T(8,128)(2,1)S(1)}, u32[]{:S(2)}, u32[]{:S(2)}) %collective-permute-start.19) | collective-permute-done | bytes 131104 | tf_op jit(solution)/shard_map/ppermute | solution.py:303
  92.3 3.9 %collective-permute-done.5 = bf16[16,32,128]{2,1,0:T(8,128)(2,1)S(1)} collective-permute-done((bf16[16,32,128]{2,1,0:T(8,128)(2,1)S(1)}, bf16[16,32,128]{2,1,0:T(8,128)(2,1)S(1)}, u32[]{:S(2)}, u32[]{:S(2)}) %collective-permute-start.5) | collective-permute-done | bytes 131104 | tf_op jit(solution)/shard_map/ppermute | solution.py:303
  96.2 1.9 %collective-permute-start.6 = (bf16[16,32,128]{2,1,0:T(8,128)(2,1)S(1)}, bf16[16,32,128]{2,1,0:T(8,128)(2,1)S(1)}, u32[]{:S(2)}, u32[]{:S(2)}) collective-permute-start(bf16[16,32,128]{2,1,0:T(8,128)(2,1)S(1)} %get-tuple-element.33), channel_id=1, source_target_pairs={{0,6},{1,7},{2,4},{3,5},{4,2},{5,3},{6,0},{7,1},{8,14},{9,15},{10,... | collective-permute-start | bytes 393224 | tf_op jit(solution)/shard_map/ppermute | solution.py:303
  98.1 4.0 %collective-permute-done.6 = bf16[16,32,128]{2,1,0:T(8,128)(2,1)S(1)} collective-permute-done((bf16[16,32,128]{2,1,0:T(8,128)(2,1)S(1)}, bf16[16,32,128]{2,1,0:T(8,128)(2,1)S(1)}, u32[]{:S(2)}, u32[]{:S(2)}) %collective-permute-start.6) | collective-permute-done | bytes 131104 | tf_op jit(solution)/shard_map/ppermute | solution.py:303
  102.3 2.2 %collective-permute-done.7 = bf16[96,32,128]{2,1,0:T(8,128)(2,1)S(1)} collective-permute-done((bf16[96,32,128]{2,1,0:T(8,128)(2,1)S(1)}, bf16[96,32,128]{2,1,0:T(8,128)(2,1)S(1)}, u32[]{:S(2)}, u32[]{:S(2)}) %collective-permute-start.7) | collective-permute-done | bytes 786464 | tf_op jit(solution)/shard_map/ppermute | solution.py:313
  105.8 2.7 %shard_map.77.refs_0_ = f32[12,64,128]{2,1,0:T(8,128)S(1)} custom-call(s32[3,64]{1,0:T(4,128)S(1)} %slots.1.slot_ref, bf16[128,32,128]{2,1,0:T(8,128)(2,1)S(1)} %slice_dynamic-update-slice_fusion.win_ref, f32[64,128]{1,0:T(8,128)S(1)} %copy-done, f32[64,128]{1,0:T(8,128)S(1)} %copy-done.1), custom_call_target="tpu_custom_call" | custom-call | tf_op jit(solution)/shard_map/pallas_call | solution.py:264
  108.5 2.7 %shard_map.78.refs_0_ = f32[12,64,128]{2,1,0:T(8,128)S(1)} custom-call(s32[3,64]{1,0:T(4,128)S(1)} %slots.1.slot_ref, bf16[128,32,128]{2,1,0:T(8,128)(2,1)S(1)} %get-tuple-element.46.win_ref, f32[12,64,128]{2,1,0:T(8,128)S(1)} %shard_map.77.refs_0_), custom_call_target="tpu_custom_call" | custom-call | tf_op jit(solution)/shard_map/pallas_call | solution.py:264
  111.3 3.5 %shard_map.79 = (f32[64,2,128]{2,1,0:T(2,128)}, f32[64,4,128]{2,1,0:T(4,128)}) custom-call(s32[3,64]{1,0:T(4,128)S(1)} %slots.1.slot_ref, bf16[128,32,128]{2,1,0:T(8,128)(2,1)S(1)} %constant_dynamic-update-slice_fusion.12.win_ref, f32[12,64,128]{2,1,0:T(8,128)S(1)} %shard_map.78.refs_0_), custom_call_target="tpu_custom_call" | custom-call | tf_op jit(solution)/shard_map/pallas_call | solution.py:264
  (77 shorter events, 15.3 us)
Async XLA Ops:
  2.5 14.4 %all-to-all-start = ((s32[8,1,128]{2,1,0:T(1,128)}), s32[8,1,128]{2,1,0:T(1,128)S(1)}, u32[]{:S(2)}, u32[]{:S(2)}) async-start(s32[8,1,128]{2,1,0:T(1,128)} %bitcast.20), calls=%async_computation | async-start | bytes 8192 | tf_op jit(solution)/shard_map/all_to_all | solution.py:292
  8.8 47.4 %collective-permute-start.8 = (bf16[2,256,256]{2,1,0:T(8,128)(2,1)S(1)}, bf16[2,256,256]{2,1,0:T(8,128)(2,1)S(1)}, u32[]{:S(2)}, u32[]{:S(2)}) collective-permute-start(bf16[2,256,256]{2,1,0:T(8,128)(2,1)S(1)} %get-tuple-element.48.refs_1_), channel_id=1, source_target_pairs={{0,8},{1,9},{2,10},{3,11},{4,12},{5,13},{6,14},{7,15},{8,0},{9,1},... | collective-permute-start | bytes 786440 | tf_op jit(solution)/shard_map/ppermute | solution.py:321
  11.5 50.0 %collective-permute-start.3 = (bf16[2,256,256]{2,1,0:T(8,128)(2,1)S(1)}, bf16[2,256,256]{2,1,0:T(8,128)(2,1)S(1)}, u32[]{:S(2)}, u32[]{:S(2)}) collective-permute-start(bf16[2,256,256]{2,1,0:T(8,128)(2,1)S(1)} %get-tuple-element.49.refs_0_), channel_id=1, source_target_pairs={{0,8},{1,9},{2,10},{3,11},{4,12},{5,13},{6,14},{7,15},{8,0},{9,1},... | collective-permute-start | bytes 786440 | tf_op jit(solution)/shard_map/ppermute | solution.py:321
  12.8 47.2 %collective-permute-start.16 = (bf16[2,256,256]{2,1,0:T(8,128)(2,1)S(1)}, bf16[2,256,256]{2,1,0:T(8,128)(2,1)S(1)}, u32[]{:S(2)}, u32[]{:S(2)}) collective-permute-start(bf16[2,256,256]{2,1,0:T(8,128)(2,1)S(1)} %slice_bitcast_fusion.refs_0_), channel_id=1, source_target_pairs={{0,8},{1,9},{2,10},{3,11},{4,12},{5,13},{6,14},{7,15},{8,0},{9,1},... | collective-permute-start | bytes 786440 | tf_op jit(solution)/shard_map/ppermute | solution.py:321
  19.3 44.9 %collective-permute-start = (bf16[32,32,128]{2,1,0:T(8,128)(2,1)S(1)}, bf16[32,32,128]{2,1,0:T(8,128)(2,1)S(1)}, u32[]{:S(2)}, u32[]{:S(2)}) collective-permute-start(bf16[32,32,128]{2,1,0:T(8,128)(2,1)S(1)} %get-tuple-element.27), channel_id=1, source_target_pairs={{0,2},{1,3},{2,0},{3,1},{4,6},{5,7},{6,4},{7,5},{8,10},{9,11},{10,... | collective-permute-start | bytes 786440 | tf_op jit(solution)/shard_map/ppermute | solution.py:303
  21.4 8.7 %collective-permute-start.13 = (bf16[16,32,128]{2,1,0:T(8,128)(2,1)S(1)}, bf16[16,32,128]{2,1,0:T(8,128)(2,1)S(1)}, u32[]{:S(2)}, u32[]{:S(2)}) collective-permute-start(bf16[16,32,128]{2,1,0:T(8,128)(2,1)S(1)} %get-tuple-element.39), channel_id=1, source_target_pairs={{0,2},{1,3},{2,0},{3,1},{4,6},{5,7},{6,4},{7,5},{8,10},{9,11},{10,... | collective-permute-start | bytes 393224 | tf_op jit(solution)/shard_map/ppermute | solution.py:303
  30.0 19.4 %collective-permute-start.14 = (bf16[16,32,128]{2,1,0:T(8,128)(2,1)S(1)}, bf16[16,32,128]{2,1,0:T(8,128)(2,1)S(1)}, u32[]{:S(2)}, u32[]{:S(2)}) collective-permute-start(bf16[16,32,128]{2,1,0:T(8,128)(2,1)S(1)} %get-tuple-element.40), channel_id=1, source_target_pairs={{0,4},{1,5},{2,6},{3,7},{4,0},{5,1},{6,2},{7,3},{8,12},{9,13},{10,... | collective-permute-start | bytes 393224 | tf_op jit(solution)/shard_map/ppermute | solution.py:303
  49.4 6.3 %collective-permute-start.15 = (bf16[16,32,128]{2,1,0:T(8,128)(2,1)S(1)}, bf16[16,32,128]{2,1,0:T(8,128)(2,1)S(1)}, u32[]{:S(2)}, u32[]{:S(2)}) collective-permute-start(bf16[16,32,128]{2,1,0:T(8,128)(2,1)S(1)} %get-tuple-element.41), channel_id=1, source_target_pairs={{0,6},{1,7},{2,4},{3,5},{4,2},{5,3},{6,0},{7,1},{8,14},{9,15},{10,... | collective-permute-start | bytes 393224 | tf_op jit(solution)/shard_map/ppermute | solution.py:303
  55.7 10.2 %collective-permute-start.1 = (bf16[32,32,128]{2,1,0:T(8,128)(2,1)S(1)}, bf16[32,32,128]{2,1,0:T(8,128)(2,1)S(1)}, u32[]{:S(2)}, u32[]{:S(2)}) collective-permute-start(bf16[32,32,128]{2,1,0:T(8,128)(2,1)S(1)} %get-tuple-element.28), channel_id=1, source_target_pairs={{0,4},{1,5},{2,6},{3,7},{4,0},{5,1},{6,2},{7,3},{8,12},{9,13},{10,... | collective-permute-start | bytes 786440 | tf_op jit(solution)/shard_map/ppermute | solution.py:303
  56.2 15.4 %collective-permute-start.2 = (bf16[32,32,128]{2,1,0:T(8,128)(2,1)S(1)}, bf16[32,32,128]{2,1,0:T(8,128)(2,1)S(1)}, u32[]{:S(2)}, u32[]{:S(2)}) collective-permute-start(bf16[32,32,128]{2,1,0:T(8,128)(2,1)S(1)} %get-tuple-element.29), channel_id=1, source_target_pairs={{0,6},{1,7},{2,4},{3,5},{4,2},{5,3},{6,0},{7,1},{8,14},{9,15},{10,... | collective-permute-start | bytes 786440 | tf_op jit(solution)/shard_map/ppermute | solution.py:303
  60.0 44.8 %collective-permute-start.11 = (bf16[16,32,128]{2,1,0:T(8,128)(2,1)S(1)}, bf16[16,32,128]{2,1,0:T(8,128)(2,1)S(1)}, u32[]{:S(2)}, u32[]{:S(2)}) collective-permute-start(bf16[16,32,128]{2,1,0:T(8,128)(2,1)S(1)} %get-tuple-element.37), channel_id=1, source_target_pairs={{0,6},{1,7},{2,4},{3,5},{4,2},{5,3},{6,0},{7,1},{8,14},{9,15},{10,... | collective-permute-start | bytes 393224 | tf_op jit(solution)/shard_map/ppermute | solution.py:303
  61.4 43.3 %collective-permute-start.10 = (bf16[16,32,128]{2,1,0:T(8,128)(2,1)S(1)}, bf16[16,32,128]{2,1,0:T(8,128)(2,1)S(1)}, u32[]{:S(2)}, u32[]{:S(2)}) collective-permute-start(bf16[16,32,128]{2,1,0:T(8,128)(2,1)S(1)} %get-tuple-element.36), channel_id=1, source_target_pairs={{0,4},{1,5},{2,6},{3,7},{4,0},{5,1},{6,2},{7,3},{8,12},{9,13},{10,... | collective-permute-start | bytes 393224 | tf_op jit(solution)/shard_map/ppermute | solution.py:303
  64.1 40.6 %collective-permute-start.9 = (bf16[16,32,128]{2,1,0:T(8,128)(2,1)S(1)}, bf16[16,32,128]{2,1,0:T(8,128)(2,1)S(1)}, u32[]{:S(2)}, u32[]{:S(2)}) collective-permute-start(bf16[16,32,128]{2,1,0:T(8,128)(2,1)S(1)} %get-tuple-element.35), channel_id=1, source_target_pairs={{0,2},{1,3},{2,0},{3,1},{4,6},{5,7},{6,4},{7,5},{8,10},{9,11},{10,... | collective-permute-start | bytes 393224 | tf_op jit(solution)/shard_map/ppermute | solution.py:303
  65.9 26.3 %collective-permute-start.4 = (bf16[16,32,128]{2,1,0:T(8,128)(2,1)S(1)}, bf16[16,32,128]{2,1,0:T(8,128)(2,1)S(1)}, u32[]{:S(2)}, u32[]{:S(2)}) collective-permute-start(bf16[16,32,128]{2,1,0:T(8,128)(2,1)S(1)} %get-tuple-element.31), channel_id=1, source_target_pairs={{0,2},{1,3},{2,0},{3,1},{4,6},{5,7},{6,4},{7,5},{8,10},{9,11},{10,... | collective-permute-start | bytes 393224 | tf_op jit(solution)/shard_map/ppermute | solution.py:303
  71.6 8.8 %collective-permute-start.17 = (bf16[16,32,128]{2,1,0:T(8,128)(2,1)S(1)}, bf16[16,32,128]{2,1,0:T(8,128)(2,1)S(1)}, u32[]{:S(2)}, u32[]{:S(2)}) collective-permute-start(bf16[16,32,128]{2,1,0:T(8,128)(2,1)S(1)} %get-tuple-element.43), channel_id=1, source_target_pairs={{0,2},{1,3},{2,0},{3,1},{4,6},{5,7},{6,4},{7,5},{8,10},{9,11},{10,... | collective-permute-start | bytes 393224 | tf_op jit(solution)/shard_map/ppermute | solution.py:303
  80.4 5.0 %collective-permute-start.18 = (bf16[16,32,128]{2,1,0:T(8,128)(2,1)S(1)}, bf16[16,32,128]{2,1,0:T(8,128)(2,1)S(1)}, u32[]{:S(2)}, u32[]{:S(2)}) collective-permute-start(bf16[16,32,128]{2,1,0:T(8,128)(2,1)S(1)} %get-tuple-element.44), channel_id=1, source_target_pairs={{0,4},{1,5},{2,6},{3,7},{4,0},{5,1},{6,2},{7,3},{8,12},{9,13},{10,... | collective-permute-start | bytes 393224 | tf_op jit(solution)/shard_map/ppermute | solution.py:303
  85.4 5.9 %collective-permute-start.19 = (bf16[16,32,128]{2,1,0:T(8,128)(2,1)S(1)}, bf16[16,32,128]{2,1,0:T(8,128)(2,1)S(1)}, u32[]{:S(2)}, u32[]{:S(2)}) collective-permute-start(bf16[16,32,128]{2,1,0:T(8,128)(2,1)S(1)} %get-tuple-element.45), channel_id=1, source_target_pairs={{0,6},{1,7},{2,4},{3,5},{4,2},{5,3},{6,0},{7,1},{8,14},{9,15},{10,... | collective-permute-start | bytes 393224 | tf_op jit(solution)/shard_map/ppermute | solution.py:303
  91.3 5.0 %collective-permute-start.5 = (bf16[16,32,128]{2,1,0:T(8,128)(2,1)S(1)}, bf16[16,32,128]{2,1,0:T(8,128)(2,1)S(1)}, u32[]{:S(2)}, u32[]{:S(2)}) collective-permute-start(bf16[16,32,128]{2,1,0:T(8,128)(2,1)S(1)} %get-tuple-element.32), channel_id=1, source_target_pairs={{0,4},{1,5},{2,6},{3,7},{4,0},{5,1},{6,2},{7,3},{8,12},{9,13},{10,... | collective-permute-start | bytes 393224 | tf_op jit(solution)/shard_map/ppermute | solution.py:303
  92.2 10.0 %collective-permute-start.20 = (bf16[64,32,128]{2,1,0:T(8,128)(2,1)S(1)}, bf16[64,32,128]{2,1,0:T(8,128)(2,1)S(1)}, u32[]{:S(2)}, u32[]{:S(2)}) collective-permute-start(bf16[64,32,128]{2,1,0:T(8,128)(2,1)S(1)} %constant_dynamic-update-slice_fusion.29), channel_id=1, source_target_pairs={{0,1},{1,0},{2,3},{3,2},{4,5},{5,4},{6,7},{7,6},{8,9},{9,8},{10,11... | collective-permute-start | bytes 1572872 | tf_op jit(solution)/shard_map/ppermute | solution.py:313
  96.2 5.9 %collective-permute-start.6 = (bf16[16,32,128]{2,1,0:T(8,128)(2,1)S(1)}, bf16[16,32,128]{2,1,0:T(8,128)(2,1)S(1)}, u32[]{:S(2)}, u32[]{:S(2)}) collective-permute-start(bf16[16,32,128]{2,1,0:T(8,128)(2,1)S(1)} %get-tuple-element.33), channel_id=1, source_target_pairs={{0,6},{1,7},{2,4},{3,5},{4,2},{5,3},{6,0},{7,1},{8,14},{9,15},{10,... | collective-permute-start | bytes 393224 | tf_op jit(solution)/shard_map/ppermute | solution.py:303
  102.1 2.4 %collective-permute-start.7 = (bf16[96,32,128]{2,1,0:T(8,128)(2,1)S(1)}, bf16[96,32,128]{2,1,0:T(8,128)(2,1)S(1)}, u32[]{:S(2)}, u32[]{:S(2)}) collective-permute-start(bf16[96,32,128]{2,1,0:T(8,128)(2,1)S(1)} %constant_dynamic-update-slice_fusion), channel_id=1, source_target_pairs={{0,1},{1,0},{2,3},{3,2},{4,5},{5,4},{6,7},{7,6},{8,9},{9,8},{10,11... | collective-permute-start | bytes 2359304 | tf_op jit(solution)/shard_map/ppermute | solution.py:313
  104.8 6.4 %collective-permute-start.12 = (bf16[32,32,128]{2,1,0:T(8,128)(2,1)S(1)}, bf16[32,32,128]{2,1,0:T(8,128)(2,1)S(1)}, u32[]{:S(2)}, u32[]{:S(2)}) collective-permute-start(bf16[32,32,128]{2,1,0:T(8,128)(2,1)S(1)} %pad_maximum_fusion), channel_id=1, source_target_pairs={{0,1},{1,0},{2,3},{3,2},{4,5},{5,4},{6,7},{7,6},{8,9},{9,8},{10,11... | collective-permute-start | bytes 786440 | tf_op jit(solution)/shard_map/ppermute | solution.py:313
  105.1 0.8 copy-start
  105.1 0.8 copy-start.1
  (1 other events, 0.7 us)

commit v9 on v8

--- a/solution.py
+++ b/solution.py
@@ -299,8 +299,11 @@
             got = got.reshape(relays, count, cap, 2 * WR, WC)
             return [([got[:, at].reshape(relays * cap, 2 * WR, WC)], []) for at in range(count)]
         got = [parts[0]]
-        for m in range(1, chips):
-            got.append(lax.ppermute(parts[m], "sky", swap(2 * m)))
+        step = relays // len(parts)
+        for m in range(1, len(parts)):
+            got.append(lax.ppermute(parts[m], "sky", swap(step * m)))
+        if step == 1:
+            return [(got[::2] + got[1::2], [])]
 
         def pieces(at):
             return [part[at * cap : (at + 1) * cap] for part in got]
@@ -320,9 +323,10 @@
     def mirror(plane):
         return lax.ppermute(sheets[plane], "sky", mirror_pairs)
 
-    def cut_sent(planes, mirrored, tiles_of):
-        parts = cut(planes, cap, outs, mirrored, place, asked, tiles_of)
-        return ship(parts, len(planes))
+    def cut_sent(plane, mirrored, sheet, straight=False):
+        count = outs * 2 if straight and not direct else outs
+        parts = cut((plane,), cap, count, mirrored, place, asked, (sheet,))
+        return ship(parts, 1)[0]
 
     index = lax.axis_index("sky").astype(jnp.int32)
     place = jnp.stack([index // relays, jnp.zeros_like(index) if direct else index % relays])
@@ -333,20 +337,15 @@
     mirrors = [mirror(plane) for plane in range(PLANES)]
     asked = exchange(requests)
     slots = find_slots(place, tiles, peers, cap, direct)
-    rest = tuple(range(1, PLANES))
-    own = cut_sent((0,), False, sheets[:1])
-    far = cut_sent((0,), True, mirrors[:1])
-    own += cut_sent(rest, False, sheets[1:])
-    for plane in rest:
-        far += cut_sent((plane,), True, mirrors[plane : plane + 1])
+    own, far = [], []
+    for plane in range(PLANES):
+        own.append(cut_sent(plane, False, sheets[plane]))
+        far.append(cut_sent(plane, True, mirrors[plane], plane == PLANES - 1))
     state = (start_x, start_y)
-    held = {}
     for plane in range(PLANES):
-        news = [("own", plane)] if plane == 0 else [("own", k) for k in rest] if plane == 1 else []
-        news.append(("far", plane))
-        source = {"own": own, "far": far}
-        held.update(zip(news, across([source[kind][k][1] for kind, k in news])))
-        windows = own[plane][0] + held["own", plane] + far[plane][0] + held["far", plane]
+        sets = (own[plane], far[plane])
+        held = iter(across([other for _, other in sets if other]))
+        windows = sum((mine + (next(held) if other else []) for mine, other in sets), [])
         state = interp(plane, slots, jnp.concatenate(windows, axis=0), state)
     return state
 

time: 115 us -> 108 us (0.939)
  waiting for transfers between devices: 64 us -> 46.6 us
  starting transfers between devices: 28.5 us -> 37.9 us
    ppermute x15 -> x22, waiting for transfers between devices: 61.9 us -> 46.5 us  [ship(): got.append(lax.ppermute(parts[m], 'sky', swap(step * m)))]
    ppermute x15 -> x22, starting transfers between devices: 17.3 us -> 26.4 us  [ship(): got.append(lax.ppermute(parts[m], 'sky', swap(step * m)))]
    ppermute x3, waiting for transfers between devices: 2.17 us -> 0.01 us  [across(): got = lax.ppermute(jnp.concatenate(sum(lists, []), axis=0), 'sky', swap(1))]
    pallas_call x5 -> x6, Pallas kernels: 5.63 us -> 6.31 us  [cut(): pl.pallas_call(functools.partial(cut_kernel, planes, cap, mirrored), out_...]
  transfers between devices with their start and end apart: 22 -> 29, of which waited for: 10 -> 14; matrix products, arithmetic and copies ran while one was open for 2% -> 2% of each run, Pallas kernels for 10% -> 7%
where the time goes in v9:
time: 108 us; the launch traced here: 107 us
  waiting for transfers between devices  46.6 us (43%)
  starting transfers between devices  37.9 us (35%)
  Pallas kernels  17.8 us (16%)
  local copies, waits for them, and re-layouts  4.05 us (4%)
    ppermute x22, waiting for transfers between devices, ship(): got.append(lax.ppermute(parts[m], 'sky', swap(step * m)))  46.5 us
    ppermute x22, starting transfers between devices, ship(): got.append(lax.ppermute(parts[m], 'sky', swap(step * m)))  26.4 us
    pallas_call x3, Pallas kernels, interp(): pl.pallas_call(functools.partial(interp_kernel, plane), out_shape=out_sha...  8.98 us
    pallas_call x6, Pallas kernels, cut(): pl.pallas_call(functools.partial(cut_kernel, planes, cap, mirrored), out_...  6.31 us
    ppermute x3, starting transfers between devices, mirror(): return lax.ppermute(sheets[plane], 'sky', mirror_pairs)  5.64 us
    all_to_all x1, starting transfers between devices, exchange(): lax.all_to_all(x, 'sky', split_axis=0, concat_axis=0, axis_index_groups=g...  5.28 us
  transfers between devices with their start and end apart: 29, of which 14 were waited for; matrix products, arithmetic and copies ran while one was open for 2% of the time, Pallas kernels for 7%

profile of v9, /device:TPU:0, one launch (start us, length us, event | category | flops | bytes accessed | tf_op | source)
XLA Modules:
  0.0 107.4 jit_solution(795394622516298647)
XLA Ops:
  0.6 1.8 %want.1 = s32[8,128]{1,0:T(8,128)} custom-call(s32[3,1,64]{2,1,0:T(1,128)} %bitcast.19, s32[3,64]{1,0:T(4,128)} %row_ref.1, s32[3,64]{1,0:T(4,128)} %col_ref.1), custom_call_target="tpu_custom_call" | custom-call | tf_op jit(solution)/shard_map/want/pallas_call | solution.py:65
  2.5 5.3 %all-to-all-start = ((s32[8,1,128]{2,1,0:T(1,128)}), s32[8,1,128]{2,1,0:T(1,128)S(1)}, u32[]{:S(2)}, u32[]{:S(2)}) async-start(s32[8,1,128]{2,1,0:T(1,128)} %bitcast.21), calls=%async_computation | async-start | bytes 8192 | tf_op jit(solution)/shard_map/all_to_all | solution.py:292
  8.7 2.7 %collective-permute-start.23 = (bf16[2,256,256]{2,1,0:T(8,128)(2,1)S(1)}, bf16[2,256,256]{2,1,0:T(8,128)(2,1)S(1)}, u32[]{:S(2)}, u32[]{:S(2)}) collective-permute-start(bf16[2,256,256]{2,1,0:T(8,128)(2,1)S(1)} %slice_bitcast_fusion.refs_0_), channel_id=1, source_target_pairs={{0,8},{1,9},{2,10},{3,11},{4,12},{5,13},{6,14},{7,15},{8,0},{9,1},... | collective-permute-start | bytes 786440 | tf_op jit(solution)/shard_map/ppermute | solution.py:324
  12.8 2.6 %collective-permute-start.4 = (bf16[2,256,256]{2,1,0:T(8,128)(2,1)S(1)}, bf16[2,256,256]{2,1,0:T(8,128)(2,1)S(1)}, u32[]{:S(2)}, u32[]{:S(2)}) collective-permute-start(bf16[2,256,256]{2,1,0:T(8,128)(2,1)S(1)} %get-tuple-element.63.refs_0_), channel_id=1, source_target_pairs={{0,8},{1,9},{2,10},{3,11},{4,12},{5,13},{6,14},{7,15},{8,0},{9,1},... | collective-permute-start | bytes 786440 | tf_op jit(solution)/shard_map/ppermute | solution.py:324
  20.1 2.1 %collective-permute-start.20 = (bf16[16,32,128]{2,1,0:T(8,128)(2,1)S(1)}, bf16[16,32,128]{2,1,0:T(8,128)(2,1)S(1)}, u32[]{:S(2)}, u32[]{:S(2)}) collective-permute-start(bf16[16,32,128]{2,1,0:T(8,128)(2,1)S(1)} %get-tuple-element.55), channel_id=1, source_target_pairs={{0,2},{1,3},{2,0},{3,1},{4,6},{5,7},{6,4},{7,5},{8,10},{9,11},{10,... | collective-permute-start | bytes 393224 | tf_op jit(solution)/shard_map/ppermute | solution.py:304
  22.3 5.7 %collective-permute-done = bf16[16,32,128]{2,1,0:T(8,128)(2,1)S(1)} collective-permute-done((bf16[16,32,128]{2,1,0:T(8,128)(2,1)S(1)}, bf16[16,32,128]{2,1,0:T(8,128)(2,1)S(1)}, u32[]{:S(2)}, u32[]{:S(2)}) %collective-permute-start) | collective-permute-done | bytes 131104 | tf_op jit(solution)/shard_map/ppermute | solution.py:304
  28.0 1.6 %collective-permute-start.1 = (bf16[16,32,128]{2,1,0:T(8,128)(2,1)S(1)}, bf16[16,32,128]{2,1,0:T(8,128)(2,1)S(1)}, u32[]{:S(2)}, u32[]{:S(2)}) collective-permute-start(bf16[16,32,128]{2,1,0:T(8,128)(2,1)S(1)} %get-tuple-element.36), channel_id=1, source_target_pairs={{0,4},{1,5},{2,6},{3,7},{4,0},{5,1},{6,2},{7,3},{8,12},{9,13},{10,... | collective-permute-start | bytes 393224 | tf_op jit(solution)/shard_map/ppermute | solution.py:304
  29.6 19.6 %collective-permute-done.1 = bf16[16,32,128]{2,1,0:T(8,128)(2,1)S(1)} collective-permute-done((bf16[16,32,128]{2,1,0:T(8,128)(2,1)S(1)}, bf16[16,32,128]{2,1,0:T(8,128)(2,1)S(1)}, u32[]{:S(2)}, u32[]{:S(2)}) %collective-permute-start.1) | collective-permute-done | bytes 131104 | tf_op jit(solution)/shard_map/ppermute | solution.py:304
  49.8 6.7 %collective-permute-done.2 = bf16[16,32,128]{2,1,0:T(8,128)(2,1)S(1)} collective-permute-done((bf16[16,32,128]{2,1,0:T(8,128)(2,1)S(1)}, bf16[16,32,128]{2,1,0:T(8,128)(2,1)S(1)}, u32[]{:S(2)}, u32[]{:S(2)}) %collective-permute-start.2) | collective-permute-done | bytes 131104 | tf_op jit(solution)/shard_map/ppermute | solution.py:304
  56.5 3.2 %collective-permute-start.22 = (bf16[16,32,128]{2,1,0:T(8,128)(2,1)S(1)}, bf16[16,32,128]{2,1,0:T(8,128)(2,1)S(1)}, u32[]{:S(2)}, u32[]{:S(2)}) collective-permute-start(bf16[16,32,128]{2,1,0:T(8,128)(2,1)S(1)} %get-tuple-element.57), channel_id=1, source_target_pairs={{0,6},{1,7},{2,4},{3,5},{4,2},{5,3},{6,0},{7,1},{8,14},{9,15},{10,... | collective-permute-start | bytes 393224 | tf_op jit(solution)/shard_map/ppermute | solution.py:304
  59.7 2.7 %collective-permute-done.21 = bf16[16,32,128]{2,1,0:T(8,128)(2,1)S(1)} collective-permute-done((bf16[16,32,128]{2,1,0:T(8,128)(2,1)S(1)}, bf16[16,32,128]{2,1,0:T(8,128)(2,1)S(1)}, u32[]{:S(2)}, u32[]{:S(2)}) %collective-permute-start.21) | collective-permute-done | bytes 131104 | tf_op jit(solution)/shard_map/ppermute | solution.py:304
  62.4 2.1 %collective-permute-start.12 = (bf16[16,32,128]{2,1,0:T(8,128)(2,1)S(1)}, bf16[16,32,128]{2,1,0:T(8,128)(2,1)S(1)}, u32[]{:S(2)}, u32[]{:S(2)}) collective-permute-start(bf16[16,32,128]{2,1,0:T(8,128)(2,1)S(1)} %get-tuple-element.47), channel_id=1, source_target_pairs={{0,2},{1,3},{2,0},{3,1},{4,6},{5,7},{6,4},{7,5},{8,10},{9,11},{10,... | collective-permute-start | bytes 393224 | tf_op jit(solution)/shard_map/ppermute | solution.py:304
  64.5 1.5 %collective-permute-done.22 = bf16[16,32,128]{2,1,0:T(8,128)(2,1)S(1)} collective-permute-done((bf16[16,32,128]{2,1,0:T(8,128)(2,1)S(1)}, bf16[16,32,128]{2,1,0:T(8,128)(2,1)S(1)}, u32[]{:S(2)}, u32[]{:S(2)}) %collective-permute-start.22) | collective-permute-done | bytes 131104 | tf_op jit(solution)/shard_map/ppermute | solution.py:304
  67.5 1.5 %collective-permute-start.14 = (bf16[16,32,128]{2,1,0:T(8,128)(2,1)S(1)}, bf16[16,32,128]{2,1,0:T(8,128)(2,1)S(1)}, u32[]{:S(2)}, u32[]{:S(2)}) collective-permute-start(bf16[16,32,128]{2,1,0:T(8,128)(2,1)S(1)} %get-tuple-element.49), channel_id=1, source_target_pairs={{0,6},{1,7},{2,4},{3,5},{4,2},{5,3},{6,0},{7,1},{8,14},{9,15},{10,... | collective-permute-start | bytes 393224 | tf_op jit(solution)/shard_map/ppermute | solution.py:304
  69.0 2.0 %collective-permute-done.13 = bf16[16,32,128]{2,1,0:T(8,128)(2,1)S(1)} collective-permute-done((bf16[16,32,128]{2,1,0:T(8,128)(2,1)S(1)}, bf16[16,32,128]{2,1,0:T(8,128)(2,1)S(1)}, u32[]{:S(2)}, u32[]{:S(2)}) %collective-permute-start.13) | collective-permute-done | bytes 131104 | tf_op jit(solution)/shard_map/ppermute | solution.py:304
  71.0 2.3 %collective-permute-done.14 = bf16[16,32,128]{2,1,0:T(8,128)(2,1)S(1)} collective-permute-done((bf16[16,32,128]{2,1,0:T(8,128)(2,1)S(1)}, bf16[16,32,128]{2,1,0:T(8,128)(2,1)S(1)}, u32[]{:S(2)}, u32[]{:S(2)}) %collective-permute-start.14) | collective-permute-done | bytes 131104 | tf_op jit(solution)/shard_map/ppermute | solution.py:304
  74.4 2.1 %collective-permute-start.24 = (bf16[16,32,128]{2,1,0:T(8,128)(2,1)S(1)}, bf16[16,32,128]{2,1,0:T(8,128)(2,1)S(1)}, u32[]{:S(2)}, u32[]{:S(2)}) collective-permute-start(bf16[16,32,128]{2,1,0:T(8,128)(2,1)S(1)} %get-tuple-element.59), channel_id=1, source_target_pairs={{0,2},{1,3},{2,0},{3,1},{4,6},{5,7},{6,4},{7,5},{8,10},{9,11},{10,... | collective-permute-start | bytes 393224 | tf_op jit(solution)/shard_map/ppermute | solution.py:304
  76.5 1.5 %collective-permute-start.26 = (bf16[16,32,128]{2,1,0:T(8,128)(2,1)S(1)}, bf16[16,32,128]{2,1,0:T(8,128)(2,1)S(1)}, u32[]{:S(2)}, u32[]{:S(2)}) collective-permute-start(bf16[16,32,128]{2,1,0:T(8,128)(2,1)S(1)} %get-tuple-element.61), channel_id=1, source_target_pairs={{0,6},{1,7},{2,4},{3,5},{4,2},{5,3},{6,0},{7,1},{8,14},{9,15},{10,... | collective-permute-start | bytes 393224 | tf_op jit(solution)/shard_map/ppermute | solution.py:304
  79.2 2.0 %collective-permute-start.16 = (bf16[16,32,128]{2,1,0:T(8,128)(2,1)S(1)}, bf16[16,32,128]{2,1,0:T(8,128)(2,1)S(1)}, u32[]{:S(2)}, u32[]{:S(2)}) collective-permute-start(bf16[16,32,128]{2,1,0:T(8,128)(2,1)S(1)} %get-tuple-element.51), channel_id=1, source_target_pairs={{0,2},{1,3},{2,0},{3,1},{4,6},{5,7},{6,4},{7,5},{8,10},{9,11},{10,... | collective-permute-start | bytes 393224 | tf_op jit(solution)/shard_map/ppermute | solution.py:304
  84.0 3.1 %collective-permute-start.5 = (bf16[8,32,128]{2,1,0:T(8,128)(2,1)S(1)}, bf16[8,32,128]{2,1,0:T(8,128)(2,1)S(1)}, u32[]{:S(2)}, u32[]{:S(2)}) collective-permute-start(bf16[8,32,128]{2,1,0:T(8,128)(2,1)S(1)} %get-tuple-element.39), channel_id=1, source_target_pairs={{0,2},{1,3},{2,0},{3,1},{4,6},{5,7},{6,4},{7,5},{8,10},{9,11},{10,... | collective-permute-start | bytes 196616 | tf_op jit(solution)/shard_map/ppermute | solution.py:304
  90.3 2.0 %collective-permute-start.9 = (bf16[8,32,128]{2,1,0:T(8,128)(2,1)S(1)}, bf16[8,32,128]{2,1,0:T(8,128)(2,1)S(1)}, u32[]{:S(2)}, u32[]{:S(2)}) collective-permute-start(bf16[8,32,128]{2,1,0:T(8,128)(2,1)S(1)} %get-tuple-element.43), channel_id=1, source_target_pairs={{0,3},{1,2},{2,1},{3,0},{4,7},{5,6},{6,5},{7,4},{8,11},{9,10},{10,... | collective-permute-start | bytes 196616 | tf_op jit(solution)/shard_map/ppermute | solution.py:304
  98.4 2.7 %shard_map.77.refs_0_ = f32[12,64,128]{2,1,0:T(8,128)S(1)} custom-call(s32[3,64]{1,0:T(4,128)S(1)} %slots.1.slot_ref, bf16[128,32,128]{2,1,0:T(8,128)(2,1)S(1)} %slice_dynamic-update-slice_fusion.win_ref, f32[64,128]{1,0:T(8,128)S(1)} %copy-done, f32[64,128]{1,0:T(8,128)S(1)} %copy-done.1), custom_call_target="tpu_custom_call" | custom-call | tf_op jit(solution)/shard_map/pallas_call | solution.py:264
  101.2 2.7 %shard_map.78.refs_0_ = f32[12,64,128]{2,1,0:T(8,128)S(1)} custom-call(s32[3,64]{1,0:T(4,128)S(1)} %slots.1.slot_ref, bf16[128,32,128]{2,1,0:T(8,128)(2,1)S(1)} %slice_dynamic-update-slice_fusion.2.win_ref, f32[12,64,128]{2,1,0:T(8,128)S(1)} %shard_map.77.refs_0_), custom_call_target="tpu_custom_call" | custom-call | tf_op jit(solution)/shard_map/pallas_call | solution.py:264
  103.9 3.5 %shard_map.79 = (f32[64,2,128]{2,1,0:T(2,128)}, f32[64,4,128]{2,1,0:T(4,128)}) custom-call(s32[3,64]{1,0:T(4,128)S(1)} %slots.1.slot_ref, bf16[128,32,128]{2,1,0:T(8,128)(2,1)S(1)} %constant_dynamic-update-slice_fusion.win_ref, f32[12,64,128]{2,1,0:T(8,128)S(1)} %shard_map.78.refs_0_), custom_call_target="tpu_custom_call" | custom-call | tf_op jit(solution)/shard_map/pallas_call | solution.py:264
  (96 shorter events, 23.5 us)
Async XLA Ops:
  2.5 14.4 %all-to-all-start = ((s32[8,1,128]{2,1,0:T(1,128)}), s32[8,1,128]{2,1,0:T(1,128)S(1)}, u32[]{:S(2)}, u32[]{:S(2)}) async-start(s32[8,1,128]{2,1,0:T(1,128)} %bitcast.21), calls=%async_computation | async-start | bytes 8192 | tf_op jit(solution)/shard_map/all_to_all | solution.py:292
  8.7 64.6 %collective-permute-start.23 = (bf16[2,256,256]{2,1,0:T(8,128)(2,1)S(1)}, bf16[2,256,256]{2,1,0:T(8,128)(2,1)S(1)}, u32[]{:S(2)}, u32[]{:S(2)}) collective-permute-start(bf16[2,256,256]{2,1,0:T(8,128)(2,1)S(1)} %slice_bitcast_fusion.refs_0_), channel_id=1, source_target_pairs={{0,8},{1,9},{2,10},{3,11},{4,12},{5,13},{6,14},{7,15},{8,0},{9,1},... | collective-permute-start | bytes 786440 | tf_op jit(solution)/shard_map/ppermute | solution.py:324
  12.4 64.1 %collective-permute-start.15 = (bf16[2,256,256]{2,1,0:T(8,128)(2,1)S(1)}, bf16[2,256,256]{2,1,0:T(8,128)(2,1)S(1)}, u32[]{:S(2)}, u32[]{:S(2)}) collective-permute-start(bf16[2,256,256]{2,1,0:T(8,128)(2,1)S(1)} %get-tuple-element.62.refs_0_), channel_id=1, source_target_pairs={{0,8},{1,9},{2,10},{3,11},{4,12},{5,13},{6,14},{7,15},{8,0},{9,1},... | collective-permute-start | bytes 786440 | tf_op jit(solution)/shard_map/ppermute | solution.py:324
  12.8 66.3 %collective-permute-start.4 = (bf16[2,256,256]{2,1,0:T(8,128)(2,1)S(1)}, bf16[2,256,256]{2,1,0:T(8,128)(2,1)S(1)}, u32[]{:S(2)}, u32[]{:S(2)}) collective-permute-start(bf16[2,256,256]{2,1,0:T(8,128)(2,1)S(1)} %get-tuple-element.63.refs_0_), channel_id=1, source_target_pairs={{0,8},{1,9},{2,10},{3,11},{4,12},{5,13},{6,14},{7,15},{8,0},{9,1},... | collective-permute-start | bytes 786440 | tf_op jit(solution)/shard_map/ppermute | solution.py:324
  20.1 36.4 %collective-permute-start.20 = (bf16[16,32,128]{2,1,0:T(8,128)(2,1)S(1)}, bf16[16,32,128]{2,1,0:T(8,128)(2,1)S(1)}, u32[]{:S(2)}, u32[]{:S(2)}) collective-permute-start(bf16[16,32,128]{2,1,0:T(8,128)(2,1)S(1)} %get-tuple-element.55), channel_id=1, source_target_pairs={{0,2},{1,3},{2,0},{3,1},{4,6},{5,7},{6,4},{7,5},{8,10},{9,11},{10,... | collective-permute-start | bytes 393224 | tf_op jit(solution)/shard_map/ppermute | solution.py:304
  22.2 5.8 %collective-permute-start = (bf16[16,32,128]{2,1,0:T(8,128)(2,1)S(1)}, bf16[16,32,128]{2,1,0:T(8,128)(2,1)S(1)}, u32[]{:S(2)}, u32[]{:S(2)}) collective-permute-start(bf16[16,32,128]{2,1,0:T(8,128)(2,1)S(1)} %get-tuple-element.35), channel_id=1, source_target_pairs={{0,2},{1,3},{2,0},{3,1},{4,6},{5,7},{6,4},{7,5},{8,10},{9,11},{10,... | collective-permute-start | bytes 393224 | tf_op jit(solution)/shard_map/ppermute | solution.py:304
  28.0 21.2 %collective-permute-start.1 = (bf16[16,32,128]{2,1,0:T(8,128)(2,1)S(1)}, bf16[16,32,128]{2,1,0:T(8,128)(2,1)S(1)}, u32[]{:S(2)}, u32[]{:S(2)}) collective-permute-start(bf16[16,32,128]{2,1,0:T(8,128)(2,1)S(1)} %get-tuple-element.36), channel_id=1, source_target_pairs={{0,4},{1,5},{2,6},{3,7},{4,0},{5,1},{6,2},{7,3},{8,12},{9,13},{10,... | collective-permute-start | bytes 393224 | tf_op jit(solution)/shard_map/ppermute | solution.py:304
  49.2 7.3 %collective-permute-start.2 = (bf16[16,32,128]{2,1,0:T(8,128)(2,1)S(1)}, bf16[16,32,128]{2,1,0:T(8,128)(2,1)S(1)}, u32[]{:S(2)}, u32[]{:S(2)}) collective-permute-start(bf16[16,32,128]{2,1,0:T(8,128)(2,1)S(1)} %get-tuple-element.37), channel_id=1, source_target_pairs={{0,6},{1,7},{2,4},{3,5},{4,2},{5,3},{6,0},{7,1},{8,14},{9,15},{10,... | collective-permute-start | bytes 393224 | tf_op jit(solution)/shard_map/ppermute | solution.py:304
  56.5 5.9 %collective-permute-start.21 = (bf16[16,32,128]{2,1,0:T(8,128)(2,1)S(1)}, bf16[16,32,128]{2,1,0:T(8,128)(2,1)S(1)}, u32[]{:S(2)}, u32[]{:S(2)}) collective-permute-start(bf16[16,32,128]{2,1,0:T(8,128)(2,1)S(1)} %get-tuple-element.56), channel_id=1, source_target_pairs={{0,4},{1,5},{2,6},{3,7},{4,0},{5,1},{6,2},{7,3},{8,12},{9,13},{10,... | collective-permute-start | bytes 393224 | tf_op jit(solution)/shard_map/ppermute | solution.py:304
  56.5 9.5 %collective-permute-start.22 = (bf16[16,32,128]{2,1,0:T(8,128)(2,1)S(1)}, bf16[16,32,128]{2,1,0:T(8,128)(2,1)S(1)}, u32[]{:S(2)}, u32[]{:S(2)}) collective-permute-start(bf16[16,32,128]{2,1,0:T(8,128)(2,1)S(1)} %get-tuple-element.57), channel_id=1, source_target_pairs={{0,6},{1,7},{2,4},{3,5},{4,2},{5,3},{6,0},{7,1},{8,14},{9,15},{10,... | collective-permute-start | bytes 393224 | tf_op jit(solution)/shard_map/ppermute | solution.py:304
  62.4 5.1 %collective-permute-start.12 = (bf16[16,32,128]{2,1,0:T(8,128)(2,1)S(1)}, bf16[16,32,128]{2,1,0:T(8,128)(2,1)S(1)}, u32[]{:S(2)}, u32[]{:S(2)}) collective-permute-start(bf16[16,32,128]{2,1,0:T(8,128)(2,1)S(1)} %get-tuple-element.47), channel_id=1, source_target_pairs={{0,2},{1,3},{2,0},{3,1},{4,6},{5,7},{6,4},{7,5},{8,10},{9,11},{10,... | collective-permute-start | bytes 393224 | tf_op jit(solution)/shard_map/ppermute | solution.py:304
  66.0 5.0 %collective-permute-start.13 = (bf16[16,32,128]{2,1,0:T(8,128)(2,1)S(1)}, bf16[16,32,128]{2,1,0:T(8,128)(2,1)S(1)}, u32[]{:S(2)}, u32[]{:S(2)}) collective-permute-start(bf16[16,32,128]{2,1,0:T(8,128)(2,1)S(1)} %get-tuple-element.48), channel_id=1, source_target_pairs={{0,4},{1,5},{2,6},{3,7},{4,0},{5,1},{6,2},{7,3},{8,12},{9,13},{10,... | collective-permute-start | bytes 393224 | tf_op jit(solution)/shard_map/ppermute | solution.py:304
  67.5 5.9 %collective-permute-start.14 = (bf16[16,32,128]{2,1,0:T(8,128)(2,1)S(1)}, bf16[16,32,128]{2,1,0:T(8,128)(2,1)S(1)}, u32[]{:S(2)}, u32[]{:S(2)}) collective-permute-start(bf16[16,32,128]{2,1,0:T(8,128)(2,1)S(1)} %get-tuple-element.49), channel_id=1, source_target_pairs={{0,6},{1,7},{2,4},{3,5},{4,2},{5,3},{6,0},{7,1},{8,14},{9,15},{10,... | collective-permute-start | bytes 393224 | tf_op jit(solution)/shard_map/ppermute | solution.py:304
  71.0 19.3 %collective-permute-start.3 = (bf16[32,32,128]{2,1,0:T(8,128)(2,1)S(1)}, bf16[32,32,128]{2,1,0:T(8,128)(2,1)S(1)}, u32[]{:S(2)}, u32[]{:S(2)}) collective-permute-start(bf16[32,32,128]{2,1,0:T(8,128)(2,1)S(1)} %pad_maximum_fusion), channel_id=1, source_target_pairs={{0,1},{1,0},{2,3},{3,2},{4,5},{5,4},{6,7},{7,6},{8,9},{9,8},{10,11... | collective-permute-start | bytes 786440 | tf_op jit(solution)/shard_map/ppermute | solution.py:316
  74.4 8.9 %collective-permute-start.24 = (bf16[16,32,128]{2,1,0:T(8,128)(2,1)S(1)}, bf16[16,32,128]{2,1,0:T(8,128)(2,1)S(1)}, u32[]{:S(2)}, u32[]{:S(2)}) collective-permute-start(bf16[16,32,128]{2,1,0:T(8,128)(2,1)S(1)} %get-tuple-element.59), channel_id=1, source_target_pairs={{0,2},{1,3},{2,0},{3,1},{4,6},{5,7},{6,4},{7,5},{8,10},{9,11},{10,... | collective-permute-start | bytes 393224 | tf_op jit(solution)/shard_map/ppermute | solution.py:304
  76.5 6.8 %collective-permute-start.25 = (bf16[16,32,128]{2,1,0:T(8,128)(2,1)S(1)}, bf16[16,32,128]{2,1,0:T(8,128)(2,1)S(1)}, u32[]{:S(2)}, u32[]{:S(2)}) collective-permute-start(bf16[16,32,128]{2,1,0:T(8,128)(2,1)S(1)} %get-tuple-element.60), channel_id=1, source_target_pairs={{0,4},{1,5},{2,6},{3,7},{4,0},{5,1},{6,2},{7,3},{8,12},{9,13},{10,... | collective-permute-start | bytes 393224 | tf_op jit(solution)/shard_map/ppermute | solution.py:304
  76.5 7.5 %collective-permute-start.26 = (bf16[16,32,128]{2,1,0:T(8,128)(2,1)S(1)}, bf16[16,32,128]{2,1,0:T(8,128)(2,1)S(1)}, u32[]{:S(2)}, u32[]{:S(2)}) collective-permute-start(bf16[16,32,128]{2,1,0:T(8,128)(2,1)S(1)} %get-tuple-element.61), channel_id=1, source_target_pairs={{0,6},{1,7},{2,4},{3,5},{4,2},{5,3},{6,0},{7,1},{8,14},{9,15},{10,... | collective-permute-start | bytes 393224 | tf_op jit(solution)/shard_map/ppermute | solution.py:304
  79.2 7.9 %collective-permute-start.16 = (bf16[16,32,128]{2,1,0:T(8,128)(2,1)S(1)}, bf16[16,32,128]{2,1,0:T(8,128)(2,1)S(1)}, u32[]{:S(2)}, u32[]{:S(2)}) collective-permute-start(bf16[16,32,128]{2,1,0:T(8,128)(2,1)S(1)} %get-tuple-element.51), channel_id=1, source_target_pairs={{0,2},{1,3},{2,0},{3,1},{4,6},{5,7},{6,4},{7,5},{8,10},{9,11},{10,... | collective-permute-start | bytes 393224 | tf_op jit(solution)/shard_map/ppermute | solution.py:304
  83.3 5.8 %collective-permute-start.17 = (bf16[16,32,128]{2,1,0:T(8,128)(2,1)S(1)}, bf16[16,32,128]{2,1,0:T(8,128)(2,1)S(1)}, u32[]{:S(2)}, u32[]{:S(2)}) collective-permute-start(bf16[16,32,128]{2,1,0:T(8,128)(2,1)S(1)} %get-tuple-element.52), channel_id=1, source_target_pairs={{0,4},{1,5},{2,6},{3,7},{4,0},{5,1},{6,2},{7,3},{8,12},{9,13},{10,... | collective-permute-start | bytes 393224 | tf_op jit(solution)/shard_map/ppermute | solution.py:304
  83.4 6.8 %collective-permute-start.18 = (bf16[16,32,128]{2,1,0:T(8,128)(2,1)S(1)}, bf16[16,32,128]{2,1,0:T(8,128)(2,1)S(1)}, u32[]{:S(2)}, u32[]{:S(2)}) collective-permute-start(bf16[16,32,128]{2,1,0:T(8,128)(2,1)S(1)} %get-tuple-element.53), channel_id=1, source_target_pairs={{0,6},{1,7},{2,4},{3,5},{4,2},{5,3},{6,0},{7,1},{8,14},{9,15},{10,... | collective-permute-start | bytes 393224 | tf_op jit(solution)/shard_map/ppermute | solution.py:304
  84.0 8.3 %collective-permute-start.5 = (bf16[8,32,128]{2,1,0:T(8,128)(2,1)S(1)}, bf16[8,32,128]{2,1,0:T(8,128)(2,1)S(1)}, u32[]{:S(2)}, u32[]{:S(2)}) collective-permute-start(bf16[8,32,128]{2,1,0:T(8,128)(2,1)S(1)} %get-tuple-element.39), channel_id=1, source_target_pairs={{0,2},{1,3},{2,0},{3,1},{4,6},{5,7},{6,4},{7,5},{8,10},{9,11},{10,... | collective-permute-start | bytes 196616 | tf_op jit(solution)/shard_map/ppermute | solution.py:304
  87.1 5.6 %collective-permute-start.6 = (bf16[8,32,128]{2,1,0:T(8,128)(2,1)S(1)}, bf16[8,32,128]{2,1,0:T(8,128)(2,1)S(1)}, u32[]{:S(2)}, u32[]{:S(2)}) collective-permute-start(bf16[8,32,128]{2,1,0:T(8,128)(2,1)S(1)} %get-tuple-element.40), channel_id=1, source_target_pairs={{0,4},{1,5},{2,6},{3,7},{4,0},{5,1},{6,2},{7,3},{8,12},{9,13},{10,... | collective-permute-start | bytes 196616 | tf_op jit(solution)/shard_map/ppermute | solution.py:304
  89.1 5.3 %collective-permute-start.7 = (bf16[8,32,128]{2,1,0:T(8,128)(2,1)S(1)}, bf16[8,32,128]{2,1,0:T(8,128)(2,1)S(1)}, u32[]{:S(2)}, u32[]{:S(2)}) collective-permute-start(bf16[8,32,128]{2,1,0:T(8,128)(2,1)S(1)} %get-tuple-element.41), channel_id=1, source_target_pairs={{0,6},{1,7},{2,4},{3,5},{4,2},{5,3},{6,0},{7,1},{8,14},{9,15},{10,... | collective-permute-start | bytes 196616 | tf_op jit(solution)/shard_map/ppermute | solution.py:304
  90.3 5.2 %collective-permute-start.9 = (bf16[8,32,128]{2,1,0:T(8,128)(2,1)S(1)}, bf16[8,32,128]{2,1,0:T(8,128)(2,1)S(1)}, u32[]{:S(2)}, u32[]{:S(2)}) collective-permute-start(bf16[8,32,128]{2,1,0:T(8,128)(2,1)S(1)} %get-tuple-element.43), channel_id=1, source_target_pairs={{0,3},{1,2},{2,1},{3,0},{4,7},{5,6},{6,5},{7,4},{8,11},{9,10},{10,... | collective-permute-start | bytes 196616 | tf_op jit(solution)/shard_map/ppermute | solution.py:304
  (8 other events, 21.4 us)

commit v10 on v9

--- a/solution.py
+++ b/solution.py
@@ -94,8 +94,8 @@
     )(place, tile_map)
 
 
-def cut_kernel(planes, cap, mirrored, place_ref, req_ref, *refs):
-    sheet_refs, out_refs, half_ref = refs[: len(planes)], refs[len(planes) : -1], refs[-1]
+def cut_kernel(plane, cap, kinds, place_ref, req_ref, *refs):
+    sheet_refs, out_refs, half_ref = refs[: len(kinds)], refs[len(kinds) : -1], refs[-1]
     parts = sheet_refs[0].shape[-1] // WC
     for at, sheet_ref in enumerate(sheet_refs):
         for c in range(2):
@@ -104,20 +104,20 @@
                 half_ref[(at * 2 + c) * parts + h] = part.astype(jnp.float32)
     lane = lax.broadcasted_iota(jnp.int32, (WR, WC), 1)
     me = place_ref[1]
-    side = 1 - place_ref[0] if mirrored else place_ref[0]
+    sides = [1 - place_ref[0] if mirrored else place_ref[0] for mirrored in kinds]
     span = req_ref.shape[0] // len(out_refs)
 
     def one(now, carry):
         for m, out_ref in enumerate(out_refs):
             source = (m * span + now) ^ me
-            for at, k in enumerate(planes):
+            for at, side in enumerate(sides):
                 for place in range(cap):
-                    packed = req_ref[source, (2 * k + side) * cap + place]
+                    packed = req_ref[source, (2 * plane + side) * cap + place]
                     row = packed >> 16
                     col = packed & 65535
                     turn = (WC - col) & (WC - 1)
                     left = lane < WC - col
-                    slot = (now * len(planes) + at) * cap + place
+                    slot = (now * len(kinds) + at) * cap + place
                     for c in range(2):
                         part = [
                             pltpu.roll(half_ref[(at * 2 + c) * parts + h, pl.ds(row, WR), :], turn, 1)
@@ -131,15 +131,15 @@
     lax.fori_loop(0, span, one, 0)
 
 
-def cut(planes, cap, outs, mirrored, place, requests, sheets):
-    count = requests.shape[0] // outs * len(planes) * cap
+def cut(plane, cap, outs, kinds, place, requests, sheets):
+    count = requests.shape[0] // outs * len(kinds) * cap
     height, width = sheets[0].shape[-2:]
     return pl.pallas_call(
-        functools.partial(cut_kernel, planes, cap, mirrored),
+        functools.partial(cut_kernel, plane, cap, kinds),
         out_shape=(jax.ShapeDtypeStruct((count, 2 * WR, WC), jnp.bfloat16),) * outs,
-        in_specs=[whole(SMEM), whole(SMEM)] + [whole()] * len(planes),
+        in_specs=[whole(SMEM), whole(SMEM)] + [whole()] * len(kinds),
         out_specs=(whole(),) * outs,
-        scratch_shapes=[VMEM((len(planes) * 2 * width // WC, height, WC), jnp.float32)],
+        scratch_shapes=[VMEM((len(kinds) * 2 * width // WC, height, WC), jnp.float32)],
         compiler_params=GRANT,
         name="cut",
     )(place, requests, *sheets)
@@ -302,17 +302,17 @@
         step = relays // len(parts)
         for m in range(1, len(parts)):
             got.append(lax.ppermute(parts[m], "sky", swap(step * m)))
+
+        def pieces(at, of=got):
+            return [part[at * cap : (at + 1) * cap] for part in of]
+
         if step == 1:
-            return [(got[::2] + got[1::2], [])]
-
-        def pieces(at):
-            return [part[at * cap : (at + 1) * cap] for part in got]
-
+            return [(pieces(at, got[::2] + got[1::2]), []) for at in range(count)]
         return [(pieces(at), pieces(count + at)) for at in range(count)]
 
     def across(lists):
-        if direct:
-            return [[] for _ in lists]
+        if not lists:
+            return []
         got = lax.ppermute(jnp.concatenate(sum(lists, []), axis=0), "sky", swap(1))
         size = chips * cap
         return [[got[at * size : (at + 1) * size]] for at in range(len(lists))]
@@ -323,10 +323,11 @@
     def mirror(plane):
         return lax.ppermute(sheets[plane], "sky", mirror_pairs)
 
-    def cut_sent(plane, mirrored, sheet, straight=False):
+    def cut_sent(plane, kinds, straight=False):
         count = outs * 2 if straight and not direct else outs
-        parts = cut((plane,), cap, count, mirrored, place, asked, (sheet,))
-        return ship(parts, 1)[0]
+        tiles_of = [mirrors[plane] if mirrored else sheets[plane] for mirrored in kinds]
+        parts = cut(plane, cap, count, kinds, place, asked, tiles_of)
+        return ship(parts, len(kinds))
 
     index = lax.axis_index("sky").astype(jnp.int32)
     place = jnp.stack([index // relays, jnp.zeros_like(index) if direct else index % relays])
@@ -337,13 +338,12 @@
     mirrors = [mirror(plane) for plane in range(PLANES)]
     asked = exchange(requests)
     slots = find_slots(place, tiles, peers, cap, direct)
-    own, far = [], []
-    for plane in range(PLANES):
-        own.append(cut_sent(plane, False, sheets[plane]))
-        far.append(cut_sent(plane, True, mirrors[plane], plane == PLANES - 1))
+    sent = [cut_sent(0, (False,)) + cut_sent(0, (True,))]
+    for plane in range(1, PLANES):
+        sent.append(cut_sent(plane, (False, True), plane == PLANES - 1))
     state = (start_x, start_y)
     for plane in range(PLANES):
-        sets = (own[plane], far[plane])
+        sets = sent[plane]
         held = iter(across([other for _, other in sets if other]))
         windows = sum((mine + (next(held) if other else []) for mine, other in sets), [])
         state = interp(plane, slots, jnp.concatenate(windows, axis=0), state)

time: 108 us -> 92.9 us (0.86)
  waiting for transfers between devices: 46.6 us -> 38.5 us
  starting transfers between devices: 37.9 us -> 32.7 us
  Pallas kernels: 17.8 us -> 16.2 us
    ppermute x22 -> x16, waiting for transfers between devices: 46.5 us -> 34.9 us  [ship(): got.append(lax.ppermute(parts[m], 'sky', swap(step * m)))]
    ppermute x22 -> x16, starting transfers between devices: 26.4 us -> 21.4 us  [ship(): got.append(lax.ppermute(parts[m], 'sky', swap(step * m)))]
    ppermute x3, waiting for transfers between devices: 0.01 us -> 3.61 us  [mirror(): return lax.ppermute(sheets[plane], 'sky', mirror_pairs)]
    pallas_call x6 -> x4, Pallas kernels: 6.31 us -> 4.78 us  [cut(): pl.pallas_call(functools.partial(cut_kernel, plane, cap, kinds), out_shap...]
  transfers between devices with their start and end apart: 29 -> 22, of which waited for: 14 -> 12; matrix products, arithmetic and copies ran while one was open for 2% -> 3% of each run, Pallas kernels for 7% -> 9%
where the time goes in v10:
time: 92.9 us; the launch traced here: 92.6 us
  waiting for transfers between devices  38.5 us (41%)
  starting transfers between devices  32.7 us (35%)
  Pallas kernels  16.2 us (17%)
  local copies, waits for them, and re-layouts  4.07 us (4%)
  between operations  0.98 us (1%)
    ppermute x16, waiting for transfers between devices, ship(): got.append(lax.ppermute(parts[m], 'sky', swap(step * m)))  34.9 us
    ppermute x16, starting transfers between devices, ship(): got.append(lax.ppermute(parts[m], 'sky', swap(step * m)))  21.4 us
    pallas_call x3, Pallas kernels, interp(): pl.pallas_call(functools.partial(interp_kernel, plane), out_shape=out_sha...  8.92 us
    ppermute x3, starting transfers between devices, mirror(): return lax.ppermute(sheets[plane], 'sky', mirror_pairs)  5.64 us
    all_to_all x1, starting transfers between devices, exchange(): lax.all_to_all(x, 'sky', split_axis=0, concat_axis=0, axis_index_groups=g...  5.28 us
    pallas_call x4, Pallas kernels, cut(): pl.pallas_call(functools.partial(cut_kernel, plane, cap, kinds), out_shap...  4.78 us
    ppermute x3, waiting for transfers between devices, mirror(): return lax.ppermute(sheets[plane], 'sky', mirror_pairs)  3.61 us
    squeeze x2, local copies, waits for them, and re-layouts, tile(): return sheet[plane]  2.03 us
  transfers between devices with their start and end apart: 22, of which 12 were waited for; matrix products, arithmetic and copies ran while one was open for 3% of the time, Pallas kernels for 9%

profile of v10, /device:TPU:0, one launch (start us, length us, event | category | flops | bytes accessed | tf_op | source)
XLA Modules:
  0.0 92.6 jit_solution(17754526265710283551)
XLA Ops:
  0.6 1.8 %want.1 = s32[8,128]{1,0:T(8,128)} custom-call(s32[3,1,64]{2,1,0:T(1,128)} %bitcast.17, s32[3,64]{1,0:T(4,128)} %row_ref.1, s32[3,64]{1,0:T(4,128)} %col_ref.1), custom_call_target="tpu_custom_call" | custom-call | tf_op jit(solution)/shard_map/want/pallas_call | solution.py:65
  2.5 5.3 %all-to-all-start = ((s32[8,1,128]{2,1,0:T(1,128)}), s32[8,1,128]{2,1,0:T(1,128)S(1)}, u32[]{:S(2)}, u32[]{:S(2)}) async-start(s32[8,1,128]{2,1,0:T(1,128)} %bitcast.19), calls=%async_computation | async-start | bytes 8192 | tf_op jit(solution)/shard_map/all_to_all | solution.py:292
  8.7 2.7 %collective-permute-start.16 = (bf16[2,256,256]{2,1,0:T(8,128)(2,1)S(1)}, bf16[2,256,256]{2,1,0:T(8,128)(2,1)S(1)}, u32[]{:S(2)}, u32[]{:S(2)}) collective-permute-start(bf16[2,256,256]{2,1,0:T(8,128)(2,1)S(1)} %slice_bitcast_fusion.refs_0_), channel_id=1, source_target_pairs={{0,8},{1,9},{2,10},{3,11},{4,12},{5,13},{6,14},{7,15},{8,0},{9,1},... | collective-permute-start | bytes 786440 | tf_op jit(solution)/shard_map/ppermute | solution.py:324
  12.8 2.6 %collective-permute-start = (bf16[2,256,256]{2,1,0:T(8,128)(2,1)S(1)}, bf16[2,256,256]{2,1,0:T(8,128)(2,1)S(1)}, u32[]{:S(2)}, u32[]{:S(2)}) collective-permute-start(bf16[2,256,256]{2,1,0:T(8,128)(2,1)S(1)} %get-tuple-element.47.refs_0_), channel_id=1, source_target_pairs={{0,8},{1,9},{2,10},{3,11},{4,12},{5,13},{6,14},{7,15},{8,0},{9,1},... | collective-permute-start | bytes 786440 | tf_op jit(solution)/shard_map/ppermute | solution.py:324
  17.9 2.1 %collective-permute-start.13 = (bf16[16,32,128]{2,1,0:T(8,128)(2,1)S(1)}, bf16[16,32,128]{2,1,0:T(8,128)(2,1)S(1)}, u32[]{:S(2)}, u32[]{:S(2)}) collective-permute-start(bf16[16,32,128]{2,1,0:T(8,128)(2,1)S(1)} %get-tuple-element.39), channel_id=1, source_target_pairs={{0,2},{1,3},{2,0},{3,1},{4,6},{5,7},{6,4},{7,5},{8,10},{9,11},{10,... | collective-permute-start | bytes 393224 | tf_op jit(solution)/shard_map/ppermute | solution.py:304
  20.0 1.5 %collective-permute-start.14 = (bf16[16,32,128]{2,1,0:T(8,128)(2,1)S(1)}, bf16[16,32,128]{2,1,0:T(8,128)(2,1)S(1)}, u32[]{:S(2)}, u32[]{:S(2)}) collective-permute-start(bf16[16,32,128]{2,1,0:T(8,128)(2,1)S(1)} %get-tuple-element.40), channel_id=1, source_target_pairs={{0,4},{1,5},{2,6},{3,7},{4,0},{5,1},{6,2},{7,3},{8,12},{9,13},{10,... | collective-permute-start | bytes 393224 | tf_op jit(solution)/shard_map/ppermute | solution.py:304
  21.5 1.6 %collective-permute-done.13 = bf16[16,32,128]{2,1,0:T(8,128)(2,1)S(1)} collective-permute-done((bf16[16,32,128]{2,1,0:T(8,128)(2,1)S(1)}, bf16[16,32,128]{2,1,0:T(8,128)(2,1)S(1)}, u32[]{:S(2)}, u32[]{:S(2)}) %collective-permute-start.13) | collective-permute-done | bytes 131104 | tf_op jit(solution)/shard_map/ppermute | solution.py:304
  23.0 2.8 %collective-permute-start.15 = (bf16[16,32,128]{2,1,0:T(8,128)(2,1)S(1)}, bf16[16,32,128]{2,1,0:T(8,128)(2,1)S(1)}, u32[]{:S(2)}, u32[]{:S(2)}) collective-permute-start(bf16[16,32,128]{2,1,0:T(8,128)(2,1)S(1)} %get-tuple-element.41), channel_id=1, source_target_pairs={{0,6},{1,7},{2,4},{3,5},{4,2},{5,3},{6,0},{7,1},{8,14},{9,15},{10,... | collective-permute-start | bytes 393224 | tf_op jit(solution)/shard_map/ppermute | solution.py:304
  25.9 6.3 %collective-permute-done.14 = bf16[16,32,128]{2,1,0:T(8,128)(2,1)S(1)} collective-permute-done((bf16[16,32,128]{2,1,0:T(8,128)(2,1)S(1)}, bf16[16,32,128]{2,1,0:T(8,128)(2,1)S(1)}, u32[]{:S(2)}, u32[]{:S(2)}) %collective-permute-start.14) | collective-permute-done | bytes 131104 | tf_op jit(solution)/shard_map/ppermute | solution.py:304
  32.2 2.3 %collective-permute-done.15 = bf16[16,32,128]{2,1,0:T(8,128)(2,1)S(1)} collective-permute-done((bf16[16,32,128]{2,1,0:T(8,128)(2,1)S(1)}, bf16[16,32,128]{2,1,0:T(8,128)(2,1)S(1)}, u32[]{:S(2)}, u32[]{:S(2)}) %collective-permute-start.15) | collective-permute-done | bytes 131104 | tf_op jit(solution)/shard_map/ppermute | solution.py:304
  36.8 2.1 %collective-permute-start.17 = (bf16[16,32,128]{2,1,0:T(8,128)(2,1)S(1)}, bf16[16,32,128]{2,1,0:T(8,128)(2,1)S(1)}, u32[]{:S(2)}, u32[]{:S(2)}) collective-permute-start(bf16[16,32,128]{2,1,0:T(8,128)(2,1)S(1)} %get-tuple-element.43), channel_id=1, source_target_pairs={{0,2},{1,3},{2,0},{3,1},{4,6},{5,7},{6,4},{7,5},{8,10},{9,11},{10,... | collective-permute-start | bytes 393224 | tf_op jit(solution)/shard_map/ppermute | solution.py:304
  42.8 2.1 %collective-permute-start.9 = (bf16[32,32,128]{2,1,0:T(8,128)(2,1)S(1)}, bf16[32,32,128]{2,1,0:T(8,128)(2,1)S(1)}, u32[]{:S(2)}, u32[]{:S(2)}) collective-permute-start(bf16[32,32,128]{2,1,0:T(8,128)(2,1)S(1)} %get-tuple-element.35), channel_id=1, source_target_pairs={{0,2},{1,3},{2,0},{3,1},{4,6},{5,7},{6,4},{7,5},{8,10},{9,11},{10,... | collective-permute-start | bytes 786440 | tf_op jit(solution)/shard_map/ppermute | solution.py:304
  44.9 1.7 %collective-permute-done.refs_1_ = bf16[2,256,256]{2,1,0:T(8,128)(2,1)S(1)} collective-permute-done((bf16[2,256,256]{2,1,0:T(8,128)(2,1)S(1)}, bf16[2,256,256]{2,1,0:T(8,128)(2,1)S(1)}, u32[]{:S(2)}, u32[]{:S(2)}) %collective-permute-start) | collective-permute-done | bytes 262176 | tf_op jit(solution)/shard_map/ppermute | solution.py:324
  48.5 2.5 %collective-permute-start.11 = (bf16[32,32,128]{2,1,0:T(8,128)(2,1)S(1)}, bf16[32,32,128]{2,1,0:T(8,128)(2,1)S(1)}, u32[]{:S(2)}, u32[]{:S(2)}) collective-permute-start(bf16[32,32,128]{2,1,0:T(8,128)(2,1)S(1)} %get-tuple-element.37), channel_id=1, source_target_pairs={{0,6},{1,7},{2,4},{3,5},{4,2},{5,3},{6,0},{7,1},{8,14},{9,15},{10,... | collective-permute-start | bytes 786440 | tf_op jit(solution)/shard_map/ppermute | solution.py:304
  51.6 1.7 %collective-permute-done.19 = bf16[16,32,128]{2,1,0:T(8,128)(2,1)S(1)} collective-permute-done((bf16[16,32,128]{2,1,0:T(8,128)(2,1)S(1)}, bf16[16,32,128]{2,1,0:T(8,128)(2,1)S(1)}, u32[]{:S(2)}, u32[]{:S(2)}) %collective-permute-start.19) | collective-permute-done | bytes 131104 | tf_op jit(solution)/shard_map/ppermute | solution.py:304
  53.3 2.8 %collective-permute-done.1 = bf16[16,32,128]{2,1,0:T(8,128)(2,1)S(1)} collective-permute-done((bf16[16,32,128]{2,1,0:T(8,128)(2,1)S(1)}, bf16[16,32,128]{2,1,0:T(8,128)(2,1)S(1)}, u32[]{:S(2)}, u32[]{:S(2)}) %collective-permute-start.1) | collective-permute-done | bytes 131104 | tf_op jit(solution)/shard_map/ppermute | solution.py:304
  56.1 5.3 %collective-permute-start.3 = (bf16[16,32,128]{2,1,0:T(8,128)(2,1)S(1)}, bf16[16,32,128]{2,1,0:T(8,128)(2,1)S(1)}, u32[]{:S(2)}, u32[]{:S(2)}) collective-permute-start(bf16[16,32,128]{2,1,0:T(8,128)(2,1)S(1)} %get-tuple-element.29), channel_id=1, source_target_pairs={{0,6},{1,7},{2,4},{3,5},{4,2},{5,3},{6,0},{7,1},{8,14},{9,15},{10,... | collective-permute-start | bytes 393224 | tf_op jit(solution)/shard_map/ppermute | solution.py:304
  61.4 4.8 %collective-permute-done.2 = bf16[16,32,128]{2,1,0:T(8,128)(2,1)S(1)} collective-permute-done((bf16[16,32,128]{2,1,0:T(8,128)(2,1)S(1)}, bf16[16,32,128]{2,1,0:T(8,128)(2,1)S(1)}, u32[]{:S(2)}, u32[]{:S(2)}) %collective-permute-start.2) | collective-permute-done | bytes 131104 | tf_op jit(solution)/shard_map/ppermute | solution.py:304
  66.3 3.7 %collective-permute-done.3 = bf16[16,32,128]{2,1,0:T(8,128)(2,1)S(1)} collective-permute-done((bf16[16,32,128]{2,1,0:T(8,128)(2,1)S(1)}, bf16[16,32,128]{2,1,0:T(8,128)(2,1)S(1)}, u32[]{:S(2)}, u32[]{:S(2)}) %collective-permute-start.3) | collective-permute-done | bytes 131104 | tf_op jit(solution)/shard_map/ppermute | solution.py:304
  70.2 5.4 %collective-permute-done.5 = bf16[16,32,128]{2,1,0:T(8,128)(2,1)S(1)} collective-permute-done((bf16[16,32,128]{2,1,0:T(8,128)(2,1)S(1)}, bf16[16,32,128]{2,1,0:T(8,128)(2,1)S(1)}, u32[]{:S(2)}, u32[]{:S(2)}) %collective-permute-start.5) | collective-permute-done | bytes 131104 | tf_op jit(solution)/shard_map/ppermute | solution.py:304
  75.8 6.2 %collective-permute-done.7 = bf16[16,32,128]{2,1,0:T(8,128)(2,1)S(1)} collective-permute-done((bf16[16,32,128]{2,1,0:T(8,128)(2,1)S(1)}, bf16[16,32,128]{2,1,0:T(8,128)(2,1)S(1)}, u32[]{:S(2)}, u32[]{:S(2)}) %collective-permute-start.7) | collective-permute-done | bytes 131104 | tf_op jit(solution)/shard_map/ppermute | solution.py:304
  83.5 2.7 %shard_map.77.refs_0_ = f32[12,64,128]{2,1,0:T(8,128)S(1)} custom-call(s32[3,64]{1,0:T(4,128)S(1)} %slots.1.slot_ref, bf16[128,32,128]{2,1,0:T(8,128)(2,1)S(1)} %slice_dynamic-update-slice_fusion.win_ref, f32[64,128]{1,0:T(8,128)S(1)} %copy-done, f32[64,128]{1,0:T(8,128)S(1)} %copy-done.1), custom_call_target="tpu_custom_call" | custom-call | tf_op jit(solution)/shard_map/pallas_call | solution.py:264
  86.3 2.7 %shard_map.78.refs_0_ = f32[12,64,128]{2,1,0:T(8,128)S(1)} custom-call(s32[3,64]{1,0:T(4,128)S(1)} %slots.1.slot_ref, bf16[128,32,128]{2,1,0:T(8,128)(2,1)S(1)} %slice_dynamic-update-slice_fusion.2.win_ref, f32[12,64,128]{2,1,0:T(8,128)S(1)} %shard_map.77.refs_0_), custom_call_target="tpu_custom_call" | custom-call | tf_op jit(solution)/shard_map/pallas_call | solution.py:264
  89.1 3.5 %shard_map.79 = (f32[64,2,128]{2,1,0:T(2,128)}, f32[64,4,128]{2,1,0:T(4,128)}) custom-call(s32[3,64]{1,0:T(4,128)S(1)} %slots.1.slot_ref, bf16[128,32,128]{2,1,0:T(8,128)(2,1)S(1)} %constant_dynamic-update-slice_fusion.win_ref, f32[12,64,128]{2,1,0:T(8,128)S(1)} %shard_map.78.refs_0_), custom_call_target="tpu_custom_call" | custom-call | tf_op jit(solution)/shard_map/pallas_call | solution.py:264
  (82 shorter events, 15.4 us)
Async XLA Ops:
  2.5 14.4 %all-to-all-start = ((s32[8,1,128]{2,1,0:T(1,128)}), s32[8,1,128]{2,1,0:T(1,128)S(1)}, u32[]{:S(2)}, u32[]{:S(2)}) async-start(s32[8,1,128]{2,1,0:T(1,128)} %bitcast.19), calls=%async_computation | async-start | bytes 8192 | tf_op jit(solution)/shard_map/all_to_all | solution.py:292
  8.7 27.0 %collective-permute-start.16 = (bf16[2,256,256]{2,1,0:T(8,128)(2,1)S(1)}, bf16[2,256,256]{2,1,0:T(8,128)(2,1)S(1)}, u32[]{:S(2)}, u32[]{:S(2)}) collective-permute-start(bf16[2,256,256]{2,1,0:T(8,128)(2,1)S(1)} %slice_bitcast_fusion.refs_0_), channel_id=1, source_target_pairs={{0,8},{1,9},{2,10},{3,11},{4,12},{5,13},{6,14},{7,15},{8,0},{9,1},... | collective-permute-start | bytes 786440 | tf_op jit(solution)/shard_map/ppermute | solution.py:324
  12.4 29.0 %collective-permute-start.8 = (bf16[2,256,256]{2,1,0:T(8,128)(2,1)S(1)}, bf16[2,256,256]{2,1,0:T(8,128)(2,1)S(1)}, u32[]{:S(2)}, u32[]{:S(2)}) collective-permute-start(bf16[2,256,256]{2,1,0:T(8,128)(2,1)S(1)} %get-tuple-element.46.refs_0_), channel_id=1, source_target_pairs={{0,8},{1,9},{2,10},{3,11},{4,12},{5,13},{6,14},{7,15},{8,0},{9,1},... | collective-permute-start | bytes 786440 | tf_op jit(solution)/shard_map/ppermute | solution.py:324
  12.8 33.7 %collective-permute-start = (bf16[2,256,256]{2,1,0:T(8,128)(2,1)S(1)}, bf16[2,256,256]{2,1,0:T(8,128)(2,1)S(1)}, u32[]{:S(2)}, u32[]{:S(2)}) collective-permute-start(bf16[2,256,256]{2,1,0:T(8,128)(2,1)S(1)} %get-tuple-element.47.refs_0_), channel_id=1, source_target_pairs={{0,8},{1,9},{2,10},{3,11},{4,12},{5,13},{6,14},{7,15},{8,0},{9,1},... | collective-permute-start | bytes 786440 | tf_op jit(solution)/shard_map/ppermute | solution.py:324
  17.9 5.1 %collective-permute-start.13 = (bf16[16,32,128]{2,1,0:T(8,128)(2,1)S(1)}, bf16[16,32,128]{2,1,0:T(8,128)(2,1)S(1)}, u32[]{:S(2)}, u32[]{:S(2)}) collective-permute-start(bf16[16,32,128]{2,1,0:T(8,128)(2,1)S(1)} %get-tuple-element.39), channel_id=1, source_target_pairs={{0,2},{1,3},{2,0},{3,1},{4,6},{5,7},{6,4},{7,5},{8,10},{9,11},{10,... | collective-permute-start | bytes 393224 | tf_op jit(solution)/shard_map/ppermute | solution.py:304
  20.0 12.2 %collective-permute-start.14 = (bf16[16,32,128]{2,1,0:T(8,128)(2,1)S(1)}, bf16[16,32,128]{2,1,0:T(8,128)(2,1)S(1)}, u32[]{:S(2)}, u32[]{:S(2)}) collective-permute-start(bf16[16,32,128]{2,1,0:T(8,128)(2,1)S(1)} %get-tuple-element.40), channel_id=1, source_target_pairs={{0,4},{1,5},{2,6},{3,7},{4,0},{5,1},{6,2},{7,3},{8,12},{9,13},{10,... | collective-permute-start | bytes 393224 | tf_op jit(solution)/shard_map/ppermute | solution.py:304
  23.0 11.5 %collective-permute-start.15 = (bf16[16,32,128]{2,1,0:T(8,128)(2,1)S(1)}, bf16[16,32,128]{2,1,0:T(8,128)(2,1)S(1)}, u32[]{:S(2)}, u32[]{:S(2)}) collective-permute-start(bf16[16,32,128]{2,1,0:T(8,128)(2,1)S(1)} %get-tuple-element.41), channel_id=1, source_target_pairs={{0,6},{1,7},{2,4},{3,5},{4,2},{5,3},{6,0},{7,1},{8,14},{9,15},{10,... | collective-permute-start | bytes 393224 | tf_op jit(solution)/shard_map/ppermute | solution.py:304
  36.8 11.7 %collective-permute-start.17 = (bf16[16,32,128]{2,1,0:T(8,128)(2,1)S(1)}, bf16[16,32,128]{2,1,0:T(8,128)(2,1)S(1)}, u32[]{:S(2)}, u32[]{:S(2)}) collective-permute-start(bf16[16,32,128]{2,1,0:T(8,128)(2,1)S(1)} %get-tuple-element.43), channel_id=1, source_target_pairs={{0,2},{1,3},{2,0},{3,1},{4,6},{5,7},{6,4},{7,5},{8,10},{9,11},{10,... | collective-permute-start | bytes 393224 | tf_op jit(solution)/shard_map/ppermute | solution.py:304
  38.9 12.2 %collective-permute-start.18 = (bf16[16,32,128]{2,1,0:T(8,128)(2,1)S(1)}, bf16[16,32,128]{2,1,0:T(8,128)(2,1)S(1)}, u32[]{:S(2)}, u32[]{:S(2)}) collective-permute-start(bf16[16,32,128]{2,1,0:T(8,128)(2,1)S(1)} %get-tuple-element.44), channel_id=1, source_target_pairs={{0,4},{1,5},{2,6},{3,7},{4,0},{5,1},{6,2},{7,3},{8,12},{9,13},{10,... | collective-permute-start | bytes 393224 | tf_op jit(solution)/shard_map/ppermute | solution.py:304
  39.6 13.6 %collective-permute-start.19 = (bf16[16,32,128]{2,1,0:T(8,128)(2,1)S(1)}, bf16[16,32,128]{2,1,0:T(8,128)(2,1)S(1)}, u32[]{:S(2)}, u32[]{:S(2)}) collective-permute-start(bf16[16,32,128]{2,1,0:T(8,128)(2,1)S(1)} %get-tuple-element.45), channel_id=1, source_target_pairs={{0,6},{1,7},{2,4},{3,5},{4,2},{5,3},{6,0},{7,1},{8,14},{9,15},{10,... | collective-permute-start | bytes 393224 | tf_op jit(solution)/shard_map/ppermute | solution.py:304
  42.8 39.4 %collective-permute-start.9 = (bf16[32,32,128]{2,1,0:T(8,128)(2,1)S(1)}, bf16[32,32,128]{2,1,0:T(8,128)(2,1)S(1)}, u32[]{:S(2)}, u32[]{:S(2)}) collective-permute-start(bf16[32,32,128]{2,1,0:T(8,128)(2,1)S(1)} %get-tuple-element.35), channel_id=1, source_target_pairs={{0,2},{1,3},{2,0},{3,1},{4,6},{5,7},{6,4},{7,5},{8,10},{9,11},{10,... | collective-permute-start | bytes 786440 | tf_op jit(solution)/shard_map/ppermute | solution.py:304
  46.6 35.6 %collective-permute-start.10 = (bf16[32,32,128]{2,1,0:T(8,128)(2,1)S(1)}, bf16[32,32,128]{2,1,0:T(8,128)(2,1)S(1)}, u32[]{:S(2)}, u32[]{:S(2)}) collective-permute-start(bf16[32,32,128]{2,1,0:T(8,128)(2,1)S(1)} %get-tuple-element.36), channel_id=1, source_target_pairs={{0,4},{1,5},{2,6},{3,7},{4,0},{5,1},{6,2},{7,3},{8,12},{9,13},{10,... | collective-permute-start | bytes 786440 | tf_op jit(solution)/shard_map/ppermute | solution.py:304
  48.5 33.7 %collective-permute-start.11 = (bf16[32,32,128]{2,1,0:T(8,128)(2,1)S(1)}, bf16[32,32,128]{2,1,0:T(8,128)(2,1)S(1)}, u32[]{:S(2)}, u32[]{:S(2)}) collective-permute-start(bf16[32,32,128]{2,1,0:T(8,128)(2,1)S(1)} %get-tuple-element.37), channel_id=1, source_target_pairs={{0,6},{1,7},{2,4},{3,5},{4,2},{5,3},{6,0},{7,1},{8,14},{9,15},{10,... | collective-permute-start | bytes 786440 | tf_op jit(solution)/shard_map/ppermute | solution.py:304
  51.1 5.0 %collective-permute-start.1 = (bf16[16,32,128]{2,1,0:T(8,128)(2,1)S(1)}, bf16[16,32,128]{2,1,0:T(8,128)(2,1)S(1)}, u32[]{:S(2)}, u32[]{:S(2)}) collective-permute-start(bf16[16,32,128]{2,1,0:T(8,128)(2,1)S(1)} %get-tuple-element.27), channel_id=1, source_target_pairs={{0,2},{1,3},{2,0},{3,1},{4,6},{5,7},{6,4},{7,5},{8,10},{9,11},{10,... | collective-permute-start | bytes 393224 | tf_op jit(solution)/shard_map/ppermute | solution.py:304
  53.3 13.0 %collective-permute-start.2 = (bf16[16,32,128]{2,1,0:T(8,128)(2,1)S(1)}, bf16[16,32,128]{2,1,0:T(8,128)(2,1)S(1)}, u32[]{:S(2)}, u32[]{:S(2)}) collective-permute-start(bf16[16,32,128]{2,1,0:T(8,128)(2,1)S(1)} %get-tuple-element.28), channel_id=1, source_target_pairs={{0,4},{1,5},{2,6},{3,7},{4,0},{5,1},{6,2},{7,3},{8,12},{9,13},{10,... | collective-permute-start | bytes 393224 | tf_op jit(solution)/shard_map/ppermute | solution.py:304
  56.1 13.9 %collective-permute-start.3 = (bf16[16,32,128]{2,1,0:T(8,128)(2,1)S(1)}, bf16[16,32,128]{2,1,0:T(8,128)(2,1)S(1)}, u32[]{:S(2)}, u32[]{:S(2)}) collective-permute-start(bf16[16,32,128]{2,1,0:T(8,128)(2,1)S(1)} %get-tuple-element.29), channel_id=1, source_target_pairs={{0,6},{1,7},{2,4},{3,5},{4,2},{5,3},{6,0},{7,1},{8,14},{9,15},{10,... | collective-permute-start | bytes 393224 | tf_op jit(solution)/shard_map/ppermute | solution.py:304
  66.3 3.8 %collective-permute-start.4 = (bf16[16,32,128]{2,1,0:T(8,128)(2,1)S(1)}, bf16[16,32,128]{2,1,0:T(8,128)(2,1)S(1)}, u32[]{:S(2)}, u32[]{:S(2)}) collective-permute-start(bf16[16,32,128]{2,1,0:T(8,128)(2,1)S(1)} %get-tuple-element.30), channel_id=1, source_target_pairs={{0,1},{1,0},{2,3},{3,2},{4,5},{5,4},{6,7},{7,6},{8,9},{9,8},{10,11... | collective-permute-start | bytes 393224 | tf_op jit(solution)/shard_map/ppermute | solution.py:304
  70.0 5.6 %collective-permute-start.5 = (bf16[16,32,128]{2,1,0:T(8,128)(2,1)S(1)}, bf16[16,32,128]{2,1,0:T(8,128)(2,1)S(1)}, u32[]{:S(2)}, u32[]{:S(2)}) collective-permute-start(bf16[16,32,128]{2,1,0:T(8,128)(2,1)S(1)} %get-tuple-element.31), channel_id=1, source_target_pairs={{0,3},{1,2},{2,1},{3,0},{4,7},{5,6},{6,5},{7,4},{8,11},{9,10},{10,... | collective-permute-start | bytes 393224 | tf_op jit(solution)/shard_map/ppermute | solution.py:304
  70.1 5.5 %collective-permute-start.6 = (bf16[16,32,128]{2,1,0:T(8,128)(2,1)S(1)}, bf16[16,32,128]{2,1,0:T(8,128)(2,1)S(1)}, u32[]{:S(2)}, u32[]{:S(2)}) collective-permute-start(bf16[16,32,128]{2,1,0:T(8,128)(2,1)S(1)} %get-tuple-element.32), channel_id=1, source_target_pairs={{0,5},{1,4},{2,7},{3,6},{4,1},{5,0},{6,3},{7,2},{8,13},{9,12},{10,... | collective-permute-start | bytes 393224 | tf_op jit(solution)/shard_map/ppermute | solution.py:304
  75.6 6.4 %collective-permute-start.7 = (bf16[16,32,128]{2,1,0:T(8,128)(2,1)S(1)}, bf16[16,32,128]{2,1,0:T(8,128)(2,1)S(1)}, u32[]{:S(2)}, u32[]{:S(2)}) collective-permute-start(bf16[16,32,128]{2,1,0:T(8,128)(2,1)S(1)} %get-tuple-element.33), channel_id=1, source_target_pairs={{0,7},{1,6},{2,5},{3,4},{4,3},{5,2},{6,1},{7,0},{8,15},{9,14},{10,... | collective-permute-start | bytes 393224 | tf_op jit(solution)/shard_map/ppermute | solution.py:304
  75.6 6.9 %collective-permute-start.20 = (bf16[64,32,128]{2,1,0:T(8,128)(2,1)S(1)}, bf16[64,32,128]{2,1,0:T(8,128)(2,1)S(1)}, u32[]{:S(2)}, u32[]{:S(2)}) collective-permute-start(bf16[64,32,128]{2,1,0:T(8,128)(2,1)S(1)} %constant_dynamic-update-slice_fusion.32), channel_id=1, source_target_pairs={{0,1},{1,0},{2,3},{3,2},{4,5},{5,4},{6,7},{7,6},{8,9},{9,8},{10,11... | collective-permute-start | bytes 1572872 | tf_op jit(solution)/shard_map/ppermute | solution.py:316
  82.4 3.8 %collective-permute-start.12 = (bf16[64,32,128]{2,1,0:T(8,128)(2,1)S(1)}, bf16[64,32,128]{2,1,0:T(8,128)(2,1)S(1)}, u32[]{:S(2)}, u32[]{:S(2)}) collective-permute-start(bf16[64,32,128]{2,1,0:T(8,128)(2,1)S(1)} %get-tuple-element.48), channel_id=1, source_target_pairs={{0,1},{1,0},{2,3},{3,2},{4,5},{5,4},{6,7},{7,6},{8,9},{9,8},{10,11... | collective-permute-start | bytes 1572872 | tf_op jit(solution)/shard_map/ppermute | solution.py:316
  82.7 0.8 copy-start
  82.7 0.8 copy-start.1
  (1 other events, 0.7 us)

commit v11 on v10

--- a/solution.py
+++ b/solution.py
@@ -94,8 +94,9 @@
     )(place, tile_map)
 
 
-def cut_kernel(plane, cap, kinds, place_ref, req_ref, *refs):
+def cut_kernel(kinds, cap, place_ref, req_ref, *refs):
     sheet_refs, out_refs, half_ref = refs[: len(kinds)], refs[len(kinds) : -1], refs[-1]
+    legs = len(out_refs) // len(kinds)
     parts = sheet_refs[0].shape[-1] // WC
     for at, sheet_ref in enumerate(sheet_refs):
         for c in range(2):
@@ -104,26 +105,25 @@
                 half_ref[(at * 2 + c) * parts + h] = part.astype(jnp.float32)
     lane = lax.broadcasted_iota(jnp.int32, (WR, WC), 1)
     me = place_ref[1]
-    sides = [1 - place_ref[0] if mirrored else place_ref[0] for mirrored in kinds]
-    span = req_ref.shape[0] // len(out_refs)
+    span = req_ref.shape[0] // legs
 
     def one(now, carry):
-        for m, out_ref in enumerate(out_refs):
-            source = (m * span + now) ^ me
-            for at, side in enumerate(sides):
+        for at, (plane, mirrored) in enumerate(kinds):
+            side = 1 - place_ref[0] if mirrored else place_ref[0]
+            for m in range(legs):
+                source = (m * span + now) ^ me
                 for place in range(cap):
                     packed = req_ref[source, (2 * plane + side) * cap + place]
                     row = packed >> 16
                     col = packed & 65535
                     turn = (WC - col) & (WC - 1)
                     left = lane < WC - col
-                    slot = (now * len(kinds) + at) * cap + place
                     for c in range(2):
                         part = [
                             pltpu.roll(half_ref[(at * 2 + c) * parts + h, pl.ds(row, WR), :], turn, 1)
                             for h in range(parts)
                         ]
-                        out_ref[slot, c * WR : (c + 1) * WR, :] = jnp.where(
+                        out_refs[at * legs + m][now * cap + place, c * WR : (c + 1) * WR, :] = jnp.where(
                             left, part[0], part[1]
                         ).astype(jnp.bfloat16)
         return carry
@@ -131,18 +131,19 @@
     lax.fori_loop(0, span, one, 0)
 
 
-def cut(plane, cap, outs, kinds, place, requests, sheets):
-    count = requests.shape[0] // outs * len(kinds) * cap
+def cut(kinds, cap, legs, place, requests, sheets):
+    count = requests.shape[0] // legs * cap
     height, width = sheets[0].shape[-2:]
-    return pl.pallas_call(
-        functools.partial(cut_kernel, plane, cap, kinds),
-        out_shape=(jax.ShapeDtypeStruct((count, 2 * WR, WC), jnp.bfloat16),) * outs,
+    outs = pl.pallas_call(
+        functools.partial(cut_kernel, kinds, cap),
+        out_shape=(jax.ShapeDtypeStruct((count, 2 * WR, WC), jnp.bfloat16),) * (legs * len(kinds)),
         in_specs=[whole(SMEM), whole(SMEM)] + [whole()] * len(kinds),
-        out_specs=(whole(),) * outs,
+        out_specs=(whole(),) * (legs * len(kinds)),
         scratch_shapes=[VMEM((len(kinds) * 2 * width // WC, height, WC), jnp.float32)],
         compiler_params=GRANT,
         name="cut",
     )(place, requests, *sheets)
+    return [outs[at * legs : (at + 1) * legs] for at in range(len(kinds))]
 
 
 def taps(pos):
@@ -293,22 +294,14 @@
             x, "sky", split_axis=0, concat_axis=0, axis_index_groups=groups, tiled=True
         )
 
-    def ship(parts, count):
+    def ship(parts):
         if direct:
-            got = exchange(parts[0].reshape(relays, -1, 2 * WR, WC))
-            got = got.reshape(relays, count, cap, 2 * WR, WC)
-            return [([got[:, at].reshape(relays * cap, 2 * WR, WC)], []) for at in range(count)]
+            got = exchange(parts[0].reshape(relays, cap, 2 * WR, WC))
+            return [got.reshape(relays * cap, 2 * WR, WC)], []
         got = [parts[0]]
-        step = relays // len(parts)
-        for m in range(1, len(parts)):
-            got.append(lax.ppermute(parts[m], "sky", swap(step * m)))
-
-        def pieces(at, of=got):
-            return [part[at * cap : (at + 1) * cap] for part in of]
-
-        if step == 1:
-            return [(pieces(at, got[::2] + got[1::2]), []) for at in range(count)]
-        return [(pieces(at), pieces(count + at)) for at in range(count)]
+        for m in range(1, chips):
+            got.append(lax.ppermute(parts[m], "sky", swap(2 * m)))
+        return [part[:cap] for part in got], [part[cap:] for part in got]
 
     def across(lists):
         if not lists:
@@ -323,11 +316,11 @@
     def mirror(plane):
         return lax.ppermute(sheets[plane], "sky", mirror_pairs)
 
-    def cut_sent(plane, kinds, straight=False):
-        count = outs * 2 if straight and not direct else outs
-        tiles_of = [mirrors[plane] if mirrored else sheets[plane] for mirrored in kinds]
-        parts = cut(plane, cap, count, kinds, place, asked, tiles_of)
-        return ship(parts, len(kinds))
+    def cut_sent(*kinds):
+        tiles_of = [mirrors[plane] if mirrored else sheets[plane] for plane, mirrored in kinds]
+        parts = cut(kinds, cap, outs, place, asked, tiles_of)
+        for (plane, mirrored), part in zip(kinds, parts):
+            sent[plane, mirrored] = ship(part)
 
     index = lax.axis_index("sky").astype(jnp.int32)
     place = jnp.stack([index // relays, jnp.zeros_like(index) if direct else index % relays])
@@ -338,12 +331,15 @@
     mirrors = [mirror(plane) for plane in range(PLANES)]
     asked = exchange(requests)
     slots = find_slots(place, tiles, peers, cap, direct)
-    sent = [cut_sent(0, (False,)) + cut_sent(0, (True,))]
+    sent = {}
+    cut_sent((0, False))
+    cut_sent((0, True))
+    cut_sent(*[(plane, False) for plane in range(1, PLANES)])
     for plane in range(1, PLANES):
-        sent.append(cut_sent(plane, (False, True), plane == PLANES - 1))
+        cut_sent((plane, True))
     state = (start_x, start_y)
     for plane in range(PLANES):
-        sets = sent[plane]
+        sets = (sent[plane, False], sent[plane, True])
         held = iter(across([other for _, other in sets if other]))
         windows = sum((mine + (next(held) if other else []) for mine, other in sets), [])
         state = interp(plane, slots, jnp.concatenate(windows, axis=0), state)

time: 92.9 us -> 95.8 us (1.031)
  starting transfers between devices: 32.7 us -> 36.9 us
  waiting for transfers between devices: 38.5 us -> 36.3 us
  Pallas kernels: 16.2 us -> 17.2 us
    ppermute x16 -> x18, starting transfers between devices: 21.4 us -> 25.7 us  [ship(): got.append(lax.ppermute(parts[m], 'sky', swap(2 * m)))]
    ppermute x3, waiting for transfers between devices: 3.61 us -> 0.01 us  [mirror(): return lax.ppermute(sheets[plane], 'sky', mirror_pairs)]
    ppermute x2 -> x3, waiting for transfers between devices: 0.01 us -> 1.75 us  [across(): got = lax.ppermute(jnp.concatenate(sum(lists, []), axis=0), 'sky', swap(1))]
    pallas_call x4 -> x5, Pallas kernels: 4.78 us -> 5.66 us  [cut(): pl.pallas_call(functools.partial(cut_kernel, kinds, cap), out_shape=(jax....]
    ppermute x16 -> x18, waiting for transfers between devices: 34.9 us -> 34.5 us  [ship(): got.append(lax.ppermute(parts[m], 'sky', swap(2 * m)))]
  transfers between devices with their start and end apart: 22 -> 25, of which waited for: 12 -> 16; matrix products, arithmetic and copies ran while one was open for 3% -> 3% of each run, Pallas kernels for 9% -> 7%
where the time goes in v11:
time: 95.8 us; the launch traced here: 95.4 us
  starting transfers between devices  36.9 us (39%)
  waiting for transfers between devices  36.3 us (38%)
  Pallas kernels  17.2 us (18%)
  local copies, waits for them, and re-layouts  4.09 us (4%)
  between operations  0.97 us (1%)
    ppermute x18, waiting for transfers between devices, ship(): got.append(lax.ppermute(parts[m], 'sky', swap(2 * m)))  34.5 us
    ppermute x18, starting transfers between devices, ship(): got.append(lax.ppermute(parts[m], 'sky', swap(2 * m)))  25.7 us
    pallas_call x3, Pallas kernels, interp(): pl.pallas_call(functools.partial(interp_kernel, plane), out_shape=out_sha...  8.98 us
    pallas_call x5, Pallas kernels, cut(): pl.pallas_call(functools.partial(cut_kernel, kinds, cap), out_shape=(jax....  5.66 us
    ppermute x3, starting transfers between devices, mirror(): return lax.ppermute(sheets[plane], 'sky', mirror_pairs)  5.64 us
    all_to_all x1, starting transfers between devices, exchange(): lax.all_to_all(x, 'sky', split_axis=0, concat_axis=0, axis_index_groups=g...  5.28 us
    squeeze x2, local copies, waits for them, and re-layouts, tile(): return sheet[plane]  2.03 us
  transfers between devices with their start and end apart: 25, of which 16 were waited for; matrix products, arithmetic and copies ran while one was open for 3% of the time, Pallas kernels for 7%

profile of v11, /device:TPU:0, one launch (start us, length us, event | category | flops | bytes accessed | tf_op | source)
XLA Modules:
  0.0 95.4 jit_solution(1741584950366726849)
XLA Ops:
  0.6 1.8 %want.1 = s32[8,128]{1,0:T(8,128)} custom-call(s32[3,1,64]{2,1,0:T(1,128)} %bitcast.18, s32[3,64]{1,0:T(4,128)} %row_ref.1, s32[3,64]{1,0:T(4,128)} %col_ref.1), custom_call_target="tpu_custom_call" | custom-call | tf_op jit(solution)/shard_map/want/pallas_call | solution.py:65
  2.5 5.3 %all-to-all-start = ((s32[8,1,128]{2,1,0:T(1,128)}), s32[8,1,128]{2,1,0:T(1,128)S(1)}, u32[]{:S(2)}, u32[]{:S(2)}) async-start(s32[8,1,128]{2,1,0:T(1,128)} %bitcast.20), calls=%async_computation | async-start | bytes 8192 | tf_op jit(solution)/shard_map/all_to_all | solution.py:293
  8.8 2.7 %collective-permute-start.3 = (bf16[2,256,256]{2,1,0:T(8,128)(2,1)S(1)}, bf16[2,256,256]{2,1,0:T(8,128)(2,1)S(1)}, u32[]{:S(2)}, u32[]{:S(2)}) collective-permute-start(bf16[2,256,256]{2,1,0:T(8,128)(2,1)S(1)} %get-tuple-element.54.refs_1_), channel_id=1, source_target_pairs={{0,8},{1,9},{2,10},{3,11},{4,12},{5,13},{6,14},{7,15},{8,0},{9,1},... | collective-permute-start | bytes 786440 | tf_op jit(solution)/shard_map/ppermute | solution.py:317
  12.8 2.7 %collective-permute-start.19 = (bf16[2,256,256]{2,1,0:T(8,128)(2,1)S(1)}, bf16[2,256,256]{2,1,0:T(8,128)(2,1)S(1)}, u32[]{:S(2)}, u32[]{:S(2)}) collective-permute-start(bf16[2,256,256]{2,1,0:T(8,128)(2,1)S(1)} %slice_bitcast_fusion.refs_0_), channel_id=1, source_target_pairs={{0,8},{1,9},{2,10},{3,11},{4,12},{5,13},{6,14},{7,15},{8,0},{9,1},... | collective-permute-start | bytes 786440 | tf_op jit(solution)/shard_map/ppermute | solution.py:317
  19.3 2.1 %collective-permute-start = (bf16[16,32,128]{2,1,0:T(8,128)(2,1)S(1)}, bf16[16,32,128]{2,1,0:T(8,128)(2,1)S(1)}, u32[]{:S(2)}, u32[]{:S(2)}) collective-permute-start(bf16[16,32,128]{2,1,0:T(8,128)(2,1)S(1)} %get-tuple-element.31), channel_id=1, source_target_pairs={{0,2},{1,3},{2,0},{3,1},{4,6},{5,7},{6,4},{7,5},{8,10},{9,11},{10,... | collective-permute-start | bytes 393224 | tf_op jit(solution)/shard_map/ppermute | solution.py:303
  24.4 2.8 %collective-permute-start.2 = (bf16[16,32,128]{2,1,0:T(8,128)(2,1)S(1)}, bf16[16,32,128]{2,1,0:T(8,128)(2,1)S(1)}, u32[]{:S(2)}, u32[]{:S(2)}) collective-permute-start(bf16[16,32,128]{2,1,0:T(8,128)(2,1)S(1)} %get-tuple-element.33), channel_id=1, source_target_pairs={{0,6},{1,7},{2,4},{3,5},{4,2},{5,3},{6,0},{7,1},{8,14},{9,15},{10,... | collective-permute-start | bytes 393224 | tf_op jit(solution)/shard_map/ppermute | solution.py:303
  27.3 5.0 %collective-permute-done.1 = bf16[16,32,128]{2,1,0:T(8,128)(2,1)S(1)} collective-permute-done((bf16[16,32,128]{2,1,0:T(8,128)(2,1)S(1)}, bf16[16,32,128]{2,1,0:T(8,128)(2,1)S(1)}, u32[]{:S(2)}, u32[]{:S(2)}) %collective-permute-start.1) | collective-permute-done | bytes 131104 | tf_op jit(solution)/shard_map/ppermute | solution.py:303
  32.2 2.0 %collective-permute-start.8 = (bf16[16,32,128]{2,1,0:T(8,128)(2,1)S(1)}, bf16[16,32,128]{2,1,0:T(8,128)(2,1)S(1)}, u32[]{:S(2)}, u32[]{:S(2)}) collective-permute-start(bf16[16,32,128]{2,1,0:T(8,128)(2,1)S(1)} %get-tuple-element.39), channel_id=1, source_target_pairs={{0,2},{1,3},{2,0},{3,1},{4,6},{5,7},{6,4},{7,5},{8,10},{9,11},{10,... | collective-permute-start | bytes 393224 | tf_op jit(solution)/shard_map/ppermute | solution.py:303
  34.6 3.6 %collective-permute-start.9 = (bf16[16,32,128]{2,1,0:T(8,128)(2,1)S(1)}, bf16[16,32,128]{2,1,0:T(8,128)(2,1)S(1)}, u32[]{:S(2)}, u32[]{:S(2)}) collective-permute-start(bf16[16,32,128]{2,1,0:T(8,128)(2,1)S(1)} %get-tuple-element.40), channel_id=1, source_target_pairs={{0,4},{1,5},{2,6},{3,7},{4,0},{5,1},{6,2},{7,3},{8,12},{9,13},{10,... | collective-permute-start | bytes 393224 | tf_op jit(solution)/shard_map/ppermute | solution.py:303
  38.3 2.9 %collective-permute-start.10 = (bf16[16,32,128]{2,1,0:T(8,128)(2,1)S(1)}, bf16[16,32,128]{2,1,0:T(8,128)(2,1)S(1)}, u32[]{:S(2)}, u32[]{:S(2)}) collective-permute-start(bf16[16,32,128]{2,1,0:T(8,128)(2,1)S(1)} %get-tuple-element.41), channel_id=1, source_target_pairs={{0,6},{1,7},{2,4},{3,5},{4,2},{5,3},{6,0},{7,1},{8,14},{9,15},{10,... | collective-permute-start | bytes 393224 | tf_op jit(solution)/shard_map/ppermute | solution.py:303
  41.2 8.3 %collective-permute-done.9 = bf16[16,32,128]{2,1,0:T(8,128)(2,1)S(1)} collective-permute-done((bf16[16,32,128]{2,1,0:T(8,128)(2,1)S(1)}, bf16[16,32,128]{2,1,0:T(8,128)(2,1)S(1)}, u32[]{:S(2)}, u32[]{:S(2)}) %collective-permute-start.9) | collective-permute-done | bytes 131104 | tf_op jit(solution)/shard_map/ppermute | solution.py:303
  51.1 2.2 %collective-permute-done.10 = bf16[16,32,128]{2,1,0:T(8,128)(2,1)S(1)} collective-permute-done((bf16[16,32,128]{2,1,0:T(8,128)(2,1)S(1)}, bf16[16,32,128]{2,1,0:T(8,128)(2,1)S(1)}, u32[]{:S(2)}, u32[]{:S(2)}) %collective-permute-start.10) | collective-permute-done | bytes 131104 | tf_op jit(solution)/shard_map/ppermute | solution.py:303
  53.4 2.7 %collective-permute-done.16 = bf16[16,32,128]{2,1,0:T(8,128)(2,1)S(1)} collective-permute-done((bf16[16,32,128]{2,1,0:T(8,128)(2,1)S(1)}, bf16[16,32,128]{2,1,0:T(8,128)(2,1)S(1)}, u32[]{:S(2)}, u32[]{:S(2)}) %collective-permute-start.16) | collective-permute-done | bytes 131104 | tf_op jit(solution)/shard_map/ppermute | solution.py:303
  56.1 3.6 %collective-permute-done.17 = bf16[16,32,128]{2,1,0:T(8,128)(2,1)S(1)} collective-permute-done((bf16[16,32,128]{2,1,0:T(8,128)(2,1)S(1)}, bf16[16,32,128]{2,1,0:T(8,128)(2,1)S(1)}, u32[]{:S(2)}, u32[]{:S(2)}) %collective-permute-start.17) | collective-permute-done | bytes 131104 | tf_op jit(solution)/shard_map/ppermute | solution.py:303
  59.7 2.7 %collective-permute-done.18 = bf16[16,32,128]{2,1,0:T(8,128)(2,1)S(1)} collective-permute-done((bf16[16,32,128]{2,1,0:T(8,128)(2,1)S(1)}, bf16[16,32,128]{2,1,0:T(8,128)(2,1)S(1)}, u32[]{:S(2)}, u32[]{:S(2)}) %collective-permute-start.18) | collective-permute-done | bytes 131104 | tf_op jit(solution)/shard_map/ppermute | solution.py:303
  64.4 2.6 %collective-permute-start.6 = (bf16[16,32,128]{2,1,0:T(8,128)(2,1)S(1)}, bf16[16,32,128]{2,1,0:T(8,128)(2,1)S(1)}, u32[]{:S(2)}, u32[]{:S(2)}) collective-permute-start(bf16[16,32,128]{2,1,0:T(8,128)(2,1)S(1)} %get-tuple-element.37), channel_id=1, source_target_pairs={{0,6},{1,7},{2,4},{3,5},{4,2},{5,3},{6,0},{7,1},{8,14},{9,15},{10,... | collective-permute-start | bytes 393224 | tf_op jit(solution)/shard_map/ppermute | solution.py:303
  70.3 2.7 %collective-permute-start.14 = (bf16[16,32,128]{2,1,0:T(8,128)(2,1)S(1)}, bf16[16,32,128]{2,1,0:T(8,128)(2,1)S(1)}, u32[]{:S(2)}, u32[]{:S(2)}) collective-permute-start(bf16[16,32,128]{2,1,0:T(8,128)(2,1)S(1)} %get-tuple-element.45), channel_id=1, source_target_pairs={{0,6},{1,7},{2,4},{3,5},{4,2},{5,3},{6,0},{7,1},{8,14},{9,15},{10,... | collective-permute-start | bytes 393224 | tf_op jit(solution)/shard_map/ppermute | solution.py:303
  74.2 2.1 %collective-permute-done.12 = bf16[16,32,128]{2,1,0:T(8,128)(2,1)S(1)} collective-permute-done((bf16[16,32,128]{2,1,0:T(8,128)(2,1)S(1)}, bf16[16,32,128]{2,1,0:T(8,128)(2,1)S(1)}, u32[]{:S(2)}, u32[]{:S(2)}) %collective-permute-start.12) | collective-permute-done | bytes 131104 | tf_op jit(solution)/shard_map/ppermute | solution.py:303
  77.5 2.0 %collective-permute-done.14 = bf16[16,32,128]{2,1,0:T(8,128)(2,1)S(1)} collective-permute-done((bf16[16,32,128]{2,1,0:T(8,128)(2,1)S(1)}, bf16[16,32,128]{2,1,0:T(8,128)(2,1)S(1)}, u32[]{:S(2)}, u32[]{:S(2)}) %collective-permute-start.14) | collective-permute-done | bytes 131104 | tf_op jit(solution)/shard_map/ppermute | solution.py:303
  81.0 2.4 %collective-permute-done.22 = bf16[16,32,128]{2,1,0:T(8,128)(2,1)S(1)} collective-permute-done((bf16[16,32,128]{2,1,0:T(8,128)(2,1)S(1)}, bf16[16,32,128]{2,1,0:T(8,128)(2,1)S(1)}, u32[]{:S(2)}, u32[]{:S(2)}) %collective-permute-start.22) | collective-permute-done | bytes 131104 | tf_op jit(solution)/shard_map/ppermute | solution.py:303
  83.6 1.7 %collective-permute-done.23 = bf16[64,32,128]{2,1,0:T(8,128)(2,1)S(1)} collective-permute-done((bf16[64,32,128]{2,1,0:T(8,128)(2,1)S(1)}, bf16[64,32,128]{2,1,0:T(8,128)(2,1)S(1)}, u32[]{:S(2)}, u32[]{:S(2)}) %collective-permute-start.23) | collective-permute-done | bytes 524320 | tf_op jit(solution)/shard_map/ppermute | solution.py:309
  86.2 2.7 %shard_map.77.refs_0_ = f32[12,64,128]{2,1,0:T(8,128)S(1)} custom-call(s32[3,64]{1,0:T(4,128)S(1)} %slots.1.slot_ref, bf16[128,32,128]{2,1,0:T(8,128)(2,1)S(1)} %slice_dynamic-update-slice_fusion.win_ref, f32[64,128]{1,0:T(8,128)S(1)} %copy-done, f32[64,128]{1,0:T(8,128)S(1)} %copy-done.1), custom_call_target="tpu_custom_call" | custom-call | tf_op jit(solution)/shard_map/pallas_call | solution.py:265
  89.1 2.7 %shard_map.78.refs_0_ = f32[12,64,128]{2,1,0:T(8,128)S(1)} custom-call(s32[3,64]{1,0:T(4,128)S(1)} %slots.1.slot_ref, bf16[128,32,128]{2,1,0:T(8,128)(2,1)S(1)} %slice_dynamic-update-slice_fusion.2.win_ref, f32[12,64,128]{2,1,0:T(8,128)S(1)} %shard_map.77.refs_0_), custom_call_target="tpu_custom_call" | custom-call | tf_op jit(solution)/shard_map/pallas_call | solution.py:265
  91.9 3.5 %shard_map.79 = (f32[64,2,128]{2,1,0:T(2,128)}, f32[64,4,128]{2,1,0:T(4,128)}) custom-call(s32[3,64]{1,0:T(4,128)S(1)} %slots.1.slot_ref, bf16[128,32,128]{2,1,0:T(8,128)(2,1)S(1)} %slice_dynamic-update-slice_fusion.4.win_ref, f32[12,64,128]{2,1,0:T(8,128)S(1)} %shard_map.78.refs_0_), custom_call_target="tpu_custom_call" | custom-call | tf_op jit(solution)/shard_map/pallas_call | solution.py:265
  (86 shorter events, 21.6 us)
Async XLA Ops:
  2.5 14.4 %all-to-all-start = ((s32[8,1,128]{2,1,0:T(1,128)}), s32[8,1,128]{2,1,0:T(1,128)S(1)}, u32[]{:S(2)}, u32[]{:S(2)}) async-start(s32[8,1,128]{2,1,0:T(1,128)} %bitcast.20), calls=%async_computation | async-start | bytes 8192 | tf_op jit(solution)/shard_map/all_to_all | solution.py:293
  8.8 53.6 %collective-permute-start.3 = (bf16[2,256,256]{2,1,0:T(8,128)(2,1)S(1)}, bf16[2,256,256]{2,1,0:T(8,128)(2,1)S(1)}, u32[]{:S(2)}, u32[]{:S(2)}) collective-permute-start(bf16[2,256,256]{2,1,0:T(8,128)(2,1)S(1)} %get-tuple-element.54.refs_1_), channel_id=1, source_target_pairs={{0,8},{1,9},{2,10},{3,11},{4,12},{5,13},{6,14},{7,15},{8,0},{9,1},... | collective-permute-start | bytes 786440 | tf_op jit(solution)/shard_map/ppermute | solution.py:317
  11.5 55.6 %collective-permute-start.11 = (bf16[2,256,256]{2,1,0:T(8,128)(2,1)S(1)}, bf16[2,256,256]{2,1,0:T(8,128)(2,1)S(1)}, u32[]{:S(2)}, u32[]{:S(2)}) collective-permute-start(bf16[2,256,256]{2,1,0:T(8,128)(2,1)S(1)} %get-tuple-element.55.refs_0_), channel_id=1, source_target_pairs={{0,8},{1,9},{2,10},{3,11},{4,12},{5,13},{6,14},{7,15},{8,0},{9,1},... | collective-permute-start | bytes 786440 | tf_op jit(solution)/shard_map/ppermute | solution.py:317
  12.8 56.0 %collective-permute-start.19 = (bf16[2,256,256]{2,1,0:T(8,128)(2,1)S(1)}, bf16[2,256,256]{2,1,0:T(8,128)(2,1)S(1)}, u32[]{:S(2)}, u32[]{:S(2)}) collective-permute-start(bf16[2,256,256]{2,1,0:T(8,128)(2,1)S(1)} %slice_bitcast_fusion.refs_0_), channel_id=1, source_target_pairs={{0,8},{1,9},{2,10},{3,11},{4,12},{5,13},{6,14},{7,15},{8,0},{9,1},... | collective-permute-start | bytes 786440 | tf_op jit(solution)/shard_map/ppermute | solution.py:317
  19.3 5.1 %collective-permute-start = (bf16[16,32,128]{2,1,0:T(8,128)(2,1)S(1)}, bf16[16,32,128]{2,1,0:T(8,128)(2,1)S(1)}, u32[]{:S(2)}, u32[]{:S(2)}) collective-permute-start(bf16[16,32,128]{2,1,0:T(8,128)(2,1)S(1)} %get-tuple-element.31), channel_id=1, source_target_pairs={{0,2},{1,3},{2,0},{3,1},{4,6},{5,7},{6,4},{7,5},{8,10},{9,11},{10,... | collective-permute-start | bytes 393224 | tf_op jit(solution)/shard_map/ppermute | solution.py:303
  21.4 10.9 %collective-permute-start.1 = (bf16[16,32,128]{2,1,0:T(8,128)(2,1)S(1)}, bf16[16,32,128]{2,1,0:T(8,128)(2,1)S(1)}, u32[]{:S(2)}, u32[]{:S(2)}) collective-permute-start(bf16[16,32,128]{2,1,0:T(8,128)(2,1)S(1)} %get-tuple-element.32), channel_id=1, source_target_pairs={{0,4},{1,5},{2,6},{3,7},{4,0},{5,1},{6,2},{7,3},{8,12},{9,13},{10,... | collective-permute-start | bytes 393224 | tf_op jit(solution)/shard_map/ppermute | solution.py:303
  24.4 10.2 %collective-permute-start.2 = (bf16[16,32,128]{2,1,0:T(8,128)(2,1)S(1)}, bf16[16,32,128]{2,1,0:T(8,128)(2,1)S(1)}, u32[]{:S(2)}, u32[]{:S(2)}) collective-permute-start(bf16[16,32,128]{2,1,0:T(8,128)(2,1)S(1)} %get-tuple-element.33), channel_id=1, source_target_pairs={{0,6},{1,7},{2,4},{3,5},{4,2},{5,3},{6,0},{7,1},{8,14},{9,15},{10,... | collective-permute-start | bytes 393224 | tf_op jit(solution)/shard_map/ppermute | solution.py:303
  32.2 6.0 %collective-permute-start.8 = (bf16[16,32,128]{2,1,0:T(8,128)(2,1)S(1)}, bf16[16,32,128]{2,1,0:T(8,128)(2,1)S(1)}, u32[]{:S(2)}, u32[]{:S(2)}) collective-permute-start(bf16[16,32,128]{2,1,0:T(8,128)(2,1)S(1)} %get-tuple-element.39), channel_id=1, source_target_pairs={{0,2},{1,3},{2,0},{3,1},{4,6},{5,7},{6,4},{7,5},{8,10},{9,11},{10,... | collective-permute-start | bytes 393224 | tf_op jit(solution)/shard_map/ppermute | solution.py:303
  34.6 14.9 %collective-permute-start.9 = (bf16[16,32,128]{2,1,0:T(8,128)(2,1)S(1)}, bf16[16,32,128]{2,1,0:T(8,128)(2,1)S(1)}, u32[]{:S(2)}, u32[]{:S(2)}) collective-permute-start(bf16[16,32,128]{2,1,0:T(8,128)(2,1)S(1)} %get-tuple-element.40), channel_id=1, source_target_pairs={{0,4},{1,5},{2,6},{3,7},{4,0},{5,1},{6,2},{7,3},{8,12},{9,13},{10,... | collective-permute-start | bytes 393224 | tf_op jit(solution)/shard_map/ppermute | solution.py:303
  38.3 15.1 %collective-permute-start.10 = (bf16[16,32,128]{2,1,0:T(8,128)(2,1)S(1)}, bf16[16,32,128]{2,1,0:T(8,128)(2,1)S(1)}, u32[]{:S(2)}, u32[]{:S(2)}) collective-permute-start(bf16[16,32,128]{2,1,0:T(8,128)(2,1)S(1)} %get-tuple-element.41), channel_id=1, source_target_pairs={{0,6},{1,7},{2,4},{3,5},{4,2},{5,3},{6,0},{7,1},{8,14},{9,15},{10,... | collective-permute-start | bytes 393224 | tf_op jit(solution)/shard_map/ppermute | solution.py:303
  49.5 6.6 %collective-permute-start.16 = (bf16[16,32,128]{2,1,0:T(8,128)(2,1)S(1)}, bf16[16,32,128]{2,1,0:T(8,128)(2,1)S(1)}, u32[]{:S(2)}, u32[]{:S(2)}) collective-permute-start(bf16[16,32,128]{2,1,0:T(8,128)(2,1)S(1)} %get-tuple-element.47), channel_id=1, source_target_pairs={{0,2},{1,3},{2,0},{3,1},{4,6},{5,7},{6,4},{7,5},{8,10},{9,11},{10,... | collective-permute-start | bytes 393224 | tf_op jit(solution)/shard_map/ppermute | solution.py:303
  53.4 6.3 %collective-permute-start.17 = (bf16[16,32,128]{2,1,0:T(8,128)(2,1)S(1)}, bf16[16,32,128]{2,1,0:T(8,128)(2,1)S(1)}, u32[]{:S(2)}, u32[]{:S(2)}) collective-permute-start(bf16[16,32,128]{2,1,0:T(8,128)(2,1)S(1)} %get-tuple-element.48), channel_id=1, source_target_pairs={{0,4},{1,5},{2,6},{3,7},{4,0},{5,1},{6,2},{7,3},{8,12},{9,13},{10,... | collective-permute-start | bytes 393224 | tf_op jit(solution)/shard_map/ppermute | solution.py:303
  56.1 6.3 %collective-permute-start.18 = (bf16[16,32,128]{2,1,0:T(8,128)(2,1)S(1)}, bf16[16,32,128]{2,1,0:T(8,128)(2,1)S(1)}, u32[]{:S(2)}, u32[]{:S(2)}) collective-permute-start(bf16[16,32,128]{2,1,0:T(8,128)(2,1)S(1)} %get-tuple-element.49), channel_id=1, source_target_pairs={{0,6},{1,7},{2,4},{3,5},{4,2},{5,3},{6,0},{7,1},{8,14},{9,15},{10,... | collective-permute-start | bytes 393224 | tf_op jit(solution)/shard_map/ppermute | solution.py:303
  63.5 6.8 %collective-permute-start.4 = (bf16[16,32,128]{2,1,0:T(8,128)(2,1)S(1)}, bf16[16,32,128]{2,1,0:T(8,128)(2,1)S(1)}, u32[]{:S(2)}, u32[]{:S(2)}) collective-permute-start(bf16[16,32,128]{2,1,0:T(8,128)(2,1)S(1)} %get-tuple-element.35), channel_id=1, source_target_pairs={{0,2},{1,3},{2,0},{3,1},{4,6},{5,7},{6,4},{7,5},{8,10},{9,11},{10,... | collective-permute-start | bytes 393224 | tf_op jit(solution)/shard_map/ppermute | solution.py:303
  64.1 8.9 %collective-permute-start.5 = (bf16[16,32,128]{2,1,0:T(8,128)(2,1)S(1)}, bf16[16,32,128]{2,1,0:T(8,128)(2,1)S(1)}, u32[]{:S(2)}, u32[]{:S(2)}) collective-permute-start(bf16[16,32,128]{2,1,0:T(8,128)(2,1)S(1)} %get-tuple-element.36), channel_id=1, source_target_pairs={{0,4},{1,5},{2,6},{3,7},{4,0},{5,1},{6,2},{7,3},{8,12},{9,13},{10,... | collective-permute-start | bytes 393224 | tf_op jit(solution)/shard_map/ppermute | solution.py:303
  64.4 9.5 %collective-permute-start.6 = (bf16[16,32,128]{2,1,0:T(8,128)(2,1)S(1)}, bf16[16,32,128]{2,1,0:T(8,128)(2,1)S(1)}, u32[]{:S(2)}, u32[]{:S(2)}) collective-permute-start(bf16[16,32,128]{2,1,0:T(8,128)(2,1)S(1)} %get-tuple-element.37), channel_id=1, source_target_pairs={{0,6},{1,7},{2,4},{3,5},{4,2},{5,3},{6,0},{7,1},{8,14},{9,15},{10,... | collective-permute-start | bytes 393224 | tf_op jit(solution)/shard_map/ppermute | solution.py:303
  68.1 8.2 %collective-permute-start.12 = (bf16[16,32,128]{2,1,0:T(8,128)(2,1)S(1)}, bf16[16,32,128]{2,1,0:T(8,128)(2,1)S(1)}, u32[]{:S(2)}, u32[]{:S(2)}) collective-permute-start(bf16[16,32,128]{2,1,0:T(8,128)(2,1)S(1)} %get-tuple-element.43), channel_id=1, source_target_pairs={{0,2},{1,3},{2,0},{3,1},{4,6},{5,7},{6,4},{7,5},{8,10},{9,11},{10,... | collective-permute-start | bytes 393224 | tf_op jit(solution)/shard_map/ppermute | solution.py:303
  68.8 8.6 %collective-permute-start.13 = (bf16[16,32,128]{2,1,0:T(8,128)(2,1)S(1)}, bf16[16,32,128]{2,1,0:T(8,128)(2,1)S(1)}, u32[]{:S(2)}, u32[]{:S(2)}) collective-permute-start(bf16[16,32,128]{2,1,0:T(8,128)(2,1)S(1)} %get-tuple-element.44), channel_id=1, source_target_pairs={{0,4},{1,5},{2,6},{3,7},{4,0},{5,1},{6,2},{7,3},{8,12},{9,13},{10,... | collective-permute-start | bytes 393224 | tf_op jit(solution)/shard_map/ppermute | solution.py:303
  70.3 9.3 %collective-permute-start.14 = (bf16[16,32,128]{2,1,0:T(8,128)(2,1)S(1)}, bf16[16,32,128]{2,1,0:T(8,128)(2,1)S(1)}, u32[]{:S(2)}, u32[]{:S(2)}) collective-permute-start(bf16[16,32,128]{2,1,0:T(8,128)(2,1)S(1)} %get-tuple-element.45), channel_id=1, source_target_pairs={{0,6},{1,7},{2,4},{3,5},{4,2},{5,3},{6,0},{7,1},{8,14},{9,15},{10,... | collective-permute-start | bytes 393224 | tf_op jit(solution)/shard_map/ppermute | solution.py:303
  73.0 7.8 %collective-permute-start.20 = (bf16[16,32,128]{2,1,0:T(8,128)(2,1)S(1)}, bf16[16,32,128]{2,1,0:T(8,128)(2,1)S(1)}, u32[]{:S(2)}, u32[]{:S(2)}) collective-permute-start(bf16[16,32,128]{2,1,0:T(8,128)(2,1)S(1)} %get-tuple-element.51), channel_id=1, source_target_pairs={{0,2},{1,3},{2,0},{3,1},{4,6},{5,7},{6,4},{7,5},{8,10},{9,11},{10,... | collective-permute-start | bytes 393224 | tf_op jit(solution)/shard_map/ppermute | solution.py:303
  73.9 7.0 %collective-permute-start.21 = (bf16[16,32,128]{2,1,0:T(8,128)(2,1)S(1)}, bf16[16,32,128]{2,1,0:T(8,128)(2,1)S(1)}, u32[]{:S(2)}, u32[]{:S(2)}) collective-permute-start(bf16[16,32,128]{2,1,0:T(8,128)(2,1)S(1)} %get-tuple-element.52), channel_id=1, source_target_pairs={{0,4},{1,5},{2,6},{3,7},{4,0},{5,1},{6,2},{7,3},{8,12},{9,13},{10,... | collective-permute-start | bytes 393224 | tf_op jit(solution)/shard_map/ppermute | solution.py:303
  76.3 7.0 %collective-permute-start.22 = (bf16[16,32,128]{2,1,0:T(8,128)(2,1)S(1)}, bf16[16,32,128]{2,1,0:T(8,128)(2,1)S(1)}, u32[]{:S(2)}, u32[]{:S(2)}) collective-permute-start(bf16[16,32,128]{2,1,0:T(8,128)(2,1)S(1)} %get-tuple-element.53), channel_id=1, source_target_pairs={{0,6},{1,7},{2,4},{3,5},{4,2},{5,3},{6,0},{7,1},{8,14},{9,15},{10,... | collective-permute-start | bytes 393224 | tf_op jit(solution)/shard_map/ppermute | solution.py:303
  77.4 6.0 %collective-permute-start.7 = (bf16[64,32,128]{2,1,0:T(8,128)(2,1)S(1)}, bf16[64,32,128]{2,1,0:T(8,128)(2,1)S(1)}, u32[]{:S(2)}, u32[]{:S(2)}) collective-permute-start(bf16[64,32,128]{2,1,0:T(8,128)(2,1)S(1)} %constant_dynamic-update-slice_fusion), channel_id=1, source_target_pairs={{0,1},{1,0},{2,3},{3,2},{4,5},{5,4},{6,7},{7,6},{8,9},{9,8},{10,11... | collective-permute-start | bytes 1572872 | tf_op jit(solution)/shard_map/ppermute | solution.py:309
  79.6 4.0 %collective-permute-start.15 = (bf16[64,32,128]{2,1,0:T(8,128)(2,1)S(1)}, bf16[64,32,128]{2,1,0:T(8,128)(2,1)S(1)}, u32[]{:S(2)}, u32[]{:S(2)}) collective-permute-start(bf16[64,32,128]{2,1,0:T(8,128)(2,1)S(1)} %constant_dynamic-update-slice_fusion.16), channel_id=1, source_target_pairs={{0,1},{1,0},{2,3},{3,2},{4,5},{5,4},{6,7},{7,6},{8,9},{9,8},{10,11... | collective-permute-start | bytes 1572872 | tf_op jit(solution)/shard_map/ppermute | solution.py:309
  (4 other events, 4.2 us)

commit v12 on v10

--- a/solution.py
+++ b/solution.py
@@ -71,26 +71,26 @@
     )(tile_map, row_anchor, col_anchor)
 
 
-def slot_kernel(peers, cap, direct, place_ref, tile_ref, slot_ref):
+def slot_kernel(planes, peers, cap, direct, place_ref, tile_ref, slot_ref):
     relays = peers // 2
-    for k in range(PLANES):
+    for at, k in enumerate(planes):
         tile, _, rank = ranks(peers, tile_ref, k)
         side = tile // relays
         relay = (tile - side * relays) ^ place_ref[1]
         if not direct:
             relay = (relay & 1) * (relays // 2) + (relay >> 1)
         far = (side != place_ref[0]).astype(jnp.int32)
-        slot_ref[k : k + 1, :] = (far * relays + relay) * cap + rank
-
-
-def find_slots(place, tile_map, peers, cap, direct):
+        slot_ref[at : at + 1, :] = (far * relays + relay) * cap + rank
+
+
+def find_slots(planes, place, tile_map, peers, cap, direct):
     return pl.pallas_call(
-        functools.partial(slot_kernel, peers, cap, direct),
-        out_shape=jax.ShapeDtypeStruct((PLANES, tile_map.shape[2]), jnp.int32),
+        functools.partial(slot_kernel, planes, peers, cap, direct),
+        out_shape=jax.ShapeDtypeStruct((len(planes), tile_map.shape[2]), jnp.int32),
         in_specs=[whole(SMEM), whole()],
         out_specs=whole(),
         compiler_params=GRANT,
-        name="slots",
+        name="find",
     )(place, tile_map)
 
 
@@ -160,7 +160,7 @@
     return cell, value, slope
 
 
-def interp_kernel(plane, slot_ref, win_ref, *refs):
+def interp_kernel(plane, at_slots, slot_ref, win_ref, *refs):
     first, last = plane == 0, plane == PLANES - 1
     if first:
         x_ref, y_ref = refs[:2]
@@ -210,7 +210,7 @@
             return value.reshape(size, rays), slope.reshape(size, rays)
 
         kern = jnp.concatenate(spread(0, WC, jnp.bfloat16), axis=1)
-        mixed = jnp.dot(win_ref[slot_ref[plane, b]], kern, preferred_element_type=jnp.float32)
+        mixed = jnp.dot(win_ref[slot_ref[at_slots, b]], kern, preferred_element_type=jnp.float32)
         ky, kyd = spread(9, WR, jnp.float32)
         for c in range(2):
             part = mixed[c * WR : (c + 1) * WR]
@@ -251,7 +251,8 @@
             state_out[j] = value
 
 
-def interp(plane, slots, windows, state):
+def interp(plane, found, windows, state):
+    slots, at_slots = found
     nblk = slots.shape[1]
     rays = state[0].shape[-1]
     if plane == PLANES - 1:
@@ -262,7 +263,7 @@
     else:
         out_shape = (jax.ShapeDtypeStruct((12, nblk, rays), jnp.float32),)
     return pl.pallas_call(
-        functools.partial(interp_kernel, plane),
+        functools.partial(interp_kernel, plane, at_slots),
         out_shape=out_shape,
         in_specs=[whole(SMEM), whole()] + [whole()] * len(state),
         out_specs=(whole(),) * len(out_shape),
@@ -337,16 +338,19 @@
     sheets = [tile(0, gradients)] + [tile(plane, late) for plane in range(1, PLANES)]
     mirrors = [mirror(plane) for plane in range(PLANES)]
     asked = exchange(requests)
-    slots = find_slots(place, tiles, peers, cap, direct)
-    sent = [cut_sent(0, (False,)) + cut_sent(0, (True,))]
-    for plane in range(1, PLANES):
-        sent.append(cut_sent(plane, (False, True), plane == PLANES - 1))
+    slots = [(find_slots((0,), place, tiles, peers, cap, direct), 0)]
+    more = find_slots(tuple(range(1, PLANES)), place, tiles, peers, cap, direct)
+    slots += [(more, at) for at in range(PLANES - 1)]
+    sent = []
+    for plane in range(PLANES - 1):
+        sent.append(cut_sent(plane, (False,)) + cut_sent(plane, (True,)))
+    sent.append(cut_sent(PLANES - 1, (False, True), True))
     state = (start_x, start_y)
     for plane in range(PLANES):
         sets = sent[plane]
         held = iter(across([other for _, other in sets if other]))
         windows = sum((mine + (next(held) if other else []) for mine, other in sets), [])
-        state = interp(plane, slots, jnp.concatenate(windows, axis=0), state)
+        state = interp(plane, slots[plane], jnp.concatenate(windows, axis=0), state)
     return state
 
 

time: 92.9 us -> 91.7 us (0.987)
  waiting for transfers between devices: 38.5 us -> 19.3 us
  starting transfers between devices: 32.7 us -> 49.3 us
  Pallas kernels: 16.2 us -> 17.7 us
    ppermute x16 -> x19, starting transfers between devices: 21.4 us -> 37.7 us  [ship(): got.append(lax.ppermute(parts[m], 'sky', swap(step * m)))]
    ppermute x16 -> x19, waiting for transfers between devices: 34.9 us -> 19.3 us  [ship(): got.append(lax.ppermute(parts[m], 'sky', swap(step * m)))]
    ppermute x3, waiting for transfers between devices: 3.61 us -> 0.01 us  [mirror(): return lax.ppermute(sheets[plane], 'sky', mirror_pairs)]
    pallas_call x4 -> x5, Pallas kernels: 4.78 us -> 5.54 us  [cut(): pl.pallas_call(functools.partial(cut_kernel, plane, cap, kinds), out_shap...]
    pallas_call x4 -> x5, Pallas kernels: 9.62 us -> 10.3 us  [the longest x3 8.92 us: interp(): pl.pallas_call(functools.partial(interp_kernel, plane, at_slots), out_sha...]
  transfers between devices with their start and end apart: 22 -> 25, of which waited for: 12 -> 11; matrix products, arithmetic and copies ran while one was open for 3% -> 3% of each run, Pallas kernels for 9% -> 8%
where the time goes in v12:
time: 91.7 us; the launch traced here: 91.4 us
  starting transfers between devices  49.3 us (54%)
  waiting for transfers between devices  19.3 us (21%)
  Pallas kernels  17.7 us (19%)
  local copies, waits for them, and re-layouts  4.06 us (4%)
  between operations  1 us (1%)
    ppermute x19, starting transfers between devices, ship(): got.append(lax.ppermute(parts[m], 'sky', swap(step * m)))  37.7 us
    ppermute x19, waiting for transfers between devices, ship(): got.append(lax.ppermute(parts[m], 'sky', swap(step * m)))  19.3 us
    pallas_call x3, Pallas kernels, interp(): pl.pallas_call(functools.partial(interp_kernel, plane, at_slots), out_sha...  8.92 us
    ppermute x3, starting transfers between devices, mirror(): return lax.ppermute(sheets[plane], 'sky', mirror_pairs)  5.64 us
    pallas_call x5, Pallas kernels, cut(): pl.pallas_call(functools.partial(cut_kernel, plane, cap, kinds), out_shap...  5.54 us
    all_to_all x1, starting transfers between devices, exchange(): lax.all_to_all(x, 'sky', split_axis=0, concat_axis=0, axis_index_groups=g...  5.28 us
    squeeze x2, local copies, waits for them, and re-layouts, tile(): return sheet[plane]  2.03 us
    unnamed x45, local copies, waits for them, and re-layouts  1.92 us
  transfers between devices with their start and end apart: 25, of which 11 were waited for; matrix products, arithmetic and copies ran while one was open for 3% of the time, Pallas kernels for 8%

profile of v12, /device:TPU:0, one launch (start us, length us, event | category | flops | bytes accessed | tf_op | source)
XLA Modules:
  0.0 91.4 jit_solution(4783350625900220739)
XLA Ops:
  0.6 1.8 %want.1 = s32[8,128]{1,0:T(8,128)} custom-call(s32[3,1,64]{2,1,0:T(1,128)} %bitcast.18, s32[3,64]{1,0:T(4,128)} %row_ref.1, s32[3,64]{1,0:T(4,128)} %col_ref.1), custom_call_target="tpu_custom_call" | custom-call | tf_op jit(solution)/shard_map/want/pallas_call | solution.py:65
  2.5 5.3 %all-to-all-start = ((s32[8,1,128]{2,1,0:T(1,128)}), s32[8,1,128]{2,1,0:T(1,128)S(1)}, u32[]{:S(2)}, u32[]{:S(2)}) async-start(s32[8,1,128]{2,1,0:T(1,128)} %bitcast.21), calls=%async_computation | async-start | bytes 8192 | tf_op jit(solution)/shard_map/all_to_all | solution.py:293
  8.7 2.7 %collective-permute-start.19 = (bf16[2,256,256]{2,1,0:T(8,128)(2,1)S(1)}, bf16[2,256,256]{2,1,0:T(8,128)(2,1)S(1)}, u32[]{:S(2)}, u32[]{:S(2)}) collective-permute-start(bf16[2,256,256]{2,1,0:T(8,128)(2,1)S(1)} %slice_bitcast_fusion.refs_0_), channel_id=1, source_target_pairs={{0,8},{1,9},{2,10},{3,11},{4,12},{5,13},{6,14},{7,15},{8,0},{9,1},... | collective-permute-start | bytes 786440 | tf_op jit(solution)/shard_map/ppermute | solution.py:325
  12.8 2.6 %collective-permute-start = (bf16[2,256,256]{2,1,0:T(8,128)(2,1)S(1)}, bf16[2,256,256]{2,1,0:T(8,128)(2,1)S(1)}, u32[]{:S(2)}, u32[]{:S(2)}) collective-permute-start(bf16[2,256,256]{2,1,0:T(8,128)(2,1)S(1)} %get-tuple-element.55.refs_0_), channel_id=1, source_target_pairs={{0,8},{1,9},{2,10},{3,11},{4,12},{5,13},{6,14},{7,15},{8,0},{9,1},... | collective-permute-start | bytes 786440 | tf_op jit(solution)/shard_map/ppermute | solution.py:325
  19.6 2.1 %collective-permute-start.16 = (bf16[16,32,128]{2,1,0:T(8,128)(2,1)S(1)}, bf16[16,32,128]{2,1,0:T(8,128)(2,1)S(1)}, u32[]{:S(2)}, u32[]{:S(2)}) collective-permute-start(bf16[16,32,128]{2,1,0:T(8,128)(2,1)S(1)} %get-tuple-element.47), channel_id=1, source_target_pairs={{0,2},{1,3},{2,0},{3,1},{4,6},{5,7},{6,4},{7,5},{8,10},{9,11},{10,... | collective-permute-start | bytes 393224 | tf_op jit(solution)/shard_map/ppermute | solution.py:305
  21.7 1.5 %collective-permute-start.17 = (bf16[16,32,128]{2,1,0:T(8,128)(2,1)S(1)}, bf16[16,32,128]{2,1,0:T(8,128)(2,1)S(1)}, u32[]{:S(2)}, u32[]{:S(2)}) collective-permute-start(bf16[16,32,128]{2,1,0:T(8,128)(2,1)S(1)} %get-tuple-element.48), channel_id=1, source_target_pairs={{0,4},{1,5},{2,6},{3,7},{4,0},{5,1},{6,2},{7,3},{8,12},{9,13},{10,... | collective-permute-start | bytes 393224 | tf_op jit(solution)/shard_map/ppermute | solution.py:305
  23.2 1.6 %collective-permute-done.16 = bf16[16,32,128]{2,1,0:T(8,128)(2,1)S(1)} collective-permute-done((bf16[16,32,128]{2,1,0:T(8,128)(2,1)S(1)}, bf16[16,32,128]{2,1,0:T(8,128)(2,1)S(1)}, u32[]{:S(2)}, u32[]{:S(2)}) %collective-permute-start.16) | collective-permute-done | bytes 131104 | tf_op jit(solution)/shard_map/ppermute | solution.py:305
  24.8 2.8 %collective-permute-start.18 = (bf16[16,32,128]{2,1,0:T(8,128)(2,1)S(1)}, bf16[16,32,128]{2,1,0:T(8,128)(2,1)S(1)}, u32[]{:S(2)}, u32[]{:S(2)}) collective-permute-start(bf16[16,32,128]{2,1,0:T(8,128)(2,1)S(1)} %get-tuple-element.49), channel_id=1, source_target_pairs={{0,6},{1,7},{2,4},{3,5},{4,2},{5,3},{6,0},{7,1},{8,14},{9,15},{10,... | collective-permute-start | bytes 393224 | tf_op jit(solution)/shard_map/ppermute | solution.py:305
  27.6 4.5 %collective-permute-done.17 = bf16[16,32,128]{2,1,0:T(8,128)(2,1)S(1)} collective-permute-done((bf16[16,32,128]{2,1,0:T(8,128)(2,1)S(1)}, bf16[16,32,128]{2,1,0:T(8,128)(2,1)S(1)}, u32[]{:S(2)}, u32[]{:S(2)}) %collective-permute-start.17) | collective-permute-done | bytes 131104 | tf_op jit(solution)/shard_map/ppermute | solution.py:305
  32.1 2.0 %collective-permute-start.8 = (bf16[16,32,128]{2,1,0:T(8,128)(2,1)S(1)}, bf16[16,32,128]{2,1,0:T(8,128)(2,1)S(1)}, u32[]{:S(2)}, u32[]{:S(2)}) collective-permute-start(bf16[16,32,128]{2,1,0:T(8,128)(2,1)S(1)} %get-tuple-element.39), channel_id=1, source_target_pairs={{0,2},{1,3},{2,0},{3,1},{4,6},{5,7},{6,4},{7,5},{8,10},{9,11},{10,... | collective-permute-start | bytes 393224 | tf_op jit(solution)/shard_map/ppermute | solution.py:305
  34.5 11.9 %collective-permute-start.9 = (bf16[16,32,128]{2,1,0:T(8,128)(2,1)S(1)}, bf16[16,32,128]{2,1,0:T(8,128)(2,1)S(1)}, u32[]{:S(2)}, u32[]{:S(2)}) collective-permute-start(bf16[16,32,128]{2,1,0:T(8,128)(2,1)S(1)} %get-tuple-element.40), channel_id=1, source_target_pairs={{0,4},{1,5},{2,6},{3,7},{4,0},{5,1},{6,2},{7,3},{8,12},{9,13},{10,... | collective-permute-start | bytes 393224 | tf_op jit(solution)/shard_map/ppermute | solution.py:305
  46.4 3.6 %collective-permute-start.10 = (bf16[16,32,128]{2,1,0:T(8,128)(2,1)S(1)}, bf16[16,32,128]{2,1,0:T(8,128)(2,1)S(1)}, u32[]{:S(2)}, u32[]{:S(2)}) collective-permute-start(bf16[16,32,128]{2,1,0:T(8,128)(2,1)S(1)} %get-tuple-element.41), channel_id=1, source_target_pairs={{0,6},{1,7},{2,4},{3,5},{4,2},{5,3},{6,0},{7,1},{8,14},{9,15},{10,... | collective-permute-start | bytes 393224 | tf_op jit(solution)/shard_map/ppermute | solution.py:305
  50.8 3.5 %collective-permute-done.10 = bf16[16,32,128]{2,1,0:T(8,128)(2,1)S(1)} collective-permute-done((bf16[16,32,128]{2,1,0:T(8,128)(2,1)S(1)}, bf16[16,32,128]{2,1,0:T(8,128)(2,1)S(1)}, u32[]{:S(2)}, u32[]{:S(2)}) %collective-permute-start.10) | collective-permute-done | bytes 131104 | tf_op jit(solution)/shard_map/ppermute | solution.py:305
  55.6 2.1 %collective-permute-start.21 = (bf16[16,32,128]{2,1,0:T(8,128)(2,1)S(1)}, bf16[16,32,128]{2,1,0:T(8,128)(2,1)S(1)}, u32[]{:S(2)}, u32[]{:S(2)}) collective-permute-start(bf16[16,32,128]{2,1,0:T(8,128)(2,1)S(1)} %get-tuple-element.52), channel_id=1, source_target_pairs={{0,4},{1,5},{2,6},{3,7},{4,0},{5,1},{6,2},{7,3},{8,12},{9,13},{10,... | collective-permute-start | bytes 393224 | tf_op jit(solution)/shard_map/ppermute | solution.py:305
  60.3 2.0 %collective-permute-start.13 = (bf16[16,32,128]{2,1,0:T(8,128)(2,1)S(1)}, bf16[16,32,128]{2,1,0:T(8,128)(2,1)S(1)}, u32[]{:S(2)}, u32[]{:S(2)}) collective-permute-start(bf16[16,32,128]{2,1,0:T(8,128)(2,1)S(1)} %get-tuple-element.44), channel_id=1, source_target_pairs={{0,4},{1,5},{2,6},{3,7},{4,0},{5,1},{6,2},{7,3},{8,12},{9,13},{10,... | collective-permute-start | bytes 393224 | tf_op jit(solution)/shard_map/ppermute | solution.py:305
  62.4 1.3 %cut.5 = (bf16[16,32,128]{2,1,0:T(8,128)(2,1)S(1)}, bf16[16,32,128]{2,1,0:T(8,128)(2,1)S(1)}, bf16[16,32,128]{2,1,0:T(8,128)(2,1)S(1)}, bf16[16,32,128]{2,1,0:T(...) custom-call(s32[2]{0:T(128)S(1)} %pad_add_fusion.place_ref, ...), custom_call_target="tpu_custom_call" | custom-call | tf_op jit(solution)/shard_map/cut/pallas_call | solution.py:137
  65.4 2.1 %collective-permute-start.2 = (bf16[16,32,128]{2,1,0:T(8,128)(2,1)S(1)}, bf16[16,32,128]{2,1,0:T(8,128)(2,1)S(1)}, u32[]{:S(2)}, u32[]{:S(2)}) collective-permute-start(bf16[16,32,128]{2,1,0:T(8,128)(2,1)S(1)} %get-tuple-element.32), channel_id=1, source_target_pairs={{0,4},{1,5},{2,6},{3,7},{4,0},{5,1},{6,2},{7,3},{8,12},{9,13},{10,... | collective-permute-start | bytes 393224 | tf_op jit(solution)/shard_map/ppermute | solution.py:305
  67.9 1.6 %collective-permute-start.3 = (bf16[16,32,128]{2,1,0:T(8,128)(2,1)S(1)}, bf16[16,32,128]{2,1,0:T(8,128)(2,1)S(1)}, u32[]{:S(2)}, u32[]{:S(2)}) collective-permute-start(bf16[16,32,128]{2,1,0:T(8,128)(2,1)S(1)} %get-tuple-element.33), channel_id=1, source_target_pairs={{0,6},{1,7},{2,4},{3,5},{4,2},{5,3},{6,0},{7,1},{8,14},{9,15},{10,... | collective-permute-start | bytes 393224 | tf_op jit(solution)/shard_map/ppermute | solution.py:305
  70.8 1.3 %collective-permute-done.1 = bf16[16,32,128]{2,1,0:T(8,128)(2,1)S(1)} collective-permute-done((bf16[16,32,128]{2,1,0:T(8,128)(2,1)S(1)}, bf16[16,32,128]{2,1,0:T(8,128)(2,1)S(1)}, u32[]{:S(2)}, u32[]{:S(2)}) %collective-permute-start.1) | collective-permute-done | bytes 131104 | tf_op jit(solution)/shard_map/ppermute | solution.py:305
  72.6 2.1 %collective-permute-start.7 = (bf16[16,32,128]{2,1,0:T(8,128)(2,1)S(1)}, bf16[16,32,128]{2,1,0:T(8,128)(2,1)S(1)}, u32[]{:S(2)}, u32[]{:S(2)}) collective-permute-start(bf16[16,32,128]{2,1,0:T(8,128)(2,1)S(1)} %get-tuple-element.37), channel_id=1, source_target_pairs={{0,7},{1,6},{2,5},{3,4},{4,3},{5,2},{6,1},{7,0},{8,15},{9,14},{10,... | collective-permute-start | bytes 393224 | tf_op jit(solution)/shard_map/ppermute | solution.py:305
  77.7 3.5 %collective-permute-done.7 = bf16[16,32,128]{2,1,0:T(8,128)(2,1)S(1)} collective-permute-done((bf16[16,32,128]{2,1,0:T(8,128)(2,1)S(1)}, bf16[16,32,128]{2,1,0:T(8,128)(2,1)S(1)}, u32[]{:S(2)}, u32[]{:S(2)}) %collective-permute-start.7) | collective-permute-done | bytes 131104 | tf_op jit(solution)/shard_map/ppermute | solution.py:305
  82.4 2.7 %shard_map.77.refs_0_ = f32[12,64,128]{2,1,0:T(8,128)S(1)} custom-call(s32[1,64]{1,0:T(1,128)S(1)} %find.3.slot_ref, bf16[128,32,128]{2,1,0:T(8,128)(2,1)S(1)} %slice_dynamic-update-slice_fusion.win_ref, f32[64,128]{1,0:T(8,128)S(1)} %copy-done, f32[64,128]{1,0:T(8,128)S(1)} %copy-done.1), custom_call_target="tpu_custom_call" | custom-call | tf_op jit(solution)/shard_map/pallas_call | solution.py:265
  85.2 2.7 %shard_map.78.refs_0_ = f32[12,64,128]{2,1,0:T(8,128)S(1)} custom-call(s32[2,64]{1,0:T(2,128)S(1)} %find.2.slot_ref, bf16[128,32,128]{2,1,0:T(8,128)(2,1)S(1)} %slice_dynamic-update-slice_fusion.2.win_ref, f32[12,64,128]{2,1,0:T(8,128)S(1)} %shard_map.77.refs_0_), custom_call_target="tpu_custom_call" | custom-call | tf_op jit(solution)/shard_map/pallas_call | solution.py:265
  87.9 3.5 %shard_map.79 = (f32[64,2,128]{2,1,0:T(2,128)}, f32[64,4,128]{2,1,0:T(4,128)}) custom-call(s32[2,64]{1,0:T(2,128)S(1)} %find.2.slot_ref, bf16[128,32,128]{2,1,0:T(8,128)(2,1)S(1)} %constant_dynamic-update-slice_fusion.win_ref, f32[12,64,128]{2,1,0:T(8,128)S(1)} %shard_map.78.refs_0_), custom_call_target="tpu_custom_call" | custom-call | tf_op jit(solution)/shard_map/pallas_call | solution.py:265
  (90 shorter events, 19.7 us)
Async XLA Ops:
  2.5 15.0 %all-to-all-start = ((s32[8,1,128]{2,1,0:T(1,128)}), s32[8,1,128]{2,1,0:T(1,128)S(1)}, u32[]{:S(2)}, u32[]{:S(2)}) async-start(s32[8,1,128]{2,1,0:T(1,128)} %bitcast.21), calls=%async_computation | async-start | bytes 8192 | tf_op jit(solution)/shard_map/all_to_all | solution.py:293
  8.7 45.6 %collective-permute-start.19 = (bf16[2,256,256]{2,1,0:T(8,128)(2,1)S(1)}, bf16[2,256,256]{2,1,0:T(8,128)(2,1)S(1)}, u32[]{:S(2)}, u32[]{:S(2)}) collective-permute-start(bf16[2,256,256]{2,1,0:T(8,128)(2,1)S(1)} %slice_bitcast_fusion.refs_0_), channel_id=1, source_target_pairs={{0,8},{1,9},{2,10},{3,11},{4,12},{5,13},{6,14},{7,15},{8,0},{9,1},... | collective-permute-start | bytes 786440 | tf_op jit(solution)/shard_map/ppermute | solution.py:325
  12.4 46.5 %collective-permute-start.11 = (bf16[2,256,256]{2,1,0:T(8,128)(2,1)S(1)}, bf16[2,256,256]{2,1,0:T(8,128)(2,1)S(1)}, u32[]{:S(2)}, u32[]{:S(2)}) collective-permute-start(bf16[2,256,256]{2,1,0:T(8,128)(2,1)S(1)} %get-tuple-element.54.refs_0_), channel_id=1, source_target_pairs={{0,8},{1,9},{2,10},{3,11},{4,12},{5,13},{6,14},{7,15},{8,0},{9,1},... | collective-permute-start | bytes 786440 | tf_op jit(solution)/shard_map/ppermute | solution.py:325
  12.8 47.5 %collective-permute-start = (bf16[2,256,256]{2,1,0:T(8,128)(2,1)S(1)}, bf16[2,256,256]{2,1,0:T(8,128)(2,1)S(1)}, u32[]{:S(2)}, u32[]{:S(2)}) collective-permute-start(bf16[2,256,256]{2,1,0:T(8,128)(2,1)S(1)} %get-tuple-element.55.refs_0_), channel_id=1, source_target_pairs={{0,8},{1,9},{2,10},{3,11},{4,12},{5,13},{6,14},{7,15},{8,0},{9,1},... | collective-permute-start | bytes 786440 | tf_op jit(solution)/shard_map/ppermute | solution.py:325
  21.7 10.4 %collective-permute-start.17 = (bf16[16,32,128]{2,1,0:T(8,128)(2,1)S(1)}, bf16[16,32,128]{2,1,0:T(8,128)(2,1)S(1)}, u32[]{:S(2)}, u32[]{:S(2)}) collective-permute-start(bf16[16,32,128]{2,1,0:T(8,128)(2,1)S(1)} %get-tuple-element.48), channel_id=1, source_target_pairs={{0,4},{1,5},{2,6},{3,7},{4,0},{5,1},{6,2},{7,3},{8,12},{9,13},{10,... | collective-permute-start | bytes 393224 | tf_op jit(solution)/shard_map/ppermute | solution.py:305
  24.8 9.7 %collective-permute-start.18 = (bf16[16,32,128]{2,1,0:T(8,128)(2,1)S(1)}, bf16[16,32,128]{2,1,0:T(8,128)(2,1)S(1)}, u32[]{:S(2)}, u32[]{:S(2)}) collective-permute-start(bf16[16,32,128]{2,1,0:T(8,128)(2,1)S(1)} %get-tuple-element.49), channel_id=1, source_target_pairs={{0,6},{1,7},{2,4},{3,5},{4,2},{5,3},{6,0},{7,1},{8,14},{9,15},{10,... | collective-permute-start | bytes 393224 | tf_op jit(solution)/shard_map/ppermute | solution.py:305
  32.1 14.3 %collective-permute-start.8 = (bf16[16,32,128]{2,1,0:T(8,128)(2,1)S(1)}, bf16[16,32,128]{2,1,0:T(8,128)(2,1)S(1)}, u32[]{:S(2)}, u32[]{:S(2)}) collective-permute-start(bf16[16,32,128]{2,1,0:T(8,128)(2,1)S(1)} %get-tuple-element.39), channel_id=1, source_target_pairs={{0,2},{1,3},{2,0},{3,1},{4,6},{5,7},{6,4},{7,5},{8,10},{9,11},{10,... | collective-permute-start | bytes 393224 | tf_op jit(solution)/shard_map/ppermute | solution.py:305
  34.5 16.3 %collective-permute-start.9 = (bf16[16,32,128]{2,1,0:T(8,128)(2,1)S(1)}, bf16[16,32,128]{2,1,0:T(8,128)(2,1)S(1)}, u32[]{:S(2)}, u32[]{:S(2)}) collective-permute-start(bf16[16,32,128]{2,1,0:T(8,128)(2,1)S(1)} %get-tuple-element.40), channel_id=1, source_target_pairs={{0,4},{1,5},{2,6},{3,7},{4,0},{5,1},{6,2},{7,3},{8,12},{9,13},{10,... | collective-permute-start | bytes 393224 | tf_op jit(solution)/shard_map/ppermute | solution.py:305
  46.4 7.8 %collective-permute-start.10 = (bf16[16,32,128]{2,1,0:T(8,128)(2,1)S(1)}, bf16[16,32,128]{2,1,0:T(8,128)(2,1)S(1)}, u32[]{:S(2)}, u32[]{:S(2)}) collective-permute-start(bf16[16,32,128]{2,1,0:T(8,128)(2,1)S(1)} %get-tuple-element.41), channel_id=1, source_target_pairs={{0,6},{1,7},{2,4},{3,5},{4,2},{5,3},{6,0},{7,1},{8,14},{9,15},{10,... | collective-permute-start | bytes 393224 | tf_op jit(solution)/shard_map/ppermute | solution.py:305
  55.4 8.3 %collective-permute-start.20 = (bf16[16,32,128]{2,1,0:T(8,128)(2,1)S(1)}, bf16[16,32,128]{2,1,0:T(8,128)(2,1)S(1)}, u32[]{:S(2)}, u32[]{:S(2)}) collective-permute-start(bf16[16,32,128]{2,1,0:T(8,128)(2,1)S(1)} %get-tuple-element.51), channel_id=1, source_target_pairs={{0,2},{1,3},{2,0},{3,1},{4,6},{5,7},{6,4},{7,5},{8,10},{9,11},{10,... | collective-permute-start | bytes 393224 | tf_op jit(solution)/shard_map/ppermute | solution.py:305
  55.6 9.4 %collective-permute-start.21 = (bf16[16,32,128]{2,1,0:T(8,128)(2,1)S(1)}, bf16[16,32,128]{2,1,0:T(8,128)(2,1)S(1)}, u32[]{:S(2)}, u32[]{:S(2)}) collective-permute-start(bf16[16,32,128]{2,1,0:T(8,128)(2,1)S(1)} %get-tuple-element.52), channel_id=1, source_target_pairs={{0,4},{1,5},{2,6},{3,7},{4,0},{5,1},{6,2},{7,3},{8,12},{9,13},{10,... | collective-permute-start | bytes 393224 | tf_op jit(solution)/shard_map/ppermute | solution.py:305
  57.7 7.6 %collective-permute-start.22 = (bf16[16,32,128]{2,1,0:T(8,128)(2,1)S(1)}, bf16[16,32,128]{2,1,0:T(8,128)(2,1)S(1)}, u32[]{:S(2)}, u32[]{:S(2)}) collective-permute-start(bf16[16,32,128]{2,1,0:T(8,128)(2,1)S(1)} %get-tuple-element.53), channel_id=1, source_target_pairs={{0,6},{1,7},{2,4},{3,5},{4,2},{5,3},{6,0},{7,1},{8,14},{9,15},{10,... | collective-permute-start | bytes 393224 | tf_op jit(solution)/shard_map/ppermute | solution.py:305
  60.0 7.9 %collective-permute-start.12 = (bf16[16,32,128]{2,1,0:T(8,128)(2,1)S(1)}, bf16[16,32,128]{2,1,0:T(8,128)(2,1)S(1)}, u32[]{:S(2)}, u32[]{:S(2)}) collective-permute-start(bf16[16,32,128]{2,1,0:T(8,128)(2,1)S(1)} %get-tuple-element.43), channel_id=1, source_target_pairs={{0,2},{1,3},{2,0},{3,1},{4,6},{5,7},{6,4},{7,5},{8,10},{9,11},{10,... | collective-permute-start | bytes 393224 | tf_op jit(solution)/shard_map/ppermute | solution.py:305
  60.3 9.2 %collective-permute-start.13 = (bf16[16,32,128]{2,1,0:T(8,128)(2,1)S(1)}, bf16[16,32,128]{2,1,0:T(8,128)(2,1)S(1)}, u32[]{:S(2)}, u32[]{:S(2)}) collective-permute-start(bf16[16,32,128]{2,1,0:T(8,128)(2,1)S(1)} %get-tuple-element.44), channel_id=1, source_target_pairs={{0,4},{1,5},{2,6},{3,7},{4,0},{5,1},{6,2},{7,3},{8,12},{9,13},{10,... | collective-permute-start | bytes 393224 | tf_op jit(solution)/shard_map/ppermute | solution.py:305
  63.7 7.0 %collective-permute-start.14 = (bf16[16,32,128]{2,1,0:T(8,128)(2,1)S(1)}, bf16[16,32,128]{2,1,0:T(8,128)(2,1)S(1)}, u32[]{:S(2)}, u32[]{:S(2)}) collective-permute-start(bf16[16,32,128]{2,1,0:T(8,128)(2,1)S(1)} %get-tuple-element.45), channel_id=1, source_target_pairs={{0,6},{1,7},{2,4},{3,5},{4,2},{5,3},{6,0},{7,1},{8,14},{9,15},{10,... | collective-permute-start | bytes 393224 | tf_op jit(solution)/shard_map/ppermute | solution.py:305
  65.0 7.0 %collective-permute-start.1 = (bf16[16,32,128]{2,1,0:T(8,128)(2,1)S(1)}, bf16[16,32,128]{2,1,0:T(8,128)(2,1)S(1)}, u32[]{:S(2)}, u32[]{:S(2)}) collective-permute-start(bf16[16,32,128]{2,1,0:T(8,128)(2,1)S(1)} %get-tuple-element.31), channel_id=1, source_target_pairs={{0,2},{1,3},{2,0},{3,1},{4,6},{5,7},{6,4},{7,5},{8,10},{9,11},{10,... | collective-permute-start | bytes 393224 | tf_op jit(solution)/shard_map/ppermute | solution.py:305
  65.4 7.2 %collective-permute-start.2 = (bf16[16,32,128]{2,1,0:T(8,128)(2,1)S(1)}, bf16[16,32,128]{2,1,0:T(8,128)(2,1)S(1)}, u32[]{:S(2)}, u32[]{:S(2)}) collective-permute-start(bf16[16,32,128]{2,1,0:T(8,128)(2,1)S(1)} %get-tuple-element.32), channel_id=1, source_target_pairs={{0,4},{1,5},{2,6},{3,7},{4,0},{5,1},{6,2},{7,3},{8,12},{9,13},{10,... | collective-permute-start | bytes 393224 | tf_op jit(solution)/shard_map/ppermute | solution.py:305
  67.9 6.8 %collective-permute-start.3 = (bf16[16,32,128]{2,1,0:T(8,128)(2,1)S(1)}, bf16[16,32,128]{2,1,0:T(8,128)(2,1)S(1)}, u32[]{:S(2)}, u32[]{:S(2)}) collective-permute-start(bf16[16,32,128]{2,1,0:T(8,128)(2,1)S(1)} %get-tuple-element.33), channel_id=1, source_target_pairs={{0,6},{1,7},{2,4},{3,5},{4,2},{5,3},{6,0},{7,1},{8,14},{9,15},{10,... | collective-permute-start | bytes 393224 | tf_op jit(solution)/shard_map/ppermute | solution.py:305
  69.5 5.3 %collective-permute-start.4 = (bf16[16,32,128]{2,1,0:T(8,128)(2,1)S(1)}, bf16[16,32,128]{2,1,0:T(8,128)(2,1)S(1)}, u32[]{:S(2)}, u32[]{:S(2)}) collective-permute-start(bf16[16,32,128]{2,1,0:T(8,128)(2,1)S(1)} %get-tuple-element.34), channel_id=1, source_target_pairs={{0,1},{1,0},{2,3},{3,2},{4,5},{5,4},{6,7},{7,6},{8,9},{9,8},{10,11... | collective-permute-start | bytes 393224 | tf_op jit(solution)/shard_map/ppermute | solution.py:305
  70.8 5.8 %collective-permute-start.5 = (bf16[16,32,128]{2,1,0:T(8,128)(2,1)S(1)}, bf16[16,32,128]{2,1,0:T(8,128)(2,1)S(1)}, u32[]{:S(2)}, u32[]{:S(2)}) collective-permute-start(bf16[16,32,128]{2,1,0:T(8,128)(2,1)S(1)} %get-tuple-element.35), channel_id=1, source_target_pairs={{0,3},{1,2},{2,1},{3,0},{4,7},{5,6},{6,5},{7,4},{8,11},{9,10},{10,... | collective-permute-start | bytes 393224 | tf_op jit(solution)/shard_map/ppermute | solution.py:305
  72.1 5.6 %collective-permute-start.6 = (bf16[16,32,128]{2,1,0:T(8,128)(2,1)S(1)}, bf16[16,32,128]{2,1,0:T(8,128)(2,1)S(1)}, u32[]{:S(2)}, u32[]{:S(2)}) collective-permute-start(bf16[16,32,128]{2,1,0:T(8,128)(2,1)S(1)} %get-tuple-element.36), channel_id=1, source_target_pairs={{0,5},{1,4},{2,7},{3,6},{4,1},{5,0},{6,3},{7,2},{8,13},{9,12},{10,... | collective-permute-start | bytes 393224 | tf_op jit(solution)/shard_map/ppermute | solution.py:305
  72.6 8.6 %collective-permute-start.7 = (bf16[16,32,128]{2,1,0:T(8,128)(2,1)S(1)}, bf16[16,32,128]{2,1,0:T(8,128)(2,1)S(1)}, u32[]{:S(2)}, u32[]{:S(2)}) collective-permute-start(bf16[16,32,128]{2,1,0:T(8,128)(2,1)S(1)} %get-tuple-element.37), channel_id=1, source_target_pairs={{0,7},{1,6},{2,5},{3,4},{4,3},{5,2},{6,1},{7,0},{8,15},{9,14},{10,... | collective-permute-start | bytes 393224 | tf_op jit(solution)/shard_map/ppermute | solution.py:305
  74.7 6.7 %collective-permute-start.23 = (bf16[64,32,128]{2,1,0:T(8,128)(2,1)S(1)}, bf16[64,32,128]{2,1,0:T(8,128)(2,1)S(1)}, u32[]{:S(2)}, u32[]{:S(2)}) collective-permute-start(bf16[64,32,128]{2,1,0:T(8,128)(2,1)S(1)} %constant_dynamic-update-slice_fusion.32), channel_id=1, source_target_pairs={{0,1},{1,0},{2,3},{3,2},{4,5},{5,4},{6,7},{7,6},{8,9},{9,8},{10,11... | collective-permute-start | bytes 1572872 | tf_op jit(solution)/shard_map/ppermute | solution.py:317
  74.8 6.7 %collective-permute-start.15 = (bf16[64,32,128]{2,1,0:T(8,128)(2,1)S(1)}, bf16[64,32,128]{2,1,0:T(8,128)(2,1)S(1)}, u32[]{:S(2)}, u32[]{:S(2)}) collective-permute-start(bf16[64,32,128]{2,1,0:T(8,128)(2,1)S(1)} %constant_dynamic-update-slice_fusion.16), channel_id=1, source_target_pairs={{0,1},{1,0},{2,3},{3,2},{4,5},{5,4},{6,7},{7,6},{8,9},{9,8},{10,11... | collective-permute-start | bytes 1572872 | tf_op jit(solution)/shard_map/ppermute | solution.py:317
  (4 other events, 7.3 us)

commit v13 on v9

--- a/solution.py
+++ b/solution.py
@@ -71,7 +71,14 @@
     )(tile_map, row_anchor, col_anchor)
 
 
-def slot_kernel(peers, cap, direct, place_ref, tile_ref, slot_ref):
+def slot_kernel(peers, cap, direct, place_ref, tile_ref, *refs):
+    start_refs, slot_ref, moved_refs, sem = refs[:2], refs[2], refs[3:5], refs[5]
+    moves = [
+        pltpu.make_async_copy(src, dst, sem.at[at])
+        for at, (src, dst) in enumerate(zip(start_refs, moved_refs))
+    ]
+    for move in moves:
+        move.start()
     relays = peers // 2
     for k in range(PLANES):
         tile, _, rank = ranks(peers, tile_ref, k)
@@ -81,17 +88,22 @@
             relay = (relay & 1) * (relays // 2) + (relay >> 1)
         far = (side != place_ref[0]).astype(jnp.int32)
         slot_ref[k : k + 1, :] = (far * relays + relay) * cap + rank
-
-
-def find_slots(place, tile_map, peers, cap, direct):
+    for move in moves:
+        move.wait()
+
+
+def find_slots(place, tile_map, start, peers, cap, direct):
+    shapes = [jax.ShapeDtypeStruct((PLANES, tile_map.shape[2]), jnp.int32)]
+    shapes += [jax.ShapeDtypeStruct(x.shape, x.dtype) for x in start]
     return pl.pallas_call(
         functools.partial(slot_kernel, peers, cap, direct),
-        out_shape=jax.ShapeDtypeStruct((PLANES, tile_map.shape[2]), jnp.int32),
-        in_specs=[whole(SMEM), whole()],
-        out_specs=whole(),
+        out_shape=tuple(shapes),
+        in_specs=[whole(SMEM), whole()] + [whole(pltpu.MemorySpace.HBM)] * 2,
+        out_specs=(whole(),) * 3,
+        scratch_shapes=[pltpu.SemaphoreType.DMA((2,))],
         compiler_params=GRANT,
         name="slots",
-    )(place, tile_map)
+    )(place, tile_map, *start)
 
 
 def cut_kernel(planes, cap, mirrored, place_ref, req_ref, *refs):
@@ -311,8 +323,8 @@
         return [(pieces(at), pieces(count + at)) for at in range(count)]
 
     def across(lists):
-        if direct:
-            return [[] for _ in lists]
+        if not lists:
+            return []
         got = lax.ppermute(jnp.concatenate(sum(lists, []), axis=0), "sky", swap(1))
         size = chips * cap
         return [[got[at * size : (at + 1) * size]] for at in range(len(lists))]
@@ -336,12 +348,11 @@
     sheets = [tile(0, gradients)] + [tile(plane, late) for plane in range(1, PLANES)]
     mirrors = [mirror(plane) for plane in range(PLANES)]
     asked = exchange(requests)
-    slots = find_slots(place, tiles, peers, cap, direct)
+    slots, *state = find_slots(place, tiles, (start_x, start_y), peers, cap, direct)
     own, far = [], []
     for plane in range(PLANES):
         own.append(cut_sent(plane, False, sheets[plane]))
         far.append(cut_sent(plane, True, mirrors[plane], plane == PLANES - 1))
-    state = (start_x, start_y)
     for plane in range(PLANES):
         sets = (own[plane], far[plane])
         held = iter(across([other for _, other in sets if other]))

time: 108 us -> 108 us (level)
  waiting for transfers between devices: 46.6 us -> 51.7 us
  starting transfers between devices: 37.9 us -> 33.2 us
    ppermute x22, waiting for transfers between devices: 46.5 us -> 51.7 us  [ship(): got.append(lax.ppermute(parts[m], 'sky', swap(step * m)))]
    ppermute x22, starting transfers between devices: 26.4 us -> 21.6 us  [ship(): got.append(lax.ppermute(parts[m], 'sky', swap(step * m)))]
  transfers between devices with their start and end apart: 29 -> 29, of which waited for: 14 -> 13; matrix products, arithmetic and copies ran while one was open for 2% -> 2% of each run, Pallas kernels for 7% -> 7%
where the time goes in v13:
time: 108 us; the launch traced here: 107 us
  waiting for transfers between devices  51.7 us (48%)
  starting transfers between devices  33.2 us (31%)
  Pallas kernels  17.9 us (17%)
  local copies, waits for them, and re-layouts  3.34 us (3%)
    ppermute x22, waiting for transfers between devices, ship(): got.append(lax.ppermute(parts[m], 'sky', swap(step * m)))  51.7 us
    ppermute x22, starting transfers between devices, ship(): got.append(lax.ppermute(parts[m], 'sky', swap(step * m)))  21.6 us
    pallas_call x3, Pallas kernels, interp(): pl.pallas_call(functools.partial(interp_kernel, plane), out_shape=out_sha...  8.98 us
    pallas_call x6, Pallas kernels, cut(): pl.pallas_call(functools.partial(cut_kernel, planes, cap, mirrored), out_...  6.31 us
    ppermute x3, starting transfers between devices, mirror(): return lax.ppermute(sheets[plane], 'sky', mirror_pairs)  5.64 us
    all_to_all x1, starting transfers between devices, exchange(): lax.all_to_all(x, 'sky', split_axis=0, concat_axis=0, axis_index_groups=g...  5.28 us
  transfers between devices with their start and end apart: 29, of which 13 were waited for; matrix products, arithmetic and copies ran while one was open for 2% of the time, Pallas kernels for 7%

profile of v13, /device:TPU:0, one launch (start us, length us, event | category | flops | bytes accessed | tf_op | source)
XLA Modules:
  0.0 107.3 jit_solution(13869154868289914188)
XLA Ops:
  0.6 1.8 %want.1 = s32[8,128]{1,0:T(8,128)} custom-call(s32[3,1,64]{2,1,0:T(1,128)} %bitcast.19, s32[3,64]{1,0:T(4,128)} %row_ref.1, s32[3,64]{1,0:T(4,128)} %col_ref.1), custom_call_target="tpu_custom_call" | custom-call | tf_op jit(solution)/shard_map/want/pallas_call | solution.py:65
  2.5 5.3 %all-to-all-start = ((s32[8,1,128]{2,1,0:T(1,128)}), s32[8,1,128]{2,1,0:T(1,128)S(1)}, u32[]{:S(2)}, u32[]{:S(2)}) async-start(s32[8,1,128]{2,1,0:T(1,128)} %bitcast.21), calls=%async_computation | async-start | bytes 8192 | tf_op jit(solution)/shard_map/all_to_all | solution.py:304
  8.7 2.7 %collective-permute-start.23 = (bf16[2,256,256]{2,1,0:T(8,128)(2,1)S(1)}, bf16[2,256,256]{2,1,0:T(8,128)(2,1)S(1)}, u32[]{:S(2)}, u32[]{:S(2)}) collective-permute-start(bf16[2,256,256]{2,1,0:T(8,128)(2,1)S(1)} %slice_bitcast_fusion.refs_0_), channel_id=1, source_target_pairs={{0,8},{1,9},{2,10},{3,11},{4,12},{5,13},{6,14},{7,15},{8,0},{9,1},... | collective-permute-start | bytes 786440 | tf_op jit(solution)/shard_map/ppermute | solution.py:336
  11.4 1.1 slice_bitcast_fusion.1
  12.9 2.6 %collective-permute-start.4 = (bf16[2,256,256]{2,1,0:T(8,128)(2,1)S(1)}, bf16[2,256,256]{2,1,0:T(8,128)(2,1)S(1)}, u32[]{:S(2)}, u32[]{:S(2)}) collective-permute-start(bf16[2,256,256]{2,1,0:T(8,128)(2,1)S(1)} %get-tuple-element.69.refs_0_), channel_id=1, source_target_pairs={{0,8},{1,9},{2,10},{3,11},{4,12},{5,13},{6,14},{7,15},{8,0},{9,1},... | collective-permute-start | bytes 786440 | tf_op jit(solution)/shard_map/ppermute | solution.py:336
  18.0 1.1 cut.8
  20.2 2.1 %collective-permute-start.20 = (bf16[16,32,128]{2,1,0:T(8,128)(2,1)S(1)}, bf16[16,32,128]{2,1,0:T(8,128)(2,1)S(1)}, u32[]{:S(2)}, u32[]{:S(2)}) collective-permute-start(bf16[16,32,128]{2,1,0:T(8,128)(2,1)S(1)} %get-tuple-element.59), channel_id=1, source_target_pairs={{0,2},{1,3},{2,0},{3,1},{4,6},{5,7},{6,4},{7,5},{8,10},{9,11},{10,... | collective-permute-start | bytes 393224 | tf_op jit(solution)/shard_map/ppermute | solution.py:316
  22.4 5.7 %collective-permute-done = bf16[16,32,128]{2,1,0:T(8,128)(2,1)S(1)} collective-permute-done((bf16[16,32,128]{2,1,0:T(8,128)(2,1)S(1)}, bf16[16,32,128]{2,1,0:T(8,128)(2,1)S(1)}, u32[]{:S(2)}, u32[]{:S(2)}) %collective-permute-start) | collective-permute-done | bytes 131104 | tf_op jit(solution)/shard_map/ppermute | solution.py:316
  28.1 1.6 %collective-permute-start.1 = (bf16[16,32,128]{2,1,0:T(8,128)(2,1)S(1)}, bf16[16,32,128]{2,1,0:T(8,128)(2,1)S(1)}, u32[]{:S(2)}, u32[]{:S(2)}) collective-permute-start(bf16[16,32,128]{2,1,0:T(8,128)(2,1)S(1)} %get-tuple-element.40), channel_id=1, source_target_pairs={{0,4},{1,5},{2,6},{3,7},{4,0},{5,1},{6,2},{7,3},{8,12},{9,13},{10,... | collective-permute-start | bytes 393224 | tf_op jit(solution)/shard_map/ppermute | solution.py:316
  29.8 19.6 %collective-permute-done.1 = bf16[16,32,128]{2,1,0:T(8,128)(2,1)S(1)} collective-permute-done((bf16[16,32,128]{2,1,0:T(8,128)(2,1)S(1)}, bf16[16,32,128]{2,1,0:T(8,128)(2,1)S(1)}, u32[]{:S(2)}, u32[]{:S(2)}) %collective-permute-start.1) | collective-permute-done | bytes 131104 | tf_op jit(solution)/shard_map/ppermute | solution.py:316
  49.4 6.6 %collective-permute-done.2 = bf16[16,32,128]{2,1,0:T(8,128)(2,1)S(1)} collective-permute-done((bf16[16,32,128]{2,1,0:T(8,128)(2,1)S(1)}, bf16[16,32,128]{2,1,0:T(8,128)(2,1)S(1)}, u32[]{:S(2)}, u32[]{:S(2)}) %collective-permute-start.2) | collective-permute-done | bytes 131104 | tf_op jit(solution)/shard_map/ppermute | solution.py:316
  57.0 5.4 %collective-permute-done.21 = bf16[16,32,128]{2,1,0:T(8,128)(2,1)S(1)} collective-permute-done((bf16[16,32,128]{2,1,0:T(8,128)(2,1)S(1)}, bf16[16,32,128]{2,1,0:T(8,128)(2,1)S(1)}, u32[]{:S(2)}, u32[]{:S(2)}) %collective-permute-start.21) | collective-permute-done | bytes 131104 | tf_op jit(solution)/shard_map/ppermute | solution.py:316
  63.0 1.7 %collective-permute-start.13 = (bf16[16,32,128]{2,1,0:T(8,128)(2,1)S(1)}, bf16[16,32,128]{2,1,0:T(8,128)(2,1)S(1)}, u32[]{:S(2)}, u32[]{:S(2)}) collective-permute-start(bf16[16,32,128]{2,1,0:T(8,128)(2,1)S(1)} %get-tuple-element.52), channel_id=1, source_target_pairs={{0,4},{1,5},{2,6},{3,7},{4,0},{5,1},{6,2},{7,3},{8,12},{9,13},{10,... | collective-permute-start | bytes 393224 | tf_op jit(solution)/shard_map/ppermute | solution.py:316
  64.8 2.5 %collective-permute-done.12 = bf16[16,32,128]{2,1,0:T(8,128)(2,1)S(1)} collective-permute-done((bf16[16,32,128]{2,1,0:T(8,128)(2,1)S(1)}, bf16[16,32,128]{2,1,0:T(8,128)(2,1)S(1)}, u32[]{:S(2)}, u32[]{:S(2)}) %collective-permute-start.12) | collective-permute-done | bytes 131104 | tf_op jit(solution)/shard_map/ppermute | solution.py:316
  68.3 4.9 %collective-permute-done.14 = bf16[16,32,128]{2,1,0:T(8,128)(2,1)S(1)} collective-permute-done((bf16[16,32,128]{2,1,0:T(8,128)(2,1)S(1)}, bf16[16,32,128]{2,1,0:T(8,128)(2,1)S(1)}, u32[]{:S(2)}, u32[]{:S(2)}) %collective-permute-start.14) | collective-permute-done | bytes 131104 | tf_op jit(solution)/shard_map/ppermute | solution.py:316
  75.7 2.1 %collective-permute-start.26 = (bf16[16,32,128]{2,1,0:T(8,128)(2,1)S(1)}, bf16[16,32,128]{2,1,0:T(8,128)(2,1)S(1)}, u32[]{:S(2)}, u32[]{:S(2)}) collective-permute-start(bf16[16,32,128]{2,1,0:T(8,128)(2,1)S(1)} %get-tuple-element.65), channel_id=1, source_target_pairs={{0,6},{1,7},{2,4},{3,5},{4,2},{5,3},{6,0},{7,1},{8,14},{9,15},{10,... | collective-permute-start | bytes 393224 | tf_op jit(solution)/shard_map/ppermute | solution.py:316
  81.4 4.0 %collective-permute-start.18 = (bf16[16,32,128]{2,1,0:T(8,128)(2,1)S(1)}, bf16[16,32,128]{2,1,0:T(8,128)(2,1)S(1)}, u32[]{:S(2)}, u32[]{:S(2)}) collective-permute-start(bf16[16,32,128]{2,1,0:T(8,128)(2,1)S(1)} %get-tuple-element.57), channel_id=1, source_target_pairs={{0,6},{1,7},{2,4},{3,5},{4,2},{5,3},{6,0},{7,1},{8,14},{9,15},{10,... | collective-permute-start | bytes 393224 | tf_op jit(solution)/shard_map/ppermute | solution.py:316
  86.8 2.5 %collective-permute-start.7 = (bf16[8,32,128]{2,1,0:T(8,128)(2,1)S(1)}, bf16[8,32,128]{2,1,0:T(8,128)(2,1)S(1)}, u32[]{:S(2)}, u32[]{:S(2)}) collective-permute-start(bf16[8,32,128]{2,1,0:T(8,128)(2,1)S(1)} %get-tuple-element.45), channel_id=1, source_target_pairs={{0,6},{1,7},{2,4},{3,5},{4,2},{5,3},{6,0},{7,1},{8,14},{9,15},{10,... | collective-permute-start | bytes 196616 | tf_op jit(solution)/shard_map/ppermute | solution.py:316
  89.3 1.2 %collective-permute-done.18 = bf16[16,32,128]{2,1,0:T(8,128)(2,1)S(1)} collective-permute-done((bf16[16,32,128]{2,1,0:T(8,128)(2,1)S(1)}, bf16[16,32,128]{2,1,0:T(8,128)(2,1)S(1)}, u32[]{:S(2)}, u32[]{:S(2)}) %collective-permute-start.18) | collective-permute-done | bytes 131104 | tf_op jit(solution)/shard_map/ppermute | solution.py:316
  91.9 2.3 %collective-permute-start.11 = (bf16[8,32,128]{2,1,0:T(8,128)(2,1)S(1)}, bf16[8,32,128]{2,1,0:T(8,128)(2,1)S(1)}, u32[]{:S(2)}, u32[]{:S(2)}) collective-permute-start(bf16[8,32,128]{2,1,0:T(8,128)(2,1)S(1)} %get-tuple-element.49), channel_id=1, source_target_pairs={{0,7},{1,6},{2,5},{3,4},{4,3},{5,2},{6,1},{7,0},{8,15},{9,14},{10,... | collective-permute-start | bytes 196616 | tf_op jit(solution)/shard_map/ppermute | solution.py:316
  95.2 2.7 %collective-permute-done.11 = bf16[8,32,128]{2,1,0:T(8,128)(2,1)S(1)} collective-permute-done((bf16[8,32,128]{2,1,0:T(8,128)(2,1)S(1)}, bf16[8,32,128]{2,1,0:T(8,128)(2,1)S(1)}, u32[]{:S(2)}, u32[]{:S(2)}) %collective-permute-start.11) | collective-permute-done | bytes 65568 | tf_op jit(solution)/shard_map/ppermute | solution.py:316
  98.2 2.7 %shard_map.77.refs_0_ = f32[12,64,128]{2,1,0:T(8,128)S(1)} custom-call(s32[3,64]{1,0:T(4,128)S(1)} %get-tuple-element.35.slot_ref, bf16[128,32,128]{2,1,0:T(8,128)(2,1)S(1)} %slice_dynamic-update-slice_fusion.win_ref, f32[64,128]{1,0:T(8,128)S(1)} %get-tuple-element.66.refs_0_, f32[64,128]{1,0:T(8,128)S(1)} %get-tuple-element.67.refs_1_), custom_call_target="tpu_custom_call" | custom-call | tf_op jit(solution)/shard_map/pallas_call | solution.py:276
  101.1 2.7 %shard_map.78.refs_0_ = f32[12,64,128]{2,1,0:T(8,128)S(1)} custom-call(s32[3,64]{1,0:T(4,128)S(1)} %get-tuple-element.35.slot_ref, bf16[128,32,128]{2,1,0:T(8,128)(2,1)S(1)} %slice_dynamic-update-slice_fusion.2.win_ref, f32[12,64,128]{2,1,0:T(8,128)S(1)} %shard_map.77.refs_0_), custom_call_target="tpu_custom_call" | custom-call | tf_op jit(solution)/shard_map/pallas_call | solution.py:276
  103.8 3.5 %shard_map.79 = (f32[64,2,128]{2,1,0:T(2,128)}, f32[64,4,128]{2,1,0:T(4,128)}) custom-call(s32[3,64]{1,0:T(4,128)S(1)} %get-tuple-element.35.slot_ref, bf16[128,32,128]{2,1,0:T(8,128)(2,1)S(1)} %constant_dynamic-update-slice_fusion.win_ref, f32[12,64,128]{2,1,0:T(8,128)S(1)} %shard_map.78.refs_0_), custom_call_target="tpu_custom_call" | custom-call | tf_op jit(solution)/shard_map/pallas_call | solution.py:276
  (96 shorter events, 17.7 us)
Async XLA Ops:
  2.5 14.5 %all-to-all-start = ((s32[8,1,128]{2,1,0:T(1,128)}), s32[8,1,128]{2,1,0:T(1,128)S(1)}, u32[]{:S(2)}, u32[]{:S(2)}) async-start(s32[8,1,128]{2,1,0:T(1,128)} %bitcast.21), calls=%async_computation | async-start | bytes 8192 | tf_op jit(solution)/shard_map/all_to_all | solution.py:304
  8.7 64.5 %collective-permute-start.23 = (bf16[2,256,256]{2,1,0:T(8,128)(2,1)S(1)}, bf16[2,256,256]{2,1,0:T(8,128)(2,1)S(1)}, u32[]{:S(2)}, u32[]{:S(2)}) collective-permute-start(bf16[2,256,256]{2,1,0:T(8,128)(2,1)S(1)} %slice_bitcast_fusion.refs_0_), channel_id=1, source_target_pairs={{0,8},{1,9},{2,10},{3,11},{4,12},{5,13},{6,14},{7,15},{8,0},{9,1},... | collective-permute-start | bytes 786440 | tf_op jit(solution)/shard_map/ppermute | solution.py:336
  12.4 63.2 %collective-permute-start.15 = (bf16[2,256,256]{2,1,0:T(8,128)(2,1)S(1)}, bf16[2,256,256]{2,1,0:T(8,128)(2,1)S(1)}, u32[]{:S(2)}, u32[]{:S(2)}) collective-permute-start(bf16[2,256,256]{2,1,0:T(8,128)(2,1)S(1)} %get-tuple-element.68.refs_0_), channel_id=1, source_target_pairs={{0,8},{1,9},{2,10},{3,11},{4,12},{5,13},{6,14},{7,15},{8,0},{9,1},... | collective-permute-start | bytes 786440 | tf_op jit(solution)/shard_map/ppermute | solution.py:336
  12.9 66.1 %collective-permute-start.4 = (bf16[2,256,256]{2,1,0:T(8,128)(2,1)S(1)}, bf16[2,256,256]{2,1,0:T(8,128)(2,1)S(1)}, u32[]{:S(2)}, u32[]{:S(2)}) collective-permute-start(bf16[2,256,256]{2,1,0:T(8,128)(2,1)S(1)} %get-tuple-element.69.refs_0_), channel_id=1, source_target_pairs={{0,8},{1,9},{2,10},{3,11},{4,12},{5,13},{6,14},{7,15},{8,0},{9,1},... | collective-permute-start | bytes 786440 | tf_op jit(solution)/shard_map/ppermute | solution.py:336
  20.2 35.8 %collective-permute-start.20 = (bf16[16,32,128]{2,1,0:T(8,128)(2,1)S(1)}, bf16[16,32,128]{2,1,0:T(8,128)(2,1)S(1)}, u32[]{:S(2)}, u32[]{:S(2)}) collective-permute-start(bf16[16,32,128]{2,1,0:T(8,128)(2,1)S(1)} %get-tuple-element.59), channel_id=1, source_target_pairs={{0,2},{1,3},{2,0},{3,1},{4,6},{5,7},{6,4},{7,5},{8,10},{9,11},{10,... | collective-permute-start | bytes 393224 | tf_op jit(solution)/shard_map/ppermute | solution.py:316
  22.3 5.8 %collective-permute-start = (bf16[16,32,128]{2,1,0:T(8,128)(2,1)S(1)}, bf16[16,32,128]{2,1,0:T(8,128)(2,1)S(1)}, u32[]{:S(2)}, u32[]{:S(2)}) collective-permute-start(bf16[16,32,128]{2,1,0:T(8,128)(2,1)S(1)} %get-tuple-element.39), channel_id=1, source_target_pairs={{0,2},{1,3},{2,0},{3,1},{4,6},{5,7},{6,4},{7,5},{8,10},{9,11},{10,... | collective-permute-start | bytes 393224 | tf_op jit(solution)/shard_map/ppermute | solution.py:316
  28.1 21.2 %collective-permute-start.1 = (bf16[16,32,128]{2,1,0:T(8,128)(2,1)S(1)}, bf16[16,32,128]{2,1,0:T(8,128)(2,1)S(1)}, u32[]{:S(2)}, u32[]{:S(2)}) collective-permute-start(bf16[16,32,128]{2,1,0:T(8,128)(2,1)S(1)} %get-tuple-element.40), channel_id=1, source_target_pairs={{0,4},{1,5},{2,6},{3,7},{4,0},{5,1},{6,2},{7,3},{8,12},{9,13},{10,... | collective-permute-start | bytes 393224 | tf_op jit(solution)/shard_map/ppermute | solution.py:316
  49.4 6.6 %collective-permute-start.2 = (bf16[16,32,128]{2,1,0:T(8,128)(2,1)S(1)}, bf16[16,32,128]{2,1,0:T(8,128)(2,1)S(1)}, u32[]{:S(2)}, u32[]{:S(2)}) collective-permute-start(bf16[16,32,128]{2,1,0:T(8,128)(2,1)S(1)} %get-tuple-element.41), channel_id=1, source_target_pairs={{0,6},{1,7},{2,4},{3,5},{4,2},{5,3},{6,0},{7,1},{8,14},{9,15},{10,... | collective-permute-start | bytes 393224 | tf_op jit(solution)/shard_map/ppermute | solution.py:316
  56.0 6.3 %collective-permute-start.21 = (bf16[16,32,128]{2,1,0:T(8,128)(2,1)S(1)}, bf16[16,32,128]{2,1,0:T(8,128)(2,1)S(1)}, u32[]{:S(2)}, u32[]{:S(2)}) collective-permute-start(bf16[16,32,128]{2,1,0:T(8,128)(2,1)S(1)} %get-tuple-element.60), channel_id=1, source_target_pairs={{0,4},{1,5},{2,6},{3,7},{4,0},{5,1},{6,2},{7,3},{8,12},{9,13},{10,... | collective-permute-start | bytes 393224 | tf_op jit(solution)/shard_map/ppermute | solution.py:316
  56.0 7.0 %collective-permute-start.22 = (bf16[16,32,128]{2,1,0:T(8,128)(2,1)S(1)}, bf16[16,32,128]{2,1,0:T(8,128)(2,1)S(1)}, u32[]{:S(2)}, u32[]{:S(2)}) collective-permute-start(bf16[16,32,128]{2,1,0:T(8,128)(2,1)S(1)} %get-tuple-element.61), channel_id=1, source_target_pairs={{0,6},{1,7},{2,4},{3,5},{4,2},{5,3},{6,0},{7,1},{8,14},{9,15},{10,... | collective-permute-start | bytes 393224 | tf_op jit(solution)/shard_map/ppermute | solution.py:316
  62.3 5.0 %collective-permute-start.12 = (bf16[16,32,128]{2,1,0:T(8,128)(2,1)S(1)}, bf16[16,32,128]{2,1,0:T(8,128)(2,1)S(1)}, u32[]{:S(2)}, u32[]{:S(2)}) collective-permute-start(bf16[16,32,128]{2,1,0:T(8,128)(2,1)S(1)} %get-tuple-element.51), channel_id=1, source_target_pairs={{0,2},{1,3},{2,0},{3,1},{4,6},{5,7},{6,4},{7,5},{8,10},{9,11},{10,... | collective-permute-start | bytes 393224 | tf_op jit(solution)/shard_map/ppermute | solution.py:316
  63.0 5.1 %collective-permute-start.13 = (bf16[16,32,128]{2,1,0:T(8,128)(2,1)S(1)}, bf16[16,32,128]{2,1,0:T(8,128)(2,1)S(1)}, u32[]{:S(2)}, u32[]{:S(2)}) collective-permute-start(bf16[16,32,128]{2,1,0:T(8,128)(2,1)S(1)} %get-tuple-element.52), channel_id=1, source_target_pairs={{0,4},{1,5},{2,6},{3,7},{4,0},{5,1},{6,2},{7,3},{8,12},{9,13},{10,... | collective-permute-start | bytes 393224 | tf_op jit(solution)/shard_map/ppermute | solution.py:316
  67.3 5.9 %collective-permute-start.14 = (bf16[16,32,128]{2,1,0:T(8,128)(2,1)S(1)}, bf16[16,32,128]{2,1,0:T(8,128)(2,1)S(1)}, u32[]{:S(2)}, u32[]{:S(2)}) collective-permute-start(bf16[16,32,128]{2,1,0:T(8,128)(2,1)S(1)} %get-tuple-element.53), channel_id=1, source_target_pairs={{0,6},{1,7},{2,4},{3,5},{4,2},{5,3},{6,0},{7,1},{8,14},{9,15},{10,... | collective-permute-start | bytes 393224 | tf_op jit(solution)/shard_map/ppermute | solution.py:316
  68.2 22.4 %collective-permute-start.3 = (bf16[32,32,128]{2,1,0:T(8,128)(2,1)S(1)}, bf16[32,32,128]{2,1,0:T(8,128)(2,1)S(1)}, u32[]{:S(2)}, u32[]{:S(2)}) collective-permute-start(bf16[32,32,128]{2,1,0:T(8,128)(2,1)S(1)} %pad_maximum_fusion), channel_id=1, source_target_pairs={{0,1},{1,0},{2,3},{3,2},{4,5},{5,4},{6,7},{7,6},{8,9},{9,8},{10,11... | collective-permute-start | bytes 786440 | tf_op jit(solution)/shard_map/ppermute | solution.py:328
  74.3 7.0 %collective-permute-start.24 = (bf16[16,32,128]{2,1,0:T(8,128)(2,1)S(1)}, bf16[16,32,128]{2,1,0:T(8,128)(2,1)S(1)}, u32[]{:S(2)}, u32[]{:S(2)}) collective-permute-start(bf16[16,32,128]{2,1,0:T(8,128)(2,1)S(1)} %get-tuple-element.63), channel_id=1, source_target_pairs={{0,2},{1,3},{2,0},{3,1},{4,6},{5,7},{6,4},{7,5},{8,10},{9,11},{10,... | collective-permute-start | bytes 393224 | tf_op jit(solution)/shard_map/ppermute | solution.py:316
  74.9 6.5 %collective-permute-start.25 = (bf16[16,32,128]{2,1,0:T(8,128)(2,1)S(1)}, bf16[16,32,128]{2,1,0:T(8,128)(2,1)S(1)}, u32[]{:S(2)}, u32[]{:S(2)}) collective-permute-start(bf16[16,32,128]{2,1,0:T(8,128)(2,1)S(1)} %get-tuple-element.64), channel_id=1, source_target_pairs={{0,4},{1,5},{2,6},{3,7},{4,0},{5,1},{6,2},{7,3},{8,12},{9,13},{10,... | collective-permute-start | bytes 393224 | tf_op jit(solution)/shard_map/ppermute | solution.py:316
  75.7 9.8 %collective-permute-start.26 = (bf16[16,32,128]{2,1,0:T(8,128)(2,1)S(1)}, bf16[16,32,128]{2,1,0:T(8,128)(2,1)S(1)}, u32[]{:S(2)}, u32[]{:S(2)}) collective-permute-start(bf16[16,32,128]{2,1,0:T(8,128)(2,1)S(1)} %get-tuple-element.65), channel_id=1, source_target_pairs={{0,6},{1,7},{2,4},{3,5},{4,2},{5,3},{6,0},{7,1},{8,14},{9,15},{10,... | collective-permute-start | bytes 393224 | tf_op jit(solution)/shard_map/ppermute | solution.py:316
  78.9 7.6 %collective-permute-start.16 = (bf16[16,32,128]{2,1,0:T(8,128)(2,1)S(1)}, bf16[16,32,128]{2,1,0:T(8,128)(2,1)S(1)}, u32[]{:S(2)}, u32[]{:S(2)}) collective-permute-start(bf16[16,32,128]{2,1,0:T(8,128)(2,1)S(1)} %get-tuple-element.55), channel_id=1, source_target_pairs={{0,2},{1,3},{2,0},{3,1},{4,6},{5,7},{6,4},{7,5},{8,10},{9,11},{10,... | collective-permute-start | bytes 393224 | tf_op jit(solution)/shard_map/ppermute | solution.py:316
  81.2 5.6 %collective-permute-start.17 = (bf16[16,32,128]{2,1,0:T(8,128)(2,1)S(1)}, bf16[16,32,128]{2,1,0:T(8,128)(2,1)S(1)}, u32[]{:S(2)}, u32[]{:S(2)}) collective-permute-start(bf16[16,32,128]{2,1,0:T(8,128)(2,1)S(1)} %get-tuple-element.56), channel_id=1, source_target_pairs={{0,4},{1,5},{2,6},{3,7},{4,0},{5,1},{6,2},{7,3},{8,12},{9,13},{10,... | collective-permute-start | bytes 393224 | tf_op jit(solution)/shard_map/ppermute | solution.py:316
  81.4 9.1 %collective-permute-start.18 = (bf16[16,32,128]{2,1,0:T(8,128)(2,1)S(1)}, bf16[16,32,128]{2,1,0:T(8,128)(2,1)S(1)}, u32[]{:S(2)}, u32[]{:S(2)}) collective-permute-start(bf16[16,32,128]{2,1,0:T(8,128)(2,1)S(1)} %get-tuple-element.57), channel_id=1, source_target_pairs={{0,6},{1,7},{2,4},{3,5},{4,2},{5,3},{6,0},{7,1},{8,14},{9,15},{10,... | collective-permute-start | bytes 393224 | tf_op jit(solution)/shard_map/ppermute | solution.py:316
  85.5 5.7 %collective-permute-start.5 = (bf16[8,32,128]{2,1,0:T(8,128)(2,1)S(1)}, bf16[8,32,128]{2,1,0:T(8,128)(2,1)S(1)}, u32[]{:S(2)}, u32[]{:S(2)}) collective-permute-start(bf16[8,32,128]{2,1,0:T(8,128)(2,1)S(1)} %get-tuple-element.43), channel_id=1, source_target_pairs={{0,2},{1,3},{2,0},{3,1},{4,6},{5,7},{6,4},{7,5},{8,10},{9,11},{10,... | collective-permute-start | bytes 196616 | tf_op jit(solution)/shard_map/ppermute | solution.py:316
  86.5 5.4 %collective-permute-start.6 = (bf16[8,32,128]{2,1,0:T(8,128)(2,1)S(1)}, bf16[8,32,128]{2,1,0:T(8,128)(2,1)S(1)}, u32[]{:S(2)}, u32[]{:S(2)}) collective-permute-start(bf16[8,32,128]{2,1,0:T(8,128)(2,1)S(1)} %get-tuple-element.44), channel_id=1, source_target_pairs={{0,4},{1,5},{2,6},{3,7},{4,0},{5,1},{6,2},{7,3},{8,12},{9,13},{10,... | collective-permute-start | bytes 196616 | tf_op jit(solution)/shard_map/ppermute | solution.py:316
  86.8 7.4 %collective-permute-start.7 = (bf16[8,32,128]{2,1,0:T(8,128)(2,1)S(1)}, bf16[8,32,128]{2,1,0:T(8,128)(2,1)S(1)}, u32[]{:S(2)}, u32[]{:S(2)}) collective-permute-start(bf16[8,32,128]{2,1,0:T(8,128)(2,1)S(1)} %get-tuple-element.45), channel_id=1, source_target_pairs={{0,6},{1,7},{2,4},{3,5},{4,2},{5,3},{6,0},{7,1},{8,14},{9,15},{10,... | collective-permute-start | bytes 196616 | tf_op jit(solution)/shard_map/ppermute | solution.py:316
  91.9 6.1 %collective-permute-start.11 = (bf16[8,32,128]{2,1,0:T(8,128)(2,1)S(1)}, bf16[8,32,128]{2,1,0:T(8,128)(2,1)S(1)}, u32[]{:S(2)}, u32[]{:S(2)}) collective-permute-start(bf16[8,32,128]{2,1,0:T(8,128)(2,1)S(1)} %get-tuple-element.49), channel_id=1, source_target_pairs={{0,7},{1,6},{2,5},{3,4},{4,3},{5,2},{6,1},{7,0},{8,15},{9,14},{10,... | collective-permute-start | bytes 196616 | tf_op jit(solution)/shard_map/ppermute | solution.py:316
  (8 other events, 27.6 us)

commit v14 on v13

--- a/solution.py
+++ b/solution.py
@@ -42,33 +42,41 @@
     return tile, hit, jnp.sum(before * hit, axis=0, keepdims=True).astype(jnp.int32)
 
 
-def want_kernel(peers, cap, tile_ref, row_ref, col_ref, req_ref):
+def want_kernel(peers, cap, near, place_ref, tile_ref, row_ref, col_ref, req_ref):
     nblk = tile_ref.shape[2]
     relays, lanes = req_ref.shape
     lane = lax.broadcasted_iota(jnp.int32, (lanes, nblk), 0)
     rows = jnp.zeros((relays, lanes), jnp.float32)
     cols = jnp.zeros((relays, lanes), jnp.float32)
     for k in range(PLANES):
-        tile, hit, rank = ranks(peers, tile_ref, k)
-        here = lane == (rank + (tile // relays + 2 * k) * cap)
+        tile, _, rank = ranks(peers, tile_ref, k)
+        side = tile // relays
+        relay = tile - side * relays
+        group = side + 2 * k
+        if near and k == 0:
+            turn = ((relay ^ place_ref[1]) & near) * (side == place_ref[0]).astype(jnp.int32)
+            relay = relay ^ turn
+            group = jnp.where(turn != 0, 2 * PLANES + side, group)
+        here = lane == (rank + group * cap)
         zero = jnp.zeros((), jnp.float32)
         row = jnp.where(here, row_ref[k : k + 1, :].astype(jnp.float32), zero)
         col = jnp.where(here, col_ref[k : k + 1, :].astype(jnp.float32), zero)
-        fold = (hit[:relays] + hit[relays:]).astype(jnp.bfloat16)
+        fold = lax.broadcasted_iota(jnp.int32, (relays, nblk), 0) == relay
+        fold = fold.astype(jnp.float32).astype(jnp.bfloat16)
         rows += dot_last(fold, row.astype(jnp.bfloat16))
         cols += dot_last(fold, col.astype(jnp.bfloat16))
     req_ref[...] = rows.astype(jnp.int32) * 65536 + cols.astype(jnp.int32)
 
 
-def want(tile_map, row_anchor, col_anchor, peers, cap):
-    lanes = -(-PLANES * 2 * cap // 128) * 128
+def want(place, tile_map, row_anchor, col_anchor, peers, cap, near):
+    lanes = -(-(PLANES + 1) * 2 * cap // 128) * 128
     return pl.pallas_call(
-        functools.partial(want_kernel, peers, cap),
+        functools.partial(want_kernel, peers, cap, near),
         out_shape=jax.ShapeDtypeStruct((peers // 2, lanes), jnp.int32),
-        in_specs=[whole()] * 3,
+        in_specs=[whole(SMEM)] + [whole()] * 3,
         out_specs=whole(),
         name="want",
-    )(tile_map, row_anchor, col_anchor)
+    )(place, tile_map, row_anchor, col_anchor)
 
 
 def slot_kernel(peers, cap, direct, place_ref, tile_ref, *refs):
@@ -106,7 +114,7 @@
     )(place, tile_map, *start)
 
 
-def cut_kernel(planes, cap, mirrored, place_ref, req_ref, *refs):
+def cut_kernel(planes, cap, mirrored, span, place_ref, req_ref, *refs):
     sheet_refs, out_refs, half_ref = refs[: len(planes)], refs[len(planes) : -1], refs[-1]
     parts = sheet_refs[0].shape[-1] // WC
     for at, sheet_ref in enumerate(sheet_refs):
@@ -117,7 +125,6 @@
     lane = lax.broadcasted_iota(jnp.int32, (WR, WC), 1)
     me = place_ref[1]
     side = 1 - place_ref[0] if mirrored else place_ref[0]
-    span = req_ref.shape[0] // len(out_refs)
 
     def one(now, carry):
         for m, out_ref in enumerate(out_refs):
@@ -143,11 +150,11 @@
     lax.fori_loop(0, span, one, 0)
 
 
-def cut(planes, cap, outs, mirrored, place, requests, sheets):
-    count = requests.shape[0] // outs * len(planes) * cap
+def cut(planes, cap, outs, span, mirrored, place, requests, sheets):
+    count = span * len(planes) * cap
     height, width = sheets[0].shape[-2:]
     return pl.pallas_call(
-        functools.partial(cut_kernel, planes, cap, mirrored),
+        functools.partial(cut_kernel, planes, cap, mirrored, span),
         out_shape=(jax.ShapeDtypeStruct((count, 2 * WR, WC), jnp.bfloat16),) * outs,
         in_specs=[whole(SMEM), whole(SMEM)] + [whole()] * len(planes),
         out_specs=(whole(),) * outs,
@@ -294,6 +301,7 @@
     chips = relays // 2
     direct = chips > 4 or chips & (chips - 1) != 0
     outs = 1 if direct else chips
+    near = relays // 2 if chips == 4 else 0
     groups = [[h * relays + r for r in range(relays)] for h in range(2)]
     mirror_pairs = [(i, (i + relays) % peers) for i in range(peers)]
 
@@ -305,13 +313,12 @@
             x, "sky", split_axis=0, concat_axis=0, axis_index_groups=groups, tiled=True
         )
 
-    def ship(parts, count):
+    def ship(parts, count, step):
         if direct:
             got = exchange(parts[0].reshape(relays, -1, 2 * WR, WC))
             got = got.reshape(relays, count, cap, 2 * WR, WC)
             return [([got[:, at].reshape(relays * cap, 2 * WR, WC)], []) for at in range(count)]
         got = [parts[0]]
-        step = relays // len(parts)
         for m in range(1, len(parts)):
             got.append(lax.ppermute(parts[m], "sky", swap(step * m)))
         if step == 1:
@@ -337,21 +344,32 @@
 
     def cut_sent(plane, mirrored, sheet, straight=False):
         count = outs * 2 if straight and not direct else outs
-        parts = cut((plane,), cap, count, mirrored, place, asked, (sheet,))
-        return ship(parts, 1)[0]
+        parts = cut((plane,), cap, count, relays // count, mirrored, place, asked, (sheet,))
+        return ship(parts, 1, relays // count)[0]
+
+    def near_sent():
+        both = (sheets[0], beside)
+        parts = cut((0, PLANES), cap, chips // 2, 2, False, place, asked, both)
+        kinds = ship(parts, 2, 2)
+        return sum([mine for mine, _ in kinds], []), sum([other for _, other in kinds], [])
 
     index = lax.axis_index("sky").astype(jnp.int32)
     place = jnp.stack([index // relays, jnp.zeros_like(index) if direct else index % relays])
     tiles = tile_map.transpose(0, 2, 1)
-    requests = want(tiles, row_anchor, col_anchor, peers, cap)
+    requests = want(place, tiles, row_anchor, col_anchor, peers, cap, near)
     requests, late = lax.optimization_barrier((requests, gradients))
     sheets = [tile(0, gradients)] + [tile(plane, late) for plane in range(1, PLANES)]
     mirrors = [mirror(plane) for plane in range(PLANES)]
+    if near:
+        beside = lax.ppermute(sheets[0], "sky", swap(near))
     asked = exchange(requests)
     slots, *state = find_slots(place, tiles, (start_x, start_y), peers, cap, direct)
     own, far = [], []
     for plane in range(PLANES):
-        own.append(cut_sent(plane, False, sheets[plane]))
+        if near and plane == 0:
+            own.append(near_sent())
+        else:
+            own.append(cut_sent(plane, False, sheets[plane]))
         far.append(cut_sent(plane, True, mirrors[plane], plane == PLANES - 1))
     for plane in range(PLANES):
         sets = (own[plane], far[plane])

time: 108 us -> 133 us (1.23)
  waiting for transfers between devices: 51.7 us -> 72.6 us
  starting transfers between devices: 33.2 us -> 37.9 us
    ppermute x22 -> x20, waiting for transfers between devices: 51.7 us -> 70.8 us  [ship(): got.append(lax.ppermute(parts[m], 'sky', swap(step * m)))]
    ppermute x22 -> x20, starting transfers between devices: 21.6 us -> 25.3 us  [ship(): got.append(lax.ppermute(parts[m], 'sky', swap(step * m)))]
    ppermute x0 -> x1, starting transfers between devices: none -> 3.12 us  [body(): beside = lax.ppermute(sheets[0], 'sky', swap(near))]
    all_to_all x1, starting transfers between devices: 5.28 us -> 3.31 us  [exchange(): lax.all_to_all(x, 'sky', split_axis=0, concat_axis=0, axis_index_groups=g...]
    ppermute x3, waiting for transfers between devices: 0.01 us -> 1.71 us  [across(): got = lax.ppermute(jnp.concatenate(sum(lists, []), axis=0), 'sky', swap(1))]
  transfers between devices with their start and end apart: 29 -> 28, of which waited for: 13 -> 18; matrix products, arithmetic and copies ran while one was open for 2% -> 2% of each run, Pallas kernels for 7% -> 7%
where the time goes in v14:
time: 133 us
  waiting for transfers between devices  72.6 us (55%)
  starting transfers between devices  37.9 us (28%)
  Pallas kernels  18 us (14%)
  local copies, waits for them, and re-layouts  2.76 us (2%)
    ppermute x20, waiting for transfers between devices, ship(): got.append(lax.ppermute(parts[m], 'sky', swap(step * m)))  70.8 us
    ppermute x20, starting transfers between devices, ship(): got.append(lax.ppermute(parts[m], 'sky', swap(step * m)))  25.3 us
    pallas_call x3, Pallas kernels, interp(): pl.pallas_call(functools.partial(interp_kernel, plane), out_shape=out_sha...  8.98 us
    pallas_call x6, Pallas kernels, cut(): pl.pallas_call(functools.partial(cut_kernel, planes, cap, mirrored, span)...  6.34 us
    ppermute x3, starting transfers between devices, mirror(): return lax.ppermute(sheets[plane], 'sky', mirror_pairs)  5.58 us
    all_to_all x1, starting transfers between devices, exchange(): lax.all_to_all(x, 'sky', split_axis=0, concat_axis=0, axis_index_groups=g...  3.31 us
    ppermute x1, starting transfers between devices, body(): beside = lax.ppermute(sheets[0], 'sky', swap(near))  3.12 us
  transfers between devices with their start and end apart: 28, of which 18 were waited for; matrix products, arithmetic and copies ran while one was open for 2% of the time, Pallas kernels for 7%

profile of v14, /device:TPU:0, one launch (start us, length us, event | category | flops | bytes accessed | tf_op | source)
XLA Modules:
  0.0 132.9 jit_solution(1727754161996269650)
XLA Ops:
  1.6 3.1 %collective-permute-start.20 = (bf16[2,256,256]{2,1,0:T(8,128)(2,1)S(1)}, bf16[2,256,256]{2,1,0:T(8,128)(2,1)S(1)}, u32[]{:S(2)}, u32[]{:S(2)}) collective-permute-start(bf16[2,256,256]{2,1,0:T(8,128)(2,1)S(1)} %slice_bitcast_fusion.refs_0_), channel_id=1, source_target_pairs={{0,4},{1,5},{2,6},{3,7},{4,0},{5,1},{6,2},{7,3},{8,12},{9,13},{10,... | collective-permute-start | bytes 786440 | tf_op jit(solution)/shard_map/ppermute | solution.py:364
  4.7 2.6 %collective-permute-start.22 = (bf16[2,256,256]{2,1,0:T(8,128)(2,1)S(1)}, bf16[2,256,256]{2,1,0:T(8,128)(2,1)S(1)}, u32[]{:S(2)}, u32[]{:S(2)}) collective-permute-start(bf16[2,256,256]{2,1,0:T(8,128)(2,1)S(1)} %slice_bitcast_fusion.refs_0_), channel_id=1, source_target_pairs={{0,8},{1,9},{2,10},{3,11},{4,12},{5,13},{6,14},{7,15},{8,0},{9,1},... | collective-permute-start | bytes 786440 | tf_op jit(solution)/shard_map/ppermute | solution.py:343
  9.9 3.3 %all-to-all-start = ((s32[8,1,128]{2,1,0:T(1,128)}), s32[8,1,128]{2,1,0:T(1,128)S(1)}, u32[]{:S(2)}, u32[]{:S(2)}) async-start(s32[8,1,128]{2,1,0:T(1,128)} %bitcast.21), calls=%async_computation | async-start | bytes 8192 | tf_op jit(solution)/shard_map/all_to_all | solution.py:312
  14.7 2.6 %collective-permute-start.4 = (bf16[2,256,256]{2,1,0:T(8,128)(2,1)S(1)}, bf16[2,256,256]{2,1,0:T(8,128)(2,1)S(1)}, u32[]{:S(2)}, u32[]{:S(2)}) collective-permute-start(bf16[2,256,256]{2,1,0:T(8,128)(2,1)S(1)} %get-tuple-element.65.refs_0_), channel_id=1, source_target_pairs={{0,8},{1,9},{2,10},{3,11},{4,12},{5,13},{6,14},{7,15},{8,0},{9,1},... | collective-permute-start | bytes 786440 | tf_op jit(solution)/shard_map/ppermute | solution.py:343
  22.3 3.3 %collective-permute-done = bf16[16,32,128]{2,1,0:T(8,128)(2,1)S(1)} collective-permute-done((bf16[16,32,128]{2,1,0:T(8,128)(2,1)S(1)}, bf16[16,32,128]{2,1,0:T(8,128)(2,1)S(1)}, u32[]{:S(2)}, u32[]{:S(2)}) %collective-permute-start) | collective-permute-done | bytes 131104 | tf_op jit(solution)/shard_map/ppermute | solution.py:323
  27.5 3.9 %collective-permute-done.1 = bf16[16,32,128]{2,1,0:T(8,128)(2,1)S(1)} collective-permute-done((bf16[16,32,128]{2,1,0:T(8,128)(2,1)S(1)}, bf16[16,32,128]{2,1,0:T(8,128)(2,1)S(1)}, u32[]{:S(2)}, u32[]{:S(2)}) %collective-permute-start.1) | collective-permute-done | bytes 131104 | tf_op jit(solution)/shard_map/ppermute | solution.py:323
  33.5 12.0 %collective-permute-done.2 = bf16[16,32,128]{2,1,0:T(8,128)(2,1)S(1)} collective-permute-done((bf16[16,32,128]{2,1,0:T(8,128)(2,1)S(1)}, bf16[16,32,128]{2,1,0:T(8,128)(2,1)S(1)}, u32[]{:S(2)}, u32[]{:S(2)}) %collective-permute-start.2) | collective-permute-done | bytes 131104 | tf_op jit(solution)/shard_map/ppermute | solution.py:323
  45.4 3.8 %collective-permute-start.12 = (bf16[16,32,128]{2,1,0:T(8,128)(2,1)S(1)}, bf16[16,32,128]{2,1,0:T(8,128)(2,1)S(1)}, u32[]{:S(2)}, u32[]{:S(2)}) collective-permute-start(bf16[16,32,128]{2,1,0:T(8,128)(2,1)S(1)} %get-tuple-element.49), channel_id=1, source_target_pairs={{0,2},{1,3},{2,0},{3,1},{4,6},{5,7},{6,4},{7,5},{8,10},{9,11},{10,... | collective-permute-start | bytes 393224 | tf_op jit(solution)/shard_map/ppermute | solution.py:323
  49.2 2.9 %collective-permute-done.12 = bf16[16,32,128]{2,1,0:T(8,128)(2,1)S(1)} collective-permute-done((bf16[16,32,128]{2,1,0:T(8,128)(2,1)S(1)}, bf16[16,32,128]{2,1,0:T(8,128)(2,1)S(1)}, u32[]{:S(2)}, u32[]{:S(2)}) %collective-permute-start.12) | collective-permute-done | bytes 131104 | tf_op jit(solution)/shard_map/ppermute | solution.py:323
  52.8 5.2 %collective-permute-done.13 = bf16[16,32,128]{2,1,0:T(8,128)(2,1)S(1)} collective-permute-done((bf16[16,32,128]{2,1,0:T(8,128)(2,1)S(1)}, bf16[16,32,128]{2,1,0:T(8,128)(2,1)S(1)}, u32[]{:S(2)}, u32[]{:S(2)}) %collective-permute-start.13) | collective-permute-done | bytes 131104 | tf_op jit(solution)/shard_map/ppermute | solution.py:323
  59.8 4.0 %collective-permute-done.14 = bf16[16,32,128]{2,1,0:T(8,128)(2,1)S(1)} collective-permute-done((bf16[16,32,128]{2,1,0:T(8,128)(2,1)S(1)}, bf16[16,32,128]{2,1,0:T(8,128)(2,1)S(1)}, u32[]{:S(2)}, u32[]{:S(2)}) %collective-permute-start.14) | collective-permute-done | bytes 131104 | tf_op jit(solution)/shard_map/ppermute | solution.py:323
  64.9 2.1 %collective-permute-start.21 = (bf16[32,32,128]{2,1,0:T(8,128)(2,1)S(1)}, bf16[32,32,128]{2,1,0:T(8,128)(2,1)S(1)}, u32[]{:S(2)}, u32[]{:S(2)}) collective-permute-start(bf16[32,32,128]{2,1,0:T(8,128)(2,1)S(1)} %get-tuple-element.57), channel_id=1, source_target_pairs={{0,2},{1,3},{2,0},{3,1},{4,6},{5,7},{6,4},{7,5},{8,10},{9,11},{10,... | collective-permute-start | bytes 786440 | tf_op jit(solution)/shard_map/ppermute | solution.py:323
  72.7 7.0 %collective-permute-done.16 = bf16[16,32,128]{2,1,0:T(8,128)(2,1)S(1)} collective-permute-done((bf16[16,32,128]{2,1,0:T(8,128)(2,1)S(1)}, bf16[16,32,128]{2,1,0:T(8,128)(2,1)S(1)}, u32[]{:S(2)}, u32[]{:S(2)}) %collective-permute-start.16) | collective-permute-done | bytes 131104 | tf_op jit(solution)/shard_map/ppermute | solution.py:323
  80.4 4.7 %collective-permute-done.17 = bf16[16,32,128]{2,1,0:T(8,128)(2,1)S(1)} collective-permute-done((bf16[16,32,128]{2,1,0:T(8,128)(2,1)S(1)}, bf16[16,32,128]{2,1,0:T(8,128)(2,1)S(1)}, u32[]{:S(2)}, u32[]{:S(2)}) %collective-permute-start.17) | collective-permute-done | bytes 131104 | tf_op jit(solution)/shard_map/ppermute | solution.py:323
  86.2 4.7 %collective-permute-done.18 = bf16[16,32,128]{2,1,0:T(8,128)(2,1)S(1)} collective-permute-done((bf16[16,32,128]{2,1,0:T(8,128)(2,1)S(1)}, bf16[16,32,128]{2,1,0:T(8,128)(2,1)S(1)}, u32[]{:S(2)}, u32[]{:S(2)}) %collective-permute-start.18) | collective-permute-done | bytes 131104 | tf_op jit(solution)/shard_map/ppermute | solution.py:323
  92.9 4.5 %collective-permute-done.5 = bf16[8,32,128]{2,1,0:T(8,128)(2,1)S(1)} collective-permute-done((bf16[8,32,128]{2,1,0:T(8,128)(2,1)S(1)}, bf16[8,32,128]{2,1,0:T(8,128)(2,1)S(1)}, u32[]{:S(2)}, u32[]{:S(2)}) %collective-permute-start.5) | collective-permute-done | bytes 65568 | tf_op jit(solution)/shard_map/ppermute | solution.py:323
  98.2 3.5 %collective-permute-done.6 = bf16[8,32,128]{2,1,0:T(8,128)(2,1)S(1)} collective-permute-done((bf16[8,32,128]{2,1,0:T(8,128)(2,1)S(1)}, bf16[8,32,128]{2,1,0:T(8,128)(2,1)S(1)}, u32[]{:S(2)}, u32[]{:S(2)}) %collective-permute-start.6) | collective-permute-done | bytes 65568 | tf_op jit(solution)/shard_map/ppermute | solution.py:323
  102.9 3.9 %collective-permute-done.7 = bf16[8,32,128]{2,1,0:T(8,128)(2,1)S(1)} collective-permute-done((bf16[8,32,128]{2,1,0:T(8,128)(2,1)S(1)}, bf16[8,32,128]{2,1,0:T(8,128)(2,1)S(1)}, u32[]{:S(2)}, u32[]{:S(2)}) %collective-permute-start.7) | collective-permute-done | bytes 65568 | tf_op jit(solution)/shard_map/ppermute | solution.py:323
  109.2 2.9 %collective-permute-done.9 = bf16[8,32,128]{2,1,0:T(8,128)(2,1)S(1)} collective-permute-done((bf16[8,32,128]{2,1,0:T(8,128)(2,1)S(1)}, bf16[8,32,128]{2,1,0:T(8,128)(2,1)S(1)}, u32[]{:S(2)}, u32[]{:S(2)}) %collective-permute-start.9) | collective-permute-done | bytes 65568 | tf_op jit(solution)/shard_map/ppermute | solution.py:323
  112.8 3.4 %collective-permute-done.10 = bf16[8,32,128]{2,1,0:T(8,128)(2,1)S(1)} collective-permute-done((bf16[8,32,128]{2,1,0:T(8,128)(2,1)S(1)}, bf16[8,32,128]{2,1,0:T(8,128)(2,1)S(1)}, u32[]{:S(2)}, u32[]{:S(2)}) %collective-permute-start.10) | collective-permute-done | bytes 65568 | tf_op jit(solution)/shard_map/ppermute | solution.py:323
  117.2 3.9 %collective-permute-done.11 = bf16[8,32,128]{2,1,0:T(8,128)(2,1)S(1)} collective-permute-done((bf16[8,32,128]{2,1,0:T(8,128)(2,1)S(1)}, bf16[8,32,128]{2,1,0:T(8,128)(2,1)S(1)}, u32[]{:S(2)}, u32[]{:S(2)}) %collective-permute-start.11) | collective-permute-done | bytes 65568 | tf_op jit(solution)/shard_map/ppermute | solution.py:323
  123.9 2.7 %shard_map.77.refs_0_ = f32[12,64,128]{2,1,0:T(8,128)S(1)} custom-call(s32[3,64]{1,0:T(4,128)S(1)} %get-tuple-element.33.slot_ref, bf16[128,32,128]{2,1,0:T(8,128)(2,1)S(1)} %slice_dynamic-update-slice_fusion.win_ref, f32[64,128]{1,0:T(8,128)S(1)} %get-tuple-element.62.refs_0_, f32[64,128]{1,0:T(8,128)S(1)} %get-tuple-element.63.refs_1_), custom_call_target="tpu_custom_call" | custom-call | tf_op jit(solution)/shard_map/pallas_call | solution.py:283
  126.7 2.7 %shard_map.78.refs_0_ = f32[12,64,128]{2,1,0:T(8,128)S(1)} custom-call(s32[3,64]{1,0:T(4,128)S(1)} %get-tuple-element.33.slot_ref, bf16[128,32,128]{2,1,0:T(8,128)(2,1)S(1)} %slice_dynamic-update-slice_fusion.2.win_ref, f32[12,64,128]{2,1,0:T(8,128)S(1)} %shard_map.77.refs_0_), custom_call_target="tpu_custom_call" | custom-call | tf_op jit(solution)/shard_map/pallas_call | solution.py:283
  129.4 3.5 %shard_map.79 = (f32[64,2,128]{2,1,0:T(2,128)}, f32[64,4,128]{2,1,0:T(4,128)}) custom-call(s32[3,64]{1,0:T(4,128)S(1)} %get-tuple-element.33.slot_ref, bf16[128,32,128]{2,1,0:T(8,128)(2,1)S(1)} %constant_dynamic-update-slice_fusion.win_ref, f32[12,64,128]{2,1,0:T(8,128)S(1)} %shard_map.78.refs_0_), custom_call_target="tpu_custom_call" | custom-call | tf_op jit(solution)/shard_map/pallas_call | solution.py:283
  (96 shorter events, 35.8 us)
Async XLA Ops:
  1.6 62.2 %collective-permute-start.20 = (bf16[2,256,256]{2,1,0:T(8,128)(2,1)S(1)}, bf16[2,256,256]{2,1,0:T(8,128)(2,1)S(1)}, u32[]{:S(2)}, u32[]{:S(2)}) collective-permute-start(bf16[2,256,256]{2,1,0:T(8,128)(2,1)S(1)} %slice_bitcast_fusion.refs_0_), channel_id=1, source_target_pairs={{0,4},{1,5},{2,6},{3,7},{4,0},{5,1},{6,2},{7,3},{8,12},{9,13},{10,... | collective-permute-start | bytes 786440 | tf_op jit(solution)/shard_map/ppermute | solution.py:364
  4.7 62.4 %collective-permute-start.22 = (bf16[2,256,256]{2,1,0:T(8,128)(2,1)S(1)}, bf16[2,256,256]{2,1,0:T(8,128)(2,1)S(1)}, u32[]{:S(2)}, u32[]{:S(2)}) collective-permute-start(bf16[2,256,256]{2,1,0:T(8,128)(2,1)S(1)} %slice_bitcast_fusion.refs_0_), channel_id=1, source_target_pairs={{0,8},{1,9},{2,10},{3,11},{4,12},{5,13},{6,14},{7,15},{8,0},{9,1},... | collective-permute-start | bytes 786440 | tf_op jit(solution)/shard_map/ppermute | solution.py:343
  9.9 8.3 %all-to-all-start = ((s32[8,1,128]{2,1,0:T(1,128)}), s32[8,1,128]{2,1,0:T(1,128)S(1)}, u32[]{:S(2)}, u32[]{:S(2)}) async-start(s32[8,1,128]{2,1,0:T(1,128)} %bitcast.21), calls=%async_computation | async-start | bytes 8192 | tf_op jit(solution)/shard_map/all_to_all | solution.py:312
  14.3 54.0 %collective-permute-start.15 = (bf16[2,256,256]{2,1,0:T(8,128)(2,1)S(1)}, bf16[2,256,256]{2,1,0:T(8,128)(2,1)S(1)}, u32[]{:S(2)}, u32[]{:S(2)}) collective-permute-start(bf16[2,256,256]{2,1,0:T(8,128)(2,1)S(1)} %get-tuple-element.64.refs_0_), channel_id=1, source_target_pairs={{0,8},{1,9},{2,10},{3,11},{4,12},{5,13},{6,14},{7,15},{8,0},{9,1},... | collective-permute-start | bytes 786440 | tf_op jit(solution)/shard_map/ppermute | solution.py:343
  14.7 55.6 %collective-permute-start.4 = (bf16[2,256,256]{2,1,0:T(8,128)(2,1)S(1)}, bf16[2,256,256]{2,1,0:T(8,128)(2,1)S(1)}, u32[]{:S(2)}, u32[]{:S(2)}) collective-permute-start(bf16[2,256,256]{2,1,0:T(8,128)(2,1)S(1)} %get-tuple-element.65.refs_0_), channel_id=1, source_target_pairs={{0,8},{1,9},{2,10},{3,11},{4,12},{5,13},{6,14},{7,15},{8,0},{9,1},... | collective-permute-start | bytes 786440 | tf_op jit(solution)/shard_map/ppermute | solution.py:343
  20.3 5.3 %collective-permute-start = (bf16[16,32,128]{2,1,0:T(8,128)(2,1)S(1)}, bf16[16,32,128]{2,1,0:T(8,128)(2,1)S(1)}, u32[]{:S(2)}, u32[]{:S(2)}) collective-permute-start(bf16[16,32,128]{2,1,0:T(8,128)(2,1)S(1)} %get-tuple-element.37), channel_id=1, source_target_pairs={{0,2},{1,3},{2,0},{3,1},{4,6},{5,7},{6,4},{7,5},{8,10},{9,11},{10,... | collective-permute-start | bytes 393224 | tf_op jit(solution)/shard_map/ppermute | solution.py:323
  25.6 5.8 %collective-permute-start.1 = (bf16[16,32,128]{2,1,0:T(8,128)(2,1)S(1)}, bf16[16,32,128]{2,1,0:T(8,128)(2,1)S(1)}, u32[]{:S(2)}, u32[]{:S(2)}) collective-permute-start(bf16[16,32,128]{2,1,0:T(8,128)(2,1)S(1)} %get-tuple-element.38), channel_id=1, source_target_pairs={{0,4},{1,5},{2,6},{3,7},{4,0},{5,1},{6,2},{7,3},{8,12},{9,13},{10,... | collective-permute-start | bytes 393224 | tf_op jit(solution)/shard_map/ppermute | solution.py:323
  31.4 14.1 %collective-permute-start.2 = (bf16[16,32,128]{2,1,0:T(8,128)(2,1)S(1)}, bf16[16,32,128]{2,1,0:T(8,128)(2,1)S(1)}, u32[]{:S(2)}, u32[]{:S(2)}) collective-permute-start(bf16[16,32,128]{2,1,0:T(8,128)(2,1)S(1)} %get-tuple-element.39), channel_id=1, source_target_pairs={{0,6},{1,7},{2,4},{3,5},{4,2},{5,3},{6,0},{7,1},{8,14},{9,15},{10,... | collective-permute-start | bytes 393224 | tf_op jit(solution)/shard_map/ppermute | solution.py:323
  45.4 6.7 %collective-permute-start.12 = (bf16[16,32,128]{2,1,0:T(8,128)(2,1)S(1)}, bf16[16,32,128]{2,1,0:T(8,128)(2,1)S(1)}, u32[]{:S(2)}, u32[]{:S(2)}) collective-permute-start(bf16[16,32,128]{2,1,0:T(8,128)(2,1)S(1)} %get-tuple-element.49), channel_id=1, source_target_pairs={{0,2},{1,3},{2,0},{3,1},{4,6},{5,7},{6,4},{7,5},{8,10},{9,11},{10,... | collective-permute-start | bytes 393224 | tf_op jit(solution)/shard_map/ppermute | solution.py:323
  52.2 5.8 %collective-permute-start.13 = (bf16[16,32,128]{2,1,0:T(8,128)(2,1)S(1)}, bf16[16,32,128]{2,1,0:T(8,128)(2,1)S(1)}, u32[]{:S(2)}, u32[]{:S(2)}) collective-permute-start(bf16[16,32,128]{2,1,0:T(8,128)(2,1)S(1)} %get-tuple-element.50), channel_id=1, source_target_pairs={{0,4},{1,5},{2,6},{3,7},{4,0},{5,1},{6,2},{7,3},{8,12},{9,13},{10,... | collective-permute-start | bytes 393224 | tf_op jit(solution)/shard_map/ppermute | solution.py:323
  57.9 5.9 %collective-permute-start.14 = (bf16[16,32,128]{2,1,0:T(8,128)(2,1)S(1)}, bf16[16,32,128]{2,1,0:T(8,128)(2,1)S(1)}, u32[]{:S(2)}, u32[]{:S(2)}) collective-permute-start(bf16[16,32,128]{2,1,0:T(8,128)(2,1)S(1)} %get-tuple-element.51), channel_id=1, source_target_pairs={{0,6},{1,7},{2,4},{3,5},{4,2},{5,3},{6,0},{7,1},{8,14},{9,15},{10,... | collective-permute-start | bytes 393224 | tf_op jit(solution)/shard_map/ppermute | solution.py:323
  63.8 28.3 %collective-permute-start.3 = (bf16[32,32,128]{2,1,0:T(8,128)(2,1)S(1)}, bf16[32,32,128]{2,1,0:T(8,128)(2,1)S(1)}, u32[]{:S(2)}, u32[]{:S(2)}) collective-permute-start(bf16[32,32,128]{2,1,0:T(8,128)(2,1)S(1)} %pad_maximum_fusion), channel_id=1, source_target_pairs={{0,1},{1,0},{2,3},{3,2},{4,5},{5,4},{6,7},{7,6},{8,9},{9,8},{10,11... | collective-permute-start | bytes 786440 | tf_op jit(solution)/shard_map/ppermute | solution.py:335
  64.9 56.4 %collective-permute-start.21 = (bf16[32,32,128]{2,1,0:T(8,128)(2,1)S(1)}, bf16[32,32,128]{2,1,0:T(8,128)(2,1)S(1)}, u32[]{:S(2)}, u32[]{:S(2)}) collective-permute-start(bf16[32,32,128]{2,1,0:T(8,128)(2,1)S(1)} %get-tuple-element.57), channel_id=1, source_target_pairs={{0,2},{1,3},{2,0},{3,1},{4,6},{5,7},{6,4},{7,5},{8,10},{9,11},{10,... | collective-permute-start | bytes 786440 | tf_op jit(solution)/shard_map/ppermute | solution.py:323
  68.2 53.3 %collective-permute-start.23 = (bf16[16,32,128]{2,1,0:T(8,128)(2,1)S(1)}, bf16[16,32,128]{2,1,0:T(8,128)(2,1)S(1)}, u32[]{:S(2)}, u32[]{:S(2)}) collective-permute-start(bf16[16,32,128]{2,1,0:T(8,128)(2,1)S(1)} %get-tuple-element.59), channel_id=1, source_target_pairs={{0,2},{1,3},{2,0},{3,1},{4,6},{5,7},{6,4},{7,5},{8,10},{9,11},{10,... | collective-permute-start | bytes 393224 | tf_op jit(solution)/shard_map/ppermute | solution.py:323
  68.2 53.2 %collective-permute-start.24 = (bf16[16,32,128]{2,1,0:T(8,128)(2,1)S(1)}, bf16[16,32,128]{2,1,0:T(8,128)(2,1)S(1)}, u32[]{:S(2)}, u32[]{:S(2)}) collective-permute-start(bf16[16,32,128]{2,1,0:T(8,128)(2,1)S(1)} %get-tuple-element.60), channel_id=1, source_target_pairs={{0,4},{1,5},{2,6},{3,7},{4,0},{5,1},{6,2},{7,3},{8,12},{9,13},{10,... | collective-permute-start | bytes 393224 | tf_op jit(solution)/shard_map/ppermute | solution.py:323
  70.3 9.4 %collective-permute-start.16 = (bf16[16,32,128]{2,1,0:T(8,128)(2,1)S(1)}, bf16[16,32,128]{2,1,0:T(8,128)(2,1)S(1)}, u32[]{:S(2)}, u32[]{:S(2)}) collective-permute-start(bf16[16,32,128]{2,1,0:T(8,128)(2,1)S(1)} %get-tuple-element.53), channel_id=1, source_target_pairs={{0,2},{1,3},{2,0},{3,1},{4,6},{5,7},{6,4},{7,5},{8,10},{9,11},{10,... | collective-permute-start | bytes 393224 | tf_op jit(solution)/shard_map/ppermute | solution.py:323
  79.7 5.3 %collective-permute-start.17 = (bf16[16,32,128]{2,1,0:T(8,128)(2,1)S(1)}, bf16[16,32,128]{2,1,0:T(8,128)(2,1)S(1)}, u32[]{:S(2)}, u32[]{:S(2)}) collective-permute-start(bf16[16,32,128]{2,1,0:T(8,128)(2,1)S(1)} %get-tuple-element.54), channel_id=1, source_target_pairs={{0,4},{1,5},{2,6},{3,7},{4,0},{5,1},{6,2},{7,3},{8,12},{9,13},{10,... | collective-permute-start | bytes 393224 | tf_op jit(solution)/shard_map/ppermute | solution.py:323
  85.0 5.9 %collective-permute-start.18 = (bf16[16,32,128]{2,1,0:T(8,128)(2,1)S(1)}, bf16[16,32,128]{2,1,0:T(8,128)(2,1)S(1)}, u32[]{:S(2)}, u32[]{:S(2)}) collective-permute-start(bf16[16,32,128]{2,1,0:T(8,128)(2,1)S(1)} %get-tuple-element.55), channel_id=1, source_target_pairs={{0,6},{1,7},{2,4},{3,5},{4,2},{5,3},{6,0},{7,1},{8,14},{9,15},{10,... | collective-permute-start | bytes 393224 | tf_op jit(solution)/shard_map/ppermute | solution.py:323
  90.9 30.6 %collective-permute-start.25 = (bf16[16,32,128]{2,1,0:T(8,128)(2,1)S(1)}, bf16[16,32,128]{2,1,0:T(8,128)(2,1)S(1)}, u32[]{:S(2)}, u32[]{:S(2)}) collective-permute-start(bf16[16,32,128]{2,1,0:T(8,128)(2,1)S(1)} %get-tuple-element.61), channel_id=1, source_target_pairs={{0,6},{1,7},{2,4},{3,5},{4,2},{5,3},{6,0},{7,1},{8,14},{9,15},{10,... | collective-permute-start | bytes 393224 | tf_op jit(solution)/shard_map/ppermute | solution.py:323
  92.1 5.3 %collective-permute-start.5 = (bf16[8,32,128]{2,1,0:T(8,128)(2,1)S(1)}, bf16[8,32,128]{2,1,0:T(8,128)(2,1)S(1)}, u32[]{:S(2)}, u32[]{:S(2)}) collective-permute-start(bf16[8,32,128]{2,1,0:T(8,128)(2,1)S(1)} %get-tuple-element.41), channel_id=1, source_target_pairs={{0,2},{1,3},{2,0},{3,1},{4,6},{5,7},{6,4},{7,5},{8,10},{9,11},{10,... | collective-permute-start | bytes 196616 | tf_op jit(solution)/shard_map/ppermute | solution.py:323
  97.4 4.3 %collective-permute-start.6 = (bf16[8,32,128]{2,1,0:T(8,128)(2,1)S(1)}, bf16[8,32,128]{2,1,0:T(8,128)(2,1)S(1)}, u32[]{:S(2)}, u32[]{:S(2)}) collective-permute-start(bf16[8,32,128]{2,1,0:T(8,128)(2,1)S(1)} %get-tuple-element.42), channel_id=1, source_target_pairs={{0,4},{1,5},{2,6},{3,7},{4,0},{5,1},{6,2},{7,3},{8,12},{9,13},{10,... | collective-permute-start | bytes 196616 | tf_op jit(solution)/shard_map/ppermute | solution.py:323
  101.6 5.2 %collective-permute-start.7 = (bf16[8,32,128]{2,1,0:T(8,128)(2,1)S(1)}, bf16[8,32,128]{2,1,0:T(8,128)(2,1)S(1)}, u32[]{:S(2)}, u32[]{:S(2)}) collective-permute-start(bf16[8,32,128]{2,1,0:T(8,128)(2,1)S(1)} %get-tuple-element.43), channel_id=1, source_target_pairs={{0,6},{1,7},{2,4},{3,5},{4,2},{5,3},{6,0},{7,1},{8,14},{9,15},{10,... | collective-permute-start | bytes 196616 | tf_op jit(solution)/shard_map/ppermute | solution.py:323
  108.1 4.1 %collective-permute-start.9 = (bf16[8,32,128]{2,1,0:T(8,128)(2,1)S(1)}, bf16[8,32,128]{2,1,0:T(8,128)(2,1)S(1)}, u32[]{:S(2)}, u32[]{:S(2)}) collective-permute-start(bf16[8,32,128]{2,1,0:T(8,128)(2,1)S(1)} %get-tuple-element.45), channel_id=1, source_target_pairs={{0,3},{1,2},{2,1},{3,0},{4,7},{5,6},{6,5},{7,4},{8,11},{9,10},{10,... | collective-permute-start | bytes 196616 | tf_op jit(solution)/shard_map/ppermute | solution.py:323
  116.2 5.0 %collective-permute-start.11 = (bf16[8,32,128]{2,1,0:T(8,128)(2,1)S(1)}, bf16[8,32,128]{2,1,0:T(8,128)(2,1)S(1)}, u32[]{:S(2)}, u32[]{:S(2)}) collective-permute-start(bf16[8,32,128]{2,1,0:T(8,128)(2,1)S(1)} %get-tuple-element.47), channel_id=1, source_target_pairs={{0,7},{1,6},{2,5},{3,4},{4,3},{5,2},{6,1},{7,0},{8,15},{9,14},{10,... | collective-permute-start | bytes 196616 | tf_op jit(solution)/shard_map/ppermute | solution.py:323
  (8 other events, 23.8 us)

commit v15 on v14

--- a/solution.py
+++ b/solution.py
@@ -28,6 +28,10 @@
     return lax.dot_general(
         a, b, (((1,), (1,)), ((), ())), preferred_element_type=jnp.float32
     )
+
+
+def spot(place_ref, relays, direct=False):
+    return lax.div(place_ref[0], relays), 0 if direct else lax.rem(place_ref[0], relays)
 
 
 def ranks(peers, tile_ref, plane):
@@ -54,7 +58,8 @@
         relay = tile - side * relays
         group = side + 2 * k
         if near and k == 0:
-            turn = ((relay ^ place_ref[1]) & near) * (side == place_ref[0]).astype(jnp.int32)
+            half, me = spot(place_ref, relays)
+            turn = ((relay ^ me) & near) * (side == half).astype(jnp.int32)
             relay = relay ^ turn
             group = jnp.where(turn != 0, 2 * PLANES + side, group)
         here = lane == (rank + group * cap)
@@ -88,13 +93,14 @@
     for move in moves:
         move.start()
     relays = peers // 2
+    half, me = spot(place_ref, relays, direct)
     for k in range(PLANES):
         tile, _, rank = ranks(peers, tile_ref, k)
         side = tile // relays
-        relay = (tile - side * relays) ^ place_ref[1]
+        relay = (tile - side * relays) ^ me
         if not direct:
             relay = (relay & 1) * (relays // 2) + (relay >> 1)
-        far = (side != place_ref[0]).astype(jnp.int32)
+        far = (side != half).astype(jnp.int32)
         slot_ref[k : k + 1, :] = (far * relays + relay) * cap + rank
     for move in moves:
         move.wait()
@@ -123,8 +129,8 @@
                 part = sheet_ref[c, :, h * WC : (h + 1) * WC]
                 half_ref[(at * 2 + c) * parts + h] = part.astype(jnp.float32)
     lane = lax.broadcasted_iota(jnp.int32, (WR, WC), 1)
-    me = place_ref[1]
-    side = 1 - place_ref[0] if mirrored else place_ref[0]
+    half, me = spot(place_ref, req_ref.shape[0], len(out_refs) == 1)
+    side = 1 - half if mirrored else half
 
     def one(now, carry):
         for m, out_ref in enumerate(out_refs):
@@ -354,7 +360,7 @@
         return sum([mine for mine, _ in kinds], []), sum([other for _, other in kinds], [])
 
     index = lax.axis_index("sky").astype(jnp.int32)
-    place = jnp.stack([index // relays, jnp.zeros_like(index) if direct else index % relays])
+    place = index.reshape(1)
     tiles = tile_map.transpose(0, 2, 1)
     requests = want(place, tiles, row_anchor, col_anchor, peers, cap, near)
     requests, late = lax.optimization_barrier((requests, gradients))

time: 133 us -> 134 us (level)
  waiting for transfers between devices: 72.6 us -> 87 us
  starting transfers between devices: 37.9 us -> 25.4 us
    ppermute x20, waiting for transfers between devices: 70.8 us -> 84.5 us  [ship(): got.append(lax.ppermute(parts[m], 'sky', swap(step * m)))]
    ppermute x20, starting transfers between devices: 25.3 us -> 12.8 us  [ship(): got.append(lax.ppermute(parts[m], 'sky', swap(step * m)))]
  transfers between devices with their start and end apart: 28 -> 28, of which waited for: 18 -> 19; matrix products, arithmetic and copies ran while one was open for 2% -> 1% of each run, Pallas kernels for 7% -> 6%
where the time goes in v15:
time: 134 us
  waiting for transfers between devices  87 us (65%)
  starting transfers between devices  25.4 us (19%)
  Pallas kernels  17.4 us (13%)
  local copies, waits for them, and re-layouts  2.76 us (2%)
    ppermute x20, waiting for transfers between devices, ship(): got.append(lax.ppermute(parts[m], 'sky', swap(step * m)))  84.5 us
    ppermute x20, starting transfers between devices, ship(): got.append(lax.ppermute(parts[m], 'sky', swap(step * m)))  12.8 us
    pallas_call x3, Pallas kernels, interp(): pl.pallas_call(functools.partial(interp_kernel, plane), out_shape=out_sha...  8.98 us
    pallas_call x6, Pallas kernels, cut(): pl.pallas_call(functools.partial(cut_kernel, planes, cap, mirrored, span)...  6.33 us
    ppermute x3, starting transfers between devices, mirror(): return lax.ppermute(sheets[plane], 'sky', mirror_pairs)  5.58 us
    all_to_all x1, starting transfers between devices, exchange(): lax.all_to_all(x, 'sky', split_axis=0, concat_axis=0, axis_index_groups=g...  3.31 us
    ppermute x1, starting transfers between devices, body(): beside = lax.ppermute(sheets[0], 'sky', swap(near))  3.12 us
  transfers between devices with their start and end apart: 28, of which 19 were waited for; matrix products, arithmetic and copies ran while one was open for 1% of the time, Pallas kernels for 6%

profile of v15, /device:TPU:0, one launch (start us, length us, event | category | flops | bytes accessed | tf_op | source)
XLA Modules:
  0.0 133.6 jit_solution(2771170563447064681)
XLA Ops:
  1.6 3.1 %collective-permute-start.20 = (bf16[2,256,256]{2,1,0:T(8,128)(2,1)S(1)}, bf16[2,256,256]{2,1,0:T(8,128)(2,1)S(1)}, u32[]{:S(2)}, u32[]{:S(2)}) collective-permute-start(bf16[2,256,256]{2,1,0:T(8,128)(2,1)S(1)} %slice_bitcast_fusion.refs_0_), channel_id=1, source_target_pairs={{0,4},{1,5},{2,6},{3,7},{4,0},{5,1},{6,2},{7,3},{8,12},{9,13},{10,... | collective-permute-start | bytes 786440 | tf_op jit(solution)/shard_map/ppermute | solution.py:370
  4.7 2.6 %collective-permute-start.22 = (bf16[2,256,256]{2,1,0:T(8,128)(2,1)S(1)}, bf16[2,256,256]{2,1,0:T(8,128)(2,1)S(1)}, u32[]{:S(2)}, u32[]{:S(2)}) collective-permute-start(bf16[2,256,256]{2,1,0:T(8,128)(2,1)S(1)} %slice_bitcast_fusion.refs_0_), channel_id=1, source_target_pairs={{0,8},{1,9},{2,10},{3,11},{4,12},{5,13},{6,14},{7,15},{8,0},{9,1},... | collective-permute-start | bytes 786440 | tf_op jit(solution)/shard_map/ppermute | solution.py:349
  9.1 3.3 %all-to-all-start = ((s32[8,1,128]{2,1,0:T(1,128)}), s32[8,1,128]{2,1,0:T(1,128)S(1)}, u32[]{:S(2)}, u32[]{:S(2)}) async-start(s32[8,1,128]{2,1,0:T(1,128)} %bitcast.20), calls=%async_computation | async-start | bytes 8192 | tf_op jit(solution)/shard_map/all_to_all | solution.py:318
  14.0 2.6 %collective-permute-start.4 = (bf16[2,256,256]{2,1,0:T(8,128)(2,1)S(1)}, bf16[2,256,256]{2,1,0:T(8,128)(2,1)S(1)}, u32[]{:S(2)}, u32[]{:S(2)}) collective-permute-start(bf16[2,256,256]{2,1,0:T(8,128)(2,1)S(1)} %get-tuple-element.65.refs_0_), channel_id=1, source_target_pairs={{0,8},{1,9},{2,10},{3,11},{4,12},{5,13},{6,14},{7,15},{8,0},{9,1},... | collective-permute-start | bytes 786440 | tf_op jit(solution)/shard_map/ppermute | solution.py:349
  21.0 4.4 %collective-permute-done = bf16[16,32,128]{2,1,0:T(8,128)(2,1)S(1)} collective-permute-done((bf16[16,32,128]{2,1,0:T(8,128)(2,1)S(1)}, bf16[16,32,128]{2,1,0:T(8,128)(2,1)S(1)}, u32[]{:S(2)}, u32[]{:S(2)}) %collective-permute-start) | collective-permute-done | bytes 131104 | tf_op jit(solution)/shard_map/ppermute | solution.py:329
  25.4 2.9 %collective-permute-start.1 = (bf16[16,32,128]{2,1,0:T(8,128)(2,1)S(1)}, bf16[16,32,128]{2,1,0:T(8,128)(2,1)S(1)}, u32[]{:S(2)}, u32[]{:S(2)}) collective-permute-start(bf16[16,32,128]{2,1,0:T(8,128)(2,1)S(1)} %get-tuple-element.38), channel_id=1, source_target_pairs={{0,4},{1,5},{2,6},{3,7},{4,0},{5,1},{6,2},{7,3},{8,12},{9,13},{10,... | collective-permute-start | bytes 393224 | tf_op jit(solution)/shard_map/ppermute | solution.py:329
  28.3 15.2 %collective-permute-done.1 = bf16[16,32,128]{2,1,0:T(8,128)(2,1)S(1)} collective-permute-done((bf16[16,32,128]{2,1,0:T(8,128)(2,1)S(1)}, bf16[16,32,128]{2,1,0:T(8,128)(2,1)S(1)}, u32[]{:S(2)}, u32[]{:S(2)}) %collective-permute-start.1) | collective-permute-done | bytes 131104 | tf_op jit(solution)/shard_map/ppermute | solution.py:329
  43.5 5.8 %collective-permute-done.2 = bf16[16,32,128]{2,1,0:T(8,128)(2,1)S(1)} collective-permute-done((bf16[16,32,128]{2,1,0:T(8,128)(2,1)S(1)}, bf16[16,32,128]{2,1,0:T(8,128)(2,1)S(1)}, u32[]{:S(2)}, u32[]{:S(2)}) %collective-permute-start.2) | collective-permute-done | bytes 131104 | tf_op jit(solution)/shard_map/ppermute | solution.py:329
  49.4 4.9 %collective-permute-done.12 = bf16[16,32,128]{2,1,0:T(8,128)(2,1)S(1)} collective-permute-done((bf16[16,32,128]{2,1,0:T(8,128)(2,1)S(1)}, bf16[16,32,128]{2,1,0:T(8,128)(2,1)S(1)}, u32[]{:S(2)}, u32[]{:S(2)}) %collective-permute-start.12) | collective-permute-done | bytes 131104 | tf_op jit(solution)/shard_map/ppermute | solution.py:329
  54.4 4.9 %collective-permute-done.13 = bf16[16,32,128]{2,1,0:T(8,128)(2,1)S(1)} collective-permute-done((bf16[16,32,128]{2,1,0:T(8,128)(2,1)S(1)}, bf16[16,32,128]{2,1,0:T(8,128)(2,1)S(1)}, u32[]{:S(2)}, u32[]{:S(2)}) %collective-permute-start.13) | collective-permute-done | bytes 131104 | tf_op jit(solution)/shard_map/ppermute | solution.py:329
  59.6 5.6 %collective-permute-done.14 = bf16[16,32,128]{2,1,0:T(8,128)(2,1)S(1)} collective-permute-done((bf16[16,32,128]{2,1,0:T(8,128)(2,1)S(1)}, bf16[16,32,128]{2,1,0:T(8,128)(2,1)S(1)}, u32[]{:S(2)}, u32[]{:S(2)}) %collective-permute-start.14) | collective-permute-done | bytes 131104 | tf_op jit(solution)/shard_map/ppermute | solution.py:329
  67.5 2.1 %collective-permute-start.23 = (bf16[16,32,128]{2,1,0:T(8,128)(2,1)S(1)}, bf16[16,32,128]{2,1,0:T(8,128)(2,1)S(1)}, u32[]{:S(2)}, u32[]{:S(2)}) collective-permute-start(bf16[16,32,128]{2,1,0:T(8,128)(2,1)S(1)} %get-tuple-element.59), channel_id=1, source_target_pairs={{0,2},{1,3},{2,0},{3,1},{4,6},{5,7},{6,4},{7,5},{8,10},{9,11},{10,... | collective-permute-start | bytes 393224 | tf_op jit(solution)/shard_map/ppermute | solution.py:329
  72.5 8.3 %collective-permute-done.16 = bf16[16,32,128]{2,1,0:T(8,128)(2,1)S(1)} collective-permute-done((bf16[16,32,128]{2,1,0:T(8,128)(2,1)S(1)}, bf16[16,32,128]{2,1,0:T(8,128)(2,1)S(1)}, u32[]{:S(2)}, u32[]{:S(2)}) %collective-permute-start.16) | collective-permute-done | bytes 131104 | tf_op jit(solution)/shard_map/ppermute | solution.py:329
  80.9 4.9 %collective-permute-done.17 = bf16[16,32,128]{2,1,0:T(8,128)(2,1)S(1)} collective-permute-done((bf16[16,32,128]{2,1,0:T(8,128)(2,1)S(1)}, bf16[16,32,128]{2,1,0:T(8,128)(2,1)S(1)}, u32[]{:S(2)}, u32[]{:S(2)}) %collective-permute-start.17) | collective-permute-done | bytes 131104 | tf_op jit(solution)/shard_map/ppermute | solution.py:329
  86.1 5.6 %collective-permute-done.18 = bf16[16,32,128]{2,1,0:T(8,128)(2,1)S(1)} collective-permute-done((bf16[16,32,128]{2,1,0:T(8,128)(2,1)S(1)}, bf16[16,32,128]{2,1,0:T(8,128)(2,1)S(1)}, u32[]{:S(2)}, u32[]{:S(2)}) %collective-permute-start.18) | collective-permute-done | bytes 131104 | tf_op jit(solution)/shard_map/ppermute | solution.py:329
  93.5 4.2 %collective-permute-done.5 = bf16[8,32,128]{2,1,0:T(8,128)(2,1)S(1)} collective-permute-done((bf16[8,32,128]{2,1,0:T(8,128)(2,1)S(1)}, bf16[8,32,128]{2,1,0:T(8,128)(2,1)S(1)}, u32[]{:S(2)}, u32[]{:S(2)}) %collective-permute-start.5) | collective-permute-done | bytes 65568 | tf_op jit(solution)/shard_map/ppermute | solution.py:329
  98.5 3.8 %collective-permute-done.6 = bf16[8,32,128]{2,1,0:T(8,128)(2,1)S(1)} collective-permute-done((bf16[8,32,128]{2,1,0:T(8,128)(2,1)S(1)}, bf16[8,32,128]{2,1,0:T(8,128)(2,1)S(1)}, u32[]{:S(2)}, u32[]{:S(2)}) %collective-permute-start.6) | collective-permute-done | bytes 65568 | tf_op jit(solution)/shard_map/ppermute | solution.py:329
  103.4 4.1 %collective-permute-done.7 = bf16[8,32,128]{2,1,0:T(8,128)(2,1)S(1)} collective-permute-done((bf16[8,32,128]{2,1,0:T(8,128)(2,1)S(1)}, bf16[8,32,128]{2,1,0:T(8,128)(2,1)S(1)}, u32[]{:S(2)}, u32[]{:S(2)}) %collective-permute-start.7) | collective-permute-done | bytes 65568 | tf_op jit(solution)/shard_map/ppermute | solution.py:329
  109.2 3.6 %collective-permute-done.9 = bf16[8,32,128]{2,1,0:T(8,128)(2,1)S(1)} collective-permute-done((bf16[8,32,128]{2,1,0:T(8,128)(2,1)S(1)}, bf16[8,32,128]{2,1,0:T(8,128)(2,1)S(1)}, u32[]{:S(2)}, u32[]{:S(2)}) %collective-permute-start.9) | collective-permute-done | bytes 65568 | tf_op jit(solution)/shard_map/ppermute | solution.py:329
  113.0 3.8 %collective-permute-done.10 = bf16[8,32,128]{2,1,0:T(8,128)(2,1)S(1)} collective-permute-done((bf16[8,32,128]{2,1,0:T(8,128)(2,1)S(1)}, bf16[8,32,128]{2,1,0:T(8,128)(2,1)S(1)}, u32[]{:S(2)}, u32[]{:S(2)}) %collective-permute-start.10) | collective-permute-done | bytes 65568 | tf_op jit(solution)/shard_map/ppermute | solution.py:329
  117.7 4.1 %collective-permute-done.11 = bf16[8,32,128]{2,1,0:T(8,128)(2,1)S(1)} collective-permute-done((bf16[8,32,128]{2,1,0:T(8,128)(2,1)S(1)}, bf16[8,32,128]{2,1,0:T(8,128)(2,1)S(1)}, u32[]{:S(2)}, u32[]{:S(2)}) %collective-permute-start.11) | collective-permute-done | bytes 65568 | tf_op jit(solution)/shard_map/ppermute | solution.py:329
  124.6 2.7 %shard_map.77.refs_0_ = f32[12,64,128]{2,1,0:T(8,128)S(1)} custom-call(s32[3,64]{1,0:T(4,128)S(1)} %get-tuple-element.33.slot_ref, bf16[128,32,128]{2,1,0:T(8,128)(2,1)S(1)} %slice_dynamic-update-slice_fusion.win_ref, f32[64,128]{1,0:T(8,128)S(1)} %get-tuple-element.62.refs_0_, f32[64,128]{1,0:T(8,128)S(1)} %get-tuple-element.63.refs_1_), custom_call_target="tpu_custom_call" | custom-call | tf_op jit(solution)/shard_map/pallas_call | solution.py:289
  127.4 2.7 %shard_map.78.refs_0_ = f32[12,64,128]{2,1,0:T(8,128)S(1)} custom-call(s32[3,64]{1,0:T(4,128)S(1)} %get-tuple-element.33.slot_ref, bf16[128,32,128]{2,1,0:T(8,128)(2,1)S(1)} %slice_dynamic-update-slice_fusion.2.win_ref, f32[12,64,128]{2,1,0:T(8,128)S(1)} %shard_map.77.refs_0_), custom_call_target="tpu_custom_call" | custom-call | tf_op jit(solution)/shard_map/pallas_call | solution.py:289
  130.1 3.5 %shard_map.79 = (f32[64,2,128]{2,1,0:T(2,128)}, f32[64,4,128]{2,1,0:T(4,128)}) custom-call(s32[3,64]{1,0:T(4,128)S(1)} %get-tuple-element.33.slot_ref, bf16[128,32,128]{2,1,0:T(8,128)(2,1)S(1)} %constant_dynamic-update-slice_fusion.win_ref, f32[12,64,128]{2,1,0:T(8,128)S(1)} %shard_map.78.refs_0_), custom_call_target="tpu_custom_call" | custom-call | tf_op jit(solution)/shard_map/pallas_call | solution.py:289
  (93 shorter events, 23.9 us)
Async XLA Ops:
  1.6 63.6 %collective-permute-start.20 = (bf16[2,256,256]{2,1,0:T(8,128)(2,1)S(1)}, bf16[2,256,256]{2,1,0:T(8,128)(2,1)S(1)}, u32[]{:S(2)}, u32[]{:S(2)}) collective-permute-start(bf16[2,256,256]{2,1,0:T(8,128)(2,1)S(1)} %slice_bitcast_fusion.refs_0_), channel_id=1, source_target_pairs={{0,4},{1,5},{2,6},{3,7},{4,0},{5,1},{6,2},{7,3},{8,12},{9,13},{10,... | collective-permute-start | bytes 786440 | tf_op jit(solution)/shard_map/ppermute | solution.py:370
  4.7 61.7 %collective-permute-start.22 = (bf16[2,256,256]{2,1,0:T(8,128)(2,1)S(1)}, bf16[2,256,256]{2,1,0:T(8,128)(2,1)S(1)}, u32[]{:S(2)}, u32[]{:S(2)}) collective-permute-start(bf16[2,256,256]{2,1,0:T(8,128)(2,1)S(1)} %slice_bitcast_fusion.refs_0_), channel_id=1, source_target_pairs={{0,8},{1,9},{2,10},{3,11},{4,12},{5,13},{6,14},{7,15},{8,0},{9,1},... | collective-permute-start | bytes 786440 | tf_op jit(solution)/shard_map/ppermute | solution.py:349
  9.1 8.5 %all-to-all-start = ((s32[8,1,128]{2,1,0:T(1,128)}), s32[8,1,128]{2,1,0:T(1,128)S(1)}, u32[]{:S(2)}, u32[]{:S(2)}) async-start(s32[8,1,128]{2,1,0:T(1,128)} %bitcast.20), calls=%async_computation | async-start | bytes 8192 | tf_op jit(solution)/shard_map/all_to_all | solution.py:318
  13.6 56.0 %collective-permute-start.15 = (bf16[2,256,256]{2,1,0:T(8,128)(2,1)S(1)}, bf16[2,256,256]{2,1,0:T(8,128)(2,1)S(1)}, u32[]{:S(2)}, u32[]{:S(2)}) collective-permute-start(bf16[2,256,256]{2,1,0:T(8,128)(2,1)S(1)} %get-tuple-element.64.refs_0_), channel_id=1, source_target_pairs={{0,8},{1,9},{2,10},{3,11},{4,12},{5,13},{6,14},{7,15},{8,0},{9,1},... | collective-permute-start | bytes 786440 | tf_op jit(solution)/shard_map/ppermute | solution.py:349
  14.0 56.9 %collective-permute-start.4 = (bf16[2,256,256]{2,1,0:T(8,128)(2,1)S(1)}, bf16[2,256,256]{2,1,0:T(8,128)(2,1)S(1)}, u32[]{:S(2)}, u32[]{:S(2)}) collective-permute-start(bf16[2,256,256]{2,1,0:T(8,128)(2,1)S(1)} %get-tuple-element.65.refs_0_), channel_id=1, source_target_pairs={{0,8},{1,9},{2,10},{3,11},{4,12},{5,13},{6,14},{7,15},{8,0},{9,1},... | collective-permute-start | bytes 786440 | tf_op jit(solution)/shard_map/ppermute | solution.py:349
  19.8 5.6 %collective-permute-start = (bf16[16,32,128]{2,1,0:T(8,128)(2,1)S(1)}, bf16[16,32,128]{2,1,0:T(8,128)(2,1)S(1)}, u32[]{:S(2)}, u32[]{:S(2)}) collective-permute-start(bf16[16,32,128]{2,1,0:T(8,128)(2,1)S(1)} %get-tuple-element.37), channel_id=1, source_target_pairs={{0,2},{1,3},{2,0},{3,1},{4,6},{5,7},{6,4},{7,5},{8,10},{9,11},{10,... | collective-permute-start | bytes 393224 | tf_op jit(solution)/shard_map/ppermute | solution.py:329
  25.4 18.1 %collective-permute-start.1 = (bf16[16,32,128]{2,1,0:T(8,128)(2,1)S(1)}, bf16[16,32,128]{2,1,0:T(8,128)(2,1)S(1)}, u32[]{:S(2)}, u32[]{:S(2)}) collective-permute-start(bf16[16,32,128]{2,1,0:T(8,128)(2,1)S(1)} %get-tuple-element.38), channel_id=1, source_target_pairs={{0,4},{1,5},{2,6},{3,7},{4,0},{5,1},{6,2},{7,3},{8,12},{9,13},{10,... | collective-permute-start | bytes 393224 | tf_op jit(solution)/shard_map/ppermute | solution.py:329
  43.5 5.9 %collective-permute-start.2 = (bf16[16,32,128]{2,1,0:T(8,128)(2,1)S(1)}, bf16[16,32,128]{2,1,0:T(8,128)(2,1)S(1)}, u32[]{:S(2)}, u32[]{:S(2)}) collective-permute-start(bf16[16,32,128]{2,1,0:T(8,128)(2,1)S(1)} %get-tuple-element.39), channel_id=1, source_target_pairs={{0,6},{1,7},{2,4},{3,5},{4,2},{5,3},{6,0},{7,1},{8,14},{9,15},{10,... | collective-permute-start | bytes 393224 | tf_op jit(solution)/shard_map/ppermute | solution.py:329
  49.4 5.0 %collective-permute-start.12 = (bf16[16,32,128]{2,1,0:T(8,128)(2,1)S(1)}, bf16[16,32,128]{2,1,0:T(8,128)(2,1)S(1)}, u32[]{:S(2)}, u32[]{:S(2)}) collective-permute-start(bf16[16,32,128]{2,1,0:T(8,128)(2,1)S(1)} %get-tuple-element.49), channel_id=1, source_target_pairs={{0,2},{1,3},{2,0},{3,1},{4,6},{5,7},{6,4},{7,5},{8,10},{9,11},{10,... | collective-permute-start | bytes 393224 | tf_op jit(solution)/shard_map/ppermute | solution.py:329
  54.3 5.0 %collective-permute-start.13 = (bf16[16,32,128]{2,1,0:T(8,128)(2,1)S(1)}, bf16[16,32,128]{2,1,0:T(8,128)(2,1)S(1)}, u32[]{:S(2)}, u32[]{:S(2)}) collective-permute-start(bf16[16,32,128]{2,1,0:T(8,128)(2,1)S(1)} %get-tuple-element.50), channel_id=1, source_target_pairs={{0,4},{1,5},{2,6},{3,7},{4,0},{5,1},{6,2},{7,3},{8,12},{9,13},{10,... | collective-permute-start | bytes 393224 | tf_op jit(solution)/shard_map/ppermute | solution.py:329
  59.3 5.9 %collective-permute-start.14 = (bf16[16,32,128]{2,1,0:T(8,128)(2,1)S(1)}, bf16[16,32,128]{2,1,0:T(8,128)(2,1)S(1)}, u32[]{:S(2)}, u32[]{:S(2)}) collective-permute-start(bf16[16,32,128]{2,1,0:T(8,128)(2,1)S(1)} %get-tuple-element.51), channel_id=1, source_target_pairs={{0,6},{1,7},{2,4},{3,5},{4,2},{5,3},{6,0},{7,1},{8,14},{9,15},{10,... | collective-permute-start | bytes 393224 | tf_op jit(solution)/shard_map/ppermute | solution.py:329
  65.2 26.8 %collective-permute-start.3 = (bf16[32,32,128]{2,1,0:T(8,128)(2,1)S(1)}, bf16[32,32,128]{2,1,0:T(8,128)(2,1)S(1)}, u32[]{:S(2)}, u32[]{:S(2)}) collective-permute-start(bf16[32,32,128]{2,1,0:T(8,128)(2,1)S(1)} %pad_maximum_fusion), channel_id=1, source_target_pairs={{0,1},{1,0},{2,3},{3,2},{4,5},{5,4},{6,7},{7,6},{8,9},{9,8},{10,11... | collective-permute-start | bytes 786440 | tf_op jit(solution)/shard_map/ppermute | solution.py:341
  66.3 55.7 %collective-permute-start.21 = (bf16[32,32,128]{2,1,0:T(8,128)(2,1)S(1)}, bf16[32,32,128]{2,1,0:T(8,128)(2,1)S(1)}, u32[]{:S(2)}, u32[]{:S(2)}) collective-permute-start(bf16[32,32,128]{2,1,0:T(8,128)(2,1)S(1)} %get-tuple-element.57), channel_id=1, source_target_pairs={{0,2},{1,3},{2,0},{3,1},{4,6},{5,7},{6,4},{7,5},{8,10},{9,11},{10,... | collective-permute-start | bytes 786440 | tf_op jit(solution)/shard_map/ppermute | solution.py:329
  67.5 54.6 %collective-permute-start.23 = (bf16[16,32,128]{2,1,0:T(8,128)(2,1)S(1)}, bf16[16,32,128]{2,1,0:T(8,128)(2,1)S(1)}, u32[]{:S(2)}, u32[]{:S(2)}) collective-permute-start(bf16[16,32,128]{2,1,0:T(8,128)(2,1)S(1)} %get-tuple-element.59), channel_id=1, source_target_pairs={{0,2},{1,3},{2,0},{3,1},{4,6},{5,7},{6,4},{7,5},{8,10},{9,11},{10,... | collective-permute-start | bytes 393224 | tf_op jit(solution)/shard_map/ppermute | solution.py:329
  69.6 52.6 %collective-permute-start.24 = (bf16[16,32,128]{2,1,0:T(8,128)(2,1)S(1)}, bf16[16,32,128]{2,1,0:T(8,128)(2,1)S(1)}, u32[]{:S(2)}, u32[]{:S(2)}) collective-permute-start(bf16[16,32,128]{2,1,0:T(8,128)(2,1)S(1)} %get-tuple-element.60), channel_id=1, source_target_pairs={{0,4},{1,5},{2,6},{3,7},{4,0},{5,1},{6,2},{7,3},{8,12},{9,13},{10,... | collective-permute-start | bytes 393224 | tf_op jit(solution)/shard_map/ppermute | solution.py:329
  70.8 9.9 %collective-permute-start.16 = (bf16[16,32,128]{2,1,0:T(8,128)(2,1)S(1)}, bf16[16,32,128]{2,1,0:T(8,128)(2,1)S(1)}, u32[]{:S(2)}, u32[]{:S(2)}) collective-permute-start(bf16[16,32,128]{2,1,0:T(8,128)(2,1)S(1)} %get-tuple-element.53), channel_id=1, source_target_pairs={{0,2},{1,3},{2,0},{3,1},{4,6},{5,7},{6,4},{7,5},{8,10},{9,11},{10,... | collective-permute-start | bytes 393224 | tf_op jit(solution)/shard_map/ppermute | solution.py:329
  80.7 5.1 %collective-permute-start.17 = (bf16[16,32,128]{2,1,0:T(8,128)(2,1)S(1)}, bf16[16,32,128]{2,1,0:T(8,128)(2,1)S(1)}, u32[]{:S(2)}, u32[]{:S(2)}) collective-permute-start(bf16[16,32,128]{2,1,0:T(8,128)(2,1)S(1)} %get-tuple-element.54), channel_id=1, source_target_pairs={{0,4},{1,5},{2,6},{3,7},{4,0},{5,1},{6,2},{7,3},{8,12},{9,13},{10,... | collective-permute-start | bytes 393224 | tf_op jit(solution)/shard_map/ppermute | solution.py:329
  85.8 5.9 %collective-permute-start.18 = (bf16[16,32,128]{2,1,0:T(8,128)(2,1)S(1)}, bf16[16,32,128]{2,1,0:T(8,128)(2,1)S(1)}, u32[]{:S(2)}, u32[]{:S(2)}) collective-permute-start(bf16[16,32,128]{2,1,0:T(8,128)(2,1)S(1)} %get-tuple-element.55), channel_id=1, source_target_pairs={{0,6},{1,7},{2,4},{3,5},{4,2},{5,3},{6,0},{7,1},{8,14},{9,15},{10,... | collective-permute-start | bytes 393224 | tf_op jit(solution)/shard_map/ppermute | solution.py:329
  91.6 30.5 %collective-permute-start.25 = (bf16[16,32,128]{2,1,0:T(8,128)(2,1)S(1)}, bf16[16,32,128]{2,1,0:T(8,128)(2,1)S(1)}, u32[]{:S(2)}, u32[]{:S(2)}) collective-permute-start(bf16[16,32,128]{2,1,0:T(8,128)(2,1)S(1)} %get-tuple-element.61), channel_id=1, source_target_pairs={{0,6},{1,7},{2,4},{3,5},{4,2},{5,3},{6,0},{7,1},{8,14},{9,15},{10,... | collective-permute-start | bytes 393224 | tf_op jit(solution)/shard_map/ppermute | solution.py:329
  92.0 5.7 %collective-permute-start.5 = (bf16[8,32,128]{2,1,0:T(8,128)(2,1)S(1)}, bf16[8,32,128]{2,1,0:T(8,128)(2,1)S(1)}, u32[]{:S(2)}, u32[]{:S(2)}) collective-permute-start(bf16[8,32,128]{2,1,0:T(8,128)(2,1)S(1)} %get-tuple-element.41), channel_id=1, source_target_pairs={{0,2},{1,3},{2,0},{3,1},{4,6},{5,7},{6,4},{7,5},{8,10},{9,11},{10,... | collective-permute-start | bytes 196616 | tf_op jit(solution)/shard_map/ppermute | solution.py:329
  97.7 4.6 %collective-permute-start.6 = (bf16[8,32,128]{2,1,0:T(8,128)(2,1)S(1)}, bf16[8,32,128]{2,1,0:T(8,128)(2,1)S(1)}, u32[]{:S(2)}, u32[]{:S(2)}) collective-permute-start(bf16[8,32,128]{2,1,0:T(8,128)(2,1)S(1)} %get-tuple-element.42), channel_id=1, source_target_pairs={{0,4},{1,5},{2,6},{3,7},{4,0},{5,1},{6,2},{7,3},{8,12},{9,13},{10,... | collective-permute-start | bytes 196616 | tf_op jit(solution)/shard_map/ppermute | solution.py:329
  102.3 5.2 %collective-permute-start.7 = (bf16[8,32,128]{2,1,0:T(8,128)(2,1)S(1)}, bf16[8,32,128]{2,1,0:T(8,128)(2,1)S(1)}, u32[]{:S(2)}, u32[]{:S(2)}) collective-permute-start(bf16[8,32,128]{2,1,0:T(8,128)(2,1)S(1)} %get-tuple-element.43), channel_id=1, source_target_pairs={{0,6},{1,7},{2,4},{3,5},{4,2},{5,3},{6,0},{7,1},{8,14},{9,15},{10,... | collective-permute-start | bytes 196616 | tf_op jit(solution)/shard_map/ppermute | solution.py:329
  108.8 4.1 %collective-permute-start.9 = (bf16[8,32,128]{2,1,0:T(8,128)(2,1)S(1)}, bf16[8,32,128]{2,1,0:T(8,128)(2,1)S(1)}, u32[]{:S(2)}, u32[]{:S(2)}) collective-permute-start(bf16[8,32,128]{2,1,0:T(8,128)(2,1)S(1)} %get-tuple-element.45), channel_id=1, source_target_pairs={{0,3},{1,2},{2,1},{3,0},{4,7},{5,6},{6,5},{7,4},{8,11},{9,10},{10,... | collective-permute-start | bytes 196616 | tf_op jit(solution)/shard_map/ppermute | solution.py:329
  116.9 5.0 %collective-permute-start.11 = (bf16[8,32,128]{2,1,0:T(8,128)(2,1)S(1)}, bf16[8,32,128]{2,1,0:T(8,128)(2,1)S(1)}, u32[]{:S(2)}, u32[]{:S(2)}) collective-permute-start(bf16[8,32,128]{2,1,0:T(8,128)(2,1)S(1)} %get-tuple-element.47), channel_id=1, source_target_pairs={{0,7},{1,6},{2,5},{3,4},{4,3},{5,2},{6,1},{7,0},{8,15},{9,14},{10,... | collective-permute-start | bytes 196616 | tf_op jit(solution)/shard_map/ppermute | solution.py:329
  (7 other events, 20.7 us)
